TPU v7x, 32 devices: a whole 2x2x4 slice. The times are simulated.
32 devices in a mesh: dp: 8 (over z, x), seq: 4 (over y, core).
Axes of the slice: x: 2, y: 2, z: 4, core: 2. Of those that a mesh axis runs over, the one named last changes fastest.
Arguments:
- tokens: bfloat16 [16, 2048, 1024], P('dp', 'seq'), may hold values from -6 to 6
- cotangent: bfloat16 [16, 2048, 1024], P('dp', 'seq'), may hold values from -6 to 6
- lengths: int32 [16], replicated, may hold values from 512 to 2048, as said below
- assignment: int32 [16], replicated, may hold values from 0 to 15, as said below
- mix_norm_gain: bfloat16 [1024], P('dp'), may hold values from 0.5 to 1.5
- mix_norm_bias: bfloat16 [1024], P('dp'), may hold values from -1.75 to 1.75
- shift_key: bfloat16 [1024], P('dp'), may hold values from 0 to 1
- shift_value: bfloat16 [1024], P('dp'), may hold values from 0 to 1
- shift_recept: bfloat16 [1024], P('dp'), may hold values from 0 to 1
- time_decay: bfloat16 [1024], P('dp'), may hold values from -9 to -3.390625
- time_first: bfloat16 [1024], P('dp'), may hold values from -1 to 1
- key_weight: bfloat16 [1024, 1024], P('dp'), may hold values from -1 to 1
- value_weight: bfloat16 [1024, 1024], P('dp'), may hold values from -1 to 1
- recept_weight: bfloat16 [1024, 1024], P('dp'), may hold values from -1 to 1
- output_weight: bfloat16 [1024, 1024], P('dp'), may hold values from -3 to 3
- feed_norm_gain: bfloat16 [1024], P('dp'), may hold values from 0.5 to 1.5
- feed_norm_bias: bfloat16 [1024], P('dp'), may hold values from -1.75 to 1.75
- feed_shift_key: bfloat16 [1024], P('dp'), may hold values from 0 to 1
- feed_shift_recept: bfloat16 [1024], P('dp'), may hold values from 0 to 1
- feed_key_weight: bfloat16 [1024, 4096], P('dp'), may hold values from -1 to 1
- feed_recept_weight: bfloat16 [1024, 1024], P('dp'), may hold values from -1 to 1
- feed_value_weight: bfloat16 [4096, 1024], P('dp'), may hold values from -0.09375 to 0.09375
Outputs:
- block_out: bfloat16 [16, 2048, 1024], P('dp', 'seq')
- input_grad: bfloat16 [16, 2048, 1024], P('dp', 'seq')
- grad_mix_norm_gain: float32 [1024], P('dp')
- grad_mix_norm_bias: float32 [1024], P('dp')
- grad_shift_key: float32 [1024], P('dp')
- grad_shift_value: float32 [1024], P('dp')
- grad_shift_recept: float32 [1024], P('dp')
- grad_time_decay: float32 [1024], P('dp')
- grad_time_first: float32 [1024], P('dp')
- grad_key_weight: float32 [1024, 1024], P('dp')
- grad_value_weight: float32 [1024, 1024], P('dp')
- grad_recept_weight: float32 [1024, 1024], P('dp')
- grad_output_weight: float32 [1024, 1024], P('dp')
- grad_feed_norm_gain: float32 [1024], P('dp')
- grad_feed_norm_bias: float32 [1024], P('dp')
- grad_feed_shift_key: float32 [1024], P('dp')
- grad_feed_shift_recept: float32 [1024], P('dp')
- grad_feed_key_weight: float32 [1024, 4096], P('dp')
- grad_feed_recept_weight: float32 [1024, 1024], P('dp')
- grad_feed_value_weight: float32 [4096, 1024], P('dp')
- residual_rms: float32 [], replicated
- mix_rms: float32 [], replicated
- feed_rms: float32 [], replicated
Inputs may be any that keep to these rules, and one draw needn't show every extreme that they name: lengths[i] is the valid length of sequence i; of the 2 slots of each index of dp one holds a sequence 2048 long. a permutation: slot s holds sequence assignment[s].
All inputs are finite; a program needn't handle non-finite values.
Results may differ from a plain program's by a relative error of at most 0.018.
Values may be sent and summed in bfloat16 or wider, within the bound.
No kernel may reach another device: no remote copies, remote signals or barrier semaphores. Data moves between devices by JAX's collectives and lax.ppermute only.
A program may use at most 256 MiB of HBM per device.

v0:
```python
from functools import partial

import jax
import jax.numpy as jnp
from jax import lax
from jax.sharding import PartitionSpec as P

D = 1024
BLOCK = 32


norm_eps = 1e-05


def from_behind(value, axis, by):
    devices = lax.axis_size(axis)
    pairs = [(i, i + by) for i in range(devices) if 0 <= i + by < devices]
    return lax.ppermute(value, axis, pairs)


def prefix(value, axis, join, neutral, backward):
    count, mine = (lax.axis_size(axis), lax.axis_index(axis))
    pieces = jax.tree.map(lambda part: lax.all_gather(part, axis), value)
    if backward:
        pieces = jax.tree.map(lambda part: part[::-1], pieces)
        mine = count - 1 - mine
    so_far = jax.tree.map(
        lambda part, zero: jnp.full_like(part, 0) + jnp.asarray(zero, part.dtype), value, neutral
    )

    def hop(position, so_far):
        longer = join(so_far, jax.tree.map(lambda part: part[position], pieces))
        return jax.tree.map(lambda new, old: jnp.where(position < mine, new, old), longer, so_far)

    return lax.fori_loop(0, count - 1, hop, so_far)


def norm_rows(values, gain_vec, bias_vec):
    centre = values - jnp.mean(values, axis=-1, keepdims=True)
    spread = jnp.mean(centre * centre, axis=-1, keepdims=True)
    return centre * lax.rsqrt(spread + norm_eps) * gain_vec + bias_vec


def decay_tables(fading_multiplier):
    offsets = jnp.arange(BLOCK).astype(jnp.float32)
    spacing = offsets[:, None] - offsets[None, :] - 1.0
    decay_table = jnp.where(
        (spacing >= 0.0)[:, :, None],
        jnp.exp(-jnp.maximum(spacing, 0.0)[:, :, None] * fading_multiplier),
        0.0,
    )
    falling = jnp.exp(-offsets[:, None] * fading_multiplier)
    trailing = jnp.exp(-(BLOCK - 1.0 - offsets)[:, None] * fading_multiplier)
    return (decay_table, falling, trailing, jnp.exp(-BLOCK * fading_multiplier))


def segment_forward_sweep(
    sharded_arrays_group, current_boost_array, running_recurrence, segment_entries
):
    decay_table, falling, trailing, whole_block = sharded_arrays_group
    num_state, den_state = running_recurrence
    lookup_segment_lines, content_segment_lines = segment_entries
    exponentiated_lookup = jnp.exp(lookup_segment_lines)
    weighted = exponentiated_lookup * content_segment_lines
    dividend_earlier = falling * num_state + jnp.sum(decay_table * weighted[None, :, :], axis=1)
    divisor_earlier = falling * den_state + jnp.sum(
        decay_table * exponentiated_lookup[None, :, :], axis=1
    )
    boosted_lookup_entry = jnp.exp(current_boost_array + lookup_segment_lines)
    attention_result = (dividend_earlier + boosted_lookup_entry * content_segment_lines) / (
        divisor_earlier + boosted_lookup_entry
    )
    num_after = whole_block * num_state + jnp.sum(trailing * weighted, axis=0)
    den_after = whole_block * den_state + jnp.sum(trailing * exponentiated_lookup, axis=0)
    return ((num_after, den_after), (attention_result, dividend_earlier, divisor_earlier))


def segment_backward_sweep(
    sharded_arrays_group, current_boost_array, derivative_for_running, segment_entries
):
    decay_table, falling, trailing, whole_block = sharded_arrays_group
    num_grad_end, den_grad_end = derivative_for_running
    (
        lookup_segment_lines,
        content_segment_lines,
        dividend_earlier,
        divisor_earlier,
        dividend_cotangent,
        denominator_adjoint,
    ) = segment_entries
    exponentiated_lookup = jnp.exp(lookup_segment_lines)
    boosted_lookup_entry = jnp.exp(current_boost_array + lookup_segment_lines)
    dividend_later = (
        jnp.sum(decay_table * dividend_cotangent[:, None, :], axis=0) + trailing * num_grad_end
    )
    den_next = (
        jnp.sum(decay_table * denominator_adjoint[:, None, :], axis=0) + trailing * den_grad_end
    )
    diagonal_contribution = boosted_lookup_entry * (
        content_segment_lines * dividend_cotangent + denominator_adjoint
    )
    lookup_derivative = (
        exponentiated_lookup * (content_segment_lines * dividend_later + den_next)
        + diagonal_contribution
    )
    content_derivative = (
        exponentiated_lookup * dividend_later + boosted_lookup_entry * dividend_cotangent
    )
    current_boost_derivative = jnp.sum(diagonal_contribution, axis=0)
    fading_derivative = jnp.sum(
        dividend_later * dividend_earlier + den_next * divisor_earlier, axis=0
    )
    running_recurrence_result = (
        jnp.sum(falling * dividend_cotangent, axis=0) + whole_block * num_grad_end,
        jnp.sum(falling * denominator_adjoint, axis=0) + whole_block * den_grad_end,
    )
    return (
        running_recurrence_result,
        (lookup_derivative, content_derivative, current_boost_derivative, fading_derivative),
    )


def chain_states(earlier_part, later_part):
    return (
        earlier_part[0] * later_part[0],
        later_part[0] * earlier_part[1] + later_part[1],
        later_part[0] * earlier_part[2] + later_part[2],
    )


def into_blocks(matrix_rows):
    return matrix_rows.reshape(matrix_rows.shape[0] // BLOCK, BLOCK, matrix_rows.shape[1])


def from_blocks(block_rows):
    return block_rows.reshape(block_rows.shape[0] * block_rows.shape[1], block_rows.shape[2])


def mul_plain(left_rows, right_rows):
    return jnp.dot(left_rows, right_rows, preferred_element_type=jnp.float32)


def mul_back(grad_rows, weight):
    return lax.dot_general(
        grad_rows, weight, (((1,), (1,)), ((), ())), preferred_element_type=jnp.float32
    )


def mul_weight(input_rows, grad_rows):
    return lax.dot_general(
        input_rows, grad_rows, (((0,), (0,)), ((), ())), preferred_element_type=jnp.float32
    )


def forward_pass(rows_in, valid_mask, learned_arrays_group):
    initial_layernorm_scale = learned_arrays_group[0].astype(jnp.float32)
    initial_layernorm_offset = learned_arrays_group[1].astype(jnp.float32)
    lagged_lookup_lines = learned_arrays_group[2].astype(jnp.float32)
    lagged_content_lines = learned_arrays_group[3].astype(jnp.float32)
    lagged_gating_lines = learned_arrays_group[4].astype(jnp.float32)
    fading_multiplier = jnp.exp(learned_arrays_group[5].astype(jnp.float32))
    current_boost_array = learned_arrays_group[6].astype(jnp.float32)
    latter_layernorm_scale = learned_arrays_group[11].astype(jnp.float32)
    latter_layernorm_offset = learned_arrays_group[12].astype(jnp.float32)
    channel_lagged_lookup = learned_arrays_group[13].astype(jnp.float32)
    channel_lagged_gating = learned_arrays_group[14].astype(jnp.float32)
    inputs = rows_in.astype(jnp.float32)
    span_len = inputs.shape[0]
    normed = norm_rows(inputs, initial_layernorm_scale, initial_layernorm_offset)
    earlier_row = from_behind(normed[-1:], "seq", 1)
    before = jnp.concatenate([earlier_row, normed[:-1]], axis=0)
    key_in = (normed * lagged_lookup_lines + before * (1.0 - lagged_lookup_lines)).astype(
        jnp.bfloat16
    )
    value_in = (normed * lagged_content_lines + before * (1.0 - lagged_content_lines)).astype(
        jnp.bfloat16
    )
    recept_in = (normed * lagged_gating_lines + before * (1.0 - lagged_gating_lines)).astype(
        jnp.bfloat16
    )
    lookup_line_pile = mul_plain(key_in, learned_arrays_group[7])
    content_line_pile = mul_plain(value_in, learned_arrays_group[8])
    recept_rows = mul_plain(recept_in, learned_arrays_group[9])
    sharded_arrays_group = decay_tables(fading_multiplier)
    offsets = jnp.arange(span_len).astype(jnp.float32)
    exponentiated_lookup = jnp.exp(lookup_line_pile)
    trailing_all = jnp.exp(-(span_len - 1.0 - offsets)[:, None] * fading_multiplier)
    carried = prefix(
        (
            jnp.exp(-span_len * fading_multiplier),
            jnp.sum(trailing_all * exponentiated_lookup * content_line_pile, axis=0),
            jnp.sum(trailing_all * exponentiated_lookup, axis=0),
        ),
        "seq",
        chain_states,
        (
            jnp.ones_like(fading_multiplier),
            jnp.zeros_like(fading_multiplier),
            jnp.zeros_like(fading_multiplier),
        ),
        False,
    )
    unused, block_outs = lax.scan(
        partial(segment_forward_sweep, sharded_arrays_group, current_boost_array),
        (carried[1], carried[2]),
        (into_blocks(lookup_line_pile), into_blocks(content_line_pile)),
    )
    attention_result = from_blocks(block_outs[0])
    dividend_earlier = from_blocks(block_outs[1])
    divisor_earlier = from_blocks(block_outs[2])
    recept_gate = jax.nn.sigmoid(recept_rows)
    weighted = (recept_gate * attention_result).astype(jnp.bfloat16)
    attn_out = mul_plain(weighted, learned_arrays_group[10])
    middle = inputs + attn_out
    normed_two = norm_rows(middle, latter_layernorm_scale, latter_layernorm_offset)
    earlier_two = from_behind(normed_two[-1:], "seq", 1)
    before_two = jnp.concatenate([earlier_two, normed_two[:-1]], axis=0)
    feed_key_in = (
        normed_two * channel_lagged_lookup + before_two * (1.0 - channel_lagged_lookup)
    ).astype(jnp.bfloat16)
    feed_recept_in = (
        normed_two * channel_lagged_gating + before_two * (1.0 - channel_lagged_gating)
    ).astype(jnp.bfloat16)
    hidden = mul_plain(feed_key_in, learned_arrays_group[15])
    squared = jnp.square(jax.nn.relu(hidden)).astype(jnp.bfloat16)
    feed_value = mul_plain(squared, learned_arrays_group[17])
    feed_gate = jax.nn.sigmoid(mul_plain(feed_recept_in, learned_arrays_group[16]))
    feed_out = feed_gate * feed_value
    keep_rows = valid_mask[:, None]
    summed_rows = middle + feed_out
    result = (keep_rows * summed_rows).astype(jnp.bfloat16)
    square_sums = jnp.stack(
        [
            jnp.sum(keep_rows * summed_rows * summed_rows),
            jnp.sum(keep_rows * attn_out * attn_out),
            jnp.sum(keep_rows * feed_out * feed_out),
        ]
    )
    kept_state = (
        inputs,
        normed,
        before,
        key_in,
        value_in,
        recept_in,
        lookup_line_pile,
        content_line_pile,
        attention_result,
        dividend_earlier,
        divisor_earlier,
        recept_gate,
        weighted,
        middle,
        normed_two,
        before_two,
        feed_key_in,
        feed_recept_in,
        hidden,
        squared,
        feed_value,
        feed_gate,
    )
    return (result, square_sums, kept_state)


def backward_pass(rows_cot, valid_mask, learned_arrays_group, kept_state):
    (
        inputs,
        normed,
        before,
        key_in,
        value_in,
        recept_in,
        lookup_line_pile,
        content_line_pile,
        attention_result,
        dividend_earlier,
        divisor_earlier,
        recept_gate,
        weighted,
        middle,
        normed_two,
        before_two,
        feed_key_in,
        feed_recept_in,
        hidden,
        squared,
        feed_value,
        feed_gate,
    ) = kept_state
    initial_layernorm_scale = learned_arrays_group[0].astype(jnp.float32)
    initial_layernorm_offset = learned_arrays_group[1].astype(jnp.float32)
    lagged_lookup_lines = learned_arrays_group[2].astype(jnp.float32)
    lagged_content_lines = learned_arrays_group[3].astype(jnp.float32)
    lagged_gating_lines = learned_arrays_group[4].astype(jnp.float32)
    fading_multiplier = jnp.exp(learned_arrays_group[5].astype(jnp.float32))
    current_boost_array = learned_arrays_group[6].astype(jnp.float32)
    latter_layernorm_scale = learned_arrays_group[11].astype(jnp.float32)
    latter_layernorm_offset = learned_arrays_group[12].astype(jnp.float32)
    channel_lagged_lookup = learned_arrays_group[13].astype(jnp.float32)
    channel_lagged_gating = learned_arrays_group[14].astype(jnp.float32)
    span_len = inputs.shape[0]
    out_grad = rows_cot.astype(jnp.float32) * valid_mask[:, None]
    feed_value_grad = (out_grad * feed_gate).astype(jnp.bfloat16)
    gate_grad = (out_grad * feed_value * feed_gate * (1.0 - feed_gate)).astype(jnp.bfloat16)
    squared_grad = mul_back(feed_value_grad, learned_arrays_group[17])
    grad_feed_value_w = mul_weight(squared, feed_value_grad)
    hidden_grad = (squared_grad * 2.0 * jax.nn.relu(hidden)).astype(jnp.bfloat16)
    feed_key_in_grad = mul_back(hidden_grad, learned_arrays_group[15])
    grad_feed_key_w = mul_weight(feed_key_in, hidden_grad)
    feed_recept_in_grad = mul_back(gate_grad, learned_arrays_group[16])
    grad_feed_recept_w = mul_weight(feed_recept_in, gate_grad)
    gap_two = normed_two - before_two
    grad_feed_shift_keys = jnp.sum(gap_two * feed_key_in_grad, axis=0)
    grad_feed_shift_recepts = jnp.sum(gap_two * feed_recept_in_grad, axis=0)
    normed_two_grad = (
        feed_key_in_grad * channel_lagged_lookup + feed_recept_in_grad * channel_lagged_gating
    )
    before_two_grad = feed_key_in_grad * (1.0 - channel_lagged_lookup) + feed_recept_in_grad * (
        1.0 - channel_lagged_gating
    )
    later_two = from_behind(before_two_grad[:1], "seq", -1)
    normed_two_grad = normed_two_grad + jnp.concatenate([before_two_grad[1:], later_two], axis=0)
    middle_part, grad_gain_two, grad_bias_two = jax.vjp(
        norm_rows, middle, latter_layernorm_scale, latter_layernorm_offset
    )[1](normed_two_grad)
    middle_grad = out_grad + middle_part
    attn_grad = middle_grad.astype(jnp.bfloat16)
    weighted_grad = mul_back(attn_grad, learned_arrays_group[10])
    grad_output_w = mul_weight(weighted, attn_grad)
    mix_grad = weighted_grad * recept_gate
    recept_grad = (weighted_grad * attention_result * recept_gate * (1.0 - recept_gate)).astype(
        jnp.bfloat16
    )
    boosted_lookup_entry = jnp.exp(current_boost_array + lookup_line_pile)
    divisor_combined = divisor_earlier + boosted_lookup_entry
    dividend_cotangent = mix_grad / divisor_combined
    denominator_adjoint = -dividend_cotangent * attention_result
    offsets = jnp.arange(span_len).astype(jnp.float32)
    falling_all = jnp.exp(-offsets[:, None] * fading_multiplier)
    later_state = prefix(
        (
            jnp.exp(-span_len * fading_multiplier),
            jnp.sum(falling_all * dividend_cotangent, axis=0),
            jnp.sum(falling_all * denominator_adjoint, axis=0),
        ),
        "seq",
        chain_states,
        (
            jnp.ones_like(fading_multiplier),
            jnp.zeros_like(fading_multiplier),
            jnp.zeros_like(fading_multiplier),
        ),
        True,
    )
    sharded_arrays_group = decay_tables(fading_multiplier)
    unused, segment_derivative_array = lax.scan(
        partial(segment_backward_sweep, sharded_arrays_group, current_boost_array),
        (later_state[1], later_state[2]),
        (
            into_blocks(lookup_line_pile),
            into_blocks(content_line_pile),
            into_blocks(dividend_earlier),
            into_blocks(divisor_earlier),
            into_blocks(dividend_cotangent),
            into_blocks(denominator_adjoint),
        ),
        reverse=True,
    )
    lookup_derivative = from_blocks(segment_derivative_array[0]).astype(jnp.bfloat16)
    content_derivative = from_blocks(segment_derivative_array[1]).astype(jnp.bfloat16)
    derivative_for_boost = jnp.sum(segment_derivative_array[2], axis=0)
    grad_decay = (
        -jnp.exp(-fading_multiplier)
        * fading_multiplier
        * jnp.sum(segment_derivative_array[3], axis=0)
    )
    key_in_grad = mul_back(lookup_derivative, learned_arrays_group[7])
    grad_key_w = mul_weight(key_in, lookup_derivative)
    value_in_grad = mul_back(content_derivative, learned_arrays_group[8])
    grad_value_w = mul_weight(value_in, content_derivative)
    recept_in_grad = mul_back(recept_grad, learned_arrays_group[9])
    grad_recept_w = mul_weight(recept_in, recept_grad)
    gap_one = normed - before
    grad_shift_keys = jnp.sum(gap_one * key_in_grad, axis=0)
    grad_shift_values = jnp.sum(gap_one * value_in_grad, axis=0)
    grad_shift_recepts = jnp.sum(gap_one * recept_in_grad, axis=0)
    normed_grad = (
        key_in_grad * lagged_lookup_lines
        + value_in_grad * lagged_content_lines
        + recept_in_grad * lagged_gating_lines
    )
    before_grad = (
        key_in_grad * (1.0 - lagged_lookup_lines)
        + value_in_grad * (1.0 - lagged_content_lines)
        + recept_in_grad * (1.0 - lagged_gating_lines)
    )
    later_one = from_behind(before_grad[:1], "seq", -1)
    normed_grad = normed_grad + jnp.concatenate([before_grad[1:], later_one], axis=0)
    input_part, grad_gain_one, grad_bias_one = jax.vjp(
        norm_rows, inputs, initial_layernorm_scale, initial_layernorm_offset
    )[1](normed_grad)
    in_grad = (middle_grad + input_part).astype(jnp.bfloat16)
    grad_list = (
        grad_gain_one,
        grad_bias_one,
        grad_shift_keys,
        grad_shift_values,
        grad_shift_recepts,
        grad_decay,
        derivative_for_boost,
        grad_key_w,
        grad_value_w,
        grad_recept_w,
        grad_output_w,
        grad_gain_two,
        grad_bias_two,
        grad_feed_shift_keys,
        grad_feed_shift_recepts,
        grad_feed_key_w,
        grad_feed_recept_w,
        grad_feed_value_w,
    )
    return (in_grad, grad_list)


def owner_sums(grad_list):
    owned_part = (
        lax.psum_scatter(
            grad_list[0].astype(jnp.bfloat16), "dp", scatter_dimension=0, tiled=True
        ).astype(jnp.float32),
        lax.psum_scatter(
            grad_list[1].astype(jnp.bfloat16), "dp", scatter_dimension=0, tiled=True
        ).astype(jnp.float32),
        lax.psum_scatter(
            grad_list[2].astype(jnp.bfloat16), "dp", scatter_dimension=0, tiled=True
        ).astype(jnp.float32),
        lax.psum_scatter(
            grad_list[3].astype(jnp.bfloat16), "dp", scatter_dimension=0, tiled=True
        ).astype(jnp.float32),
        lax.psum_scatter(
            grad_list[4].astype(jnp.bfloat16), "dp", scatter_dimension=0, tiled=True
        ).astype(jnp.float32),
        lax.psum_scatter(
            grad_list[5].astype(jnp.bfloat16), "dp", scatter_dimension=0, tiled=True
        ).astype(jnp.float32),
        lax.psum_scatter(
            grad_list[6].astype(jnp.bfloat16), "dp", scatter_dimension=0, tiled=True
        ).astype(jnp.float32),
        lax.psum_scatter(
            grad_list[7].astype(jnp.bfloat16), "dp", scatter_dimension=0, tiled=True
        ).astype(jnp.float32),
        lax.psum_scatter(
            grad_list[8].astype(jnp.bfloat16), "dp", scatter_dimension=0, tiled=True
        ).astype(jnp.float32),
        lax.psum_scatter(
            grad_list[9].astype(jnp.bfloat16), "dp", scatter_dimension=0, tiled=True
        ).astype(jnp.float32),
        lax.psum_scatter(
            grad_list[10].astype(jnp.bfloat16), "dp", scatter_dimension=0, tiled=True
        ).astype(jnp.float32),
        lax.psum_scatter(
            grad_list[11].astype(jnp.bfloat16), "dp", scatter_dimension=0, tiled=True
        ).astype(jnp.float32),
        lax.psum_scatter(
            grad_list[12].astype(jnp.bfloat16), "dp", scatter_dimension=0, tiled=True
        ).astype(jnp.float32),
        lax.psum_scatter(
            grad_list[13].astype(jnp.bfloat16), "dp", scatter_dimension=0, tiled=True
        ).astype(jnp.float32),
        lax.psum_scatter(
            grad_list[14].astype(jnp.bfloat16), "dp", scatter_dimension=0, tiled=True
        ).astype(jnp.float32),
        lax.psum_scatter(
            grad_list[15].astype(jnp.bfloat16), "dp", scatter_dimension=0, tiled=True
        ).astype(jnp.float32),
        lax.psum_scatter(
            grad_list[16].astype(jnp.bfloat16), "dp", scatter_dimension=0, tiled=True
        ).astype(jnp.float32),
        lax.psum_scatter(
            grad_list[17].astype(jnp.bfloat16), "dp", scatter_dimension=0, tiled=True
        ).astype(jnp.float32),
    )
    return (
        lax.psum(owned_part[0].astype(jnp.bfloat16), "seq").astype(jnp.float32),
        lax.psum(owned_part[1].astype(jnp.bfloat16), "seq").astype(jnp.float32),
        lax.psum(owned_part[2].astype(jnp.bfloat16), "seq").astype(jnp.float32),
        lax.psum(owned_part[3].astype(jnp.bfloat16), "seq").astype(jnp.float32),
        lax.psum(owned_part[4].astype(jnp.bfloat16), "seq").astype(jnp.float32),
        lax.psum(owned_part[5].astype(jnp.bfloat16), "seq").astype(jnp.float32),
        lax.psum(owned_part[6].astype(jnp.bfloat16), "seq").astype(jnp.float32),
        lax.psum(owned_part[7].astype(jnp.bfloat16), "seq").astype(jnp.float32),
        lax.psum(owned_part[8].astype(jnp.bfloat16), "seq").astype(jnp.float32),
        lax.psum(owned_part[9].astype(jnp.bfloat16), "seq").astype(jnp.float32),
        lax.psum(owned_part[10].astype(jnp.bfloat16), "seq").astype(jnp.float32),
        lax.psum(owned_part[11].astype(jnp.bfloat16), "seq").astype(jnp.float32),
        lax.psum(owned_part[12].astype(jnp.bfloat16), "seq").astype(jnp.float32),
        lax.psum(owned_part[13].astype(jnp.bfloat16), "seq").astype(jnp.float32),
        lax.psum(owned_part[14].astype(jnp.bfloat16), "seq").astype(jnp.float32),
        lax.psum(owned_part[15].astype(jnp.bfloat16), "seq").astype(jnp.float32),
        lax.psum(owned_part[16].astype(jnp.bfloat16), "seq").astype(jnp.float32),
        lax.psum(owned_part[17].astype(jnp.bfloat16), "seq").astype(jnp.float32),
    )


def add_tuples(first_set, second_set):
    return tuple(
        (first_item + second_item for first_item, second_item in zip(first_set, second_set))
    )


def per_device(
    tokens,
    cotangent,
    lengths,
    assignment,
    mix_norm_gain,
    mix_norm_bias,
    shift_key,
    shift_value,
    shift_recept,
    time_decay,
    time_first,
    key_weight,
    value_weight,
    recept_weight,
    output_weight,
    feed_norm_gain,
    feed_norm_bias,
    feed_shift_key,
    feed_shift_recept,
    feed_key_weight,
    feed_recept_weight,
    feed_value_weight,
):
    micro_count = tokens.shape[0]
    span_len = tokens.shape[1]
    slot_count = assignment.shape[0]
    slot_base = lax.axis_index("dp") * micro_count
    positions = lax.axis_index("seq") * span_len + jnp.arange(span_len)
    slot_ids = jnp.arange(slot_count)
    square_sums = jnp.zeros((3,), jnp.float32)
    totals = None
    outputs = []
    input_grads = []
    for micro_index in range(micro_count):
        gathered = (
            lax.all_gather(mix_norm_gain, "dp", axis=0, tiled=True),
            lax.all_gather(mix_norm_bias, "dp", axis=0, tiled=True),
            lax.all_gather(shift_key, "dp", axis=0, tiled=True),
            lax.all_gather(shift_value, "dp", axis=0, tiled=True),
            lax.all_gather(shift_recept, "dp", axis=0, tiled=True),
            lax.all_gather(time_decay, "dp", axis=0, tiled=True),
            lax.all_gather(time_first, "dp", axis=0, tiled=True),
            lax.all_gather(key_weight, "dp", axis=0, tiled=True),
            lax.all_gather(value_weight, "dp", axis=0, tiled=True),
            lax.all_gather(recept_weight, "dp", axis=0, tiled=True),
            lax.all_gather(output_weight, "dp", axis=0, tiled=True),
            lax.all_gather(feed_norm_gain, "dp", axis=0, tiled=True),
            lax.all_gather(feed_norm_bias, "dp", axis=0, tiled=True),
            lax.all_gather(feed_shift_key, "dp", axis=0, tiled=True),
            lax.all_gather(feed_shift_recept, "dp", axis=0, tiled=True),
            lax.all_gather(feed_key_weight, "dp", axis=0, tiled=True),
            lax.all_gather(feed_recept_weight, "dp", axis=0, tiled=True),
            lax.all_gather(feed_value_weight, "dp", axis=0, tiled=True),
        )
        sequence_id = jnp.sum(jnp.where(slot_ids == slot_base + micro_index, assignment, 0))
        sequence_len = jnp.sum(jnp.where(slot_ids == sequence_id, lengths, 0))
        valid_mask = (positions < sequence_len).astype(jnp.float32)
        result, stats_now, kept_state = forward_pass(tokens[micro_index], valid_mask, gathered)
        square_sums = square_sums + stats_now
        outputs.append(result)
        weights_back = (
            lax.all_gather(mix_norm_gain, "dp", axis=0, tiled=True),
            lax.all_gather(mix_norm_bias, "dp", axis=0, tiled=True),
            lax.all_gather(shift_key, "dp", axis=0, tiled=True),
            lax.all_gather(shift_value, "dp", axis=0, tiled=True),
            lax.all_gather(shift_recept, "dp", axis=0, tiled=True),
            lax.all_gather(time_decay, "dp", axis=0, tiled=True),
            lax.all_gather(time_first, "dp", axis=0, tiled=True),
            lax.all_gather(key_weight, "dp", axis=0, tiled=True),
            lax.all_gather(value_weight, "dp", axis=0, tiled=True),
            lax.all_gather(recept_weight, "dp", axis=0, tiled=True),
            lax.all_gather(output_weight, "dp", axis=0, tiled=True),
            lax.all_gather(feed_norm_gain, "dp", axis=0, tiled=True),
            lax.all_gather(feed_norm_bias, "dp", axis=0, tiled=True),
            lax.all_gather(feed_shift_key, "dp", axis=0, tiled=True),
            lax.all_gather(feed_shift_recept, "dp", axis=0, tiled=True),
            lax.all_gather(feed_key_weight, "dp", axis=0, tiled=True),
            lax.all_gather(feed_recept_weight, "dp", axis=0, tiled=True),
            lax.all_gather(feed_value_weight, "dp", axis=0, tiled=True),
        )
        in_grad, local_grads = backward_pass(
            cotangent[micro_index], valid_mask, weights_back, kept_state
        )
        input_grads.append(in_grad)
        totals = local_grads if totals is None else add_tuples(totals, local_grads)
    totals = owner_sums(totals)
    summed = lax.psum(square_sums, ("dp", "seq"))
    valid_count = jnp.sum(lengths).astype(jnp.float32) * D
    rms_values = jnp.sqrt(summed / valid_count)
    return (
        jnp.stack(outputs),
        jnp.stack(input_grads),
        totals[0],
        totals[1],
        totals[2],
        totals[3],
        totals[4],
        totals[5],
        totals[6],
        totals[7],
        totals[8],
        totals[9],
        totals[10],
        totals[11],
        totals[12],
        totals[13],
        totals[14],
        totals[15],
        totals[16],
        totals[17],
        rms_values[0],
        rms_values[1],
        rms_values[2],
    )


def solution(mesh):
    in_specs = (
        P("dp", "seq", None),
        P("dp", "seq", None),
        P(),
        P(),
        P("dp"),
        P("dp"),
        P("dp"),
        P("dp"),
        P("dp"),
        P("dp"),
        P("dp"),
        P("dp", None),
        P("dp", None),
        P("dp", None),
        P("dp", None),
        P("dp"),
        P("dp"),
        P("dp"),
        P("dp"),
        P("dp", None),
        P("dp", None),
        P("dp", None),
    )
    out_specs = (
        P("dp", "seq", None),
        P("dp", "seq", None),
        P("dp"),
        P("dp"),
        P("dp"),
        P("dp"),
        P("dp"),
        P("dp"),
        P("dp"),
        P("dp", None),
        P("dp", None),
        P("dp", None),
        P("dp", None),
        P("dp"),
        P("dp"),
        P("dp"),
        P("dp"),
        P("dp", None),
        P("dp", None),
        P("dp", None),
        P(),
        P(),
        P(),
    )
    return jax.shard_map(
        per_device, mesh=mesh, in_specs=in_specs, out_specs=out_specs, check_vma=False
    )
```

profile of v0, /device:TPU:0, one launch (start us, length us, event | category | flops | bytes accessed | tf_op | source)
XLA Modules:
  0.0 1431.4 jit_solution(9328425729441138005)
XLA Ops:
  11.2 22.2 %all-gather.9 = bf16[8,1,128]{2,1,0:T(2,128)(2,1)S(1)} all-gather(bf16[1,1,128]{2,1,0:T(2,128)(2,1)S(1)} %bitcast.675), channel_id=1, replica_groups=mesh['dp'=8,'seq'=4] {'dp'}, dimensions={0}, use_global_device_ids=true | all-gather | bytes 2304 | tf_op jit(solution)/shard_map/all_gather | solution.py:548
  33.5 16.3 %all-gather.10 = bf16[8,1,128]{2,1,0:T(2,128)(2,1)S(1)} all-gather(bf16[1,1,128]{2,1,0:T(2,128)(2,1)S(1)} %bitcast.676), channel_id=1, replica_groups=mesh['dp'=8,'seq'=4] {'dp'}, dimensions={0}, use_global_device_ids=true | all-gather | bytes 2304 | tf_op jit(solution)/shard_map/all_gather | solution.py:549
  53.7 3.5 collective-permute-start
  57.3 4.3 slice_bitcast_fusion
  64.5 18.2 %all-gather.13 = bf16[8,1,128]{2,1,0:T(2,128)(2,1)S(1)} all-gather(bf16[1,1,128]{2,1,0:T(2,128)(2,1)S(1)} %bitcast.677), channel_id=1, replica_groups=mesh['dp'=8,'seq'=4] {'dp'}, dimensions={0}, use_global_device_ids=true | all-gather | bytes 2304 | tf_op jit(solution)/shard_map/all_gather | solution.py:550
  82.7 16.3 %all-gather.14 = bf16[8,1,128]{2,1,0:T(2,128)(2,1)S(1)} all-gather(bf16[1,1,128]{2,1,0:T(2,128)(2,1)S(1)} %bitcast.678), channel_id=1, replica_groups=mesh['dp'=8,'seq'=4] {'dp'}, dimensions={0}, use_global_device_ids=true | all-gather | bytes 2304 | tf_op jit(solution)/shard_map/all_gather | solution.py:551
  99.0 18.2 %all-gather.12 = bf16[8,1,128]{2,1,0:T(2,128)(2,1)S(1)} all-gather(bf16[1,1,128]{2,1,0:T(2,128)(2,1)S(1)} %bitcast.679), channel_id=1, replica_groups=mesh['dp'=8,'seq'=4] {'dp'}, dimensions={0}, use_global_device_ids=true | all-gather | bytes 2304 | tf_op jit(solution)/shard_map/all_gather | solution.py:553
  117.3 16.3 %all-gather.11 = bf16[8,1,128]{2,1,0:T(2,128)(2,1)S(1)} all-gather(bf16[1,1,128]{2,1,0:T(2,128)(2,1)S(1)} %bitcast.680), channel_id=1, replica_groups=mesh['dp'=8,'seq'=4] {'dp'}, dimensions={0}, use_global_device_ids=true | all-gather | bytes 2304 | tf_op jit(solution)/shard_map/all_gather | solution.py:552
  133.7 18.2 %all-gather.19 = bf16[8,1,128]{2,1,0:T(2,128)(2,1)S(1)} all-gather(bf16[1,1,128]{2,1,0:T(2,128)(2,1)S(1)} %bitcast.681), channel_id=1, replica_groups=mesh['dp'=8,'seq'=4] {'dp'}, dimensions={0}, use_global_device_ids=true | all-gather | bytes 2304 | tf_op jit(solution)/shard_map/all_gather | solution.py:561
  151.9 16.3 %all-gather.18 = bf16[8,1,128]{2,1,0:T(2,128)(2,1)S(1)} all-gather(bf16[1,1,128]{2,1,0:T(2,128)(2,1)S(1)} %bitcast.682), channel_id=1, replica_groups=mesh['dp'=8,'seq'=4] {'dp'}, dimensions={0}, use_global_device_ids=true | all-gather | bytes 2304 | tf_op jit(solution)/shard_map/all_gather | solution.py:562
  172.1 5.2 all-gather
  177.3 18.2 %all-gather.15 = bf16[8,1,128]{2,1,0:T(2,128)(2,1)S(1)} all-gather(bf16[1,1,128]{2,1,0:T(2,128)(2,1)S(1)} %bitcast.683), channel_id=1, replica_groups=mesh['dp'=8,'seq'=4] {'dp'}, dimensions={0}, use_global_device_ids=true | all-gather | bytes 2304 | tf_op jit(solution)/shard_map/all_gather | solution.py:554
  195.5 16.4 %all-gather.16 = bf16[8,1,128]{2,1,0:T(2,128)(2,1)S(1)} all-gather(bf16[1,1,128]{2,1,0:T(2,128)(2,1)S(1)} %bitcast.684), channel_id=1, replica_groups=mesh['dp'=8,'seq'=4] {'dp'}, dimensions={0}, use_global_device_ids=true | all-gather | bytes 2304 | tf_op jit(solution)/shard_map/all_gather | solution.py:559
  211.9 18.1 %all-gather.17 = bf16[8,1,128]{2,1,0:T(2,128)(2,1)S(1)} all-gather(bf16[1,1,128]{2,1,0:T(2,128)(2,1)S(1)} %bitcast.685), channel_id=1, replica_groups=mesh['dp'=8,'seq'=4] {'dp'}, dimensions={0}, use_global_device_ids=true | all-gather | bytes 2304 | tf_op jit(solution)/shard_map/all_gather | solution.py:560
  230.1 5.1 fusion.173
  235.1 3.9 fusion.174
  242.0 4.0 fusion.162
  246.0 5.2 all-gather.1
  251.2 5.4 all-gather.2
  261.7 108.3 %while.160 = (s32[]{:T(128)}, f32[1024]{0:T(1024)S(1)}, f32[1024]{0:T(1024)S(1)}, f32[16,32,1024]{2,1,0:T(8,128)}, f32[16,32,1024]{2,1,0:T(8,128)}, /*index=5*/f...) while((s32[]{:T(128)}, f32[1024]{0:T(1024)S(1)}, ...), condition=%wide.region_13.14_spmd.clone.clone, body=%wide.region_8.13_spmd.clone.clone.sunk | while | flops 6785026 | bytes 2295709 | solution.py:203
  369.9 5.2 all-gather.3
  375.1 5.2 all-gather.4
  385.3 108.4 %while.161 = (s32[]{:T(128)}, f32[1024]{0:T(1024)S(1)}, f32[1024]{0:T(1024)S(1)}, f32[16,32,1024]{2,1,0:T(8,128)}, f32[16,32,1024]{2,1,0:T(8,128)}, /*index=5*/f...) while((s32[]{:T(128)}, f32[1024]{0:T(1024)S(1)}, ...), condition=%wide.region_29.30_spmd.clone.clone, body=%wide.region_24.29_spmd.clone.clone.sunk | while | flops 6785026 | bytes 2295709 | solution.py:203
  493.9 6.3 fusion.154
  504.1 3.5 fusion.158
  521.0 5.9 add_convert_fusion.9
  526.9 4.8 add_divide_fusion
  531.7 11.6 fusion.267
  543.3 6.7 fusion.269
  550.0 9.5 fusion.169
  559.5 7.7 fusion.170
  567.3 4.2 fusion.148
  571.5 12.7 multiply_convert_fusion.1
  584.2 8.4 fusion.270
  597.4 10.9 multiply_convert_fusion
  608.3 8.8 fusion.275
  628.6 8.1 fusion.115
  638.7 4.4 fusion.114
  653.2 7.9 multiply_reduce_fusion.15
  661.1 6.9 all-gather.5
  668.3 5.2 all-gather.6
  680.3 92.5 %while.162 = (s32[]{:T(128)}, f32[1024]{0:T(1024)S(1)}, f32[1024]{0:T(1024)S(1)}, bf16[16,32,1024]{2,1,0:T(8,128)(2,1)S(1)}, bf16[16,32,1024]{2,1,0:T(8,128)(2,1...) while((s32[]{:T(128)}, f32[1024]{0:T(1024)S(1)}, ...), condition=%wide.region_45.46_spmd.clone.clone, body=%wide.region_38.45_spmd.clone.clone.sunk | while | flops 7372803 | bytes 3250157 | solution.py:357
  772.8 5.2 all-gather.7
  778.2 5.2 all-gather.8
  783.7 3.6 fusion.255
  790.8 103.3 %while.163 = (s32[]{:T(128)}, f32[1024]{0:T(1024)S(1)}, f32[1024]{0:T(1024)S(1)}, bf16[16,32,1024]{2,1,0:T(8,128)(2,1)}, bf16[16,32,1024]{2,1,0:T(8,128)(2,1)}, ...) while((s32[]{:T(128)}, f32[1024]{0:T(1024)S(1)}, ...), condition=%wide.region_61.62_spmd.clone.clone, body=%wide.region_54.61_spmd.clone.clone.sunk | while | flops 7372803 | bytes 3249773 | solution.py:357
  894.2 3.6 fusion.180
  901.4 3.4 fusion.183
  907.8 14.0 fusion.168
  921.9 16.5 %add_convert_fusion = bf16[4096,1024]{1,0:T(8,128)(2,1)} fusion(f32[4096,1024]{1,0:T(8,128)} %fusion.168, bf16[512,1024]{1,0:T(8,128)(2,1)} %get-tuple-element.2228, f32[512,4096]{1,0:T(8,128)} %fusion.269), kind=kOutput, calls=%fused_computation.156 | convolution fusion | flops 4309647360 | bytes 34603008 | tf_op jit(solution)/shard_map/dot_general | solution.py:150
  938.9 12.9 fusion.279
  951.8 11.4 add_convert_fusion.1
  965.2 4.0 maximum_add_fusion.4
  969.2 38.1 %psum.151 = f32[3]{0:T(128)S(1)} all-reduce(f32[3]{0:T(128)S(1)} %maximum_add_fusion.4), channel_id=1, replica_groups=mesh['dp'=8,'seq'=4] {'dp','seq'}, use_global_device_ids=true, to_apply=%region_128.129 | all-reduce | flops 3 | bytes 24 | tf_op jit(solution)/shard_map/psum | solution.py:599
  1007.2 3.4 fusion.276
  1019.6 3.5 multiply_add_fusion.8
  1033.4 3.8 multiply_reduce_fusion.6
  1037.3 3.7 multiply_reduce_fusion.7
  1043.6 144.8 %reduce-scatter.20.cloned.1.call-done = bf16[512,1024]{1,0:T(8,128)(2,1)} async-done(((bf16[4096,1024]{1,0:T(8,128)(2,1)}), bf16[512,1024]{1,0:T(8,128)(2,1)}) %reduce-scatter.20.cloned.1.call-update) | async-done | bytes 1048592 | tf_op jit(solution)/shard_map/reduce_scatter | solution.py:480
  1188.4 151.9 %reduce-scatter.16.cloned.1.call-done = bf16[128,4096]{1,0:T(8,128)(2,1)} async-done(((bf16[1024,4096]{1,0:T(8,128)(2,1)}), bf16[128,4096]{1,0:T(8,128)(2,1)}) %reduce-scatter.16.cloned.1.call-update) | async-done | bytes 1048592 | tf_op jit(solution)/shard_map/reduce_scatter | solution.py:474
  1340.4 35.2 %all-reduce.11 = (bf16[1024]{0:T(1024)(128)(2,1)S(1)}, bf16[1024]{0:T(1024)(128)(2,1)S(1)}, bf16[1024]{0:T(1024)(128)(2,1)S(1)}, bf16[1024]{0:T(1024)(128)(2,1)S...) all-reduce(bf16[1024]{0:T(1024)(128)(2,1)S(1)} %add_convert_fusion., ...), channel_id=11, replica_groups=mesh['dp'=8,'seq'=4] {'dp'}, use_global_device_ids=true, to_apply=%region_66.67.clone | all-reduce | flops 11264 | bytes 45056
  1376.4 5.7 all-reduce.12
  1387.8 3.3 fusion.175
  1395.0 21.0 %all-reduce.16.cloned.1.call-done = (bf16[128,1024]{1,0:T(8,128)(2,1)}, bf16[128,1024]{1,0:T(8,128)(2,1)}, bf16[128,1024]{1,0:T(8,128)(2,1)}, bf16[128,1024]{1,0...) async-done(((bf16[128,1024]{1,0:T(8,128)(2,1)}, bf16[128,1024]{1,0:T(8,128)(2,1)}, bf16[128,1024]{1,0:T(8,128)(2,1)}, ...) | async-done | bytes 3407888 | tf_op jit(solution)/shard_map/psum | solution.py:492
  (967 shorter events, 542.5 us)
Async XLA Ops:
  7.2 26.3 %copy-start.139 = (bf16[128]{0:T(256)(128)(2,1)S(1)}, bf16[128]{0:T(256)(128)(2,1)}, u32[]{:S(2)}) copy-start(bf16[128]{0:T(256)(128)(2,1)} %param.43) | copy-start | bytes 772
  7.2 42.6 %copy-start = (bf16[2,512,1024]{2,1,0:T(8,128)(2,1)S(1)}, bf16[2,512,1024]{2,1,0:T(8,128)(2,1)}, u32[]{:S(2)}) copy-start(bf16[2,512,1024]{2,1,0:T(8,128)(2,1)} %param.38) | copy-start | bytes 6291460
  7.2 222.8 %all-gather.30.cloned.1.call-start = ((), (), s32[]{:S(2)}) async-start(), calls=%async_computation.8 | async-start | bytes 2359296 | tf_op jit(solution)/shard_map/all_gather | solution.py:555
  8.0 227.2 %all-gather.32.cloned.1.call-start = ((), (), s32[]{:S(2)}) async-start(), calls=%async_computation.9 | async-start | bytes 2359296 | tf_op jit(solution)/shard_map/all_gather | solution.py:556
  8.7 485.1 %all-gather.28.cloned.1.call-start = ((), (), s32[]{:S(2)}) async-start(), calls=%async_computation.7 | async-start | bytes 2359296 | tf_op jit(solution)/shard_map/all_gather | solution.py:557
  9.4 490.8 %all-gather.34.cloned.1.call-start = ((), (), s32[]{:S(2)}) async-start(), calls=%async_computation.10 | async-start | bytes 2359296 | tf_op jit(solution)/shard_map/all_gather | solution.py:558
  10.0 516.9 %all-gather.36.cloned.1.call-start = ((), (), s32[]{:S(2)}) async-start(), calls=%async_computation.11 | async-start | bytes 2359296 | tf_op jit(solution)/shard_map/all_gather | solution.py:564
  10.6 521.1 %all-gather.38.cloned.1.call-start = ((), (), s32[]{:S(2)}) async-start(), calls=%async_computation.12 | async-start | bytes 9437184 | tf_op jit(solution)/shard_map/all_gather | solution.py:563
  11.2 538.8 %all-gather.40.cloned.1.call-start = ((), (), s32[]{:S(2)}) async-start(), calls=%async_computation.13 | async-start | bytes 9437184 | tf_op jit(solution)/shard_map/all_gather | solution.py:565
  33.5 470.1 %copy-start.101 = (f32[8,1,128]{2,1,0:T(1,128)}, f32[8,1,128]{2,1,0:T(1,128)S(1)}, u32[]{:S(2)}) copy-start(f32[8,1,128]{2,1,0:T(1,128)S(1)} %convert_element_type.530) | copy-start | bytes 12292
  49.8 453.9 %copy-start.107 = (f32[8,1,128]{2,1,0:T(1,128)}, f32[8,1,128]{2,1,0:T(1,128)S(1)}, u32[]{:S(2)}) copy-start(f32[8,1,128]{2,1,0:T(1,128)S(1)} %convert_element_type.531) | copy-start | bytes 12292
  50.1 443.7 %copy-start.103 = (f32[512]{0:T(512)}, f32[512]{0:T(512)S(1)}, u32[]{:S(2)}) copy-start(f32[512]{0:T(512)S(1)} %get-tuple-element.2256) | copy-start | bytes 6148
  50.1 453.5 %copy-start.105 = (f32[512]{0:T(512)}, f32[512]{0:T(512)S(1)}, u32[]{:S(2)}) copy-start(f32[512]{0:T(512)S(1)} %get-tuple-element.2257) | copy-start | bytes 6148
  50.9 452.8 %copy-start.117 = (f32[512]{0:T(512)}, f32[512]{0:T(512)S(1)}, u32[]{:S(2)}) copy-start(f32[512]{0:T(512)S(1)} %fusion.228) | copy-start | bytes 6148
  50.9 442.9 %copy-start.115 = (f32[512]{0:T(512)}, f32[512]{0:T(512)S(1)}, u32[]{:S(2)}) copy-start(f32[512]{0:T(512)S(1)} %fusion.230) | copy-start | bytes 6148
  51.7 178.3 %collective-permute-start.2 = (f32[1,1024]{1,0:T(1,128)S(1)}, f32[1,1024]{1,0:T(1,128)S(1)}, u32[]{:S(2)}, u32[]{:S(2)}) collective-permute-start(f32[1,1024]{1,0:T(1,128)S(1)} %slice.96), channel_id=1, source_target_pairs={{0,1},{1,2},{2,3},{4,5},{5,6},{6,7},{8,9},{9,10},{10,11},{12,13},{... | collective-permute-start | bytes 12296 | tf_op jit(solution)/shard_map/ppermute | solution.py:18
  53.7 185.3 %collective-permute-start = (f32[1,1024]{1,0:T(1,128)S(1)}, f32[1,1024]{1,0:T(1,128)S(1)}, u32[]{:S(2)}, u32[]{:S(2)}) collective-permute-start(f32[1,1024]{1,0:T(1,128)S(1)} %slice.92), channel_id=1, source_target_pairs={{0,1},{1,2},{2,3},{4,5},{5,6},{6,7},{8,9},{9,10},{10,11},{12,13},{... | collective-permute-start | bytes 12296 | tf_op jit(solution)/shard_map/ppermute | solution.py:18
  57.2 986.2 %reduce-scatter.18.cloned.1.call-start = ((), (), s32[]{:S(2)}) async-start(), calls=%async_computation.19 | async-start | bytes 2359296 | tf_op jit(solution)/shard_map/reduce_scatter | solution.py:477
  61.6 21.1 %copy-start.141 = (bf16[128]{0:T(256)(128)(2,1)S(1)}, bf16[128]{0:T(256)(128)(2,1)}, u32[]{:S(2)}) copy-start(bf16[128]{0:T(256)(128)(2,1)} %param.45) | copy-start | bytes 772
  61.6 37.4 %copy-start.142 = (bf16[128]{0:T(256)(128)(2,1)S(1)}, bf16[128]{0:T(256)(128)(2,1)}, u32[]{:S(2)}) copy-start(bf16[128]{0:T(256)(128)(2,1)} %param.47) | copy-start | bytes 772
  61.6 55.7 %copy-start.143 = (bf16[128]{0:T(256)(128)(2,1)S(1)}, bf16[128]{0:T(256)(128)(2,1)}, u32[]{:S(2)}) copy-start(bf16[128]{0:T(256)(128)(2,1)} %param.46) | copy-start | bytes 772
  61.6 72.1 %copy-start.144 = (bf16[128]{0:T(256)(128)(2,1)S(1)}, bf16[128]{0:T(256)(128)(2,1)}, u32[]{:S(2)}) copy-start(bf16[128]{0:T(256)(128)(2,1)} %param.55) | copy-start | bytes 772
  61.6 90.3 %copy-start.145 = (bf16[128]{0:T(256)(128)(2,1)S(1)}, bf16[128]{0:T(256)(128)(2,1)}, u32[]{:S(2)}) copy-start(bf16[128]{0:T(256)(128)(2,1)} %param.56) | copy-start | bytes 772
  61.6 106.6 %copy-start.146 = (s32[16]{0:T(128)S(1)}, s32[16]{0:T(128)}, u32[]{:S(2)}) copy-start(s32[16]{0:T(128)} %param.41) | copy-start | bytes 196
  61.6 107.2 %copy-start.150 = (s32[16]{0:T(128)S(1)}, s32[16]{0:T(128)}, u32[]{:S(2)}) copy-start(s32[16]{0:T(128)} %param.40) | copy-start | bytes 196
  61.7 115.7 %copy-start.147 = (bf16[128]{0:T(256)(128)(2,1)S(1)}, bf16[128]{0:T(256)(128)(2,1)}, u32[]{:S(2)}) copy-start(bf16[128]{0:T(256)(128)(2,1)} %param.48) | copy-start | bytes 772
  61.7 133.8 %copy-start.148 = (bf16[128]{0:T(256)(128)(2,1)S(1)}, bf16[128]{0:T(256)(128)(2,1)}, u32[]{:S(2)}) copy-start(bf16[128]{0:T(256)(128)(2,1)} %param.53) | copy-start | bytes 772
  61.7 150.2 %copy-start.149 = (bf16[128]{0:T(256)(128)(2,1)S(1)}, bf16[128]{0:T(256)(128)(2,1)}, u32[]{:S(2)}) copy-start(bf16[128]{0:T(256)(128)(2,1)} %param.54) | copy-start | bytes 772
  82.7 157.9 %copy-start.109 = (f32[8,1,128]{2,1,0:T(1,128)}, f32[8,1,128]{2,1,0:T(1,128)S(1)}, u32[]{:S(2)}) copy-start(f32[8,1,128]{2,1,0:T(1,128)S(1)} %convert_element_type.534) | copy-start | bytes 12292
  82.7 157.9 %copy-start.123 = (f32[1024]{0:T(1024)}, f32[1024]{0:T(1024)S(1)}, u32[]{:S(2)}) copy-start(f32[1024]{0:T(1024)S(1)} %broadcast_subtract_fusion.3) | copy-start | bytes 12292
  99.0 140.1 %copy-start.111 = (f32[8,1,128]{2,1,0:T(1,128)}, f32[8,1,128]{2,1,0:T(1,128)S(1)}, u32[]{:S(2)}) copy-start(f32[8,1,128]{2,1,0:T(1,128)S(1)} %convert_element_type.535) | copy-start | bytes 12292
  99.0 140.1 %copy-start.125 = (f32[1024]{0:T(1024)}, f32[1024]{0:T(1024)S(1)}, u32[]{:S(2)}) copy-start(f32[1024]{0:T(1024)S(1)} %broadcast_subtract_fusion.2) | copy-start | bytes 12292
  133.7 370.0 %copy-start.113 = (f32[8,1,128]{2,1,0:T(1,128)}, f32[8,1,128]{2,1,0:T(1,128)S(1)}, u32[]{:S(2)}) copy-start(f32[8,1,128]{2,1,0:T(1,128)S(1)} %convert_element_type.532) | copy-start | bytes 12292
  133.7 370.0 %copy-start.127 = (f32[1024]{0:T(1024)}, f32[1024]{0:T(1024)S(1)}, u32[]{:S(2)}) copy-start(f32[1024]{0:T(1024)S(1)} %broadcast_subtract_fusion.4) | copy-start | bytes 12292
  230.0 263.8 %copy-start.133 = (f32[1,1024]{1,0:T(1,128)}, f32[1,1024]{1,0:T(1,128)S(1)}, u32[]{:S(2)}) copy-start(f32[1,1024]{1,0:T(1,128)S(1)} %collective-permute-done.2) | copy-start | bytes 12292
  239.0 264.6 %copy-start.131 = (f32[1,1024]{1,0:T(1,128)}, f32[1,1024]{1,0:T(1,128)S(1)}, u32[]{:S(2)}) copy-start(f32[1,1024]{1,0:T(1,128)S(1)} %collective-permute-done) | copy-start | bytes 12292
  513.1 7.9 collective-permute-start.1
  515.3 5.7 collective-permute-start.3
  531.7 11.6 copy-start.89
  531.7 11.6 copy-start.151
  550.0 9.5 copy-start.9
  623.1 13.7 collective-permute-start.4
  624.4 4.2 collective-permute-start.6
  628.5 415.0 %reduce-scatter.14.cloned.1.call-start = ((), (), s32[]{:S(2)}) async-start(), calls=%async_computation.17 | async-start | bytes 2359296 | tf_op jit(solution)/shard_map/reduce_scatter | solution.py:459
  628.6 9.4 copy-start.73
  628.6 10.0 copy-start.74
  679.7 363.8 %reduce-scatter.12.cloned.1.call-start = ((), (), s32[]{:S(2)}) async-start(), calls=%async_computation.16 | async-start | bytes 2359296 | tf_op jit(solution)/shard_map/reduce_scatter | solution.py:456
  680.2 103.4 %copy-start.102 = (f32[8,1,128]{2,1,0:T(1,128)S(1)}, f32[8,1,128]{2,1,0:T(1,128)}, u32[]{:S(2)}) copy-start(f32[8,1,128]{2,1,0:T(1,128)} %copy-done.101) | copy-start | bytes 12292
  680.2 103.4 %copy-start.106 = (f32[512]{0:T(512)S(1)}, f32[512]{0:T(512)}, u32[]{:S(2)}) copy-start(f32[512]{0:T(512)} %copy-done.105) | copy-start | bytes 6148
  680.2 103.4 %copy-start.108 = (f32[8,1,128]{2,1,0:T(1,128)S(1)}, f32[8,1,128]{2,1,0:T(1,128)}, u32[]{:S(2)}) copy-start(f32[8,1,128]{2,1,0:T(1,128)} %copy-done.107) | copy-start | bytes 12292
  680.2 103.4 %copy-start.114 = (f32[8,1,128]{2,1,0:T(1,128)S(1)}, f32[8,1,128]{2,1,0:T(1,128)}, u32[]{:S(2)}) copy-start(f32[8,1,128]{2,1,0:T(1,128)} %copy-done.113) | copy-start | bytes 12292
  680.2 103.4 %copy-start.118 = (f32[512]{0:T(512)S(1)}, f32[512]{0:T(512)}, u32[]{:S(2)}) copy-start(f32[512]{0:T(512)} %copy-done.117) | copy-start | bytes 6148
  680.2 103.4 %copy-start.128 = (f32[1024]{0:T(1024)S(1)}, f32[1024]{0:T(1024)}, u32[]{:S(2)}) copy-start(f32[1024]{0:T(1024)} %copy-done.127) | copy-start | bytes 12292
  680.3 103.4 %copy-start.132 = (f32[1,1024]{1,0:T(1,128)S(1)}, f32[1,1024]{1,0:T(1,128)}, u32[]{:S(2)}) copy-start(f32[1,1024]{1,0:T(1,128)} %copy-done.131) | copy-start | bytes 12292
  790.7 252.8 %reduce-scatter.10.cloned.1.call-start = ((), (), s32[]{:S(2)}) async-start(), calls=%async_computation.15 | async-start | bytes 2359296 | tf_op jit(solution)/shard_map/reduce_scatter | solution.py:453
  790.8 103.3 %copy-start.112 = (f32[8,1,128]{2,1,0:T(1,128)S(1)}, f32[8,1,128]{2,1,0:T(1,128)}, u32[]{:S(2)}) copy-start(f32[8,1,128]{2,1,0:T(1,128)} %copy-done.111) | copy-start | bytes 12292
  790.8 103.3 %copy-start.126 = (f32[1024]{0:T(1024)S(1)}, f32[1024]{0:T(1024)}, u32[]{:S(2)}) copy-start(f32[1024]{0:T(1024)} %copy-done.125) | copy-start | bytes 12292
  900.8 142.8 %reduce-scatter.8.cloned.1.call-start = ((), (), s32[]{:S(2)}) async-start(), calls=%async_computation.14 | async-start | bytes 2359296 | tf_op jit(solution)/shard_map/reduce_scatter | solution.py:450
  907.8 280.6 %reduce-scatter.20.cloned.1.call-start = ((), (), s32[]{:S(2)}) async-start(), calls=%async_computation.20 | async-start | bytes 9437184 | tf_op jit(solution)/shard_map/reduce_scatter | solution.py:480
  938.4 401.9 %reduce-scatter.16.cloned.1.call-start = ((), (), s32[]{:S(2)}) async-start(), calls=%async_computation.18 | async-start | bytes 9437184 | tf_op jit(solution)/shard_map/reduce_scatter | solution.py:474
  938.9 13.0 copy-start.90
  963.3 452.8 %all-reduce.16.cloned.1.call-start = ((), (), s32[]{:S(2)}) async-start(), calls=%async_computation.21 | async-start | bytes 6815744 | tf_op jit(solution)/shard_map/psum | solution.py:492
  1024.4 8.6 collective-permute-start.7
  1031.2 6.1 collective-permute-start.5
  (119 other events, 451.3 us)
Sparse Core Ops, SparseCore 0:
  10.2 52.0 all-gather.29
  64.4 47.8 all-gather.31
  114.4 47.8 all-gather.27
  164.2 47.8 all-gather.33
  214.1 47.7 all-gather.35
  263.9 123.4 all-gather.37
  389.5 123.1 all-gather.39
  628.6 67.0 reduce-scatter.17
  699.3 66.6 reduce-scatter.13
  790.8 65.1 reduce-scatter.11
  900.9 65.0 reduce-scatter.9
  969.3 67.5 reduce-scatter.7
  1040.5 147.8 reduce-scatter.19
  1192.3 147.9 reduce-scatter.15
  1343.0 72.9 all-reduce.15
where the time goes:
time: 1440 us; the launch traced here: 1430 us
  other arithmetic  437 us (30%)
  waiting for transfers between devices  322 us (22%)
  blocking collectives  322 us (22%)
  matrix products  228 us (16%)
  local copies, waits for them, and re-layouts  85.6 us (6%)
  between operations  17.8 us (1%)
  starting transfers between devices  16.3 us (1%)
    reduce_scatter x1, waiting for transfers between devices, owner_sums(): lax.psum_scatter(grad_list[15].astype(jnp.bfloat16), 'dp', scatter_dimens...  152 us
    reduce_scatter x1, waiting for transfers between devices, owner_sums(): lax.psum_scatter(grad_list[17].astype(jnp.bfloat16), 'dp', scatter_dimens...  145 us
    dynamic_update_slice x64, other arithmetic, forward_pass(): lax.scan(partial(segment_forward_sweep, sharded_arrays_group, current_boo...  120 us
    reduce_sum x32, other arithmetic, segment_forward_sweep(): jnp.sum(decay_table * exponentiated_lookup[None, :, :], axis=1)  89.5 us
    dot_general x14, matrix products, mul_weight(): lax.dot_general(input_rows, grad_rows, (((0,), (0,)), ((), ())), preferre...  84.2 us
    dot_general x14, matrix products, mul_plain(): return jnp.dot(left_rows, right_rows, preferred_element_type=jnp.float32)  74.8 us
    dot_general x14, matrix products, mul_back(): lax.dot_general(grad_rows, weight, (((1,), (1,)), ((), ())), preferred_el...  69.3 us
    reduce_sum x32, other arithmetic, segment_backward_sweep(): jnp.sum(decay_table * dividend_cotangent[:, None, :], axis=0)  53.4 us
  transfers between devices with their start and end apart: 23, of which 3 were waited for; matrix products, arithmetic and copies ran while one was open for 45% of the time, Pallas kernels for 0%

commit v1 on v0

v1 whole, which is shorter than its diff:
```python
import functools

import jax
import jax.numpy as jnp
from jax import lax
from jax.experimental import pallas as pl
from jax.experimental.pallas import tpu as pltpu
from jax.sharding import PartitionSpec as P

D = 1024
EPS = 1e-05
F32 = jnp.float32
BF16 = jnp.bfloat16


def axes_of(letter, size):
    return tuple(f"{letter}{bit}" for bit in reversed(range(size.bit_length() - 1)))


def swap(value, key):
    return lax.ppermute(value, key, [(0, 1), (1, 0)])


def place(held, key):
    rank = lambda k: (k[0] == "s", -int(k[1:]))
    return sum(1 for other in held if rank(other) < rank(key))


def join(mine, other, key, at):
    first = lax.axis_index(key) == 0
    return jnp.stack(
        [jnp.where(first, mine, other), jnp.where(first, other, mine)], axis=at
    )


def half(value, which, at):
    return lax.dynamic_index_in_dim(value, which, at, keepdims=False)


def add_low(mine, other):
    return (mine.astype(F32) + other.astype(F32)).astype(BF16)


def tie(*values):
    return lax.optimization_barrier(values)


class Growing:
    def __init__(self, value):
        self.value, self.held = value, []

    def hop(self, key, cut=None):
        at = place(self.held, key)
        other = swap(self.value, key)
        self.held.append(key)
        if cut is None:
            self.value = join(self.value, other, key, at)
        else:
            self.value = [join(m, o, key, at) for m, o in zip(cut(self.value), cut(other))]


class Shrinking:
    def __init__(self, value, held):
        self.value, self.held = value, list(held)

    def hop(self, key):
        self.held.remove(key)
        at = place(self.held, key)
        bit = lax.axis_index(key)
        got = swap(half(self.value, 1 - bit, at), key)
        self.value = add_low(half(self.value, bit, at), got)


def grow(values, key):
    for v in values:
        v.hop(key)


def settle(items, *others):
    tied = tie(*[item.value for item in items], *others)
    for item, value in zip(items, tied):
        item.value = value
    return tied[len(items) :]


ROWS = 8


def fwd_kernel(k_ref, v_ref, r_ref, rate_ref, u_ref, a0_ref, b0_ref, w_ref, a_ref, b_ref):
    rate = rate_ref[...]
    boost = jnp.exp(u_ref[...])
    width = rate.shape[1]
    row = lax.broadcasted_iota(jnp.int32, (ROWS, width), 0)
    rowf = row.astype(F32)
    falling = jnp.exp(-rowf * rate)
    one = jnp.exp(-rate)
    steps = [(s, jnp.where(row >= s, jnp.exp(-s * rate), 0.0)) for s in (1, 2, 4)]
    inner = row >= 1

    def scan(tile, carry):
        before = jnp.where(inner, pltpu.roll(tile, 1, 0), 0.0)
        for s, factor in steps:
            before = before + factor * pltpu.roll(before, s, 0)
        before = before + falling * carry
        after = one * before[ROWS - 1 :, :] + tile[ROWS - 1 :, :]
        return before, after

    def tile_of(start, carry):
        num, den = carry
        at = pl.ds(start, ROWS)
        key = k_ref[at, :]
        val = v_ref[at, :]
        power = jnp.exp(key)
        num_before, num = scan(power * val, num)
        den_before, den = scan(power, den)
        a_ref[at, :] = num_before
        b_ref[at, :] = den_before
        now = boost * power
        mixed = (num_before + now * val) / (den_before + now)
        return jax.nn.sigmoid(r_ref[at, :]) * mixed, (num, den)

    def body(i, carry):
        start = pl.multiple_of(i * (2 * ROWS), 2 * ROWS)
        low, carry = tile_of(start, carry)
        high, carry = tile_of(pl.multiple_of(start + ROWS, ROWS), carry)
        w_ref[pl.ds(start, 2 * ROWS), :] = jnp.concatenate([low, high], axis=0).astype(BF16)
        return carry

    lax.fori_loop(
        0, k_ref.shape[0] // (2 * ROWS), body, (a0_ref[...], b0_ref[...]), unroll=2
    )


def bwd_kernel(
    k_ref, v_ref, r_ref, a_ref, b_ref, dw_ref, rate_ref, u_ref, ga_ref, gb_ref,
    dk_ref, dv_ref, first_ref, decay_ref,
):
    rate = rate_ref[...]
    boost = jnp.exp(u_ref[...])
    width = rate.shape[1]
    row = lax.broadcasted_iota(jnp.int32, (ROWS, width), 0)
    rowf = row.astype(F32)
    trailing = jnp.exp(-(ROWS - 1.0 - rowf) * rate)
    one = jnp.exp(-rate)
    steps = [(s, jnp.where(row < ROWS - s, jnp.exp(-s * rate), 0.0)) for s in (1, 2, 4)]
    inner = row < ROWS - 1

    def scan(tile, carry):
        later = jnp.where(inner, pltpu.roll(tile, ROWS - 1, 0), 0.0)
        for s, factor in steps:
            later = later + factor * pltpu.roll(later, ROWS - s, 0)
        later = later + trailing * carry
        before = one * later[:1, :] + tile[:1, :]
        return later, before

    def tile_of(start, carry):
        num, den, first, decay = carry
        at = pl.ds(start, ROWS)
        key = k_ref[at, :]
        val = v_ref[at, :]
        num_before = a_ref[at, :]
        den_before = b_ref[at, :]
        power = jnp.exp(key)
        now = boost * power
        inverse = 1.0 / (den_before + now)
        mixed = (num_before + now * val) * inverse
        gate = jax.nn.sigmoid(r_ref[at, :])
        d_weighted = dw_ref[at, :]
        d_mixed = d_weighted * gate
        p = d_mixed * inverse
        q = -p * mixed
        num_later, num = scan(p, num)
        den_later, den = scan(q, den)
        diagonal = now * (val * p + q)
        d_key = power * (val * num_later + den_later) + diagonal
        d_val = power * num_later + now * p
        first = first + diagonal
        decay = decay + (num_later * num_before + den_later * den_before)
        return (d_key, d_val), (num, den, first, decay)

    count = k_ref.shape[0] // (2 * ROWS)

    def body(i, carry):
        start = pl.multiple_of((count - 1 - i) * (2 * ROWS), 2 * ROWS)
        high, carry = tile_of(pl.multiple_of(start + ROWS, ROWS), carry)
        low, carry = tile_of(start, carry)
        at = pl.ds(start, 2 * ROWS)
        for ref, a, b in zip((dk_ref, dv_ref), low, high):
            ref[at, :] = jnp.concatenate([a, b], axis=0).astype(BF16)
        return carry

    zero = jnp.zeros((ROWS, width), F32)
    done = lax.fori_loop(0, count, body, (ga_ref[...], gb_ref[...], zero, zero), unroll=2)
    first_ref[...] = done[2]
    decay_ref[...] = done[3]


WIDTH = 256


def wkv_specs(rows):
    big = pl.BlockSpec((rows, WIDTH), lambda s, c: (s, c))
    row = pl.BlockSpec((1, WIDTH), lambda s, c: (0, c))
    state = pl.BlockSpec((None, 1, WIDTH), lambda s, c: (s, 0, c))
    partial = pl.BlockSpec((None, ROWS, WIDTH), lambda s, c: (s, 0, c))
    return big, row, state, partial


def wkv_forward(keys, vals, recepts, rate, first, num, den, seqs):
    total = keys.shape[0]
    big, row, state, _ = wkv_specs(total // seqs)
    cells = total * D
    return pl.pallas_call(
        fwd_kernel,
        grid=(seqs, D // WIDTH),
        in_specs=[big, big, big, row, row, state, state],
        out_specs=[big, big, big],
        out_shape=[
            jax.ShapeDtypeStruct((total, D), BF16),
            jax.ShapeDtypeStruct((total, D), F32),
            jax.ShapeDtypeStruct((total, D), F32),
        ],
        compiler_params=pltpu.CompilerParams(vmem_limit_bytes=32 << 20),
        cost_estimate=pl.CostEstimate(
            flops=60 * cells, bytes_accessed=22 * cells, transcendentals=4 * cells
        ),
    )(keys, vals, recepts, rate, first, num, den)


def wkv_backward(keys, vals, recepts, num_before, den_before, d_weighted, rate, first, num, den, seqs):
    total = keys.shape[0]
    big, row, state, partial = wkv_specs(total // seqs)
    cells = total * D
    return pl.pallas_call(
        bwd_kernel,
        grid=(seqs, D // WIDTH),
        in_specs=[big, big, big, big, big, big, row, row, state, state],
        out_specs=[big, big, partial, partial],
        out_shape=[
            jax.ShapeDtypeStruct((total, D), BF16),
            jax.ShapeDtypeStruct((total, D), BF16),
            jax.ShapeDtypeStruct((seqs, ROWS, D), F32),
            jax.ShapeDtypeStruct((seqs, ROWS, D), F32),
        ],
        compiler_params=pltpu.CompilerParams(vmem_limit_bytes=32 << 20),
        cost_estimate=pl.CostEstimate(
            flops=90 * cells, bytes_accessed=30 * cells, transcendentals=4 * cells
        ),
    )(keys, vals, recepts, num_before, den_before, d_weighted, rate, first, num, den)


def dot(left, right):
    return jnp.dot(left, right, preferred_element_type=F32)


def dot_back(grads, weight):
    return lax.dot_general(grads, weight, (((1,), (1,)), ((), ())), preferred_element_type=F32)


def dot_weight(inputs, grads):
    return lax.dot_general(inputs, grads, (((0,), (0,)), ((), ())), preferred_element_type=F32)


def normalize(values):
    centre = values - jnp.mean(values, axis=-1, keepdims=True)
    spread = jnp.mean(centre * centre, axis=-1, keepdims=True)
    inverse = lax.rsqrt(spread + EPS)
    return centre * inverse, inverse


def from_behind(value, axes, by):
    count = lax.axis_size(axes)
    pairs = [(i, i + by) for i in range(count) if 0 <= i + by < count]
    return lax.ppermute(value, axes, pairs)


def shifted(rows, edge):
    return jnp.concatenate([edge, rows[:, :-1]], axis=1)


def pulled(rows, edge):
    return jnp.concatenate([rows[:, 1:], edge], axis=1)


def blend(now, before, share):
    return (now * share + before * (1.0 - share)).astype(BF16)


def earlier_state(decay, num, den, axes, backward):
    count = lax.axis_size(axes)
    mine = lax.axis_index(axes)
    packed = lax.all_gather(jnp.concatenate([num, den], axis=0), axes)
    seqs = num.shape[0]
    state = jnp.zeros_like(packed[0])
    for hop in range(count - 1):
        source = count - 1 - hop if backward else hop
        longer = decay * state + packed[source]
        keep = source > mine if backward else source < mine
        state = jnp.where(keep, longer, state)
    return state[:seqs, None, :], state[seqs:, None, :]


def per_device(
    dp_axes, seq_axes,
    tokens, cotangent, lengths, assignment,
    mix_norm_gain, mix_norm_bias, shift_key, shift_value, shift_recept, time_decay, time_first,
    key_weight, value_weight, recept_weight, output_weight,
    feed_norm_gain, feed_norm_bias, feed_shift_key, feed_shift_recept,
    feed_key_weight, feed_recept_weight, feed_value_weight,
):
    seqs, span, _ = tokens.shape
    total = seqs * span
    dp, seq = lax.axis_size(dp_axes), lax.axis_size(seq_axes)
    my_dp, my_seq = lax.axis_index(dp_axes), lax.axis_index(seq_axes)
    every = dp_axes + seq_axes
    z_axes, x = dp_axes[:-1], dp_axes[-1]
    y, c = seq_axes
    ff = feed_key_weight.shape[1]
    wide, thin = ff // 2, D // 2
    flat = lambda v: v.reshape(total, v.shape[-1])
    deep = lambda v: v.reshape(seqs, span, v.shape[-1])

    shard = D // dp
    quarter = shard // seq

    def own_rows(weight):
        return lax.dynamic_slice_in_dim(weight, my_seq * quarter, quarter, 0)

    hid = feed_value_weight.shape[0]
    w_fv = lax.all_gather(
        half(feed_value_weight.reshape(2, hid // 2, D), lax.axis_index(c), 0),
        dp_axes + (c,), axis=0, tiled=True,
    )
    vectors = Growing(
        jnp.stack(
            [
                mix_norm_gain, mix_norm_bias, shift_key, shift_value, shift_recept, time_decay, time_first,
                feed_norm_gain, feed_norm_bias, feed_shift_key, feed_shift_recept,
            ]
        )
    )
    kv = Growing(jnp.stack([own_rows(key_weight), own_rows(value_weight)]))
    ro = Growing(jnp.stack([own_rows(recept_weight), own_rows(output_weight)]))
    fk_own, fr_own = own_rows(feed_key_weight), own_rows(feed_recept_weight)
    f1 = Growing(jnp.concatenate([fk_own[:, :wide], fr_own[:, :thin]], axis=1))
    f2 = Growing(jnp.concatenate([fk_own[:, wide:], fr_own[:, thin:]], axis=1))
    edge1 = from_behind(tokens[:, -1:], seq_axes, 1)

    both = lambda v: [v[..., 0, :, :], v[..., 1, :, :]]
    cols = lambda v: [v[..., :wide], v[..., wide:]]
    for z in z_axes:
        grow([vectors, kv, ro], z)
        settle([vectors, kv, ro])
    vectors.hop(x)
    kv.hop(x)
    ro.hop(y)
    f1.hop(z_axes[0])
    f2.hop(z_axes[0])
    settle([vectors, kv, ro, f1, f2])
    kv.hop(y)
    ro.hop(x)
    for z in z_axes[1:]:
        grow([f1, f2], z)
    settle([kv, ro, f1, f2])
    f1.hop(x)
    f2.hop(y)
    kv.hop(c, both)
    ro.hop(c, both)
    w_k, w_v, w_r, w_o, f1.value, f2.value = tie(*kv.value, *ro.value, f1.value, f2.value)
    w_k, w_v, w_r, w_o = [w.reshape(D, D) for w in (w_k, w_v, w_r, w_o)]
    f1.hop(y)
    f2.hop(x)

    vectors = jnp.swapaxes(vectors.value.reshape(dp, 11, D // dp), 0, 1).reshape(11, D).astype(F32)
    gain1, bias1, mix_k, mix_v, mix_r, log_rate, first, gain2, bias2, fmix_k, fmix_r = [
        vectors[i : i + 1] for i in range(11)
    ]
    rate = jnp.exp(log_rate)
    lam = jnp.exp(-rate)

    slot_ids = jnp.arange(assignment.shape[0])
    my_slots = my_dp * seqs + jnp.arange(seqs)
    seq_ids = jnp.sum(jnp.where(slot_ids[None, :] == my_slots[:, None], assignment[None, :], 0), axis=1)
    my_lens = jnp.sum(jnp.where(slot_ids[None, :] == seq_ids[:, None], lengths[None, :], 0), axis=1)
    positions = my_seq * span + jnp.arange(span)
    valid = flat((positions[None, :] < my_lens[:, None]).astype(F32)[..., None])
    inside = (my_seq > 0).astype(F32)

    xin = tokens.astype(F32)
    edge1 = (normalize(edge1.astype(F32))[0] * gain1 + bias1) * inside
    n1, inv1 = normalize(xin)
    a = n1 * gain1 + bias1
    a_prev = shifted(a, edge1)
    key_in = flat(blend(a, a_prev, mix_k))
    value_in = flat(blend(a, a_prev, mix_v))
    recept_in = flat(blend(a, a_prev, mix_r))
    keys = dot(key_in, w_k)
    vals = dot(value_in, w_v)
    recepts = dot(recept_in, w_r)

    offsets = jnp.arange(span).astype(F32)[:, None]
    power = deep(jnp.exp(keys))
    left = jnp.exp(-(span - 1.0 - offsets) * rate)
    span_decay = jnp.exp(-span * rate)
    num_end = jnp.sum(left * power * deep(vals), axis=1)
    den_end = jnp.sum(left * power, axis=1)
    num_end, den_end = settle([f1, f2], num_end, den_end)
    f1.hop(c, cols)
    f2.hop(c, cols)
    num0, den0 = earlier_state(span_decay, num_end, den_end, seq_axes, False)
    weighted, num_before, den_before = wkv_forward(keys, vals, recepts, rate, first, num0, den0, seqs)
    attn = dot(weighted, w_o)
    middle = flat(xin) + attn

    w_fk1, w_fr1 = [w.reshape(D, -1) for w in f1.value]
    w_fk2, w_fr2 = [w.reshape(D, -1) for w in f2.value]
    w_fr = jnp.concatenate([w_fr1, w_fr2], axis=1)
    edge2 = from_behind(deep(middle)[:, -1:], seq_axes, 1)
    edge2 = (normalize(edge2)[0] * gain2 + bias2) * inside
    n2, inv2 = normalize(middle)
    b = n2 * gain2 + bias2
    b_prev = flat(shifted(deep(b), edge2))
    feed_key_in = blend(b, b_prev, fmix_k)
    feed_recept_in = blend(b, b_prev, fmix_r)
    sq1 = jnp.square(jax.nn.relu(dot(feed_key_in, w_fk1))).astype(BF16)
    sq2 = jnp.square(jax.nn.relu(dot(feed_key_in, w_fk2))).astype(BF16)
    gate = jax.nn.sigmoid(dot(feed_recept_in, w_fr))
    feed_value = dot(sq1, w_fv[:wide]) + dot(sq2, w_fv[wide:])
    feed = gate * feed_value
    result = middle + feed
    block_out = deep((valid * result).astype(BF16))
    stats = jnp.stack(
        [jnp.sum(valid * result * result), jnp.sum(valid * attn * attn), jnp.sum(valid * feed * feed)]
    )

    g = flat(cotangent).astype(F32) * valid
    d_fval = (g * gate).astype(BF16)
    d_fgate = (g * feed * (1.0 - gate)).astype(BF16)
    gfv = jnp.concatenate([dot_weight(sq1, d_fval).astype(BF16), dot_weight(sq2, d_fval).astype(BF16)], axis=0)
    gfv = lax.psum_scatter(gfv, dp_axes + (c,), scatter_dimension=0, tiled=True)
    gfr = dot_weight(feed_recept_in, d_fgate).astype(BF16)
    dh1 = (2.0 * jnp.sqrt(sq1.astype(F32)) * dot_back(d_fval, w_fv[:wide])).astype(BF16)
    dh2 = (2.0 * jnp.sqrt(sq2.astype(F32)) * dot_back(d_fval, w_fv[wide:])).astype(BF16)
    gfk1 = dot_weight(feed_key_in, dh1).astype(BF16)
    gfk2 = dot_weight(feed_key_in, dh2).astype(BF16)

    lead = (2,) * len(every)
    split = lambda g_: Shrinking(g_.reshape(lead + (quarter, g_.shape[1])), every)
    r1 = split(jnp.concatenate([gfk1, gfr[:, :thin]], axis=1))
    r2 = split(jnp.concatenate([gfk2, gfr[:, thin:]], axis=1))
    dh1, dh2 = settle([r1, r2], dh1, dh2)

    r1.hop(c)
    r2.hop(c)
    d_fk = dot_back(dh1, w_fk1) + dot_back(dh2, w_fk2)
    d_fr = dot_back(d_fgate, w_fr)
    d_fk, d_fr = settle([r1, r2], d_fk, d_fr)

    r1.hop(y)
    r2.hop(x)
    gap2 = b - b_prev
    grad_fmix_k = jnp.sum(gap2 * d_fk, axis=0)
    grad_fmix_r = jnp.sum(gap2 * d_fr, axis=0)
    later = deep(d_fk * (1.0 - fmix_k) + d_fr * (1.0 - fmix_r))
    db = d_fk * fmix_k + d_fr * fmix_r + flat(pulled(later, from_behind(later[:, :1], seq_axes, -1)))
    grad_gain2 = jnp.sum(n2 * db, axis=0)
    grad_bias2 = jnp.sum(db, axis=0)
    h2 = db * gain2
    d_middle = g + inv2 * (
        h2 - jnp.mean(h2, axis=-1, keepdims=True) - n2 * jnp.mean(h2 * n2, axis=-1, keepdims=True)
    )
    d_attn = d_middle.astype(BF16)
    d_weighted = dot_back(d_attn, w_o)
    ro_o = split(dot_weight(weighted, d_attn).astype(BF16))
    (d_weighted,) = settle([r1, r2, ro_o], d_weighted)

    r1.hop(x)
    r2.hop(y)
    ro_o.hop(c)
    now = jnp.exp(first + keys)
    inverse = 1.0 / (den_before + now)
    mixed = (num_before + now * vals) * inverse
    recept = jax.nn.sigmoid(recepts)
    d_recepts = (d_weighted * mixed * recept * (1.0 - recept)).astype(BF16)
    p = deep(d_weighted * recept * inverse)
    q = -p * deep(mixed)
    fall = jnp.exp(-offsets * rate)
    ga0, gb0 = earlier_state(
        span_decay, jnp.sum(fall * p, axis=1), jnp.sum(fall * q, axis=1), seq_axes, True
    )
    ro_r = split(dot_weight(recept_in, d_recepts).astype(BF16))
    ga0, gb0 = settle([r1, r2, ro_o, ro_r], ga0, gb0)

    z1, z2 = z_axes[-1], z_axes[:-1]
    r1.hop(z1)
    r2.hop(z1)
    ro_o.hop(y)
    ro_r.hop(c)
    d_keys, d_vals, first_part, decay_part = wkv_backward(
        keys, vals, recepts, num_before, den_before, d_weighted, rate, first, ga0, gb0, seqs
    )
    d_keys, d_vals = settle([r1, r2, ro_o, ro_r], d_keys, d_vals)

    for z in reversed(z2):
        r1.hop(z)
        r2.hop(z)
    ro_o.hop(x)
    ro_r.hop(x)
    r_k = split(dot_weight(key_in, d_keys).astype(BF16))
    r_v = split(dot_weight(value_in, d_vals).astype(BF16))
    d_keys, d_vals = settle([r1, r2, ro_o, ro_r, r_k, r_v], d_keys, d_vals)

    r_k.hop(c)
    r_v.hop(c)
    ro_o.hop(z1)
    ro_r.hop(y)
    out_f = Growing(jnp.stack([r1.value, r2.value]))
    out_f.hop(y)
    d_ki = dot_back(d_keys, w_k)
    d_vi = dot_back(d_vals, w_v)
    d_ri = dot_back(d_recepts, w_r)
    d_ki, d_vi, d_ri, gfv = settle([r_k, r_v, ro_o, ro_r, out_f], d_ki, d_vi, d_ri, gfv)

    r_k.hop(y)
    r_v.hop(x)
    for z in reversed(z2):
        ro_o.hop(z)
    ro_r.hop(z1)
    out_f.hop(c)
    gap1 = flat(a - a_prev)
    grad_mix_k = jnp.sum(gap1 * d_ki, axis=0)
    grad_mix_v = jnp.sum(gap1 * d_vi, axis=0)
    grad_mix_r = jnp.sum(gap1 * d_ri, axis=0)
    later = deep(d_ki * (1.0 - mix_k) + d_vi * (1.0 - mix_v) + d_ri * (1.0 - mix_r))
    da = d_ki * mix_k + d_vi * mix_v + d_ri * mix_r + flat(
        pulled(later, from_behind(later[:, :1], seq_axes, -1))
    )
    n1f, inv1f = flat(n1), flat(inv1)
    grad_gain1 = jnp.sum(n1f * da, axis=0)
    grad_bias1 = jnp.sum(da, axis=0)
    h1 = da * gain1
    d_x = inv1f * (
        h1 - jnp.mean(h1, axis=-1, keepdims=True) - n1f * jnp.mean(h1 * n1f, axis=-1, keepdims=True)
    )
    input_grad = deep((d_middle + d_x).astype(BF16))

    small = jnp.stack(
        [
            grad_gain1, grad_bias1, grad_mix_k, grad_mix_v, grad_mix_r,
            -(lam * rate)[0] * jnp.sum(decay_part, axis=(0, 1)), jnp.sum(first_part, axis=(0, 1)),
            grad_gain2, grad_bias2, grad_fmix_k, grad_fmix_r,
            jnp.pad(stats, (0, D - 3)),
        ]
    )
    small, input_grad = settle([r_k, r_v, ro_o, ro_r, out_f], small, input_grad)
    r_k.hop(x)
    r_v.hop(y)
    for z in reversed(z2):
        ro_r.hop(z)
    out_or = Growing(jnp.stack([ro_o.value, ro_r.value]))
    gfv = add_low(gfv, swap(gfv, y))
    small = small + swap(small, every[0])
    (small, gfv) = settle([r_k, r_v, out_or], small, gfv)
    r_k.hop(z1)
    r_v.hop(z1)
    out_or.hop(y)
    out_v = Growing(gfv)
    out_v.hop(c)
    small = small + swap(small, every[1])
    (small,) = settle([r_k, r_v, out_or, out_v], small)
    for z in reversed(z2):
        r_k.hop(z)
        r_v.hop(z)
    out_or.hop(c)
    small = small + swap(small, every[2])
    out_kv = Growing(jnp.stack([r_k.value, r_v.value]))
    (small,) = settle([out_kv, out_or], small)
    out_kv.hop(y)
    for key in every[3:]:
        small = small + swap(small, key)
    out_kv.hop(c)

    wide_out = lambda v, i: v[:, :, i].reshape(shard, -1)
    fk_r1, fk_r2 = wide_out(out_f.value, 0), wide_out(out_f.value, 1)
    grad_fk = jnp.concatenate([fk_r1[:, :wide], fk_r2[:, :wide]], axis=1).astype(F32)
    grad_fr = jnp.concatenate([fk_r1[:, wide:], fk_r2[:, wide:]], axis=1).astype(F32)
    grad_fv = out_v.value.reshape(hid, D).astype(F32)
    grad_o, grad_r = [wide_out(out_or.value, i).astype(F32) for i in range(2)]
    grad_k, grad_v = [wide_out(out_kv.value, i).astype(F32) for i in range(2)]
    rows = lax.dynamic_slice_in_dim(small[:11], my_dp * shard, shard, 1)
    rms = jnp.sqrt(small[11, :3] / (jnp.sum(lengths).astype(F32) * D))
    v = [rows[i] for i in range(11)]
    return (
        block_out, input_grad,
        v[0], v[1], v[2], v[3], v[4], v[5], v[6],
        grad_k, grad_v, grad_r, grad_o,
        v[7], v[8], v[9], v[10],
        grad_fk, grad_fr, grad_fv,
        rms[0], rms[1], rms[2],
    )


def solution(mesh):
    dp_axes, seq_axes = axes_of("d", mesh.shape["dp"]), axes_of("s", mesh.shape["seq"])
    names = dp_axes + seq_axes
    fine = jax.sharding.Mesh(mesh.devices.reshape((2,) * len(names)), names)
    big, vec, mat = P(dp_axes, seq_axes, None), P(dp_axes), P(dp_axes, None)
    args = (big, big, P(), P()) + (vec,) * 7 + (mat,) * 4 + (vec,) * 4 + (mat,) * 3
    outs = (big, big) + (vec,) * 7 + (mat,) * 4 + (vec,) * 4 + (mat,) * 3 + (P(),) * 3
    return jax.shard_map(
        functools.partial(per_device, dp_axes, seq_axes),
        mesh=fine, in_specs=args, out_specs=outs, check_vma=False,
    )
```

time: 1440 us -> 631 us (0.44)
  blocking collectives: 322 us -> 13.6 us
  other arithmetic: 437 us -> 134 us
  waiting for transfers between devices: 322 us -> 172 us
  matrix products: 228 us -> 145 us
  starting transfers between devices: 16.3 us -> 70.5 us
  local copies, waits for them, and re-layouts: 85.6 us -> 45.2 us
  Pallas kernels: 0 us -> 26.5 us
    reduce_scatter x7 -> x1, waiting for transfers between devices: 297 us -> 0.02 us  [per_device(): gfv = lax.psum_scatter(gfv, dp_axes + (c,), scatter_dimension=0, tiled=True)]
    all_gather x20 -> x2, blocking collectives: 243 us -> 13.6 us  [earlier_state(): packed = lax.all_gather(jnp.concatenate([num, den], axis=0), axes)]
    reduce_sum x144 -> x17, other arithmetic: 247 us -> 33.9 us  [the longest x1 9.6 us: per_device(): jnp.sum(valid * result * result)]
    ppermute x8 -> x70, waiting for transfers between devices: 0.02 us -> 172 us  [the longest x66 172 us: swap(): return lax.ppermute(value, key, [(0, 1), (1, 0)])]
    dynamic_update_slice x64 -> x0, other arithmetic: 120 us -> none  [forward_pass(): lax.scan(partial(segment_forward_sweep, sharded_arrays_group, current_boo...]
    dot_general x42 -> x27, matrix products: 228 us -> 145 us  [the longest x9 53.1 us: dot_back(): lax.dot_general(grads, weight, (((1,), (1,)), ((), ())), preferred_elemen...]
    ppermute x8 -> x70, starting transfers between devices: 15.1 us -> 70.4 us  [the longest x66 64.2 us: swap(): return lax.ppermute(value, key, [(0, 1), (1, 0)])]
    psum x2 -> x0, blocking collectives: 43.8 us -> none  [the longest x1 38.1 us: per_device(): summed = lax.psum(square_sums, ('dp', 'seq'))]
  transfers between devices with their start and end apart: 23 -> 72, of which waited for: 3 -> 34; matrix products, arithmetic and copies ran while one was open for 45% -> 41% of each run, Pallas kernels for 0% -> 4%
where the time goes in v1:
time: 631 us; the launch traced here: 624 us
  waiting for transfers between devices  172 us (27%)
  matrix products  145 us (23%)
  other arithmetic  134 us (21%)
  starting transfers between devices  70.5 us (11%)
  local copies, waits for them, and re-layouts  45.2 us (7%)
  Pallas kernels  26.5 us (4%)
  between operations  17.8 us (3%)
  blocking collectives  13.6 us (2%)
    ppermute x66, waiting for transfers between devices, swap(): return lax.ppermute(value, key, [(0, 1), (1, 0)])  172 us
    ppermute x66, starting transfers between devices, swap(): return lax.ppermute(value, key, [(0, 1), (1, 0)])  64.2 us
    dot_general x9, matrix products, dot_back(): lax.dot_general(grads, weight, (((1,), (1,)), ((), ())), preferred_elemen...  53.1 us
    dot_general x9, matrix products, dot(): return jnp.dot(left, right, preferred_element_type=F32)  50.4 us
    dot_general x9, matrix products, dot_weight(): lax.dot_general(inputs, grads, (((0,), (0,)), ((), ())), preferred_elemen...  41.6 us
    convert_element_type x28, other arithmetic, add_low(): return (mine.astype(F32) + other.astype(F32)).astype(BF16)  25.2 us
    another operation x61, other arithmetic, join(): jnp.stack([jnp.where(first, mine, other), jnp.where(first, other, mine)],...  23.8 us
    squeeze x30, local copies, waits for them, and re-layouts, half(): return lax.dynamic_index_in_dim(value, which, at, keepdims=False)  14.5 us
  transfers between devices with their start and end apart: 72, of which 34 were waited for; matrix products, arithmetic and copies ran while one was open for 41% of the time, Pallas kernels for 4%

profile of v1, /device:TPU:0, one launch (start us, length us, event | category | flops | bytes accessed | tf_op | source)
XLA Modules:
  0.0 624.5 jit_solution(17106820861305543851)
XLA Ops:
  7.3 2.8 stack.431
  10.1 4.0 collective-permute-start
  22.0 2.6 collective-permute-start.2
  34.2 2.6 collective-permute-start.10
  43.5 2.9 collective-permute-done.9
  46.4 9.3 %collective-permute-done.10 = bf16[32,2560]{1,0:T(8,128)(2,1)S(1)} collective-permute-done((bf16[32,2560]{1,0:T(8,128)(2,1)}, bf16[32,2560]{1,0:T(8,128)(2,1)S(1)}, u32[]{:S(2)}, u32[]{:S(2)}) %collective-permute-start.10) | collective-permute-done | bytes 163872 | tf_op jit(solution)/shard_map/ppermute | solution.py:21
  56.8 12.3 %collective-permute-done.4 = bf16[2,2,32,1024]{3,2,1,0:T(8,128)(2,1)S(1)} collective-permute-done((bf16[2,2,32,1024]{3,2,1,0:T(8,128)(2,1)S(1)}, bf16[2,2,32,1024]{3,2,1,0:T(8,128)(2,1)S(1)}, u32[]{:S(2)}, u32[]{:S(2)}) %collective-permute-start.4) | collective-permute-done | bytes 262176 | tf_op jit(solution)/shard_map/ppermute | solution.py:21
  69.2 6.6 %collective-permute-done.5 = bf16[2,2,32,1024]{3,2,1,0:T(8,128)(2,1)S(1)} collective-permute-done((bf16[2,2,32,1024]{3,2,1,0:T(8,128)(2,1)S(1)}, bf16[2,2,32,1024]{3,2,1,0:T(8,128)(2,1)S(1)}, u32[]{:S(2)}, u32[]{:S(2)}) %collective-permute-start.5) | collective-permute-done | bytes 262176 | tf_op jit(solution)/shard_map/ppermute | solution.py:21
  79.7 23.3 %collective-permute-done.7 = bf16[2,2,2,32,1024]{4,3,2,1,0:T(8,128)(2,1)S(1)} collective-permute-done((bf16[2,2,2,32,1024]{4,3,2,1,0:T(8,128)(2,1)S(1)}, bf16[2,2,2,32,1024]{4,3,2,1,0:T(8,128)(2,1)S(1)}, u32[]{:S(2)}, u32[]{:S(2)}) %collective-permute-start.7) | collective-permute-done | bytes 524320 | tf_op jit(solution)/shard_map/ppermute | solution.py:21
  109.8 7.9 %collective-permute-done.14 = bf16[2,32,2560]{2,1,0:T(8,128)(2,1)S(1)} collective-permute-done((bf16[2,32,2560]{2,1,0:T(8,128)(2,1)S(1)}, bf16[2,32,2560]{2,1,0:T(8,128)(2,1)S(1)}, u32[]{:S(2)}, u32[]{:S(2)}) %collective-permute-start.14) | collective-permute-done | bytes 327712 | tf_op jit(solution)/shard_map/ppermute | solution.py:21
  117.8 15.5 %collective-permute-done.15 = bf16[2,32,2560]{2,1,0:T(8,128)(2,1)S(1)} collective-permute-done((bf16[2,32,2560]{2,1,0:T(8,128)(2,1)S(1)}, bf16[2,32,2560]{2,1,0:T(8,128)(2,1)S(1)}, u32[]{:S(2)}, u32[]{:S(2)}) %collective-permute-start.15) | collective-permute-done | bytes 327712 | tf_op jit(solution)/shard_map/ppermute | solution.py:21
  136.0 6.7 %fusion.32 = (f32[2,512,1024]{2,1,0:T(8,128)}, bf16[2,512,1024]{2,1,0:T(8,128)(2,1)S(1)}, bf16[2,512,1024]{2,1,0:T(8,128)(2,1)S(1)}, bf16[2,512,1024]{2,1,0:T(8,128)(2,1)S(1)}, f32[2,512,1024]{2,1,0:T(8,128)}) fusion(f32[2,511,1024]{2,1,0:T(8,128)S(1)} %bitcast.627, f32[2,1,1024]{2,1,0:T(1,128)S(1)} %add_multiply_fusion.3, f32[1024]{0:T(1024)S(1)} %get-tuple-element.350, ...), kind=kLoop, calls=%fused_computation.123 | loop fusion | flops 19922944 | bytes 21012480 | tf_op jit(solution)/shard_map/sub | solution.py:530
  144.1 7.3 %collective-permute-done.18 = bf16[2,2,32,2560]{3,2,1,0:T(8,128)(2,1)S(1)} collective-permute-done((bf16[2,2,32,2560]{3,2,1,0:T(8,128)(2,1)S(1)}, bf16[2,2,32,2560]{3,2,1,0:T(8,128)(2,1)S(1)}, u32[]{:S(2)}, u32[]{:S(2)}) %collective-permute-start.18) | collective-permute-done | bytes 655392 | tf_op jit(solution)/shard_map/ppermute | solution.py:21
  151.5 7.0 %collective-permute-done.19 = bf16[2,2,32,2560]{3,2,0,1:T(8,128)(2,1)S(1)} collective-permute-done((bf16[2,2,32,2560]{3,2,0,1:T(8,128)(2,1)S(1)}, bf16[2,2,32,2560]{3,2,0,1:T(8,128)(2,1)S(1)}, u32[]{:S(2)}, u32[]{:S(2)}) %collective-permute-start.19) | collective-permute-done | bytes 655392 | tf_op jit(solution)/shard_map/ppermute | solution.py:21
  165.1 4.4 fusion.94.r_ref
  169.8 2.7 multiply_reduce_fusion.9
  172.5 17.0 %collective-permute-done.20 = bf16[2,2,2,32,2560]{4,3,2,1,0:T(8,128)(2,1)S(1)} collective-permute-done((bf16[2,2,2,32,2560]{4,3,2,1,0:T(8,128)(2,1)S(1)}, bf16[2,2,2,32,2560]{4,3,2,1,0:T(8,128)(2,1)S(1)}, u32[]{:S(2)}, u32[]{:S(2)}) %collective-permute-start.20) | collective-permute-done | bytes 1310752 | tf_op jit(solution)/shard_map/ppermute | solution.py:21
  193.3 5.2 all-gather.3
  199.2 12.3 %shard_map.389 = (bf16[1024,1024]{1,0:T(8,128)(2,1)S(1)}, f32[1024,1024]{1,0:T(8,128)S(1)}, f32[1024,1024]{1,0:T(8,128)S(1)}) custom-call(f32[1024,1024]{1,0:T(8,128)S(1)} %get-tuple-element.369.k_ref, f32[1024,1024]{1,0:T(8,128)S(1)} %fusion.93.v_ref, f32[1024,1024]{1,0:T(8,128)} %fusion.94.r_ref, f32[1,1024]{1,0:T(1,128)S(1)} %bitcast.612, ...), custom_call_target="tpu_custom_call" | custom-call | flops 62914560 | bytes 23068672 | tf_op jit(solution)/shard_map/pallas_call | solution.py:213
  211.6 4.9 fusion.86
  219.6 2.7 multiply_add_fusion.2
  222.7 2.9 pad_maximum_fusion.4
  228.5 4.0 select_bitcast_fusion.3
  233.5 4.0 select_bitcast_fusion.1
  242.6 4.7 add_divide_fusion.2
  247.3 6.1 multiply_convert_fusion.2
  253.4 6.2 multiply_convert_fusion.3
  259.8 10.2 %fusion.24 = f32[1024,1024]{1,0:T(8,128)} fusion(bf16[1024,2048]{1,0:T(8,128)(2,1)} %multiply_convert_fusion.3, bf16[1,4096,1024]{2,1,0:T(8,128)(2,1)} %all-gather.7.cloned.1.call-done), kind=kOutput, calls=%fused_computation.90 | convolution fusion | flops 4294967296 | bytes 12582912 | tf_op jit(solution)/shard_map/dot_general | solution.py:253
  270.0 8.8 %fusion.8 = (bf16[1024,1024]{1,0:T(8,128)(2,1)}, bf16[1024,1024]{1,0:T(8,128)(2,1)S(1)}, f32[1024,1024]{1,0:T(8,128)}) fusion(f32[1024,1024]{1,0:T(8,128)S(1)} %copy-done.130, bf16[2,512,1024]{2,1,0:T(8,128)(2,1)S(1)} %copy-done.60, f32[1024]{0:T(1024)S(1)} %bitcast.678, f32[1024,1024]{1,0:T(8,128)} %fusion.24, bf16[1024,2048]{1,0:T(8,128)(2,1)S(1)} %copy-done.128, ...), kind=kOutput, calls=%fused_computation.30 | convolution fusion | flops 4305453056 | bytes 27267072 | tf_op jit(solution)/shard_map/dot_general | solution.py:253
  278.8 10.3 %convolution_convert_fusion.1 = bf16[2048,1024]{1,0:T(8,128)(2,1)} fusion(bf16[1024,2048]{1,0:T(8,128)(2,1)} %multiply_convert_fusion.3, bf16[1024,1024]{1,0:T(8,128)(2,1)} %get-tuple-element.246), kind=kOutput, calls=%fused_computation.87 | convolution fusion | flops 4297064448 | bytes 10485760 | tf_op jit(solution)/shard_map/dot_general | solution.py:261
  289.1 6.6 %convolution_convert_fusion = bf16[2048,1024]{1,0:T(8,128)(2,1)} fusion(bf16[1024,2048]{1,0:T(8,128)(2,1)S(1)} %copy-done.128, bf16[1024,1024]{1,0:T(8,128)(2,1)S(1)} %copy-done.131), kind=kOutput, calls=%fused_computation.86 | convolution fusion | flops 4297064448 | bytes 10485760 | tf_op jit(solution)/shard_map/dot_general | solution.py:261
  299.3 7.8 %pad_maximum_fusion = bf16[4096,1024]{1,0:T(8,128)(2,1)} fusion(bf16[2048,1024]{1,0:T(8,128)(2,1)} %convolution_convert_fusion, bf16[2048,1024]{1,0:T(8,128)(2,1)} %convolution_convert_fusion.1), kind=kLoop, calls=%fused_computation | loop fusion | flops 16777216 | bytes 16777216 | tf_op jit(solution)/shard_map/concatenate | solution.py:439
  307.2 10.4 %multiply_convert_fusion.1 = bf16[1024,2048]{1,0:T(8,128)(2,1)S(1)} fusion(bf16[1024,2048]{1,0:T(8,128)(2,1)} %multiply_convert_fusion.3, bf16[1024,1024]{1,0:T(8,128)(2,1)} %get-tuple-element.246, bf16[1,4096,1024]{2,1,0:T(8,128)(2,1)} %all-gather.7.cloned.1.call-done), kind=kOutput, calls=%fused_computation.2 | convolution fusion | flops 4303355904 | bytes 14680064 | tf_op jit(solution)/shard_map/dot_general | solution.py:257
  319.6 4.9 convolution_convert_fusion.3
  324.6 8.9 %multiply_convert_fusion = bf16[1024,2048]{1,0:T(8,128)(2,1)S(1)} fusion(bf16[1024,2048]{1,0:T(8,128)(2,1)S(1)} %copy-done.129, bf16[1024,1024]{1,0:T(8,128)(2,1)S(1)} %copy-done.132, bf16[1,4096,1024]{2,1,0:T(8,128)(2,1)} %all-gather.7.cloned.1.call-done), kind=kOutput, calls=%fused_computation.1 | convolution fusion | flops 4303355904 | bytes 14680064 | tf_op jit(solution)/shard_map/dot_general | solution.py:257
  333.5 6.3 %convolution_convert_fusion.2 = bf16[1024,2048]{1,0:T(8,128)(2,1)} fusion(bf16[1024,1024]{1,0:T(8,128)(2,1)S(1)} %copy-done.63, bf16[1024,2048]{1,0:T(8,128)(2,1)S(1)} %multiply_convert_fusion), kind=kOutput, calls=%fused_computation.88 | convolution fusion | flops 4297064448 | bytes 10485760 | tf_op jit(solution)/shard_map/dot_general | solution.py:261
  340.2 2.9 pad_maximum_fusion.2
  348.6 6.1 fusion.95
  357.0 7.6 %convolution_add_fusion = f32[1024,1024]{1,0:T(8,128)S(1)} fusion(f32[1024,1024]{1,0:T(8,128)} %fusion.95, bf16[1024,2048]{1,0:T(8,128)(2,1)} %copy-done.123, bf16[1024,2048]{1,0:T(8,128)(2,1)S(1)} %bitcast.635), kind=kOutput, calls=%fused_computation.124 | convolution fusion | flops 4296015872 | bytes 16777216 | tf_op jit(solution)/shard_map/dot_general | solution.py:257
  365.6 4.0 fusion.1
  370.1 2.8 multiply_reduce_fusion
  378.3 2.5 collective-permute-start.27
  381.1 9.6 %fusion.2 = (f32[]{:T(128)}, f32[]{:T(128)}, f32[1024]{0:T(1024)S(1)}, f32[1024]{0:T(1024)S(1)}, f32[1024]{0:T(1024)S(1)}, /*index=5*/f32[1024]{0:T(1024)S(1)}, ...) fusion(f32[1024]{0:T(1024)S(1)} %bitcast.679, f32[1024,1024]{1,0:T(8,128)S(1)} %copy-done.19, ...), kind=kLoop, calls=%fused_computation.15 | loop fusion | flops 25161724 | bytes 31498252 | tf_op jit(solution)/shard_map/reduce_sum | solution.py:433
  392.6 2.7 select_maximum_fusion
  397.9 4.5 fusion.40.dw_ref
  402.4 10.9 %collective-permute-done.28 = bf16[2,2,2,32,2560]{4,3,0,1,2:T(8,128)(2,1)} collective-permute-done((bf16[2,2,2,32,2560]{4,3,0,1,2:T(8,128)(2,1)}, bf16[2,2,2,32,2560]{4,3,0,1,2:T(8,128)(2,1)}, u32[]{:S(2)}, u32[]{:S(2)}) %collective-permute-start.28) | collective-permute-done | bytes 1310752 | tf_op jit(solution)/shard_map/ppermute | solution.py:21
  421.2 6.8 %multiply_reduce_fusion.4 = (f32[2,1024]{1,0:T(2,128)S(1)}, f32[2,1024]{1,0:T(2,128)S(1)}, f32[1024,1024]{1,0:T(8,128)}) fusion(f32[512,1024]{1,0:T(8,128)} %get-tuple-element.364, f32[1024,1024]{1,0:T(8,128)S(1)} %copy-done.12, f32[1024,1024]{1,0:T(8,128)S(1)} %copy-done.9, f32[1024,1024]{1,0:T(8,128)S(1)} %copy-done.4, f32[1024,1024]{1,0:T(8,128)S(1)} %copy-done.6, ...), kind=kLoop, calls=%fused_computation.63 | loop fusion | flops 17821696 | bytes 31477760 | tf_op jit(solution)/shard_map/reduce_sum | solution.py:489
  428.1 8.3 %all-gather.4 = f32[4,4,1024]{2,1,0:T(4,128)S(1)} all-gather(f32[1,4,1024]{2,1,0:T(4,128)S(1)} %maximum_bitcast_fusion.1), channel_id=4, replica_groups=mesh['d2'=2,'d1'=2,'d0'=2,'s1'=2,'s0'=2] {'s1','s0'}, dimensions={0}, use_global_device_ids=true | all-gather | bytes 81920 | tf_op jit(solution)/shard_map/all_gather | solution.py:292
  436.4 5.3 multiply_convert_fusion.5
  441.8 3.8 convolution_convert_fusion.6
  445.6 4.4 fusion.98
  453.5 2.6 fusion.31
  456.1 14.2 %shard_map.390 = (bf16[1024,1024]{1,0:T(8,128)(2,1)S(1)}, bf16[1024,1024]{1,0:T(8,128)(2,1)S(1)}, f32[2,8,1024]{2,1,0:T(8,128)S(1)}, f32[2,8,1024]{2,1,0:T(8,128)S(1)}) custom-call(f32[1024,1024]{1,0:T(8,128)S(1)} %copy-done.7, f32[1024,1024]{1,0:T(8,128)S(1)} %copy-done.4, f32[1024,1024]{1,0:T(8,128)S(1)} %copy-done.2, f32[1024,1024]{1,0:T(8,128)S(1)} %copy-done.10, ...), custom_call_target="tpu_custom_call" | custom-call | flops 94371840 | bytes 31457280 | tf_op jit(solution)/shard_map/pallas_call | solution.py:234
  477.8 4.5 collective-permute-done.34
  482.4 6.4 %collective-permute-done.33 = bf16[2,32,2560]{2,1,0:T(8,128)(2,1)S(1)} collective-permute-done((bf16[2,32,2560]{2,1,0:T(8,128)(2,1)S(1)}, bf16[2,32,2560]{2,1,0:T(8,128)(2,1)S(1)}, u32[]{:S(2)}, u32[]{:S(2)}) %collective-permute-start.33) | collective-permute-done | bytes 327712 | tf_op jit(solution)/shard_map/ppermute | solution.py:21
  501.8 3.6 collective-permute-done.38
  505.5 3.2 collective-permute-done.37
  509.0 9.1 %collective-permute-done.40 = bf16[2,2,2,32,1024]{4,3,0,1,2:T(8,128)(2,1)S(1)} collective-permute-done((bf16[2,2,2,32,1024]{4,3,0,1,2:T(8,128)(2,1)S(1)}, bf16[2,2,2,32,1024]{4,3,0,1,2:T(8,128)(2,1)S(1)}, u32[]{:S(2)}, u32[]{:S(2)}) %collective-permute-start.40) | collective-permute-done | bytes 524320 | tf_op jit(solution)/shard_map/ppermute | solution.py:21
  522.2 4.4 fusion.96
  526.6 4.3 fusion.97
  534.3 7.9 %fusion.13 = (f32[1024]{0:T(1024)}, f32[1024]{0:T(1024)}, f32[1024]{0:T(1024)}, f32[1024,1024]{1,0:T(8,128)S(1)}) fusion(f32[1024,1024]{1,0:T(8,128)} %fusion.98, f32[2,512,1024]{2,1,0:T(8,128)} %get-tuple-element.242, f32[1024,1024]{1,0:T(8,128)} %fusion.97, f32[1024,1024]{1,0:T(8,128)} %fusion.96, f32[1024]{0:T(1024)S(1)} %copy-done.112, ...), kind=kLoop, calls=%fused_computation.38 | loop fusion | flops 11531264 | bytes 20996096 | tf_op jit(solution)/shard_map/reduce_sum | solution.py:533
  555.3 3.6 fusion.15
  559.0 2.6 fusion.19
  567.6 8.3 %collective-permute-done.56 = bf16[256,1024]{1,0:T(8,128)(2,1)} collective-permute-done((bf16[256,1024]{1,0:T(8,128)(2,1)}, bf16[256,1024]{1,0:T(8,128)(2,1)}, u32[]{:S(2)}, u32[]{:S(2)}) %collective-permute-start.56) | collective-permute-done | bytes 524320 | tf_op jit(solution)/shard_map/ppermute | solution.py:21
  (622 shorter events, 187.4 us)
Async XLA Ops:
  7.2 252.5 %all-gather.7.cloned.1.call-start = ((), (), s32[]{:S(2)}) async-start(), calls=%async_computation.2 | async-start | bytes 8912896 | tf_op jit(solution)/shard_map/all_gather | solution.py:330
  10.1 24.2 %collective-permute-start = (bf16[11,128]{1,0:T(8,128)(2,1)}, bf16[11,128]{1,0:T(8,128)(2,1)}, u32[]{:S(2)}, u32[]{:S(2)}) collective-permute-start(bf16[11,128]{1,0:T(8,128)(2,1)} %stack.431), channel_id=1, source_target_pairs={{0,16},{16,0},{1,17},{17,1},{2,18},{18,2},{3,19},{19,3},{4,20},{20... | collective-permute-start | bytes 8456 | tf_op jit(solution)/shard_map/ppermute | solution.py:21
  15.5 22.1 %collective-permute-start.11 = (bf16[2,1,1024]{2,1,0:T(2,128)(2,1)}, bf16[2,1,1024]{2,1,0:T(2,128)(2,1)S(1)}, u32[]{:S(2)}, u32[]{:S(2)}) collective-permute-start(bf16[2,1,1024]{2,1,0:T(2,128)(2,1)} %slice.262), channel_id=1, source_target_pairs={{0,1},{1,2},{2,3},{4,5},{5,6},{6,7},{8,9},{9,10},{10,11},{12,13},{... | collective-permute-start | bytes 12296 | tf_op jit(solution)/shard_map/ppermute | solution.py:274
  19.3 18.6 %collective-permute-start.1 = (bf16[2,32,1024]{2,1,0:T(8,128)(2,1)}, bf16[2,32,1024]{2,1,0:T(8,128)(2,1)}, u32[]{:S(2)}, u32[]{:S(2)}) collective-permute-start(bf16[2,32,1024]{2,1,0:T(8,128)(2,1)} %pad_maximum_fusion.44), channel_id=1, source_target_pairs={{0,16},{16,0},{1,17},{17,1},{2,18},{18,2},{3,19},{19,3},{4,20},{20... | collective-permute-start | bytes 393224 | tf_op jit(solution)/shard_map/ppermute | solution.py:21
  22.0 15.9 %collective-permute-start.2 = (bf16[2,32,1024]{2,1,0:T(8,128)(2,1)}, bf16[2,32,1024]{2,1,0:T(8,128)(2,1)}, u32[]{:S(2)}, u32[]{:S(2)}) collective-permute-start(bf16[2,32,1024]{2,1,0:T(8,128)(2,1)} %pad_maximum_fusion.45), channel_id=1, source_target_pairs={{0,16},{16,0},{1,17},{17,1},{2,18},{18,2},{3,19},{19,3},{4,20},{20... | collective-permute-start | bytes 393224 | tf_op jit(solution)/shard_map/ppermute | solution.py:21
  27.7 18.7 %collective-permute-start.9 = (bf16[32,2560]{1,0:T(8,128)(2,1)}, bf16[32,2560]{1,0:T(8,128)(2,1)}, u32[]{:S(2)}, u32[]{:S(2)}) collective-permute-start(bf16[32,2560]{1,0:T(8,128)(2,1)} %pad_maximum_fusion.42), channel_id=1, source_target_pairs={{0,16},{16,0},{1,17},{17,1},{2,18},{18,2},{3,19},{19,3},{4,20},{20... | collective-permute-start | bytes 491528 | tf_op jit(solution)/shard_map/ppermute | solution.py:21
  28.9 505.4 %reduce-scatter.2.cloned.1.call-start = ((), (), s32[]{:S(2)}) async-start(), calls=%async_computation.1 | async-start | bytes 8912896 | tf_op jit(solution)/shard_map/reduce_scatter | solution.py:440
  34.2 21.5 %collective-permute-start.10 = (bf16[32,2560]{1,0:T(8,128)(2,1)}, bf16[32,2560]{1,0:T(8,128)(2,1)S(1)}, u32[]{:S(2)}, u32[]{:S(2)}) collective-permute-start(bf16[32,2560]{1,0:T(8,128)(2,1)} %pad_maximum_fusion.43), channel_id=1, source_target_pairs={{0,16},{16,0},{1,17},{17,1},{2,18},{18,2},{3,19},{19,3},{4,20},{20... | collective-permute-start | bytes 491528 | tf_op jit(solution)/shard_map/ppermute | solution.py:21
  40.7 28.4 %collective-permute-start.4 = (bf16[2,2,32,1024]{3,2,1,0:T(8,128)(2,1)S(1)}, bf16[2,2,32,1024]{3,2,1,0:T(8,128)(2,1)S(1)}, u32[]{:S(2)}, u32[]{:S(2)}) collective-permute-start(bf16[2,2,32,1024]{3,2,1,0:T(8,128)(2,1)S(1)} %pad_maximum_fusion.38), channel_id=1, source_target_pairs={{0,8},{8,0},{1,9},{9,1},{2,10},{10,2},{3,11},{11,3},{4,12},{12,4},... | collective-permute-start | bytes 786440 | tf_op jit(solution)/shard_map/ppermute | solution.py:21
  41.1 34.7 %collective-permute-start.5 = (bf16[2,2,32,1024]{3,2,1,0:T(8,128)(2,1)S(1)}, bf16[2,2,32,1024]{3,2,1,0:T(8,128)(2,1)S(1)}, u32[]{:S(2)}, u32[]{:S(2)}) collective-permute-start(bf16[2,2,32,1024]{3,2,1,0:T(8,128)(2,1)S(1)} %pad_maximum_fusion.39), channel_id=1, source_target_pairs={{0,8},{8,0},{1,9},{9,1},{2,10},{10,2},{3,11},{11,3},{4,12},{12,4},... | collective-permute-start | bytes 786440 | tf_op jit(solution)/shard_map/ppermute | solution.py:21
  77.4 25.5 %collective-permute-start.7 = (bf16[2,2,2,32,1024]{4,3,2,1,0:T(8,128)(2,1)S(1)}, bf16[2,2,2,32,1024]{4,3,2,1,0:T(8,128)(2,1)S(1)}, u32[]{:S(2)}, u32[]{:S(2)}) collective-permute-start(bf16[2,2,2,32,1024]{4,3,2,1,0:T(8,128)(2,1)S(1)} %pad_maximum_fusion.31), channel_id=1, source_target_pairs={{0,4},{4,0},{1,5},{5,1},{2,6},{6,2},{3,7},{7,3},{8,12},{12,8},{9,1... | collective-permute-start | bytes 1572872 | tf_op jit(solution)/shard_map/ppermute | solution.py:21
  78.0 25.2 %collective-permute-start.8 = (bf16[2,2,2,32,1024]{4,3,2,0,1:T(8,128)(2,1)S(1)}, bf16[2,2,2,32,1024]{4,3,2,0,1:T(8,128)(2,1)S(1)}, u32[]{:S(2)}, u32[]{:S(2)}) collective-permute-start(bf16[2,2,2,32,1024]{4,3,2,0,1:T(8,128)(2,1)S(1)} %pad_maximum_fusion.32), channel_id=1, source_target_pairs={{0,2},{2,0},{1,3},{3,1},{4,6},{6,4},{5,7},{7,5},{8,10},{10,8},{9,1... | collective-permute-start | bytes 1572872 | tf_op jit(solution)/shard_map/ppermute | solution.py:21
  104.1 13.5 %collective-permute-start.14 = (bf16[2,32,2560]{2,1,0:T(8,128)(2,1)S(1)}, bf16[2,32,2560]{2,1,0:T(8,128)(2,1)S(1)}, u32[]{:S(2)}, u32[]{:S(2)}) collective-permute-start(bf16[2,32,2560]{2,1,0:T(8,128)(2,1)S(1)} %pad_maximum_fusion.34), channel_id=1, source_target_pairs={{0,8},{8,0},{1,9},{9,1},{2,10},{10,2},{3,11},{11,3},{4,12},{12,4},... | collective-permute-start | bytes 983048 | tf_op jit(solution)/shard_map/ppermute | solution.py:21
  104.2 29.1 %collective-permute-start.15 = (bf16[2,32,2560]{2,1,0:T(8,128)(2,1)S(1)}, bf16[2,32,2560]{2,1,0:T(8,128)(2,1)S(1)}, u32[]{:S(2)}, u32[]{:S(2)}) collective-permute-start(bf16[2,32,2560]{2,1,0:T(8,128)(2,1)S(1)} %pad_maximum_fusion.35), channel_id=1, source_target_pairs={{0,8},{8,0},{1,9},{9,1},{2,10},{10,2},{3,11},{11,3},{4,12},{12,4},... | collective-permute-start | bytes 983048 | tf_op jit(solution)/shard_map/ppermute | solution.py:21
  106.2 27.3 %collective-permute-start.12 = (bf16[2,2,2,2,32,1024]{5,4,3,2,1,0:T(8,128)(2,1)S(1)}, bf16[2,2,2,2,32,1024]{5,4,3,2,1,0:T(8,128)(2,1)S(1)}, u32[]{:S(2)}, u32[]{:S(2)}) collective-permute-start(bf16[2,2,2,2,32,1024]{5,4,3,2,1,0:T(8,128)(2,1)S(1)} %pad_maximum_fusion.23), channel_id=1, source_target_pairs={{0,2},{2,0},{1,3},{3,1},{4,6},{6,4},{5,7},{7,5},{8,10},{10,8},{9,1... | collective-permute-start | bytes 3145736 | tf_op jit(solution)/shard_map/ppermute | solution.py:21
  106.2 28.9 %collective-permute-start.13 = (bf16[2,2,2,2,32,1024]{5,4,3,0,1,2:T(8,128)(2,1)S(1)}, bf16[2,2,2,2,32,1024]{5,4,3,0,1,2:T(8,128)(2,1)S(1)}, u32[]{:S(2)}, u32[]{:S(2)}) collective-permute-start(bf16[2,2,2,2,32,1024]{5,4,3,0,1,2:T(8,128)(2,1)S(1)} %pad_maximum_fusion.24), channel_id=1, source_target_pairs={{0,4},{4,0},{1,5},{5,1},{2,6},{6,2},{3,7},{7,3},{8,12},{12,8},{9,1... | collective-permute-start | bytes 3145736 | tf_op jit(solution)/shard_map/ppermute | solution.py:21
  135.5 15.9 %collective-permute-start.18 = (bf16[2,2,32,2560]{3,2,1,0:T(8,128)(2,1)S(1)}, bf16[2,2,32,2560]{3,2,1,0:T(8,128)(2,1)S(1)}, u32[]{:S(2)}, u32[]{:S(2)}) collective-permute-start(bf16[2,2,32,2560]{3,2,1,0:T(8,128)(2,1)S(1)} %pad_maximum_fusion.28), channel_id=1, source_target_pairs={{0,4},{4,0},{1,5},{5,1},{2,6},{6,2},{3,7},{7,3},{8,12},{12,8},{9,1... | collective-permute-start | bytes 1966088 | tf_op jit(solution)/shard_map/ppermute | solution.py:21
  142.7 15.9 %collective-permute-start.19 = (bf16[2,2,32,2560]{3,2,0,1:T(8,128)(2,1)S(1)}, bf16[2,2,32,2560]{3,2,0,1:T(8,128)(2,1)S(1)}, u32[]{:S(2)}, u32[]{:S(2)}) collective-permute-start(bf16[2,2,32,2560]{3,2,0,1:T(8,128)(2,1)S(1)} %pad_maximum_fusion.29), channel_id=1, source_target_pairs={{0,2},{2,0},{1,3},{3,1},{4,6},{6,4},{5,7},{7,5},{8,10},{10,8},{9,1... | collective-permute-start | bytes 1966088 | tf_op jit(solution)/shard_map/ppermute | solution.py:21
  143.6 15.3 %collective-permute-start.16 = (bf16[2,2,2,2,2,32,1024]{6,5,4,3,2,1,0:T(8,128)(2,1)S(1)}, bf16[2,2,2,2,2,32,1024]{6,5,4,3,2,1,0:T(8,128)(2,1)S(1)}, u32[]{:S(2)}, u32[]{:S(2)}) collective-permute-start(bf16[2,2,2,2,2,32,1024]{6,5,4,3,2,1,0:T(8,128)(2,1)S(1)} %pad_maximum_fusion.11), channel_id=1, source_target_pairs={{0,1},{1,0},{2,3},{3,2},{4,5},{5,4},{6,7},{7,6},{8,9},{9,8},{10,11... | collective-permute-start | bytes 6291464 | tf_op jit(solution)/shard_map/ppermute | solution.py:21
  143.6 16.1 %collective-permute-start.17 = (bf16[2,2,2,2,2,32,1024]{6,5,4,0,1,3,2:T(8,128)(2,1)S(1)}, bf16[2,2,2,2,2,32,1024]{6,5,4,0,1,3,2:T(8,128)(2,1)S(1)}, u32[]{:S(2)}, u32[]{:S(2)}) collective-permute-start(bf16[2,2,2,2,2,32,1024]{6,5,4,0,1,3,2:T(8,128)(2,1)S(1)} %pad_maximum_fusion.12), channel_id=1, source_target_pairs={{0,1},{1,0},{2,3},{3,2},{4,5},{5,4},{6,7},{7,6},{8,9},{9,8},{10,11... | collective-permute-start | bytes 6291464 | tf_op jit(solution)/shard_map/ppermute | solution.py:21
  160.5 29.0 %collective-permute-start.20 = (bf16[2,2,2,32,2560]{4,3,2,1,0:T(8,128)(2,1)S(1)}, bf16[2,2,2,32,2560]{4,3,2,1,0:T(8,128)(2,1)S(1)}, u32[]{:S(2)}, u32[]{:S(2)}) collective-permute-start(bf16[2,2,2,32,2560]{4,3,2,1,0:T(8,128)(2,1)S(1)} %pad_maximum_fusion.20), channel_id=1, source_target_pairs={{0,2},{2,0},{1,3},{3,1},{4,6},{6,4},{5,7},{7,5},{8,10},{10,8},{9,1... | collective-permute-start | bytes 3932168 | tf_op jit(solution)/shard_map/ppermute | solution.py:21
  161.2 30.2 %collective-permute-start.21 = (bf16[2,2,2,32,2560]{4,3,0,1,2:T(8,128)(2,1)S(1)}, bf16[2,2,2,32,2560]{4,3,0,1,2:T(8,128)(2,1)S(1)}, u32[]{:S(2)}, u32[]{:S(2)}) collective-permute-start(bf16[2,2,2,32,2560]{4,3,0,1,2:T(8,128)(2,1)S(1)} %pad_maximum_fusion.21), channel_id=1, source_target_pairs={{0,4},{4,0},{1,5},{5,1},{2,6},{6,2},{3,7},{7,3},{8,12},{12,8},{9,1... | collective-permute-start | bytes 3932168 | tf_op jit(solution)/shard_map/ppermute | solution.py:21
  198.6 29.9 %collective-permute-start.23 = (bf16[2,2,2,2,32,2560]{5,4,3,2,1,0:T(8,128)(2,1)}, bf16[2,2,2,2,32,2560]{5,4,3,2,1,0:T(8,128)(2,1)}, u32[]{:S(2)}, u32[]{:S(2)}) collective-permute-start(bf16[2,2,2,2,32,2560]{5,4,3,2,1,0:T(8,128)(2,1)} %pad_maximum_fusion.9), channel_id=1, source_target_pairs={{0,1},{1,0},{2,3},{3,2},{4,5},{5,4},{6,7},{7,6},{8,9},{9,8},{10,11... | collective-permute-start | bytes 7864328 | tf_op jit(solution)/shard_map/ppermute | solution.py:21
  199.0 34.5 %collective-permute-start.24 = (bf16[2,2,2,2,32,2560]{5,4,0,1,3,2:T(8,128)(2,1)}, bf16[2,2,2,2,32,2560]{5,4,0,1,3,2:T(8,128)(2,1)}, u32[]{:S(2)}, u32[]{:S(2)}) collective-permute-start(bf16[2,2,2,2,32,2560]{5,4,0,1,3,2:T(8,128)(2,1)} %pad_maximum_fusion.10), channel_id=1, source_target_pairs={{0,1},{1,0},{2,3},{3,2},{4,5},{5,4},{6,7},{7,6},{8,9},{9,8},{10,11... | collective-permute-start | bytes 7864328 | tf_op jit(solution)/shard_map/ppermute | solution.py:21
  216.7 5.5 collective-permute-start.22
  346.6 18.1 %collective-permute-start.26 = (bf16[2,2,2,2,32,2560]{5,4,0,1,3,2:T(8,128)(2,1)}, bf16[2,2,2,2,32,2560]{5,4,0,1,3,2:T(8,128)(2,1)S(1)}, u32[]{:S(2)}, u32[]{:S(2)}) collective-permute-start(bf16[2,2,2,2,32,2560]{5,4,0,1,3,2:T(8,128)(2,1)} %copy_bitcast_fusion), channel_id=1, source_target_pairs={{0,1},{1,0},{2,3},{3,2},{4,5},{5,4},{6,7},{7,6},{8,9},{9,8},{10,11... | collective-permute-start | bytes 7864328 | tf_op jit(solution)/shard_map/ppermute | solution.py:21
  346.8 18.8 %collective-permute-start.25 = (bf16[2,2,2,2,32,2560]{5,4,3,2,1,0:T(8,128)(2,1)}, bf16[2,2,2,2,32,2560]{5,4,3,2,1,0:T(8,128)(2,1)}, u32[]{:S(2)}, u32[]{:S(2)}) collective-permute-start(bf16[2,2,2,2,32,2560]{5,4,3,2,1,0:T(8,128)(2,1)} %dynamic-slice_bitcast_fusion), channel_id=1, source_target_pairs={{0,1},{1,0},{2,3},{3,2},{4,5},{5,4},{6,7},{7,6},{8,9},{9,8},{10,11... | collective-permute-start | bytes 7864328 | tf_op jit(solution)/shard_map/ppermute | solution.py:21
  373.4 7.4 %collective-permute-start.29 = (f32[2,1,1024]{2,1,0:T(1,128)S(1)}, f32[2,1,1024]{2,1,0:T(1,128)S(1)}, u32[]{:S(2)}, u32[]{:S(2)}) collective-permute-start(f32[2,1,1024]{2,1,0:T(1,128)S(1)} %slice.381), channel_id=1, source_target_pairs={{1,0},{2,1},{3,2},{5,4},{6,5},{7,6},{9,8},{10,9},{11,10},{13,12},{... | collective-permute-start | bytes 24584 | tf_op jit(solution)/shard_map/ppermute | solution.py:274
  375.9 37.4 %collective-permute-start.28 = (bf16[2,2,2,32,2560]{4,3,0,1,2:T(8,128)(2,1)}, bf16[2,2,2,32,2560]{4,3,0,1,2:T(8,128)(2,1)}, u32[]{:S(2)}, u32[]{:S(2)}) collective-permute-start(bf16[2,2,2,32,2560]{4,3,0,1,2:T(8,128)(2,1)} %dynamic-slice_bitcast_fusion.1), channel_id=1, source_target_pairs={{0,4},{4,0},{1,5},{5,1},{2,6},{6,2},{3,7},{7,3},{8,12},{12,8},{9,1... | collective-permute-start | bytes 3932168 | tf_op jit(solution)/shard_map/ppermute | solution.py:21
  378.3 36.8 %collective-permute-start.27 = (bf16[2,2,2,32,2560]{4,3,2,1,0:T(8,128)(2,1)}, bf16[2,2,2,32,2560]{4,3,2,1,0:T(8,128)(2,1)}, u32[]{:S(2)}, u32[]{:S(2)}) collective-permute-start(bf16[2,2,2,32,2560]{4,3,2,1,0:T(8,128)(2,1)} %dynamic-slice_bitcast_fusion.2), channel_id=1, source_target_pairs={{0,2},{2,0},{1,3},{3,1},{4,6},{6,4},{5,7},{7,5},{8,10},{10,8},{9,1... | collective-permute-start | bytes 3932168 | tf_op jit(solution)/shard_map/ppermute | solution.py:21
  418.3 31.7 %collective-permute-start.31 = (bf16[2,2,32,2560]{3,2,0,1:T(8,128)(2,1)S(1)}, bf16[2,2,32,2560]{3,2,0,1:T(8,128)(2,1)}, u32[]{:S(2)}, u32[]{:S(2)}) collective-permute-start(bf16[2,2,32,2560]{3,2,0,1:T(8,128)(2,1)S(1)} %dynamic-slice_bitcast_fusion.4), channel_id=1, source_target_pairs={{0,2},{2,0},{1,3},{3,1},{4,6},{6,4},{5,7},{7,5},{8,10},{10,8},{9,1... | collective-permute-start | bytes 1966088 | tf_op jit(solution)/shard_map/ppermute | solution.py:21
  419.0 32.4 %collective-permute-start.30 = (bf16[2,2,32,2560]{3,2,1,0:T(8,128)(2,1)}, bf16[2,2,32,2560]{3,2,1,0:T(8,128)(2,1)}, u32[]{:S(2)}, u32[]{:S(2)}) collective-permute-start(bf16[2,2,32,2560]{3,2,1,0:T(8,128)(2,1)} %dynamic-slice_bitcast_fusion.5), channel_id=1, source_target_pairs={{0,4},{4,0},{1,5},{5,1},{2,6},{6,2},{3,7},{7,3},{8,12},{12,8},{9,1... | collective-permute-start | bytes 1966088 | tf_op jit(solution)/shard_map/ppermute | solution.py:21
  421.2 32.3 %collective-permute-start.32 = (bf16[2,2,2,2,32,1024]{5,4,3,2,1,0:T(8,128)(2,1)}, bf16[2,2,2,2,32,1024]{5,4,3,2,1,0:T(8,128)(2,1)}, u32[]{:S(2)}, u32[]{:S(2)}) collective-permute-start(bf16[2,2,2,2,32,1024]{5,4,3,2,1,0:T(8,128)(2,1)} %dynamic-slice_bitcast_fusion.3), channel_id=1, source_target_pairs={{0,1},{1,0},{2,3},{3,2},{4,5},{5,4},{6,7},{7,6},{8,9},{9,8},{10,11... | collective-permute-start | bytes 3145736 | tf_op jit(solution)/shard_map/ppermute | solution.py:21
  471.7 10.6 %collective-permute-start.34 = (bf16[2,32,2560]{2,1,0:T(8,128)(2,1)S(1)}, bf16[2,32,2560]{2,1,0:T(8,128)(2,1)S(1)}, u32[]{:S(2)}, u32[]{:S(2)}) collective-permute-start(bf16[2,32,2560]{2,1,0:T(8,128)(2,1)S(1)} %dynamic-slice_bitcast_fusion.10), channel_id=1, source_target_pairs={{0,8},{8,0},{1,9},{9,1},{2,10},{10,2},{3,11},{11,3},{4,12},{12,4},... | collective-permute-start | bytes 983048 | tf_op jit(solution)/shard_map/ppermute | solution.py:21
  473.5 15.3 %collective-permute-start.33 = (bf16[2,32,2560]{2,1,0:T(8,128)(2,1)S(1)}, bf16[2,32,2560]{2,1,0:T(8,128)(2,1)S(1)}, u32[]{:S(2)}, u32[]{:S(2)}) collective-permute-start(bf16[2,32,2560]{2,1,0:T(8,128)(2,1)S(1)} %dynamic-slice_bitcast_fusion.11), channel_id=1, source_target_pairs={{0,8},{8,0},{1,9},{9,1},{2,10},{10,2},{3,11},{11,3},{4,12},{12,4},... | collective-permute-start | bytes 983048 | tf_op jit(solution)/shard_map/ppermute | solution.py:21
  476.0 13.8 %collective-permute-start.35 = (bf16[2,2,2,32,1024]{4,3,2,1,0:T(8,128)(2,1)S(1)}, bf16[2,2,2,32,1024]{4,3,2,1,0:T(8,128)(2,1)S(1)}, u32[]{:S(2)}, u32[]{:S(2)}) collective-permute-start(bf16[2,2,2,32,1024]{4,3,2,1,0:T(8,128)(2,1)S(1)} %dynamic-slice_bitcast_fusion.9), channel_id=1, source_target_pairs={{0,2},{2,0},{1,3},{3,1},{4,6},{6,4},{5,7},{7,5},{8,10},{10,8},{9,1... | collective-permute-start | bytes 1572872 | tf_op jit(solution)/shard_map/ppermute | solution.py:21
  477.7 13.4 %collective-permute-start.36 = (bf16[2,2,2,2,32,1024]{5,4,0,1,3,2:T(8,128)(2,1)S(1)}, bf16[2,2,2,2,32,1024]{5,4,0,1,3,2:T(8,128)(2,1)S(1)}, u32[]{:S(2)}, u32[]{:S(2)}) collective-permute-start(bf16[2,2,2,2,32,1024]{5,4,0,1,3,2:T(8,128)(2,1)S(1)} %copy_bitcast_fusion.3), channel_id=1, source_target_pairs={{0,1},{1,0},{2,3},{3,2},{4,5},{5,4},{6,7},{7,6},{8,9},{9,8},{10,11... | collective-permute-start | bytes 3145736 | tf_op jit(solution)/shard_map/ppermute | solution.py:21
  491.6 13.9 %collective-permute-start.38 = (bf16[32,2560]{1,0:T(8,128)(2,1)S(1)}, bf16[32,2560]{1,0:T(8,128)(2,1)S(1)}, u32[]{:S(2)}, u32[]{:S(2)}) collective-permute-start(bf16[32,2560]{1,0:T(8,128)(2,1)S(1)} %dynamic-slice_bitcast_fusion.16), channel_id=1, source_target_pairs={{0,16},{16,0},{1,17},{17,1},{2,18},{18,2},{3,19},{19,3},{4,20},{20... | collective-permute-start | bytes 491528 | tf_op jit(solution)/shard_map/ppermute | solution.py:21
  492.6 16.1 %collective-permute-start.37 = (bf16[32,2560]{1,0:T(8,128)(2,1)S(1)}, bf16[32,2560]{1,0:T(8,128)(2,1)S(1)}, u32[]{:S(2)}, u32[]{:S(2)}) collective-permute-start(bf16[32,2560]{1,0:T(8,128)(2,1)S(1)} %dynamic-slice_bitcast_fusion.17), channel_id=1, source_target_pairs={{0,16},{16,0},{1,17},{17,1},{2,18},{18,2},{3,19},{19,3},{4,20},{20... | collective-permute-start | bytes 491528 | tf_op jit(solution)/shard_map/ppermute | solution.py:21
  499.6 9.3 %collective-permute-start.39 = (bf16[2,2,32,1024]{3,2,1,0:T(8,128)(2,1)S(1)}, bf16[2,2,32,1024]{3,2,1,0:T(8,128)(2,1)S(1)}, u32[]{:S(2)}, u32[]{:S(2)}) collective-permute-start(bf16[2,2,32,1024]{3,2,1,0:T(8,128)(2,1)S(1)} %dynamic-slice_bitcast_fusion.15), channel_id=1, source_target_pairs={{0,4},{4,0},{1,5},{5,1},{2,6},{6,2},{3,7},{7,3},{8,12},{12,8},{9,1... | collective-permute-start | bytes 786440 | tf_op jit(solution)/shard_map/ppermute | solution.py:21
  501.0 17.1 %collective-permute-start.40 = (bf16[2,2,2,32,1024]{4,3,0,1,2:T(8,128)(2,1)S(1)}, bf16[2,2,2,32,1024]{4,3,0,1,2:T(8,128)(2,1)S(1)}, u32[]{:S(2)}, u32[]{:S(2)}) collective-permute-start(bf16[2,2,2,32,1024]{4,3,0,1,2:T(8,128)(2,1)S(1)} %dynamic-slice_bitcast_fusion.8), channel_id=1, source_target_pairs={{0,4},{4,0},{1,5},{5,1},{2,6},{6,2},{3,7},{7,3},{8,12},{12,8},{9,1... | collective-permute-start | bytes 1572872 | tf_op jit(solution)/shard_map/ppermute | solution.py:21
  518.3 12.6 %collective-permute-start.43 = (bf16[2,32,1024]{2,1,0:T(8,128)(2,1)S(1)}, bf16[2,32,1024]{2,1,0:T(8,128)(2,1)S(1)}, u32[]{:S(2)}, u32[]{:S(2)}) collective-permute-start(bf16[2,32,1024]{2,1,0:T(8,128)(2,1)S(1)} %dynamic-slice_bitcast_fusion.21), channel_id=1, source_target_pairs={{0,8},{8,0},{1,9},{9,1},{2,10},{10,2},{3,11},{11,3},{4,12},{12,4},... | collective-permute-start | bytes 393224 | tf_op jit(solution)/shard_map/ppermute | solution.py:21
  519.1 11.9 %collective-permute-start.44 = (bf16[2,2,32,1024]{3,2,0,1:T(8,128)(2,1)S(1)}, bf16[2,2,32,1024]{3,2,0,1:T(8,128)(2,1)S(1)}, u32[]{:S(2)}, u32[]{:S(2)}) collective-permute-start(bf16[2,2,32,1024]{3,2,0,1:T(8,128)(2,1)S(1)} %dynamic-slice_bitcast_fusion.14), channel_id=1, source_target_pairs={{0,2},{2,0},{1,3},{3,1},{4,6},{6,4},{5,7},{7,5},{8,10},{10,8},{9,1... | collective-permute-start | bytes 786440 | tf_op jit(solution)/shard_map/ppermute | solution.py:21
  519.5 12.7 %collective-permute-start.45 = (bf16[2,32,2560]{2,1,0:T(8,128)(2,1)S(1)}, bf16[2,32,2560]{2,1,0:T(8,128)(2,1)S(1)}, u32[]{:S(2)}, u32[]{:S(2)}) collective-permute-start(bf16[2,32,2560]{2,1,0:T(8,128)(2,1)S(1)} %pad_maximum_fusion.36), channel_id=1, source_target_pairs={{0,2},{2,0},{1,3},{3,1},{4,6},{6,4},{5,7},{7,5},{8,10},{10,8},{9,1... | collective-permute-start | bytes 983048 | tf_op jit(solution)/shard_map/ppermute | solution.py:21
  521.4 11.7 %collective-permute-start.42 = (bf16[2,2,2,2,32,1024]{5,4,0,1,3,2:T(8,128)(2,1)S(1)}, bf16[2,2,2,2,32,1024]{5,4,0,1,3,2:T(8,128)(2,1)S(1)}, u32[]{:S(2)}, u32[]{:S(2)}) collective-permute-start(bf16[2,2,2,2,32,1024]{5,4,0,1,3,2:T(8,128)(2,1)S(1)} %copy_bitcast_fusion.1), channel_id=1, source_target_pairs={{0,1},{1,0},{2,3},{3,2},{4,5},{5,4},{6,7},{7,6},{8,9},{9,8},{10,11... | collective-permute-start | bytes 3145736 | tf_op jit(solution)/shard_map/ppermute | solution.py:21
  521.6 12.0 %collective-permute-start.41 = (bf16[2,2,2,2,32,1024]{5,4,0,1,2,3:T(8,128)(2,1)S(1)}, bf16[2,2,2,2,32,1024]{5,4,0,1,2,3:T(8,128)(2,1)S(1)}, u32[]{:S(2)}, u32[]{:S(2)}) collective-permute-start(bf16[2,2,2,2,32,1024]{5,4,0,1,2,3:T(8,128)(2,1)S(1)} %copy_bitcast_fusion.2), channel_id=1, source_target_pairs={{0,1},{1,0},{2,3},{3,2},{4,5},{5,4},{6,7},{7,6},{8,9},{9,8},{10,11... | collective-permute-start | bytes 3145736 | tf_op jit(solution)/shard_map/ppermute | solution.py:21
  542.2 9.9 %collective-permute-start.51 = (f32[2,1,1024]{2,1,0:T(1,128)S(1)}, f32[2,1,1024]{2,1,0:T(1,128)S(1)}, u32[]{:S(2)}, u32[]{:S(2)}) collective-permute-start(f32[2,1,1024]{2,1,0:T(1,128)S(1)} %slice.388), channel_id=1, source_target_pairs={{1,0},{2,1},{3,2},{5,4},{6,5},{7,6},{9,8},{10,9},{11,10},{13,12},{... | collective-permute-start | bytes 24584 | tf_op jit(solution)/shard_map/ppermute | solution.py:274
  544.1 18.3 %collective-permute-start.48 = (bf16[32,1024]{1,0:T(8,128)(2,1)}, bf16[32,1024]{1,0:T(8,128)(2,1)S(1)}, u32[]{:S(2)}, u32[]{:S(2)}) collective-permute-start(bf16[32,1024]{1,0:T(8,128)(2,1)} %dynamic-slice_bitcast_fusion.25), channel_id=1, source_target_pairs={{0,16},{16,0},{1,17},{17,1},{2,18},{18,2},{3,19},{19,3},{4,20},{20... | collective-permute-start | bytes 196616 | tf_op jit(solution)/shard_map/ppermute | solution.py:21
  546.7 17.2 %collective-permute-start.49 = (bf16[2,32,1024]{2,1,0:T(8,128)(2,1)}, bf16[2,32,1024]{2,1,0:T(8,128)(2,1)}, u32[]{:S(2)}, u32[]{:S(2)}) collective-permute-start(bf16[2,32,1024]{2,1,0:T(8,128)(2,1)} %dynamic-slice_bitcast_fusion.20), channel_id=1, source_target_pairs={{0,8},{8,0},{1,9},{9,1},{2,10},{10,2},{3,11},{11,3},{4,12},{12,4},... | collective-permute-start | bytes 393224 | tf_op jit(solution)/shard_map/ppermute | solution.py:21
  549.9 15.1 %collective-permute-start.47 = (bf16[2,2,2,32,1024]{4,3,0,1,2:T(8,128)(2,1)}, bf16[2,2,2,32,1024]{4,3,0,1,2:T(8,128)(2,1)}, u32[]{:S(2)}, u32[]{:S(2)}) collective-permute-start(bf16[2,2,2,32,1024]{4,3,0,1,2:T(8,128)(2,1)} %dynamic-slice_bitcast_fusion.6), channel_id=1, source_target_pairs={{0,4},{4,0},{1,5},{5,1},{2,6},{6,2},{3,7},{7,3},{8,12},{12,8},{9,1... | collective-permute-start | bytes 1572872 | tf_op jit(solution)/shard_map/ppermute | solution.py:21
  550.3 15.9 %collective-permute-start.46 = (bf16[2,2,2,32,1024]{4,3,0,1,2:T(8,128)(2,1)}, bf16[2,2,2,32,1024]{4,3,0,1,2:T(8,128)(2,1)}, u32[]{:S(2)}, u32[]{:S(2)}) collective-permute-start(bf16[2,2,2,32,1024]{4,3,0,1,2:T(8,128)(2,1)} %dynamic-slice_bitcast_fusion.7), channel_id=1, source_target_pairs={{0,2},{2,0},{1,3},{3,1},{4,6},{6,4},{5,7},{7,5},{8,10},{10,8},{9,1... | collective-permute-start | bytes 1572872 | tf_op jit(solution)/shard_map/ppermute | solution.py:21
  552.0 23.9 %collective-permute-start.56 = (bf16[256,1024]{1,0:T(8,128)(2,1)}, bf16[256,1024]{1,0:T(8,128)(2,1)}, u32[]{:S(2)}, u32[]{:S(2)}) collective-permute-start(bf16[256,1024]{1,0:T(8,128)(2,1)} %reduce-scatter.2.cloned.1.call-done), channel_id=1, source_target_pairs={{0,2},{2,0},{1,3},{3,1},{4,6},{6,4},{5,7},{7,5},{8,10},{10,8},{9,1... | collective-permute-start | bytes 1572872 | tf_op jit(solution)/shard_map/ppermute | solution.py:21
  562.4 14.9 %collective-permute-start.50 = (bf16[2,2,32,2560]{3,2,1,0:T(8,128)(2,1)}, bf16[2,2,32,2560]{3,2,1,0:T(8,128)(2,1)S(1)}, u32[]{:S(2)}, u32[]{:S(2)}) collective-permute-start(bf16[2,2,32,2560]{3,2,1,0:T(8,128)(2,1)} %pad_maximum_fusion.30), channel_id=1, source_target_pairs={{0,1},{1,0},{2,3},{3,2},{4,5},{5,4},{6,7},{7,6},{8,9},{9,8},{10,11... | collective-permute-start | bytes 1966088 | tf_op jit(solution)/shard_map/ppermute | solution.py:21
  578.0 8.8 %collective-permute-start.54 = (bf16[32,1024]{1,0:T(8,128)(2,1)S(1)}, bf16[32,1024]{1,0:T(8,128)(2,1)S(1)}, u32[]{:S(2)}, u32[]{:S(2)}) collective-permute-start(bf16[32,1024]{1,0:T(8,128)(2,1)S(1)} %dynamic-slice_bitcast_fusion.24), channel_id=1, source_target_pairs={{0,16},{16,0},{1,17},{17,1},{2,18},{18,2},{3,19},{19,3},{4,20},{20... | collective-permute-start | bytes 196616 | tf_op jit(solution)/shard_map/ppermute | solution.py:21
  580.3 6.4 %collective-permute-start.55 = (f32[12,1024]{1,0:T(8,128)S(1)}, f32[12,1024]{1,0:T(8,128)S(1)}, u32[]{:S(2)}, u32[]{:S(2)}) collective-permute-start(f32[12,1024]{1,0:T(8,128)S(1)} %stack.535), channel_id=1, source_target_pairs={{0,16},{16,0},{1,17},{17,1},{2,18},{18,2},{3,19},{19,3},{4,20},{20... | collective-permute-start | bytes 147464 | tf_op jit(solution)/shard_map/ppermute | solution.py:21
  581.0 7.2 %collective-permute-start.53 = (bf16[2,2,32,1024]{3,2,0,1:T(8,128)(2,1)S(1)}, bf16[2,2,32,1024]{3,2,0,1:T(8,128)(2,1)S(1)}, u32[]{:S(2)}, u32[]{:S(2)}) collective-permute-start(bf16[2,2,32,1024]{3,2,0,1:T(8,128)(2,1)S(1)} %dynamic-slice_bitcast_fusion.12), channel_id=1, source_target_pairs={{0,2},{2,0},{1,3},{3,1},{4,6},{6,4},{5,7},{7,5},{8,10},{10,8},{9,1... | collective-permute-start | bytes 786440 | tf_op jit(solution)/shard_map/ppermute | solution.py:21
  582.2 6.4 %collective-permute-start.52 = (bf16[2,2,32,1024]{3,2,0,1:T(8,128)(2,1)S(1)}, bf16[2,2,32,1024]{3,2,0,1:T(8,128)(2,1)S(1)}, u32[]{:S(2)}, u32[]{:S(2)}) collective-permute-start(bf16[2,2,32,1024]{3,2,0,1:T(8,128)(2,1)S(1)} %dynamic-slice_bitcast_fusion.13), channel_id=1, source_target_pairs={{0,4},{4,0},{1,5},{5,1},{2,6},{6,2},{3,7},{7,3},{8,12},{12,8},{9,1... | collective-permute-start | bytes 786440 | tf_op jit(solution)/shard_map/ppermute | solution.py:21
  588.6 5.0 collective-permute-start.61
  589.8 5.0 collective-permute-start.59
  591.4 5.0 collective-permute-start.58
  592.2 5.6 collective-permute-start.57
  598.2 6.0 collective-permute-start.63
  600.7 5.2 collective-permute-start.62
  609.0 5.0 collective-permute-start.68
  (141 other events, 2132.2 us)
Sparse Core Ops, SparseCore 0:
  29.0 106.7 all-gather.6
  307.3 108.6 reduce-scatter.1

commit v2 on v1

v2 whole, which is shorter than its diff:
```python
import functools

import jax
import jax.numpy as jnp
from jax import lax
from jax.experimental import pallas as pl
from jax.experimental.layout import Layout, with_layout_constraint
from jax.experimental.pallas import tpu as pltpu
from jax.sharding import PartitionSpec as P

D = 1024
EPS = 1e-05
F32 = jnp.float32
BF16 = jnp.bfloat16


LIGHT = pl.CostEstimate(flops=1 << 20, bytes_accessed=1 << 16, transcendentals=0)


def axes_of(letter, size):
    return tuple(f"{letter}{bit}" for bit in reversed(range(size.bit_length() - 1)))


def swap(value, key):
    return lax.ppermute(value, key, [(0, 1), (1, 0)])


def place(held, key):
    rank = lambda k: (k[0] == "s", -int(k[1:]))
    return sum(1 for other in held if rank(other) < rank(key))


def join(mine, other, key, at):
    first = lax.axis_index(key) == 0
    return jnp.stack(
        [jnp.where(first, mine, other), jnp.where(first, other, mine)], axis=at
    )


def half(value, which, at):
    return lax.dynamic_index_in_dim(value, which, at, keepdims=False)


def add_low(mine, other):
    return (mine.astype(F32) + other.astype(F32)).astype(BF16)


def tie(*values):
    return lax.optimization_barrier(values)


def row_major(value):
    return with_layout_constraint(value, Layout(tuple(range(value.ndim))))


class Moving:
    def start(self, key):
        self.prepare(key)
        self.go()

    def go(self):
        self.got = swap(self.send, self.key)

    def finish(self):
        pass


class Plain(Moving):
    def __init__(self, value, key):
        self.send, self.key = value, key


class Growing(Moving):
    def __init__(self, value):
        self.value, self.held = value, []

    def prepare(self, key):
        self.key, self.send = key, self.value

    def finish(self):
        at = place(self.held, self.key)
        self.held.append(self.key)
        self.value = join(self.value, self.got, self.key, at)


class Shrinking(Moving):
    def __init__(self, parts, merge, held):
        self.parts, self.merge, self.held = parts, merge, list(held)

    def prepare(self, key):
        self.key = key
        self.held.remove(key)
        self.at = place(self.held, key)
        self.bit = lax.axis_index(key)
        self.send = self.merge([half(p, 1 - self.bit, self.at) for p in self.parts])

    def finish(self):
        self.value = add_low(self.merge([half(p, self.bit, self.at) for p in self.parts]), self.got)
        self.parts, self.merge = [self.value], only


class Summing(Moving):
    def __init__(self, value):
        self.value = value

    def prepare(self, key):
        self.key, self.send = key, self.value

    def finish(self):
        self.value = self.value + self.got


def fire(items, *others):
    tied = tie(*[item.send for item in items], *others)
    for item, send in zip(items, tied):
        item.send = send
        item.go()
    return tied[len(items) :]


def only(parts):
    (part,) = parts
    return part


def stacked(parts):
    return jnp.stack(parts, axis=-3)


def settle(items, *others):
    tied = tie(*[item.got for item in items], *others)
    for item, got in zip(items, tied):
        item.got = got
        item.finish()
    return tied[len(items) :]


ROWS = 8


def fwd_kernel(k_ref, v_ref, r_ref, rate_ref, u_ref, a0_ref, b0_ref, w_ref, a_ref, b_ref):
    rate = rate_ref[...]
    boost = jnp.exp(u_ref[...])
    width = rate.shape[1]
    row = lax.broadcasted_iota(jnp.int32, (ROWS, width), 0)
    rowf = row.astype(F32)
    falling = jnp.exp(-rowf * rate)
    one = jnp.exp(-rate)
    steps = [(s, jnp.where(row >= s, jnp.exp(-s * rate), 0.0)) for s in (1, 2, 4)]
    inner = row >= 1

    def scan(tile, carry):
        before = jnp.where(inner, pltpu.roll(tile, 1, 0), 0.0)
        for s, factor in steps:
            before = before + factor * pltpu.roll(before, s, 0)
        before = before + falling * carry
        after = one * before[ROWS - 1 :, :] + tile[ROWS - 1 :, :]
        return before, after

    def tile_of(key, val, recept, carry):
        num, den = carry
        power = jnp.exp(key)
        num_before, num = scan(power * val, num)
        den_before, den = scan(power, den)
        now = boost * power
        mixed = (num_before + now * val) / (den_before + now)
        return (jax.nn.sigmoid(recept) * mixed, num_before, den_before), (num, den)

    def body(i, carry):
        at = pl.ds(pl.multiple_of(i * (2 * ROWS), 2 * ROWS), 2 * ROWS)
        key, val, recept = k_ref[at, :], v_ref[at, :].astype(F32), r_ref[at, :].astype(F32)
        low, carry = tile_of(key[:ROWS], val[:ROWS], recept[:ROWS], carry)
        high, carry = tile_of(key[ROWS:], val[ROWS:], recept[ROWS:], carry)
        for ref, a, b in zip((w_ref, a_ref, b_ref), low, high):
            ref[at, :] = jnp.concatenate([a, b], axis=0).astype(ref.dtype)
        return carry

    lax.fori_loop(
        0, k_ref.shape[0] // (2 * ROWS), body, (a0_ref[...], b0_ref[...]), unroll=2
    )


def bwd_kernel(
    k_ref, v_ref, a_ref, b_ref, p_ref, rate_ref, u_ref, ga_ref, gb_ref,
    dk_ref, dv_ref, first_ref, decay_ref,
):
    rate = rate_ref[...]
    boost = jnp.exp(u_ref[...])
    width = rate.shape[1]
    row = lax.broadcasted_iota(jnp.int32, (ROWS, width), 0)
    rowf = row.astype(F32)
    trailing = jnp.exp(-(ROWS - 1.0 - rowf) * rate)
    one = jnp.exp(-rate)
    steps = [(s, jnp.where(row < ROWS - s, jnp.exp(-s * rate), 0.0)) for s in (1, 2, 4)]
    inner = row < ROWS - 1

    def scan(tile, carry):
        later = jnp.where(inner, pltpu.roll(tile, ROWS - 1, 0), 0.0)
        for s, factor in steps:
            later = later + factor * pltpu.roll(later, ROWS - s, 0)
        later = later + trailing * carry
        before = one * later[:1, :] + tile[:1, :]
        return later, before

    def tile_of(tiles, carry):
        num, den, first, decay = carry
        key, val, num_before, den_before, p = tiles
        power = jnp.exp(key)
        now = boost * power
        q = -p * (num_before + now * val) / (den_before + now)
        num_later, num = scan(p, num)
        den_later, den = scan(q, den)
        diagonal = now * (val * p + q)
        d_key = power * (val * num_later + den_later) + diagonal
        d_val = power * num_later + now * p
        first = first + diagonal
        decay = decay + (num_later * num_before + den_later * den_before)
        return (d_key, d_val), (num, den, first, decay)

    count = k_ref.shape[0] // (2 * ROWS)

    def body(i, carry):
        at = pl.ds(pl.multiple_of((count - 1 - i) * (2 * ROWS), 2 * ROWS), 2 * ROWS)
        tiles = [ref[at, :].astype(F32) for ref in (k_ref, v_ref, a_ref, b_ref, p_ref)]
        high, carry = tile_of([tile[ROWS:] for tile in tiles], carry)
        low, carry = tile_of([tile[:ROWS] for tile in tiles], carry)
        for ref, a, b in zip((dk_ref, dv_ref), low, high):
            ref[at, :] = jnp.concatenate([a, b], axis=0).astype(BF16)
        return carry

    zero = jnp.zeros((ROWS, width), F32)
    done = lax.fori_loop(0, count, body, (ga_ref[...], gb_ref[...], zero, zero), unroll=2)
    first_ref[...] = done[2]
    decay_ref[...] = done[3]


def share_kernel(
    da_ref, w_ref, k_ref, v_ref, r_ref, a_ref, b_ref, rate_ref, u_ref,
    p_ref, dr_ref, ga_ref, gb_ref, dw_ref,
):
    dw_ref[...] = lax.dot_general(
        da_ref[...], w_ref[...], (((1,), (1,)), ((), ())), preferred_element_type=F32
    )
    rate = rate_ref[...]
    boost = jnp.exp(u_ref[...])
    rows = 2 * ROWS
    rowf = lax.broadcasted_iota(jnp.int32, (rows, rate.shape[1]), 0).astype(F32)
    near = jnp.exp(-rowf * rate)

    def body(i, carry):
        ga, gb = carry
        at = pl.ds(pl.multiple_of(i * rows, rows), rows)
        now = boost * jnp.exp(k_ref[at, :])
        inverse = 1.0 / (b_ref[at, :].astype(F32) + now)
        mixed = (a_ref[at, :].astype(F32) + now * v_ref[at, :].astype(F32)) * inverse
        gate = jax.nn.sigmoid(r_ref[at, :].astype(F32))
        d_mixed = dw_ref[at, :] * gate
        dr_ref[at, :] = (d_mixed * mixed * (1.0 - gate)).astype(BF16)
        p_low = (d_mixed * inverse).astype(BF16)
        p_ref[at, :] = p_low
        p = p_low.astype(F32)
        q = -p * mixed
        fall = near * jnp.exp(-(i * rows).astype(F32) * rate)
        return ga + fall * p, gb + fall * q

    zero = jnp.zeros((rows, rate.shape[1]), F32)
    ga, gb = lax.fori_loop(0, k_ref.shape[0] // rows, body, (zero, zero), unroll=2)
    ga_ref[...] = ga[:ROWS] + ga[ROWS:]
    gb_ref[...] = gb[:ROWS] + gb[ROWS:]


WIDTH = 256


def wkv_specs(rows):
    big = pl.BlockSpec((rows, WIDTH), lambda s, c: (s, c))
    row = pl.BlockSpec((1, WIDTH), lambda s, c: (0, c))
    state = pl.BlockSpec((None, 1, WIDTH), lambda s, c: (s, 0, c))
    partial = pl.BlockSpec((None, ROWS, WIDTH), lambda s, c: (s, 0, c))
    return big, row, state, partial


def wkv_forward(keys, vals, recepts, rate, first, num, den, seqs):
    total = keys.shape[0]
    big, row, state, _ = wkv_specs(total // seqs)
    cells = total * D
    return pl.pallas_call(
        fwd_kernel,
        grid=(seqs, D // WIDTH),
        in_specs=[big, big, big, row, row, state, state],
        out_specs=[big, big, big],
        out_shape=[
            jax.ShapeDtypeStruct((total, D), BF16),
            jax.ShapeDtypeStruct((total, D), F32),
            jax.ShapeDtypeStruct((total, D), F32),
        ],
        compiler_params=pltpu.CompilerParams(vmem_limit_bytes=58 << 20),
        cost_estimate=LIGHT,
    )(keys, vals, recepts, rate, first, num, den)


def wkv_backward(keys, vals, num_before, den_before, p, rate, first, num, den, seqs):
    total = keys.shape[0]
    big, row, state, partial = wkv_specs(total // seqs)
    cells = total * D
    return pl.pallas_call(
        bwd_kernel,
        grid=(seqs, D // WIDTH),
        in_specs=[big, big, big, big, big, row, row, state, state],
        out_specs=[big, big, partial, partial],
        out_shape=[
            jax.ShapeDtypeStruct((total, D), BF16),
            jax.ShapeDtypeStruct((total, D), BF16),
            jax.ShapeDtypeStruct((seqs, ROWS, D), F32),
            jax.ShapeDtypeStruct((seqs, ROWS, D), F32),
        ],
        compiler_params=pltpu.CompilerParams(vmem_limit_bytes=58 << 20),
        cost_estimate=LIGHT,
    )(keys, vals, num_before, den_before, p, rate, first, num, den)


def share_back(d_attn, weight, keys, vals, recepts, num_before, den_before, rate, first, seqs):
    total = keys.shape[0]
    span = total // seqs
    big, row, _, partial = wkv_specs(span)
    cells = total * D
    return pl.pallas_call(
        share_kernel,
        grid=(seqs, D // WIDTH),
        in_specs=[
            pl.BlockSpec((span, D), lambda s, c: (s, 0)),
            pl.BlockSpec((WIDTH, D), lambda s, c: (c, 0)),
            big, big, big, big, big, row, row,
        ],
        out_specs=[big, big, partial, partial],
        out_shape=[
            jax.ShapeDtypeStruct((total, D), BF16),
            jax.ShapeDtypeStruct((total, D), BF16),
            jax.ShapeDtypeStruct((seqs, ROWS, D), F32),
            jax.ShapeDtypeStruct((seqs, ROWS, D), F32),
        ],
        scratch_shapes=[pltpu.VMEM((span, WIDTH), F32)],
        compiler_params=pltpu.CompilerParams(vmem_limit_bytes=58 << 20),
        cost_estimate=LIGHT,
    )(d_attn, weight, keys, vals, recepts, num_before, den_before, rate, first)


PIECES = 8


def load_pieces(refs, held, sems):
    left, right = refs[:4], refs[4:]
    per = PIECES // held.shape[0]
    width = held.shape[2] // per
    copies = []
    for p in range(4):
        for side, ref in enumerate((left[p], right[p % 2].at[p // 2])):
            i = 2 * p + side
            to = held.at[i // per, :, pl.ds((i % per) * width, width)]
            copies.append(pltpu.make_async_copy(ref, to, sems.at[i]))
    return copies


def feed_kernel(s_ref, left_ref, x_ref, *rest):
    refs = rest[:6]
    fv_ref, xr_ref, fr_ref, mid_ref, cot_ref = rest[6:11]
    sq_ref, out_ref, dval_ref, dgate_ref, sums = rest[11:16]
    held, held_v, acc, gate_acc, sems, sems_v = rest[16:]
    copies = load_pieces(refs, held, sems)
    deep = held_v.shape[1]
    copies_v = [
        pltpu.make_async_copy(fv_ref.at[pl.ds(h * deep, deep)], held_v.at[h], sems_v.at[h])
        for h in range(2)
    ]
    first = pl.program_id(0) == 0
    width = held.shape[2]

    @pl.when(first)
    def _():
        for copy in copies + copies_v:
            copy.start()

    for p in range(4):

        @pl.when(first)
        def _(p=p):
            copies[2 * p].wait()
            copies[2 * p + 1].wait()

        hidden = jnp.maximum(jnp.dot(x_ref[...], held[p], preferred_element_type=F32), 0.0)
        at = pl.multiple_of(jnp.bitwise_xor(s_ref[0], p) * width, width)
        sq_ref[:, pl.ds(at, width)] = (hidden * hidden).astype(BF16)

    gate_acc[...] = jnp.dot(xr_ref[...], fr_ref[...], preferred_element_type=F32)
    total = None
    for h in range(2):

        @pl.when(first)
        def _(h=h):
            copies_v[h].wait()

        part = jnp.dot(sq_ref[:, pl.ds(h * deep, deep)], held_v[h], preferred_element_type=F32)
        total = part if total is None else total + part
    acc[...] = total

    left = left_ref[pl.program_id(0)]
    sums[...] = jnp.zeros_like(sums)

    def body(i, _):
        start = pl.multiple_of(i * 2 * ROWS, 2 * ROWS)
        at = pl.ds(start, 2 * ROWS)
        rows = start + lax.broadcasted_iota(jnp.int32, (2 * ROWS, 1), 0)
        keep = rows < left
        gate = jax.nn.sigmoid(gate_acc[at, :])
        feed = jnp.where(keep, gate * acc[at, :], 0.0)
        result = jnp.where(keep, mid_ref[at, :], 0.0) + feed
        g = jnp.where(keep, cot_ref[at, :].astype(F32), 0.0)
        out_ref[at, :] = result.astype(BF16)
        dval_ref[at, :] = (g * gate).astype(BF16)
        dgate_ref[at, :] = (g * feed * (1.0 - gate)).astype(BF16)
        sums[0] += fold(result * result)
        sums[1] += fold(feed * feed)
        return 0

    lax.fori_loop(0, mid_ref.shape[0] // (2 * ROWS), body, 0, unroll=2)


def feed_forward(my_seq, left, inputs, pieces, weight, gate_inputs, gate_weight, middle, cotangent, seqs):
    total = inputs.shape[0]
    width = 2 * pieces[0].shape[1]
    span = total // seqs
    ff = 4 * width
    big = pl.BlockSpec((span, D), lambda i, *_: (i, 0))
    return pl.pallas_call(
        feed_kernel,
        grid_spec=pltpu.PrefetchScalarGridSpec(
            num_scalar_prefetch=2,
            grid=(seqs,),
            in_specs=[big]
            + [pl.BlockSpec(memory_space=pl.ANY)] * 7
            + [big, pl.BlockSpec((D, D), lambda i, *_: (0, 0), pipeline_mode=pl.Buffered(1)), big, big],
            out_specs=[
                pl.BlockSpec((span, ff), lambda i, *_: (i, 0)), big, big, big,
                pl.BlockSpec((None, 2, ROWS, D), lambda i, *_: (i, 0, 0, 0)),
            ],
            scratch_shapes=[
                pltpu.VMEM((4, D, width), BF16),
                pltpu.VMEM((2, 2 * width, D), BF16),
                pltpu.VMEM((span, D), F32),
                pltpu.VMEM((span, D), F32),
                pltpu.SemaphoreType.DMA((PIECES,)),
                pltpu.SemaphoreType.DMA((2,)),
            ],
        ),
        out_shape=[
            jax.ShapeDtypeStruct((total, ff), BF16),
            jax.ShapeDtypeStruct((total, D), BF16),
            jax.ShapeDtypeStruct((total, D), BF16),
            jax.ShapeDtypeStruct((total, D), BF16),
            jax.ShapeDtypeStruct((seqs, 2, ROWS, D), F32),
        ],
        compiler_params=pltpu.CompilerParams(vmem_limit_bytes=60 << 20),
        cost_estimate=LIGHT,
    )(my_seq[None], left, inputs, *pieces, weight, gate_inputs, gate_weight, middle, cotangent)


CHUNK = 128


def stats_of(values):
    centre = values - jnp.mean(values, axis=-1, keepdims=True)
    inverse = lax.rsqrt(jnp.mean(centre * centre, axis=-1, keepdims=True) + EPS)
    return centre * inverse, inverse


def norm_back(grads, normed, inverse):
    return inverse * (
        grads
        - jnp.mean(grads, axis=-1, keepdims=True)
        - normed * jnp.mean(grads * normed, axis=-1, keepdims=True)
    )


def fold(values):
    return jnp.sum(values.reshape(values.shape[0] // ROWS, ROWS, values.shape[1]), axis=0)


def next_rows(values, carry):
    last = lax.broadcasted_iota(jnp.int32, values.shape, 0) == CHUNK - 1
    return jnp.where(last, carry, pltpu.roll(values, CHUNK - 1, 0))


def previous_rows(values, carry):
    first = lax.broadcasted_iota(jnp.int32, values.shape, 0) == 0
    return jnp.where(first, carry, pltpu.roll(values, 1, 0))


def mid_kernel(
    left_ref, w_ref, weight_ref, x_ref, gain_ref, bias_ref, mk_ref, mr_ref,
    mid_ref, fk_ref, fr_ref, first_ref, sq_ref,
):
    mid_ref[...] = jnp.dot(w_ref[...], weight_ref[...], preferred_element_type=F32)
    left = left_ref[pl.program_id(0)]
    gain, bias, mix_k, mix_r = gain_ref[...], bias_ref[...], mk_ref[...], mr_ref[...]
    sq_ref[...] = jnp.zeros_like(sq_ref)

    def body(i, carry):
        start = pl.multiple_of(i * CHUNK, CHUNK)
        at = pl.ds(start, CHUNK)
        attn = mid_ref[at, :]
        rows = start + lax.broadcasted_iota(jnp.int32, (CHUNK, 1), 0)
        sq_ref[...] += fold(jnp.where(rows < left, attn * attn, 0.0))
        middle = x_ref[at, :].astype(F32) + attn
        mid_ref[at, :] = middle
        b = stats_of(middle)[0] * gain + bias
        before = previous_rows(b, carry)
        fk_ref[at, :] = (b * mix_k + before * (1.0 - mix_k)).astype(BF16)
        fr_ref[at, :] = (b * mix_r + before * (1.0 - mix_r)).astype(BF16)

        @pl.when(i == 0)
        def _():
            first_ref[...] = b[:1, :]

        return b[CHUNK - 1 :, :]

    lax.fori_loop(0, x_ref.shape[0] // CHUNK, body, jnp.zeros_like(gain), unroll=2)


def mid_forward(left, weighted, weight, tokens, gain, bias, mix_k, mix_r, seqs):
    total = tokens.shape[0]
    span = total // seqs
    big = pl.BlockSpec((span, D), lambda s, _: (s, 0))
    row = pl.BlockSpec((1, D), lambda s, _: (0, 0))
    tile = lambda rows: pl.BlockSpec((None, rows, D), lambda s, _: (s, 0, 0))
    return pl.pallas_call(
        mid_kernel,
        grid_spec=pltpu.PrefetchScalarGridSpec(
            num_scalar_prefetch=1,
            grid=(seqs,),
            in_specs=[big, pl.BlockSpec((D, D), lambda s, _: (0, 0)), big, row, row, row, row],
            out_specs=[big, big, big, tile(1), tile(ROWS)],
        ),
        out_shape=[
            jax.ShapeDtypeStruct((total, D), F32),
            jax.ShapeDtypeStruct((total, D), BF16),
            jax.ShapeDtypeStruct((total, D), BF16),
            jax.ShapeDtypeStruct((seqs, 1, D), F32),
            jax.ShapeDtypeStruct((seqs, ROWS, D), F32),
        ],
        compiler_params=pltpu.CompilerParams(vmem_limit_bytes=58 << 20),
        cost_estimate=LIGHT,
    )(left, weighted, weight, tokens, gain, bias, mix_k, mix_r)


def down_kernel(s_ref, left_ref, dval_ref, fv_ref, sq_ref, *rest):
    refs = rest[:6]
    gate_ref, fr_ref, mid_ref, cot_ref, gain_ref, bias_ref, mk_ref, mr_ref = rest[6:14]
    dh_ref, out_ref, low_ref, first_k, first_r, tail_ref, sums = rest[14:21]
    held, held_v, acc_k, acc_r, sems, sems_v = rest[21:]
    copies = load_pieces(refs, held, sems)
    width = held_v.shape[1]
    places = [pl.multiple_of(jnp.bitwise_xor(s_ref[0], p) * width, width) for p in range(4)]
    copies_v = [
        pltpu.make_async_copy(fv_ref.at[pl.ds(places[p], width)], held_v.at[p], sems_v.at[p])
        for p in range(4)
    ]
    first = pl.program_id(0) == 0
    back = (((1,), (1,)), ((), ()))

    @pl.when(first)
    def _():
        for copy in copies_v + copies:
            copy.start()

    for p in range(4):

        @pl.when(first)
        def _(p=p):
            copies_v[p].wait()

        for side in range(2):
            part = pl.ds(side * (width // 2), width // 2)
            d_sq = lax.dot_general(dval_ref[...], held_v[p, part, :], back, preferred_element_type=F32)
            at = pl.multiple_of(places[p] + side * (width // 2), width // 2)
            squared = sq_ref[:, pl.ds(at, width // 2)].astype(F32)
            twice = 2.0 * squared * lax.rsqrt(jnp.maximum(squared, 1e-37))
            dh_ref[p, :, part] = (twice * d_sq).astype(BF16)

    acc_r[...] = lax.dot_general(gate_ref[...], fr_ref[...], back, preferred_element_type=F32)
    for h in range(2):

        @pl.when(first)
        def _(h=h):
            for copy in copies[4 * h : 4 * h + 4]:
                copy.wait()

        part = lax.dot_general(
            jnp.concatenate([dh_ref[2 * h], dh_ref[2 * h + 1]], axis=1), held[h],
            back, preferred_element_type=F32,
        )
        acc_k[...] = part if h == 0 else acc_k[...] + part

    left = left_ref[pl.program_id(0)]
    gain, bias, mix_k, mix_r = gain_ref[...], bias_ref[...], mk_ref[...], mr_ref[...]
    sums[...] = jnp.zeros_like(sums)
    count = mid_ref.shape[0] // CHUNK

    def body(i, carry):
        later_k, later_r = carry
        start = pl.multiple_of((count - 1 - i) * CHUNK, CHUNK)
        at = pl.ds(start, CHUNK)
        d_fk, d_fr = acc_k[at, :], acc_r[at, :]
        next_k, next_r = next_rows(d_fk, later_k), next_rows(d_fr, later_r)
        n, inverse = stats_of(mid_ref[at, :])
        b = n * gain + bias
        db = d_fk * mix_k + next_k * (1.0 - mix_k) + d_fr * mix_r + next_r * (1.0 - mix_r)
        sums[0] += fold(b * (d_fk - next_k))
        sums[1] += fold(b * (d_fr - next_r))
        sums[2] += fold(n * db)
        sums[3] += fold(db)
        rows = start + lax.broadcasted_iota(jnp.int32, (CHUNK, 1), 0)
        g = jnp.where(rows < left, cot_ref[at, :].astype(F32), 0.0)
        d_middle = g + norm_back(db * gain, n, inverse)
        out_ref[at, :] = d_middle
        low_ref[at, :] = d_middle.astype(BF16)

        @pl.when(i == 0)
        def _():
            tail_ref[0] = d_middle[CHUNK - 1 :, :]
            tail_ref[1] = n[CHUNK - 1 :, :]
            tail_ref[2] = jnp.broadcast_to(inverse[CHUNK - 1 :, :], gain.shape)

        return d_fk[:1, :], d_fr[:1, :]

    zero = jnp.zeros_like(gain)
    first_k[...], first_r[...] = lax.fori_loop(0, count, body, (zero, zero), unroll=2)


def down(
    my_seq, left, grads, weight, squared, pieces, gate_grads, gate_weight,
    middle, cotangent, gain, bias, mix_k, mix_r, seqs,
):
    total, ff = squared.shape
    span = total // seqs
    width = ff // 4
    big = pl.BlockSpec((span, D), lambda s, *_: (s, 0))
    alone = pl.BlockSpec((span, D), lambda s, *_: (s, 0), pipeline_mode=pl.Buffered(1))
    row = pl.BlockSpec((1, D), lambda s, *_: (0, 0))
    one = pl.BlockSpec((None, 1, D), lambda s, *_: (s, 0, 0))
    return pl.pallas_call(
        down_kernel,
        grid_spec=pltpu.PrefetchScalarGridSpec(
            num_scalar_prefetch=2,
            grid=(seqs,),
            in_specs=[
                big,
                pl.BlockSpec(memory_space=pl.ANY),
                pl.BlockSpec((span, ff), lambda s, *_: (s, 0), pipeline_mode=pl.Buffered(1)),
            ]
            + [pl.BlockSpec(memory_space=pl.ANY)] * 6
            + [big, pl.BlockSpec((D, D), lambda s, *_: (0, 0), pipeline_mode=pl.Buffered(1)), alone, big]
            + [row] * 4,
            out_specs=[
                pl.BlockSpec((4, span, width), lambda s, *_: (0, s, 0)),
                big, big, one, one,
                pl.BlockSpec((None, 3, 1, D), lambda s, *_: (s, 0, 0, 0)),
                pl.BlockSpec((None, 4, ROWS, D), lambda s, *_: (s, 0, 0, 0)),
            ],
            scratch_shapes=[
                pltpu.VMEM((2, D, 2 * width), BF16),
                pltpu.VMEM((4, width, D), BF16),
                pltpu.VMEM((span, D), F32),
                pltpu.VMEM((span, D), F32),
                pltpu.SemaphoreType.DMA((PIECES,)),
                pltpu.SemaphoreType.DMA((4,)),
            ],
        ),
        out_shape=[
            jax.ShapeDtypeStruct((4, total, width), BF16),
            jax.ShapeDtypeStruct((total, D), F32),
            jax.ShapeDtypeStruct((total, D), BF16),
            jax.ShapeDtypeStruct((seqs, 1, D), F32),
            jax.ShapeDtypeStruct((seqs, 1, D), F32),
            jax.ShapeDtypeStruct((seqs, 3, 1, D), F32),
            jax.ShapeDtypeStruct((seqs, 4, ROWS, D), F32),
        ],
        compiler_params=pltpu.CompilerParams(vmem_limit_bytes=60 << 20),
        cost_estimate=LIGHT,
    )(
        my_seq[None], left, grads, weight, squared, *pieces, gate_grads, gate_weight,
        middle, cotangent, gain, bias, mix_k, mix_r,
    )


def mix_kernel(
    dk_ref, dv_ref, dr_ref, wk_ref, wv_ref, wr_ref, x_ref, dm_ref,
    gain_ref, bias_ref, mk_ref, mv_ref, mr_ref,
    out_ref, firsts, tail_ref, sums, acc,
):
    for i, (grads, weight) in enumerate(((dk_ref, wk_ref), (dv_ref, wv_ref), (dr_ref, wr_ref))):
        acc[i] = lax.dot_general(
            grads[...], weight[...], (((1,), (1,)), ((), ())), preferred_element_type=F32
        )
    gain, bias = gain_ref[...], bias_ref[...]
    mixes = (mk_ref[...], mv_ref[...], mr_ref[...])
    sums[...] = jnp.zeros_like(sums)
    count = x_ref.shape[0] // CHUNK

    def body(i, carry):
        start = pl.multiple_of((count - 1 - i) * CHUNK, CHUNK)
        at = pl.ds(start, CHUNK)
        n, inverse = stats_of(x_ref[at, :].astype(F32))
        a = n * gain + bias
        da, heads = None, []
        for j in range(3):
            d = acc[j, at, :]
            later = next_rows(d, carry[j])
            sums[j] += fold(a * (d - later))
            part = d * mixes[j] + later * (1.0 - mixes[j])
            da = part if da is None else da + part
            heads.append(d[:1, :])
        sums[3] += fold(n * da)
        sums[4] += fold(da)
        total = dm_ref[at, :] + norm_back(da * gain, n, inverse)
        out_ref[at, :] = total.astype(BF16)

        @pl.when(i == 0)
        def _():
            tail_ref[0] = total[CHUNK - 1 :, :]
            tail_ref[1] = n[CHUNK - 1 :, :]
            tail_ref[2] = jnp.broadcast_to(inverse[CHUNK - 1 :, :], gain.shape)

        return tuple(heads)

    zero = jnp.zeros_like(gain)
    heads = lax.fori_loop(0, count, body, (zero, zero, zero), unroll=2)
    for j in range(3):
        firsts[j] = heads[j]


def mix_back(d_keys, d_vals, d_recepts, w_k, w_v, w_r, tokens, d_middle, gain, bias, mix_k, mix_v, mix_r, seqs):
    total = tokens.shape[0]
    span = total // seqs
    big = pl.BlockSpec((span, D), lambda s: (s, 0))
    row = pl.BlockSpec((1, D), lambda s: (0, 0))
    full = pl.BlockSpec((D, D), lambda s: (0, 0))
    return pl.pallas_call(
        mix_kernel,
        grid=(seqs,),
        in_specs=[big, big, big, full, full, full, big, big] + [row] * 5,
        out_specs=[
            big,
            pl.BlockSpec((None, 3, 1, D), lambda s: (s, 0, 0, 0)),
            pl.BlockSpec((None, 3, 1, D), lambda s: (s, 0, 0, 0)),
            pl.BlockSpec((None, 5, ROWS, D), lambda s: (s, 0, 0, 0)),
        ],
        out_shape=[
            jax.ShapeDtypeStruct((total, D), BF16),
            jax.ShapeDtypeStruct((seqs, 3, 1, D), F32),
            jax.ShapeDtypeStruct((seqs, 3, 1, D), F32),
            jax.ShapeDtypeStruct((seqs, 5, ROWS, D), F32),
        ],
        scratch_shapes=[pltpu.VMEM((3, span, D), F32)],
        compiler_params=pltpu.CompilerParams(vmem_limit_bytes=58 << 20),
        cost_estimate=LIGHT,
    )(d_keys, d_vals, d_recepts, w_k, w_v, w_r, tokens, d_middle, gain, bias, mix_k, mix_v, mix_r)


def put_rows(values, rows, at):
    seqs = rows.shape[0]
    whole = values.reshape(seqs, values.shape[0] // seqs, D)
    return lax.dynamic_update_slice(whole, rows.astype(values.dtype), (0, at, 0)).reshape(values.shape)


def cut_kernel(_, k, v, r, o, fk1, fk2, kv_out, ro_out, f1_out, f2_out):
    kv_out[0], kv_out[1] = k[...], v[...]
    ro_out[0], ro_out[1] = r[...], o[...]
    f1_out[...], f2_out[...] = fk1[...], fk2[...]


def cut(my_seq, quarter, key, value, recept, output, feed_key):
    shard, ff = feed_key.shape
    part = pl.BlockSpec((quarter, D), lambda i, at: (at[0], 0))
    side = lambda which: pl.BlockSpec((shard, ff // PIECES), lambda i, at: (0, 2 * at[0] + which))
    full = lambda *shape: pl.BlockSpec(shape, lambda i, at: (0,) * len(shape))
    shapes = [(2, quarter, D), (2, quarter, D)] + [(shard, ff // PIECES)] * 2
    return pl.pallas_call(
        cut_kernel,
        grid_spec=pltpu.PrefetchScalarGridSpec(
            num_scalar_prefetch=1,
            grid=(1,),
            in_specs=[part] * 4 + [side(0), side(1)],
            out_specs=[full(*shape) for shape in shapes],
        ),
        out_shape=[jax.ShapeDtypeStruct(shape, BF16) for shape in shapes],
    )(my_seq[None], key, value, recept, output, feed_key, feed_key)


def dot(left, right):
    return jnp.dot(left, right, preferred_element_type=F32)


def dot_back(grads, weight):
    return lax.dot_general(grads, weight, (((1,), (1,)), ((), ())), preferred_element_type=F32)


def dot_weight(inputs, grads):
    return lax.dot_general(inputs, grads, (((0,), (0,)), ((), ())), preferred_element_type=F32)


def normalize(values):
    centre = values - jnp.mean(values, axis=-1, keepdims=True)
    spread = jnp.mean(centre * centre, axis=-1, keepdims=True)
    inverse = lax.rsqrt(spread + EPS)
    return centre * inverse, inverse


def from_behind(value, axes, by):
    count = lax.axis_size(axes)
    pairs = [(i, i + by) for i in range(count) if 0 <= i + by < count]
    return lax.ppermute(value, axes, pairs)


def shifted(rows, edge):
    return jnp.concatenate([edge, rows[:, :-1]], axis=1)


def pulled(rows, edge):
    return jnp.concatenate([rows[:, 1:], edge], axis=1)


def blend(now, before, share):
    return (now * share + before * (1.0 - share)).astype(BF16)


def earlier_state(decay, num, den, axes, backward):
    count = lax.axis_size(axes)
    mine = lax.axis_index(axes)
    packed = lax.all_gather(jnp.concatenate([num, den], axis=0), axes)
    seqs = num.shape[0]
    state = jnp.zeros_like(packed[0])
    for hop in range(count - 1):
        source = count - 1 - hop if backward else hop
        longer = decay * state + packed[source]
        keep = source > mine if backward else source < mine
        state = jnp.where(keep, longer, state)
    return state[:seqs, None, :], state[seqs:, None, :]


def per_device(
    dp_axes, seq_axes,
    tokens, cotangent, lengths, assignment,
    mix_norm_gain, mix_norm_bias, shift_key, shift_value, shift_recept, time_decay, time_first,
    key_weight, value_weight, recept_weight, output_weight,
    feed_norm_gain, feed_norm_bias, feed_shift_key, feed_shift_recept,
    feed_key_weight, feed_recept_weight, feed_value_weight,
):
    seqs, span, _ = tokens.shape
    total = seqs * span
    dp, seq = lax.axis_size(dp_axes), lax.axis_size(seq_axes)
    my_dp, my_seq = lax.axis_index(dp_axes), lax.axis_index(seq_axes)
    every = dp_axes + seq_axes
    z_axes, x = dp_axes[:-1], dp_axes[-1]
    y, c = seq_axes
    ff = feed_key_weight.shape[1]
    flat = lambda v: v.reshape(total, v.shape[-1])
    deep = lambda v: v.reshape(seqs, span, v.shape[-1])

    shard = D // dp
    quarter = shard // seq

    def own_rows(weight):
        return lax.dynamic_slice_in_dim(weight, my_seq * quarter, quarter, 0)

    hid = feed_value_weight.shape[0]
    kv, ro, f1, f2 = [
        Growing(part)
        for part in cut(
            my_seq, quarter, key_weight, value_weight, recept_weight, output_weight,
            feed_key_weight,
        )
    ]
    kv.start(z_axes[0])
    ro.start(z_axes[0])
    kv.value, tokens, *vectors = tie(
        kv.value, tokens,
        mix_norm_gain, mix_norm_bias, shift_key, shift_value, shift_recept, time_decay, time_first,
        feed_norm_gain, feed_norm_bias, feed_shift_key, feed_shift_recept,
    )
    vectors = Growing(jnp.stack(vectors))
    vectors.start(z_axes[0])
    edge1 = from_behind(tokens[:, -1:], seq_axes, 1)
    for z in z_axes[1:]:
        settle([kv, ro, vectors])
        kv.start(z)
        ro.start(z)
        vectors.start(z)
    f1.value, f2.value = settle([kv, ro, vectors], f1.value, f2.value)
    kv.start(x)
    ro.start(y)
    vectors.start(x)
    f1.start(z_axes[0])
    f2.start(z_axes[0])
    halves = lambda w: half(w.reshape(2, w.shape[0] // 2, D), lax.axis_index(c), 0)
    gathered = lambda w: lax.all_gather(w, dp_axes + (c,), axis=0, tiled=True)
    (fr_part,) = settle([kv, ro, vectors, f1, f2], halves(feed_recept_weight))
    w_fr = gathered(fr_part)
    kv.start(y)
    ro.start(x)
    for z in z_axes[1:]:
        f1.start(z)
        f2.start(z)
        if z != z_axes[-1]:
            settle([f1, f2])
    (fv_part,) = settle([f1, f2, kv, ro], halves(feed_value_weight))
    w_fv = gathered(fv_part)
    kv.start(c)
    ro.start(c)
    f1.start(x)
    f2y = swap(f2.value, y)
    (f2y,) = settle([kv, ro, f1], f2y)
    pick = lambda v, i: jnp.moveaxis(v, -3, 0)[i].reshape(D, D)
    w_k, w_v, w_r, w_o = pick(kv.value, 0), pick(kv.value, 1), pick(ro.value, 0), pick(ro.value, 1)
    f1_0 = row_major(f1.value).reshape(D, -1)
    f2.value = jnp.stack([f2.value, f2y], axis=len(f2.held))

    vectors = jnp.swapaxes(vectors.value.reshape(dp, 11, D // dp), 0, 1).reshape(11, D).astype(F32)
    gain1, bias1, mix_k, mix_v, mix_r, log_rate, first, gain2, bias2, fmix_k, fmix_r = [
        vectors[i : i + 1] for i in range(11)
    ]
    rate = jnp.exp(log_rate)
    lam = jnp.exp(-rate)

    slot_ids = jnp.arange(assignment.shape[0])
    my_slots = my_dp * seqs + jnp.arange(seqs)
    seq_ids = jnp.sum(jnp.where(slot_ids[None, :] == my_slots[:, None], assignment[None, :], 0), axis=1)
    my_lens = jnp.sum(jnp.where(slot_ids[None, :] == seq_ids[:, None], lengths[None, :], 0), axis=1)
    positions = my_seq * span + jnp.arange(span)
    valid = flat((positions[None, :] < my_lens[:, None]).astype(F32)[..., None])
    inside = (my_seq > 0).astype(F32)

    xin = tokens.astype(F32)
    edge1 = (normalize(edge1.astype(F32))[0] * gain1 + bias1) * inside
    n1, inv1 = normalize(xin)
    a = n1 * gain1 + bias1
    a_prev = shifted(a, edge1)
    key_in = flat(blend(a, a_prev, mix_k))
    value_in = flat(blend(a, a_prev, mix_v))
    recept_in = flat(blend(a, a_prev, mix_r))
    keys = dot(key_in, w_k)
    vals = dot(value_in, w_v)
    recepts = dot(recept_in, w_r)

    offsets = jnp.arange(span).astype(F32)[:, None]
    power = deep(jnp.exp(keys))
    left = jnp.exp(-(span - 1.0 - offsets) * rate)
    span_decay = jnp.exp(-span * rate)
    num_end = jnp.sum(left * power * deep(vals), axis=1)
    vals, recepts = vals.astype(BF16), recepts.astype(BF16)
    den_end = jnp.sum(left * power, axis=1)
    num0, den0 = earlier_state(span_decay, num_end, den_end, seq_axes, False)
    f1_y = Plain(f1_0, y)
    f2.prepare(x)
    num0, den0 = fire([f1_y, f2], num0, den0)
    weighted, num_before, den_before = wkv_forward(keys, vals, recepts, rate, first, num0, den0, seqs)
    (weighted,) = settle([f1_y, f2], weighted)
    f1_y = f1_y.got
    f2_0 = row_major(jnp.moveaxis(f2.value, -3, 0)).reshape(2, D, -1)
    f1_c, f1_yc, f2_c = Plain(f1_0, c), Plain(f1_y, c), Plain(f2_0, c)
    (weighted,) = fire([f1_c, f1_yc, f2_c], weighted)
    last_row = tokens[:, -1].astype(F32) + dot(deep(weighted)[:, -1], w_o)
    edge2 = from_behind(last_row[:, None], seq_axes, 1)
    left_rows = (my_lens - my_seq * span).astype(jnp.int32)
    flat_tokens = flat(tokens)
    middle, feed_key_in, feed_recept_in, b_first, attn_sq = mid_forward(
        left_rows, weighted, w_o, flat_tokens, gain2, bias2, fmix_k, fmix_r, seqs
    )

    edge2 = (normalize(edge2)[0] * gain2 + bias2) * inside
    feed_key_in = put_rows(feed_key_in, blend(b_first, edge2, fmix_k), 0)
    feed_recept_in = put_rows(feed_recept_in, blend(b_first, edge2, fmix_r), 0)
    (feed_key_in,) = settle([f1_c, f1_yc, f2_c], feed_key_in)
    f1_c, f1_yc, f2_c = f1_c.got, f1_yc.got, f2_c.got
    pieces = (f1_0, f1_c, f1_y, f1_yc, f2_0, f2_c)
    sq, block_out, d_fval, d_fgate, squares = feed_forward(
        my_seq, left_rows, feed_key_in, pieces, w_fv, feed_recept_in, w_fr, middle, flat(cotangent), seqs
    )
    block_out = deep(block_out)
    stats = jnp.stack([jnp.sum(squares[:, 0]), jnp.sum(attn_sq), jnp.sum(squares[:, 1])])

    gfv = dot_weight(sq, d_fval).astype(BF16)
    gfv = lax.psum_scatter(gfv, dp_axes + (c,), scatter_dimension=0, tiled=True)
    gfr = dot_weight(feed_recept_in, d_fgate).astype(BF16)
    dh, d_middle, d_attn, first_k, first_r, tail, sums2 = down(
        my_seq, left_rows, d_fval, w_fv, sq, pieces, d_fgate, w_fr,
        middle, flat(cotangent), gain2, bias2, fmix_k, fmix_r, seqs,
    )
    gfk_1 = dot_weight(feed_key_in, dh[1]).astype(BF16)
    gfk_3 = dot_weight(feed_key_in, dh[3]).astype(BF16)

    lead = (2,) * len(every)
    split = lambda g_: Shrinking([g_.reshape(lead + (quarter, D))], only, every)
    side = ff // PIECES
    got_1, got_3 = Plain(gfk_1, c), Plain(gfk_3, c)
    (dh,) = fire([got_1, got_3], dh)
    gfk_0 = dot_weight(feed_key_in, dh[0]).astype(BF16)
    gfk_2 = dot_weight(feed_key_in, dh[2]).astype(BF16)
    edge3 = from_behind(first_k * (1.0 - fmix_k) + first_r * (1.0 - fmix_r), seq_axes, -1)
    d_middle, gfk_0, gfk_2, tail, sums2 = settle([got_1, got_3], d_middle, gfk_0, gfk_2, tail, sums2)
    low = lambda mine, got, at: add_low(mine[:, at : at + side], got.got[:, at : at + side])
    by_dp = lambda g_: g_.reshape((2,) * len(dp_axes) + (shard, g_.shape[1]))
    got_a = Plain(low(gfk_2, got_3, 0), y)
    r2 = Shrinking([by_dp(low(gfk_0, got_1, side)), by_dp(low(gfk_2, got_3, side))], stacked, dp_axes)
    r2.prepare(x)
    (d_attn,) = fire([got_a, r2], d_attn)
    a_0 = low(gfk_0, got_1, 0)

    d_last = tail[:, 0] + norm_back(edge3 * gain2, tail[:, 1], tail[:, 2])
    d_middle = put_rows(d_middle, d_last, span - 1)
    d_attn = put_rows(d_attn, d_last.astype(BF16), span - 1)
    small2 = sums2.sum((0, 2)) + jnp.concatenate(
        [
            -jnp.sum(edge2 * first_k, axis=0), -jnp.sum(edge2 * first_r, axis=0),
            jnp.sum(tail[:, 1] * edge3, axis=0), jnp.sum(edge3, axis=0),
        ]
    )
    p, d_recepts, ga_part, gb_part = share_back(
        d_attn, w_o, keys, vals, recepts, num_before, den_before, rate, first, seqs
    )
    r_o = dot_weight(weighted, d_attn).astype(BF16)
    r_r = dot_weight(recept_in, d_recepts).astype(BF16)
    ga_part, r_o, r_r = settle([r2, got_a], ga_part, r_o, r_r)

    orf = jnp.concatenate([r_o, r_r, gfr], axis=1)
    orf = lax.psum_scatter(orf, dp_axes + (c,), scatter_dimension=0, tiled=True)
    r1 = Shrinking([by_dp(add_low(a_0, got_a.got))], only, dp_axes)
    r1.prepare(x)
    b_got = Plain(r2.value[..., 1, :, :], y)
    ga0, gb0 = earlier_state(span_decay, ga_part.sum(1), gb_part.sum(1), seq_axes, True)
    ga0, gb0 = fire([r1, b_got], ga0, gb0)
    d_keys, d_vals, first_part, decay_part = wkv_backward(
        keys, vals, num_before, den_before, p, rate, first, ga0, gb0, seqs
    )
    d_keys, d_vals, gfv, first_part, decay_part = settle(
        [r1, b_got], d_keys, d_vals, gfv, first_part, decay_part
    )
    z1, z2 = z_axes[-1], z_axes[:-1]
    rows_of = lambda g_: g_.reshape(lead + (quarter, D))
    r_kv = Shrinking(
        [
            rows_of(dot_weight(key_in, d_keys).astype(BF16)),
            rows_of(dot_weight(value_in, d_vals).astype(BF16)),
        ],
        stacked, every,
    )
    r_kv.prepare(c)
    r_f = Shrinking([r1.value, add_low(r2.value[..., 0, :, :], b_got.got)], stacked, r1.held)
    r_f.prepare(z1)
    gfv_got = Plain(gfv, y)
    small2, first_part, decay_part = fire([r_kv, r_f, gfv_got], small2, first_part, decay_part)
    small2 = jnp.concatenate(
        [
            -(lam * rate) * jnp.sum(decay_part, axis=(0, 1))[None], jnp.sum(first_part, axis=(0, 1))[None],
            small2, jnp.pad(stats, (0, D - 3))[None],
        ]
    )
    d_keys, small2 = settle([r_kv, gfv_got], d_keys, small2)

    r_kv.prepare(y)
    out_v = Growing(add_low(gfv, gfv_got.got))
    out_v.prepare(c)
    d_keys, d_middle = fire([r_kv, out_v], d_keys, d_middle)
    mix_outs = mix_back(
        d_keys, d_vals, d_recepts, w_k, w_v, w_r, flat_tokens, d_middle,
        gain1, bias1, mix_k, mix_v, mix_r, seqs,
    )
    input_grad, firsts, tail1, sums1 = settle([r_kv, r_f, out_v], *mix_outs)

    r_kv.prepare(x)
    for z in reversed(z2):
        r_f.prepare(z)
        if z != z2[0]:
            r_f.go()
            settle([r_f])
    (firsts,) = fire([r_kv, r_f], firsts)
    mixes = (mix_k, mix_v, mix_r)
    edge4 = from_behind(sum(firsts[:, i] * (1.0 - m) for i, m in enumerate(mixes)), seq_axes, -1)
    input_last = (tail1[:, 0] + norm_back(edge4 * gain1, tail1[:, 1], tail1[:, 2])).astype(BF16)
    input_grad = deep(put_rows(input_grad, input_last, span - 1))
    small1 = sums1.sum((0, 2)) + jnp.concatenate(
        [
            -jnp.sum(edge1[:, None] * firsts, axis=(0, 2)),
            jnp.sum(tail1[:, 1] * edge4, axis=0), jnp.sum(edge4, axis=0),
        ]
    )

    small = jnp.concatenate([small1, small2])
    small, input_grad = settle([r_kv, r_f], small, input_grad)
    out_f = Growing(r_f.value)
    out_f.start(y)
    small = Summing(small)
    r_kv.start(z1)
    small.start(c)
    (orf,) = settle([r_kv, small, out_f], orf)
    out_f.start(c)
    for z in reversed(z2):
        r_kv.start(z)
        if z != z2[0]:
            settle([r_kv])
    small.start(y)
    orf_got = swap(orf, y)
    (orf_got,) = settle([r_kv, small, out_f], orf_got)
    orf = add_low(orf, orf_got)
    orf_c = swap(orf, c)
    own = r_kv.value
    small.start(x)
    at_y, at_c = swap(own, y), swap(own, c)
    at_both = lax.ppermute(own, (y, c), [(i, 3 - i) for i in range(4)])
    at_y, at_c, at_both, orf_c = settle([small], at_y, at_c, at_both, orf_c)
    for z in (z1, *reversed(z2)):
        small.start(z)
        small.finish()
    small = small.value
    out_kv = join(join(own, at_c, c, 0), join(at_y, at_both, c, 0), y, 0)

    wide_out = lambda v, i: v[:, :, i].reshape(shard, -1)
    out_f = out_f.value.reshape(2 * seq, shard, side)
    grad_fk = jnp.concatenate([out_f[i] for i in range(2 * seq)], axis=1).astype(F32)
    grad_fv = out_v.value.reshape(hid, D).astype(F32)
    orf = join(orf, orf_c, c, 0).reshape(shard, 3 * D).astype(F32)
    grad_o, grad_r, grad_fr = [orf[:, i * D : i * D + D] for i in range(3)]
    grad_k, grad_v = [wide_out(out_kv, i).astype(F32) for i in range(2)]
    rows = lax.dynamic_slice_in_dim(small[:11], my_dp * shard, shard, 1)
    rms = jnp.sqrt(small[11, :3] / (jnp.sum(lengths).astype(F32) * D))
    v = [rows[i] for i in range(11)]
    return (
        block_out, input_grad,
        v[3], v[4], v[0], v[1], v[2], v[5], v[6],
        grad_k, grad_v, grad_r, grad_o,
        v[9], v[10], v[7], v[8],
        grad_fk, grad_fr, grad_fv,
        rms[0], rms[1], rms[2],
    )


def solution(mesh):
    dp_axes, seq_axes = axes_of("d", mesh.shape["dp"]), axes_of("s", mesh.shape["seq"])
    names = dp_axes + seq_axes
    fine = jax.sharding.Mesh(mesh.devices.reshape((2,) * len(names)), names)
    big, vec, mat = P(dp_axes, seq_axes, None), P(dp_axes), P(dp_axes, None)
    args = (big, big, P(), P()) + (vec,) * 7 + (mat,) * 4 + (vec,) * 4 + (mat,) * 3
    outs = (big, big) + (vec,) * 7 + (mat,) * 4 + (vec,) * 4 + (mat,) * 3 + (P(),) * 3
    return jax.shard_map(
        functools.partial(per_device, dp_axes, seq_axes),
        mesh=fine, in_specs=args, out_specs=outs, check_vma=False,
    )
```

time: 631 us -> 558 us (0.88)
  Pallas kernels: 26.5 us -> 161 us
  matrix products: 145 us -> 67.1 us
  other arithmetic: 134 us -> 78.1 us
  waiting for transfers between devices: 172 us -> 118 us
  starting transfers between devices: 70.5 us -> 59.7 us
    pallas_call x0 -> x6, Pallas kernels: none -> 133 us  [the longest x1 47.9 us: down(): pl.pallas_call(down_kernel, grid_spec=pltpu.PrefetchScalarGridSpec(num_sc...]
    ppermute x66 -> x50, waiting for transfers between devices: 172 us -> 118 us  [swap(): return lax.ppermute(value, key, [(0, 1), (1, 0)])]
    dot_general x9 -> x0, matrix products: 53.1 us -> none  [dot_back(): lax.dot_general(grads, weight, (((1,), (1,)), ((), ())), preferred_elemen...]
    dot_general x9 -> x4, matrix products: 50.4 us -> 13.1 us  [dot(): return jnp.dot(left, right, preferred_element_type=F32)]
    reduce_sum x7 -> x12, other arithmetic: 30.7 us -> 5.9 us  [the longest x1 1.46 us: per_device(): jnp.sum(attn_sq)]
    ppermute x66 -> x50, starting transfers between devices: 64.2 us -> 51.4 us  [swap(): return lax.ppermute(value, key, [(0, 1), (1, 0)])]
    dot_general x9 -> x10, matrix products: 41.6 us -> 54 us  [dot_weight(): lax.dot_general(inputs, grads, (((0,), (0,)), ((), ())), preferred_elemen...]
    concatenate x8 -> x3, other arithmetic: 16 us -> 4.18 us  [the longest x1 3.42 us: per_device(): orf = jnp.concatenate([r_o, r_r, gfr], axis=1)]
  transfers between devices with their start and end apart: 72 -> 59, of which waited for: 34 -> 24; matrix products, arithmetic and copies ran while one was open for 41% -> 28% of each run, Pallas kernels for 4% -> 23%
where the time goes in v2:
time: 558 us; the launch traced here: 551 us
  Pallas kernels  161 us (29%)
  waiting for transfers between devices  118 us (21%)
  other arithmetic  78.1 us (14%)
  matrix products  67.1 us (12%)
  starting transfers between devices  59.7 us (11%)
  local copies, waits for them, and re-layouts  39.7 us (7%)
  between operations  16.7 us (3%)
  blocking collectives  10.7 us (2%)
    ppermute x50, waiting for transfers between devices, swap(): return lax.ppermute(value, key, [(0, 1), (1, 0)])  118 us
    dot_general x10, matrix products, dot_weight(): lax.dot_general(inputs, grads, (((0,), (0,)), ((), ())), preferred_elemen...  54 us
    ppermute x50, starting transfers between devices, swap(): return lax.ppermute(value, key, [(0, 1), (1, 0)])  51.4 us
    pallas_call x1, Pallas kernels, down(): pl.pallas_call(down_kernel, grid_spec=pltpu.PrefetchScalarGridSpec(num_sc...  47.9 us
    pallas_call x1, Pallas kernels, feed_forward(): pl.pallas_call(feed_kernel, grid_spec=pltpu.PrefetchScalarGridSpec(num_sc...  34.6 us
    pallas_call x1, Pallas kernels, mix_back(): pl.pallas_call(mix_kernel, grid=(seqs,), in_specs=[big, big, big, full, f...  22.1 us
    another operation x45, other arithmetic, join(): jnp.stack([jnp.where(first, mine, other), jnp.where(first, other, mine)],...  19.9 us
    convert_element_type x14, other arithmetic, add_low(): return (mine.astype(F32) + other.astype(F32)).astype(BF16)  19.8 us
  transfers between devices with their start and end apart: 59, of which 24 were waited for; matrix products, arithmetic and copies ran while one was open for 28% of the time, Pallas kernels for 23%

profile of v2, /device:TPU:0, one launch (start us, length us, event | category | flops | bytes accessed | tf_op | source)
XLA Modules:
  0.0 551.5 jit_solution(15975445611257529747)
XLA Ops:
  7.4 2.0 shard_map.389
  9.3 4.0 collective-permute-start
  13.6 2.9 collective-permute-start.2
  16.5 9.2 %collective-permute-done.2 = bf16[11,128]{1,0:T(8,128)(2,1)S(1)} collective-permute-done((bf16[11,128]{1,0:T(8,128)(2,1)S(1)}, bf16[11,128]{1,0:T(8,128)(2,1)S(1)}, u32[]{:S(2)}, u32[]{:S(2)}) %collective-permute-start.2) | collective-permute-done | bytes 2848 | tf_op jit(solution)/shard_map/ppermute | solution.py:25
  30.7 10.3 %collective-permute-done.5 = bf16[2,11,128]{2,1,0:T(8,128)(2,1)S(1)} collective-permute-done((bf16[2,11,128]{2,1,0:T(8,128)(2,1)S(1)}, bf16[2,11,128]{2,1,0:T(8,128)(2,1)S(1)}, u32[]{:S(2)}, u32[]{:S(2)}) %collective-permute-start.5) | collective-permute-done | bytes 5664 | tf_op jit(solution)/shard_map/ppermute | solution.py:25
  46.1 3.3 collective-permute-start.9
  52.9 2.4 collective-permute-done.8
  55.3 3.3 collective-permute-done.9
  58.7 1.9 collective-permute-done.10
  69.6 8.8 %collective-permute-done.12 = bf16[2,128,512]{2,1,0:T(8,128)(2,1)} collective-permute-done((bf16[2,128,512]{2,1,0:T(8,128)(2,1)}, bf16[2,128,512]{2,1,0:T(8,128)(2,1)}, u32[]{:S(2)}, u32[]{:S(2)}) %collective-permute-start.12) | collective-permute-done | bytes 262176 | tf_op jit(solution)/shard_map/ppermute | solution.py:25
  78.4 4.5 collective-permute-done.11
  82.9 3.5 collective-permute-done.13
  86.4 3.7 collective-permute-done.14
  90.1 2.2 copy.128
  94.2 2.3 collective-permute-start.19
  106.7 1.9 collective-permute-start.15
  115.4 4.1 add_convert_fusion.1
  119.5 8.2 %collective-permute-done.18 = bf16[2,2,128,512]{3,2,1,0:T(8,128)(2,1)S(1)} collective-permute-done((bf16[2,2,128,512]{3,2,1,0:T(8,128)(2,1)S(1)}, bf16[2,2,128,512]{3,2,1,0:T(8,128)(2,1)S(1)}, u32[]{:S(2)}, u32[]{:S(2)}) %collective-permute-start.18) | collective-permute-done | bytes 524320 | tf_op jit(solution)/shard_map/ppermute | solution.py:25
  127.7 5.8 %collective-permute-done.17 = bf16[2,2,128,512]{3,2,0,1:T(8,128)(2,1)S(1)} collective-permute-done((bf16[2,2,128,512]{3,2,0,1:T(8,128)(2,1)S(1)}, bf16[2,2,128,512]{3,2,0,1:T(8,128)(2,1)S(1)}, u32[]{:S(2)}, u32[]{:S(2)}) %collective-permute-start.17) | collective-permute-done | bytes 524320 | tf_op jit(solution)/shard_map/ppermute | solution.py:25
  136.7 3.7 fusion.88
  140.3 4.7 multiply_reduce_fusion
  145.0 5.4 all-gather.2
  153.4 1.8 fusion.81
  156.7 3.7 convolution_convert_fusion.6.r_ref
  160.4 13.8 %shard_map.390 = (bf16[1024,1024]{1,0:T(8,128)(2,1)}, f32[1024,1024]{1,0:T(8,128)}, f32[1024,1024]{1,0:T(8,128)}) custom-call(f32[1024,1024]{1,0:T(8,128)} %get-tuple-element.475.k_ref, bf16[1024,1024]{1,0:T(8,128)(2,1)} %get-tuple-element.476.v_ref, bf16[1024,1024]{1,0:T(8,128)(2,1)} %convolution_convert_fusion.6.r_ref, f32[1,1024]{1,0:T(1,128)} %bitcast.554, ...), custom_call_target="tpu_custom_call" | custom-call | flops 1048576 | bytes 65536 | tf_op jit(solution)/shard_map/pallas_call | solution.py:287
  174.2 2.0 collective-permute-done.20.rest_2_
  176.2 13.0 %collective-permute-done.21 = bf16[2,2,2,128,512]{4,3,1,0,2:T(8,128)(2,1)S(1)} collective-permute-done((bf16[2,2,2,128,512]{4,3,1,0,2:T(8,128)(2,1)S(1)}, bf16[2,2,2,128,512]{4,3,1,0,2:T(8,128)(2,1)S(1)}, u32[]{:S(2)}, u32[]{:S(2)}) %collective-permute-start.21) | collective-permute-done | bytes 1048608 | tf_op jit(solution)/shard_map/ppermute | solution.py:25
  191.8 1.9 copy.136
  195.6 2.5 collective-permute-start.25
  199.3 11.2 %shard_map.391 = (f32[1024,1024]{1,0:T(8,128)}, bf16[1024,1024]{1,0:T(8,128)(2,1)}, bf16[1024,1024]{1,0:T(8,128)(2,1)}, f32[2,1,1024]{2,1,0:T(1,128)}, f32[2,8,1024]{2,1,0:T(8,128)}) custom-call(s32[2]{0:T(128)} %broadcast_subtract_fusion.5.left_ref, bf16[1024,1024]{1,0:T(8,128)(2,1)} %get-tuple-element.229.w_ref, bf16[1024,1024]{1,0:T(8,128)(2,1)} %bitcast.499, ...), custom_call_target="tpu_custom_call" | custom-call | flops 1048576 | bytes 65536 | tf_op jit(solution)/shard_map/pallas_call | solution.py:535
  216.5 34.6 %shard_map.392 = (bf16[1024,4096]{1,0:T(8,128)(2,1)}, bf16[1024,1024]{1,0:T(8,128)(2,1)}, bf16[1024,1024]{1,0:T(8,128)(2,1)}, bf16[1024,1024]{1,0:T(8,128)(2,1)}, f32[2,2,8,1024]{3,2,1,0:T(8,128)}) custom-call(s32[1]{0:T(128)} %bitcast._.s_ref, s32[2]{0:T(128)} %broadcast_subtract_fusion.5.left_ref, bf16[1024,1024]{1,0:T(8,128)(2,1)} %bitcast.535, ...), custom_call_target="tpu_custom_call" | custom-call | flops 1048576 | bytes 65536 | tf_op jit(solution)/shard_map/pallas_call | solution.py:434
  251.0 15.4 %convolution_convert_fusion = bf16[4096,1024]{1,0:T(8,128)(2,1)} fusion(bf16[1024,4096]{1,0:T(8,128)(2,1)} %get-tuple-element.242.sq_ref, bf16[1024,1024]{1,0:T(8,128)(2,1)} %get-tuple-element.241.dval_ref), kind=kOutput, calls=%fused_computation | convolution fusion | flops 8594128896 | bytes 18874368 | tf_op jit(solution)/shard_map/dot_general | solution.py:808
  266.5 47.9 %shard_map.393 = (bf16[4,1024,1024]{2,1,0:T(8,128)(2,1)}, f32[1024,1024]{1,0:T(8,128)}, bf16[1024,1024]{1,0:T(8,128)(2,1)}, f32[2,1,1024]{2,1,0:T(1,128)}, f32[2...) custom-call(s32[1]{0:T(128)} %bitcast._.s_ref, s32[2]{0:T(128)} %broadcast_subtract_fusion.5.left_ref, ...), custom_call_target="tpu_custom_call" | custom-call | flops 1048576 | bytes 65536 | tf_op jit(solution)/shard_map/pallas_call | solution.py:650
  314.4 5.4 fusion.21
  319.9 5.6 %fusion.18 = bf16[1024,1024]{1,0:T(8,128)(2,1)} fusion(bf16[1024,1024]{1,0:T(8,128)(2,1)S(1)} %bitcast.537, bf16[4,1024,1024]{2,1,0:T(8,128)(2,1)} %get-tuple-element.248), kind=kOutput, calls=%fused_computation.47 | convolution fusion | flops 2148532224 | bytes 6291456 | tf_op jit(solution)/shard_map/dot_general | solution.py:808
  327.5 5.3 convolution_convert_fusion.1
  332.9 4.1 fusion.27
  337.0 4.0 fusion.24
  341.1 3.9 add_convert_fusion.6
  349.7 2.6 collective-permute-start.29
  354.5 15.1 %shard_map.394 = (bf16[1024,1024]{1,0:T(8,128)(2,1)}, bf16[1024,1024]{1,0:T(8,128)(2,1)}, f32[2,8,1024]{2,1,0:T(8,128)}, f32[2,8,1024]{2,1,0:T(8,128)}) custom-call(bf16[1024,1024]{1,0:T(8,128)(2,1)} %bitcast.532, bf16[1024,1024]{1,0:T(8,128)(2,1)} %bitcast.500, f32[1024,1024]{1,0:T(8,128)} %get-tuple-element.475.k_ref, ...), custom_call_target="tpu_custom_call" | custom-call | flops 1048576 | bytes 65536 | tf_op jit(solution)/shard_map/pallas_call | solution.py:327
  370.6 5.5 convolution_convert_fusion.5
  376.1 3.8 convolution_convert_fusion.4
  380.7 5.2 all-gather.3
  386.6 2.4 add_convert_fusion.5
  389.1 1.7 add_convert_fusion.4
  392.7 3.4 pad_maximum_fusion
  397.4 14.8 %shard_map.395 = (bf16[1024,1024]{1,0:T(8,128)(2,1)}, bf16[1024,1024]{1,0:T(8,128)(2,1)}, f32[2,8,1024]{2,1,0:T(8,128)}, f32[2,8,1024]{2,1,0:T(8,128)}) custom-call(f32[1024,1024]{1,0:T(8,128)} %get-tuple-element.475.k_ref, bf16[1024,1024]{1,0:T(8,128)(2,1)} %get-tuple-element.476.v_ref, f32[1024,1024]{1,0:T(8,128)} %get-tuple-element.262.a_ref, ...), custom_call_target="tpu_custom_call" | custom-call | flops 1048576 | bytes 65536 | tf_op jit(solution)/shard_map/pallas_call | solution.py:306
  412.3 1.7 fusion.31
  416.0 2.4 convolution_convert_fusion.3
  418.4 2.4 convolution_convert_fusion.2
  420.8 1.8 constant_dynamic-slice_fusion.7
  427.6 2.0 select_maximum_fusion
  433.6 6.7 %collective-permute-done.34 = bf16[256,1024]{1,0:T(8,128)(2,1)} collective-permute-done((bf16[256,1024]{1,0:T(8,128)(2,1)}, bf16[256,1024]{1,0:T(8,128)(2,1)}, u32[]{:S(2)}, u32[]{:S(2)}) %collective-permute-start.34) | collective-permute-done | bytes 524320 | tf_op jit(solution)/shard_map/ppermute | solution.py:25
  441.6 2.9 add_convert_fusion
  451.2 22.1 %shard_map.396 = (bf16[1024,1024]{1,0:T(8,128)(2,1)}, f32[2,3,1,1024]{3,2,1,0:T(1,128)}, f32[2,3,1,1024]{3,2,1,0:T(1,128)}, f32[2,5,8,1024]{3,2,1,0:T(8,128)}) custom-call(bf16[1024,1024]{1,0:T(8,128)(2,1)} %get-tuple-element.301.dk_ref, bf16[1024,1024]{1,0:T(8,128)(2,1)} %get-tuple-element.280.dv_ref, bf16[1024,1024]{1,0:T(8,128)(2,1)} %get-tuple-element.265.dr_ref, ...), custom_call_target="tpu_custom_call" | custom-call | flops 1048576 | bytes 65536 | tf_op jit(solution)/shard_map/pallas_call | solution.py:747
  480.5 2.5 collective-permute-start.39
  487.2 14.8 %collective-permute-done.39 = bf16[2,128,512]{2,1,0:T(8,128)(2,1)S(1)} collective-permute-done((bf16[2,128,512]{2,1,0:T(8,128)(2,1)}, bf16[2,128,512]{2,1,0:T(8,128)(2,1)S(1)}, u32[]{:S(2)}, u32[]{:S(2)}) %collective-permute-start.39) | collective-permute-done | bytes 262176 | tf_op jit(solution)/shard_map/ppermute | solution.py:25
  506.5 4.3 collective-permute-done.41
  517.4 6.0 %collective-permute-done.44 = bf16[2,32,1024]{2,1,0:T(8,128)(2,1)S(1)} collective-permute-done((bf16[2,32,1024]{2,1,0:T(8,128)(2,1)S(1)}, bf16[2,32,1024]{2,1,0:T(8,128)(2,1)S(1)}, u32[]{:S(2)}, u32[]{:S(2)}) %collective-permute-start.44) | collective-permute-done | bytes 131104 | tf_op jit(solution)/shard_map/ppermute | solution.py:25
  523.3 1.8 collective-permute-done.47
  531.8 1.8 collective-permute-done.49
  533.6 1.8 collective-permute-start.53
  540.3 3.1 collective-permute-done.54
  (502 shorter events, 127.9 us)
Async XLA Ops:
  7.2 61.5 %copy-start = (bf16[512,1024]{1,0:T(8,128)(2,1)S(1)}, bf16[512,1024]{1,0:T(8,128)(2,1)}, u32[]{:S(2)}) copy-start(bf16[512,1024]{1,0:T(8,128)(2,1)} %param.43) | copy-start | bytes 3145732
  7.3 207.8 %all-gather.9.cloned.1.call-start = ((), (), s32[]{:S(2)}) async-start(), calls=%async_computation.3 | async-start | bytes 2228224 | tf_op jit(solution)/shard_map/all_gather | solution.py:905
  9.3 16.3 %collective-permute-start = (bf16[2,32,1024]{2,1,0:T(8,128)(2,1)}, bf16[2,32,1024]{2,1,0:T(8,128)(2,1)S(1)}, u32[]{:S(2)}, u32[]{:S(2)}) collective-permute-start(bf16[2,32,1024]{2,1,0:T(8,128)(2,1)} %get-tuple-element.181), channel_id=1, source_target_pairs={{0,16},{16,0},{1,17},{17,1},{2,18},{18,2},{3,19},{19,3},{4,20},{20... | collective-permute-start | bytes 393224 | tf_op jit(solution)/shard_map/ppermute | solution.py:25
  13.4 12.3 %collective-permute-start.1 = (bf16[2,32,1024]{2,1,0:T(8,128)(2,1)}, bf16[2,32,1024]{2,1,0:T(8,128)(2,1)S(1)}, u32[]{:S(2)}, u32[]{:S(2)}) collective-permute-start(bf16[2,32,1024]{2,1,0:T(8,128)(2,1)} %get-tuple-element.182), channel_id=1, source_target_pairs={{0,16},{16,0},{1,17},{17,1},{2,18},{18,2},{3,19},{19,3},{4,20},{20... | collective-permute-start | bytes 393224 | tf_op jit(solution)/shard_map/ppermute | solution.py:25
  13.6 12.1 %collective-permute-start.2 = (bf16[11,128]{1,0:T(8,128)(2,1)S(1)}, bf16[11,128]{1,0:T(8,128)(2,1)S(1)}, u32[]{:S(2)}, u32[]{:S(2)}) collective-permute-start(bf16[11,128]{1,0:T(8,128)(2,1)S(1)} %stack.328), channel_id=1, source_target_pairs={{0,16},{16,0},{1,17},{17,1},{2,18},{18,2},{3,19},{19,3},{4,20},{20... | collective-permute-start | bytes 8456 | tf_op jit(solution)/shard_map/ppermute | solution.py:25
  27.6 13.4 %collective-permute-start.3 = (bf16[2,2,32,1024]{3,2,1,0:T(8,128)(2,1)S(1)}, bf16[2,2,32,1024]{3,2,1,0:T(8,128)(2,1)S(1)}, u32[]{:S(2)}, u32[]{:S(2)}) collective-permute-start(bf16[2,2,32,1024]{3,2,1,0:T(8,128)(2,1)S(1)} %pad_maximum_fusion.21), channel_id=1, source_target_pairs={{0,8},{8,0},{1,9},{9,1},{2,10},{10,2},{3,11},{11,3},{4,12},{12,4},... | collective-permute-start | bytes 786440 | tf_op jit(solution)/shard_map/ppermute | solution.py:25
  28.5 12.5 %collective-permute-start.4 = (bf16[2,2,32,1024]{3,2,1,0:T(8,128)(2,1)S(1)}, bf16[2,2,32,1024]{3,2,1,0:T(8,128)(2,1)S(1)}, u32[]{:S(2)}, u32[]{:S(2)}) collective-permute-start(bf16[2,2,32,1024]{3,2,1,0:T(8,128)(2,1)S(1)} %pad_maximum_fusion.22), channel_id=1, source_target_pairs={{0,8},{8,0},{1,9},{9,1},{2,10},{10,2},{3,11},{11,3},{4,12},{12,4},... | collective-permute-start | bytes 786440 | tf_op jit(solution)/shard_map/ppermute | solution.py:25
  29.8 11.1 %collective-permute-start.5 = (bf16[2,11,128]{2,1,0:T(8,128)(2,1)S(1)}, bf16[2,11,128]{2,1,0:T(8,128)(2,1)S(1)}, u32[]{:S(2)}, u32[]{:S(2)}) collective-permute-start(bf16[2,11,128]{2,1,0:T(8,128)(2,1)S(1)} %pad_maximum_fusion.30), channel_id=1, source_target_pairs={{0,8},{8,0},{1,9},{9,1},{2,10},{10,2},{3,11},{11,3},{4,12},{12,4},... | collective-permute-start | bytes 16904 | tf_op jit(solution)/shard_map/ppermute | solution.py:25
  42.5 18.1 %collective-permute-start.6 = (bf16[2,2,2,32,1024]{4,3,2,0,1:T(8,128)(2,1)}, bf16[2,2,2,32,1024]{4,3,2,0,1:T(8,128)(2,1)S(1)}, u32[]{:S(2)}, u32[]{:S(2)}) collective-permute-start(bf16[2,2,2,32,1024]{4,3,2,0,1:T(8,128)(2,1)} %pad_maximum_fusion.14), channel_id=1, source_target_pairs={{0,4},{4,0},{1,5},{5,1},{2,6},{6,2},{3,7},{7,3},{8,12},{12,8},{9,1... | collective-permute-start | bytes 1572872 | tf_op jit(solution)/shard_map/ppermute | solution.py:25
  44.6 16.0 %collective-permute-start.7 = (bf16[2,2,2,32,1024]{4,3,2,0,1:T(8,128)(2,1)}, bf16[2,2,2,32,1024]{4,3,2,0,1:T(8,128)(2,1)S(1)}, u32[]{:S(2)}, u32[]{:S(2)}) collective-permute-start(bf16[2,2,2,32,1024]{4,3,2,0,1:T(8,128)(2,1)} %pad_maximum_fusion.15), channel_id=1, source_target_pairs={{0,2},{2,0},{1,3},{3,1},{4,6},{6,4},{5,7},{7,5},{8,10},{10,8},{9,1... | collective-permute-start | bytes 1572872 | tf_op jit(solution)/shard_map/ppermute | solution.py:25
  46.1 12.6 %collective-permute-start.9 = (bf16[128,512]{1,0:T(8,128)(2,1)S(1)}, bf16[128,512]{1,0:T(8,128)(2,1)S(1)}, u32[]{:S(2)}, u32[]{:S(2)}) collective-permute-start(bf16[128,512]{1,0:T(8,128)(2,1)S(1)} %copy-done.57), channel_id=1, source_target_pairs={{0,16},{16,0},{1,17},{17,1},{2,18},{18,2},{3,19},{19,3},{4,20},{20... | collective-permute-start | bytes 393224 | tf_op jit(solution)/shard_map/ppermute | solution.py:25
  49.4 11.1 %collective-permute-start.10 = (bf16[128,512]{1,0:T(8,128)(2,1)S(1)}, bf16[128,512]{1,0:T(8,128)(2,1)}, u32[]{:S(2)}, u32[]{:S(2)}) collective-permute-start(bf16[128,512]{1,0:T(8,128)(2,1)S(1)} %copy-done.59), channel_id=1, source_target_pairs={{0,16},{16,0},{1,17},{17,1},{2,18},{18,2},{3,19},{19,3},{4,20},{20... | collective-permute-start | bytes 393224 | tf_op jit(solution)/shard_map/ppermute | solution.py:25
  50.8 4.5 collective-permute-start.8
  60.6 154.6 %all-gather.7.cloned.1.call-start = ((), (), s32[]{:S(2)}) async-start(), calls=%async_computation.2 | async-start | bytes 8912896 | tf_op jit(solution)/shard_map/all_gather | solution.py:905
  61.9 24.5 %collective-permute-start.13 = (bf16[2,2,2,2,32,1024]{5,4,3,0,1,2:T(8,128)(2,1)}, bf16[2,2,2,2,32,1024]{5,4,3,0,1,2:T(8,128)(2,1)}, u32[]{:S(2)}, u32[]{:S(2)}) collective-permute-start(bf16[2,2,2,2,32,1024]{5,4,3,0,1,2:T(8,128)(2,1)} %pad_maximum_fusion.6), channel_id=1, source_target_pairs={{0,2},{2,0},{1,3},{3,1},{4,6},{6,4},{5,7},{7,5},{8,10},{10,8},{9,1... | collective-permute-start | bytes 3145736 | tf_op jit(solution)/shard_map/ppermute | solution.py:25
  63.6 26.4 %collective-permute-start.14 = (bf16[2,2,2,2,32,1024]{5,4,3,0,1,2:T(8,128)(2,1)}, bf16[2,2,2,2,32,1024]{5,4,3,0,1,2:T(8,128)(2,1)}, u32[]{:S(2)}, u32[]{:S(2)}) collective-permute-start(bf16[2,2,2,2,32,1024]{5,4,3,0,1,2:T(8,128)(2,1)} %pad_maximum_fusion.7), channel_id=1, source_target_pairs={{0,4},{4,0},{1,5},{5,1},{2,6},{6,2},{3,7},{7,3},{8,12},{12,8},{9,1... | collective-permute-start | bytes 3145736 | tf_op jit(solution)/shard_map/ppermute | solution.py:25
  65.9 12.5 %collective-permute-start.12 = (bf16[2,128,512]{2,1,0:T(8,128)(2,1)}, bf16[2,128,512]{2,1,0:T(8,128)(2,1)}, u32[]{:S(2)}, u32[]{:S(2)}) collective-permute-start(bf16[2,128,512]{2,1,0:T(8,128)(2,1)} %pad_maximum_fusion.24), channel_id=1, source_target_pairs={{0,8},{8,0},{1,9},{9,1},{2,10},{10,2},{3,11},{11,3},{4,12},{12,4},... | collective-permute-start | bytes 786440 | tf_op jit(solution)/shard_map/ppermute | solution.py:25
  67.3 15.6 %collective-permute-start.11 = (bf16[2,128,512]{2,1,0:T(8,128)(2,1)}, bf16[2,128,512]{2,1,0:T(8,128)(2,1)}, u32[]{:S(2)}, u32[]{:S(2)}) collective-permute-start(bf16[2,128,512]{2,1,0:T(8,128)(2,1)} %pad_maximum_fusion.23), channel_id=1, source_target_pairs={{0,8},{8,0},{1,9},{9,1},{2,10},{10,2},{3,11},{11,3},{4,12},{12,4},... | collective-permute-start | bytes 786440 | tf_op jit(solution)/shard_map/ppermute | solution.py:25
  90.1 322.2 %reduce-scatter.3.cloned.1.call-start = ((), (), s32[]{:S(2)}) async-start(), calls=%async_computation.4 | async-start | bytes 8912896 | tf_op jit(solution)/shard_map/reduce_scatter | solution.py:992
  94.2 5.7 %collective-permute-start.19 = (bf16[2,1,1024]{2,0,1:T(2,128)(2,1)}, bf16[2,1,1024]{2,0,1:T(2,128)(2,1)}, u32[]{:S(2)}, u32[]{:S(2)}) collective-permute-start(bf16[2,1,1024]{2,0,1:T(2,128)(2,1)} %slice.391), channel_id=1, source_target_pairs={{0,1},{1,2},{2,3},{4,5},{5,6},{6,7},{8,9},{9,10},{10,11},{12,13},{... | collective-permute-start | bytes 12296 | tf_op jit(solution)/shard_map/ppermute | solution.py:821
  103.8 46.8 %copy-start.68 = (f32[1,1024]{1,0:T(1,128)}, f32[1,1024]{1,0:T(1,128)S(1)}, u32[]{:S(2)}) copy-start(f32[1,1024]{1,0:T(1,128)S(1)} %multiply_exponential_fusion.1) | copy-start | bytes 12292
  104.5 87.3 %copy-start.66 = (f32[1,8,128]{2,1,0:T(8,128)}, f32[1,8,128]{2,1,0:T(8,128)S(1)}, u32[]{:S(2)}) copy-start(f32[1,8,128]{2,1,0:T(8,128)S(1)} %get-tuple-element.451) | copy-start | bytes 12292
  106.7 26.9 %collective-permute-start.15 = (bf16[2,2,2,2,2,32,1024]{6,5,4,0,1,3,2:T(8,128)(2,1)S(1)}, bf16[2,2,2,2,2,32,1024]{6,5,4,0,1,3,2:T(8,128)(2,1)S(1)}, u32[]{:S(2)}, u32[]{:S(2)}) collective-permute-start(bf16[2,2,2,2,2,32,1024]{6,5,4,0,1,3,2:T(8,128)(2,1)S(1)} %pad_maximum_fusion.2), channel_id=1, source_target_pairs={{0,1},{1,0},{2,3},{3,2},{4,5},{5,4},{6,7},{7,6},{8,9},{9,8},{10,11... | collective-permute-start | bytes 6291464 | tf_op jit(solution)/shard_map/ppermute | solution.py:25
  110.1 23.4 %collective-permute-start.16 = (bf16[2,2,2,2,2,32,1024]{6,5,4,0,1,3,2:T(8,128)(2,1)S(1)}, bf16[2,2,2,2,2,32,1024]{6,5,4,0,1,3,2:T(8,128)(2,1)S(1)}, u32[]{:S(2)}, u32[]{:S(2)}) collective-permute-start(bf16[2,2,2,2,2,32,1024]{6,5,4,0,1,3,2:T(8,128)(2,1)S(1)} %pad_maximum_fusion.3), channel_id=1, source_target_pairs={{0,1},{1,0},{2,3},{3,2},{4,5},{5,4},{6,7},{7,6},{8,9},{9,8},{10,11... | collective-permute-start | bytes 6291464 | tf_op jit(solution)/shard_map/ppermute | solution.py:25
  113.5 14.2 %collective-permute-start.18 = (bf16[2,2,128,512]{3,2,1,0:T(8,128)(2,1)S(1)}, bf16[2,2,128,512]{3,2,1,0:T(8,128)(2,1)S(1)}, u32[]{:S(2)}, u32[]{:S(2)}) collective-permute-start(bf16[2,2,128,512]{3,2,1,0:T(8,128)(2,1)S(1)} %get-tuple-element.408), channel_id=1, source_target_pairs={{0,2},{2,0},{1,3},{3,1},{4,6},{6,4},{5,7},{7,5},{8,10},{10,8},{9,1... | collective-permute-start | bytes 1572872 | tf_op jit(solution)/shard_map/ppermute | solution.py:25
  114.8 18.7 %collective-permute-start.17 = (bf16[2,2,128,512]{3,2,0,1:T(8,128)(2,1)S(1)}, bf16[2,2,128,512]{3,2,0,1:T(8,128)(2,1)S(1)}, u32[]{:S(2)}, u32[]{:S(2)}) collective-permute-start(bf16[2,2,128,512]{3,2,0,1:T(8,128)(2,1)S(1)} %pad_maximum_fusion.16), channel_id=1, source_target_pairs={{0,4},{4,0},{1,5},{5,1},{2,6},{6,2},{3,7},{7,3},{8,12},{12,8},{9,1... | collective-permute-start | bytes 1572872 | tf_op jit(solution)/shard_map/ppermute | solution.py:25
  133.8 64.3 %copy-start.5 = (bf16[2,2,2,128,512]{4,3,2,1,0:T(8,128)(2,1)}, bf16[2,2,2,128,512]{4,3,2,1,0:T(8,128)(2,1)S(1)}, u32[]{:S(2)}) copy-start(bf16[2,2,2,128,512]{4,3,2,1,0:T(8,128)(2,1)S(1)} %copy.126) | copy-start | bytes 3145732
  150.6 25.6 %collective-permute-start.20 = (bf16[1024,512]{1,0:T(8,128)(2,1)S(1)}, bf16[1024,512]{1,0:T(8,128)(2,1)}, u32[]{:S(2)}, u32[]{:S(2)}) collective-permute-start(bf16[1024,512]{1,0:T(8,128)(2,1)S(1)} %bitcast.504), channel_id=1, source_target_pairs={{0,2},{2,0},{1,3},{3,1},{4,6},{6,4},{5,7},{7,5},{8,10},{10,8},{9,1... | collective-permute-start | bytes 3145736 | tf_op jit(solution)/shard_map/ppermute | solution.py:25
  152.2 37.0 %collective-permute-start.21 = (bf16[2,2,2,128,512]{4,3,1,0,2:T(8,128)(2,1)S(1)}, bf16[2,2,2,128,512]{4,3,1,0,2:T(8,128)(2,1)S(1)}, u32[]{:S(2)}, u32[]{:S(2)}) collective-permute-start(bf16[2,2,2,128,512]{4,3,1,0,2:T(8,128)(2,1)S(1)} %pad_maximum_fusion.9), channel_id=1, source_target_pairs={{0,4},{4,0},{1,5},{5,1},{2,6},{6,2},{3,7},{7,3},{8,12},{12,8},{9,1... | collective-permute-start | bytes 3145736 | tf_op jit(solution)/shard_map/ppermute | solution.py:25
  190.9 24.2 %collective-permute-start.24 = (bf16[2,1024,512]{2,1,0:T(8,128)(2,1)}, bf16[2,1024,512]{2,1,0:T(8,128)(2,1)S(1)}, u32[]{:S(2)}, u32[]{:S(2)}) collective-permute-start(bf16[2,1024,512]{2,1,0:T(8,128)(2,1)} %bitcast.95.rest_4_), channel_id=1, source_target_pairs={{0,1},{1,0},{2,3},{3,2},{4,5},{5,4},{6,7},{7,6},{8,9},{9,8},{10,11... | collective-permute-start | bytes 6291464 | tf_op jit(solution)/shard_map/ppermute | solution.py:25
  195.6 14.9 %collective-permute-start.25 = (f32[2,1,1024]{2,1,0:T(1,128)S(1)}, f32[2,1,1024]{2,1,0:T(1,128)S(1)}, u32[]{:S(2)}, u32[]{:S(2)}) collective-permute-start(f32[2,1,1024]{2,1,0:T(1,128)S(1)} %broadcast_in_dim.42), channel_id=1, source_target_pairs={{0,1},{1,2},{2,3},{4,5},{5,6},{6,7},{8,9},{9,10},{10,11},{12,13},{... | collective-permute-start | bytes 24584 | tf_op jit(solution)/shard_map/ppermute | solution.py:821
  198.1 17.0 %collective-permute-start.22 = (bf16[1024,512]{1,0:T(8,128)(2,1)S(1)}, bf16[1024,512]{1,0:T(8,128)(2,1)}, u32[]{:S(2)}, u32[]{:S(2)}) collective-permute-start(bf16[1024,512]{1,0:T(8,128)(2,1)S(1)} %bitcast.505), channel_id=1, source_target_pairs={{0,1},{1,0},{2,3},{3,2},{4,5},{5,4},{6,7},{7,6},{8,9},{9,8},{10,11... | collective-permute-start | bytes 3145736 | tf_op jit(solution)/shard_map/ppermute | solution.py:25
  199.2 15.9 %collective-permute-start.23 = (bf16[1024,512]{1,0:T(8,128)(2,1)}, bf16[1024,512]{1,0:T(8,128)(2,1)}, u32[]{:S(2)}, u32[]{:S(2)}) collective-permute-start(bf16[1024,512]{1,0:T(8,128)(2,1)} %collective-permute-done.20.rest_2_), channel_id=1, source_target_pairs={{0,1},{1,0},{2,3},{3,2},{4,5},{5,4},{6,7},{7,6},{8,9},{9,8},{10,11... | collective-permute-start | bytes 3145736 | tf_op jit(solution)/shard_map/ppermute | solution.py:25
  266.5 239.0 %reduce-scatter.5.cloned.1.call-start = ((), (), s32[]{:S(2)}) async-start(), calls=%async_computation.5 | async-start | bytes 6684672 | tf_op jit(solution)/shard_map/reduce_scatter | solution.py:1035
  266.5 47.9 %copy-start.26 = (bf16[2,512,1024]{2,1,0:T(8,128)(2,1)S(1)}, bf16[2,512,1024]{2,1,0:T(8,128)(2,1)}, u32[]{:S(2)}) copy-start(bf16[2,512,1024]{2,1,0:T(8,128)(2,1)} %dynamic_update_slice.15) | copy-start | bytes 6291460
  325.5 15.6 %collective-permute-start.26 = (bf16[1024,1024]{1,0:T(8,128)(2,1)}, bf16[1024,1024]{1,0:T(8,128)(2,1)}, u32[]{:S(2)}, u32[]{:S(2)}) collective-permute-start(bf16[1024,1024]{1,0:T(8,128)(2,1)} %fusion.18), channel_id=1, source_target_pairs={{0,1},{1,0},{2,3},{3,2},{4,5},{5,4},{6,7},{7,6},{8,9},{9,8},{10,11... | collective-permute-start | bytes 6291464 | tf_op jit(solution)/shard_map/ppermute | solution.py:25
  326.0 15.1 %collective-permute-start.27 = (bf16[1024,1024]{1,0:T(8,128)(2,1)}, bf16[1024,1024]{1,0:T(8,128)(2,1)}, u32[]{:S(2)}, u32[]{:S(2)}) collective-permute-start(bf16[1024,1024]{1,0:T(8,128)(2,1)} %fusion.21), channel_id=1, source_target_pairs={{0,1},{1,0},{2,3},{3,2},{4,5},{5,4},{6,7},{7,6},{8,9},{9,8},{10,11... | collective-permute-start | bytes 6291464 | tf_op jit(solution)/shard_map/ppermute | solution.py:25
  326.1 26.2 %collective-permute-start.30 = (f32[2,1,1024]{2,1,0:T(1,128)S(1)}, f32[2,1,1024]{2,1,0:T(1,128)S(1)}, u32[]{:S(2)}, u32[]{:S(2)}) collective-permute-start(f32[2,1,1024]{2,1,0:T(1,128)S(1)} %get-tuple-element.463), channel_id=1, source_target_pairs={{1,0},{2,1},{3,2},{5,4},{6,5},{7,6},{9,8},{10,9},{11,10},{13,12},{... | collective-permute-start | bytes 24584 | tf_op jit(solution)/shard_map/ppermute | solution.py:821
  349.6 31.0 %collective-permute-start.28 = (bf16[2,2,2,128,512]{4,3,2,1,0:T(8,128)(2,1)}, bf16[2,2,2,128,512]{4,3,2,1,0:T(8,128)(2,1)S(1)}, u32[]{:S(2)}, u32[]{:S(2)}) collective-permute-start(bf16[2,2,2,128,512]{4,3,2,1,0:T(8,128)(2,1)} %pad_maximum_fusion.10), channel_id=1, source_target_pairs={{0,4},{4,0},{1,5},{5,1},{2,6},{6,2},{3,7},{7,3},{8,12},{12,8},{9,1... | collective-permute-start | bytes 3145736 | tf_op jit(solution)/shard_map/ppermute | solution.py:25
  349.7 30.9 %collective-permute-start.29 = (bf16[1024,512]{1,0:T(8,128)(2,1)}, bf16[1024,512]{1,0:T(8,128)(2,1)}, u32[]{:S(2)}, u32[]{:S(2)}) collective-permute-start(bf16[1024,512]{1,0:T(8,128)(2,1)} %get-tuple-element.257), channel_id=1, source_target_pairs={{0,2},{2,0},{1,3},{3,1},{4,6},{6,4},{5,7},{7,5},{8,10},{10,8},{9,1... | collective-permute-start | bytes 3145736 | tf_op jit(solution)/shard_map/ppermute | solution.py:25
  390.8 21.4 %collective-permute-start.31 = (bf16[2,2,128,512]{3,2,1,0:T(8,128)(2,1)S(1)}, bf16[2,2,128,512]{3,2,1,0:T(8,128)(2,1)}, u32[]{:S(2)}, u32[]{:S(2)}) collective-permute-start(bf16[2,2,128,512]{3,2,1,0:T(8,128)(2,1)S(1)} %dynamic-slice_bitcast_fusion.2), channel_id=1, source_target_pairs={{0,4},{4,0},{1,5},{5,1},{2,6},{6,2},{3,7},{7,3},{8,12},{12,8},{9,1... | collective-permute-start | bytes 1572872 | tf_op jit(solution)/shard_map/ppermute | solution.py:25
  392.0 20.2 %collective-permute-start.32 = (bf16[2,2,128,512]{3,2,1,0:T(8,128)(2,1)S(1)}, bf16[2,2,128,512]{3,2,1,0:T(8,128)(2,1)}, u32[]{:S(2)}, u32[]{:S(2)}) collective-permute-start(bf16[2,2,128,512]{3,2,1,0:T(8,128)(2,1)S(1)} %slice_bitcast_fusion.1), channel_id=1, source_target_pairs={{0,2},{2,0},{1,3},{3,1},{4,6},{6,4},{5,7},{7,5},{8,10},{10,8},{9,1... | collective-permute-start | bytes 1572872 | tf_op jit(solution)/shard_map/ppermute | solution.py:25
  424.1 16.1 %collective-permute-start.33 = (bf16[2,2,2,2,2,32,1024]{6,5,4,3,2,1,0:T(8,128)(2,1)}, bf16[2,2,2,2,2,32,1024]{6,5,4,3,2,1,0:T(8,128)(2,1)S(1)}, u32[]{:S(2)}, u32[]{:S(2)}) collective-permute-start(bf16[2,2,2,2,2,32,1024]{6,5,4,3,2,1,0:T(8,128)(2,1)} %pad_maximum_fusion.5), channel_id=1, source_target_pairs={{0,1},{1,0},{2,3},{3,2},{4,5},{5,4},{6,7},{7,6},{8,9},{9,8},{10,11... | collective-permute-start | bytes 6291464 | tf_op jit(solution)/shard_map/ppermute | solution.py:25
  425.6 14.7 %collective-permute-start.34 = (bf16[256,1024]{1,0:T(8,128)(2,1)}, bf16[256,1024]{1,0:T(8,128)(2,1)}, u32[]{:S(2)}, u32[]{:S(2)}) collective-permute-start(bf16[256,1024]{1,0:T(8,128)(2,1)} %reduce-scatter.3.cloned.1.call-done), channel_id=1, source_target_pairs={{0,2},{2,0},{1,3},{3,1},{4,6},{6,4},{5,7},{7,5},{8,10},{10,8},{9,1... | collective-permute-start | bytes 1572872 | tf_op jit(solution)/shard_map/ppermute | solution.py:25
  446.9 26.4 %collective-permute-start.35 = (bf16[2,2,2,2,32,1024]{5,4,3,2,1,0:T(8,128)(2,1)}, bf16[2,2,2,2,32,1024]{5,4,3,2,1,0:T(8,128)(2,1)}, u32[]{:S(2)}, u32[]{:S(2)}) collective-permute-start(bf16[2,2,2,2,32,1024]{5,4,3,2,1,0:T(8,128)(2,1)} %dynamic-slice_bitcast_fusion), channel_id=1, source_target_pairs={{0,2},{2,0},{1,3},{3,1},{4,6},{6,4},{5,7},{7,5},{8,10},{10,8},{9,1... | collective-permute-start | bytes 3145736 | tf_op jit(solution)/shard_map/ppermute | solution.py:25
  448.3 24.9 %collective-permute-start.36 = (bf16[2,2,128,512]{3,2,1,0:T(8,128)(2,1)}, bf16[2,2,128,512]{3,2,1,0:T(8,128)(2,1)}, u32[]{:S(2)}, u32[]{:S(2)}) collective-permute-start(bf16[2,2,128,512]{3,2,1,0:T(8,128)(2,1)} %pad_maximum_fusion.18), channel_id=1, source_target_pairs={{0,8},{8,0},{1,9},{9,1},{2,10},{10,2},{3,11},{11,3},{4,12},{12,4},... | collective-permute-start | bytes 1572872 | tf_op jit(solution)/shard_map/ppermute | solution.py:25
  449.9 23.4 %collective-permute-start.37 = (bf16[256,1024]{1,0:T(8,128)(2,1)S(1)}, bf16[256,1024]{1,0:T(8,128)(2,1)}, u32[]{:S(2)}, u32[]{:S(2)}) collective-permute-start(bf16[256,1024]{1,0:T(8,128)(2,1)S(1)} %add_convert_fusion.11), channel_id=1, source_target_pairs={{0,1},{1,0},{2,3},{3,2},{4,5},{5,4},{6,7},{7,6},{8,9},{9,8},{10,11... | collective-permute-start | bytes 1572872 | tf_op jit(solution)/shard_map/ppermute | solution.py:25
  478.5 5.5 collective-permute-start.40
  480.5 21.5 %collective-permute-start.39 = (bf16[2,128,512]{2,1,0:T(8,128)(2,1)}, bf16[2,128,512]{2,1,0:T(8,128)(2,1)S(1)}, u32[]{:S(2)}, u32[]{:S(2)}) collective-permute-start(bf16[2,128,512]{2,1,0:T(8,128)(2,1)} %dynamic-slice_bitcast_fusion.5), channel_id=1, source_target_pairs={{0,16},{16,0},{1,17},{17,1},{2,18},{18,2},{3,19},{19,3},{4,20},{20... | collective-permute-start | bytes 786440 | tf_op jit(solution)/shard_map/ppermute | solution.py:25
  483.0 19.1 %collective-permute-start.38 = (bf16[2,2,2,32,1024]{4,3,2,1,0:T(8,128)(2,1)S(1)}, bf16[2,2,2,32,1024]{4,3,2,1,0:T(8,128)(2,1)S(1)}, u32[]{:S(2)}, u32[]{:S(2)}) collective-permute-start(bf16[2,2,2,32,1024]{4,3,2,1,0:T(8,128)(2,1)S(1)} %dynamic-slice_bitcast_fusion.1), channel_id=1, source_target_pairs={{0,4},{4,0},{1,5},{5,1},{2,6},{6,2},{3,7},{7,3},{8,12},{12,8},{9,1... | collective-permute-start | bytes 1572872 | tf_op jit(solution)/shard_map/ppermute | solution.py:25
  502.3 8.5 %collective-permute-start.41 = (bf16[2,2,32,1024]{3,2,1,0:T(8,128)(2,1)S(1)}, bf16[2,2,32,1024]{3,2,1,0:T(8,128)(2,1)}, u32[]{:S(2)}, u32[]{:S(2)}) collective-permute-start(bf16[2,2,32,1024]{3,2,1,0:T(8,128)(2,1)S(1)} %dynamic-slice_bitcast_fusion.4), channel_id=1, source_target_pairs={{0,8},{8,0},{1,9},{9,1},{2,10},{10,2},{3,11},{11,3},{4,12},{12,4},... | collective-permute-start | bytes 786440 | tf_op jit(solution)/shard_map/ppermute | solution.py:25
  502.5 8.4 %collective-permute-start.43 = (bf16[2,128,512]{2,1,0:T(8,128)(2,1)S(1)}, bf16[2,128,512]{2,1,0:T(8,128)(2,1)S(1)}, u32[]{:S(2)}, u32[]{:S(2)}) collective-permute-start(bf16[2,128,512]{2,1,0:T(8,128)(2,1)S(1)} %fusion.34), channel_id=1, source_target_pairs={{0,2},{2,0},{1,3},{3,1},{4,6},{6,4},{5,7},{7,5},{8,10},{10,8},{9,1... | collective-permute-start | bytes 786440 | tf_op jit(solution)/shard_map/ppermute | solution.py:25
  505.2 1.3 collective-permute-start.42
  511.0 14.1 %collective-permute-start.46 = (bf16[2,2,128,512]{3,2,1,0:T(8,128)(2,1)S(1)}, bf16[2,2,128,512]{3,2,1,0:T(8,128)(2,1)S(1)}, u32[]{:S(2)}, u32[]{:S(2)}) collective-permute-start(bf16[2,2,128,512]{3,2,1,0:T(8,128)(2,1)S(1)} %pad_maximum_fusion.19), channel_id=1, source_target_pairs={{0,1},{1,0},{2,3},{3,2},{4,5},{5,4},{6,7},{7,6},{8,9},{9,8},{10,11... | collective-permute-start | bytes 1572872 | tf_op jit(solution)/shard_map/ppermute | solution.py:25
  512.1 5.3 collective-permute-start.45
  513.5 11.6 %collective-permute-start.47 = (bf16[64,3072]{1,0:T(8,128)(2,1)S(1)}, bf16[64,3072]{1,0:T(8,128)(2,1)S(1)}, u32[]{:S(2)}, u32[]{:S(2)}) collective-permute-start(bf16[64,3072]{1,0:T(8,128)(2,1)S(1)} %copy-done.50), channel_id=1, source_target_pairs={{0,2},{2,0},{1,3},{3,1},{4,6},{6,4},{5,7},{7,5},{8,10},{10,8},{9,1... | collective-permute-start | bytes 1179656 | tf_op jit(solution)/shard_map/ppermute | solution.py:25
  514.2 9.1 %collective-permute-start.44 = (bf16[2,32,1024]{2,1,0:T(8,128)(2,1)S(1)}, bf16[2,32,1024]{2,1,0:T(8,128)(2,1)S(1)}, u32[]{:S(2)}, u32[]{:S(2)}) collective-permute-start(bf16[2,32,1024]{2,1,0:T(8,128)(2,1)S(1)} %dynamic-slice_bitcast_fusion.6), channel_id=1, source_target_pairs={{0,16},{16,0},{1,17},{17,1},{2,18},{18,2},{3,19},{19,3},{4,20},{20... | collective-permute-start | bytes 393224 | tf_op jit(solution)/shard_map/ppermute | solution.py:25
  525.1 6.7 %collective-permute-start.51 = (bf16[2,32,1024]{2,1,0:T(8,128)(2,1)S(1)}, bf16[2,32,1024]{2,1,0:T(8,128)(2,1)S(1)}, u32[]{:S(2)}, u32[]{:S(2)}) collective-permute-start(bf16[2,32,1024]{2,1,0:T(8,128)(2,1)S(1)} %fusion.36), channel_id=1, source_target_pairs={{0,3},{1,2},{2,1},{3,0},{4,7},{5,6},{6,5},{7,4},{8,11},{9,10},{10,... | collective-permute-start | bytes 393224 | tf_op jit(solution)/shard_map/ppermute | solution.py:1118
  525.8 6.0 %collective-permute-start.50 = (bf16[2,32,1024]{2,1,0:T(8,128)(2,1)S(1)}, bf16[2,32,1024]{2,1,0:T(8,128)(2,1)S(1)}, u32[]{:S(2)}, u32[]{:S(2)}) collective-permute-start(bf16[2,32,1024]{2,1,0:T(8,128)(2,1)S(1)} %fusion.36), channel_id=1, source_target_pairs={{0,1},{1,0},{2,3},{3,2},{4,5},{5,4},{6,7},{7,6},{8,9},{9,8},{10,11... | collective-permute-start | bytes 393224 | tf_op jit(solution)/shard_map/ppermute | solution.py:25
  526.6 7.0 %collective-permute-start.49 = (bf16[2,32,1024]{2,1,0:T(8,128)(2,1)S(1)}, bf16[2,32,1024]{2,1,0:T(8,128)(2,1)S(1)}, u32[]{:S(2)}, u32[]{:S(2)}) collective-permute-start(bf16[2,32,1024]{2,1,0:T(8,128)(2,1)S(1)} %fusion.36), channel_id=1, source_target_pairs={{0,2},{2,0},{1,3},{3,1},{4,6},{6,4},{5,7},{7,5},{8,10},{10,8},{9,1... | collective-permute-start | bytes 393224 | tf_op jit(solution)/shard_map/ppermute | solution.py:25
  527.5 4.3 collective-permute-start.48
  528.9 4.7 collective-permute-start.52
  533.6 4.3 collective-permute-start.53
  538.0 5.5 collective-permute-start.54
  (105 other events, 769.6 us)
Sparse Core Ops, SparseCore 0:
  60.7 43.6 all-gather.8
  107.2 89.1 all-gather.6
  266.6 107.7 reduce-scatter.2
  396.3 104.2 reduce-scatter.4

commit v3 on v2

--- a/solution.py
+++ b/solution.py
@@ -31,10 +31,9 @@
 
 
 def join(mine, other, key, at):
-    first = lax.axis_index(key) == 0
-    return jnp.stack(
-        [jnp.where(first, mine, other), jnp.where(first, other, mine)], axis=at
-    )
+    shape = mine.shape[:at] + (2,) + mine.shape[at:]
+    side = lax.broadcasted_iota(jnp.int32, shape, at)
+    return jnp.where(side == lax.axis_index(key), jnp.expand_dims(mine, at), jnp.expand_dims(other, at))
 
 
 def half(value, which, at):
@@ -556,7 +555,7 @@
     refs = rest[:6]
     gate_ref, fr_ref, mid_ref, cot_ref, gain_ref, bias_ref, mk_ref, mr_ref = rest[6:14]
     dh_ref, out_ref, low_ref, first_k, first_r, tail_ref, sums = rest[14:21]
-    held, held_v, acc_k, acc_r, sems, sems_v = rest[21:]
+    held, held_v, held_sq, acc_k, acc_r, sems, sems_v, sems_sq = rest[21:]
     copies = load_pieces(refs, held, sems)
     width = held_v.shape[1]
     places = [pl.multiple_of(jnp.bitwise_xor(s_ref[0], p) * width, width) for p in range(4)]
@@ -564,15 +563,31 @@
         pltpu.make_async_copy(fv_ref.at[pl.ds(places[p], width)], held_v.at[p], sems_v.at[p])
         for p in range(4)
     ]
+    span = held_sq.shape[1]
+    rows = pl.ds(pl.multiple_of(pl.program_id(0) * span, span), span)
+    copies_sq = [
+        pltpu.make_async_copy(sq_ref.at[rows, pl.ds(places[p], width)], held_sq.at[p], sems_sq.at[p])
+        for p in range(4)
+    ]
     first = pl.program_id(0) == 0
     back = (((1,), (1,)), ((), ()))
+    for copy in copies_sq[:1]:
+        copy.start()
 
     @pl.when(first)
     def _():
-        for copy in copies_v + copies:
+        copies_v[0].start()
+
+    for copy in copies_sq[1:]:
+        copy.start()
+
+    @pl.when(first)
+    def _():
+        for copy in copies_v[1:] + copies:
             copy.start()
 
     for p in range(4):
+        copies_sq[p].wait()
 
         @pl.when(first)
         def _(p=p):
@@ -581,8 +596,7 @@
         for side in range(2):
             part = pl.ds(side * (width // 2), width // 2)
             d_sq = lax.dot_general(dval_ref[...], held_v[p, part, :], back, preferred_element_type=F32)
-            at = pl.multiple_of(places[p] + side * (width // 2), width // 2)
-            squared = sq_ref[:, pl.ds(at, width // 2)].astype(F32)
+            squared = held_sq[p, :, part].astype(F32)
             twice = 2.0 * squared * lax.rsqrt(jnp.maximum(squared, 1e-37))
             dh_ref[p, :, part] = (twice * d_sq).astype(BF16)
 
@@ -655,7 +669,7 @@
             in_specs=[
                 big,
                 pl.BlockSpec(memory_space=pl.ANY),
-                pl.BlockSpec((span, ff), lambda s, *_: (s, 0), pipeline_mode=pl.Buffered(1)),
+                pl.BlockSpec(memory_space=pl.ANY),
             ]
             + [pl.BlockSpec(memory_space=pl.ANY)] * 6
             + [big, pl.BlockSpec((D, D), lambda s, *_: (0, 0), pipeline_mode=pl.Buffered(1)), alone, big]
@@ -669,9 +683,11 @@
             scratch_shapes=[
                 pltpu.VMEM((2, D, 2 * width), BF16),
                 pltpu.VMEM((4, width, D), BF16),
+                pltpu.VMEM((4, span, width), BF16),
                 pltpu.VMEM((span, D), F32),
                 pltpu.VMEM((span, D), F32),
                 pltpu.SemaphoreType.DMA((PIECES,)),
+                pltpu.SemaphoreType.DMA((4,)),
                 pltpu.SemaphoreType.DMA((4,)),
             ],
         ),
@@ -695,11 +711,26 @@
 def mix_kernel(
     dk_ref, dv_ref, dr_ref, wk_ref, wv_ref, wr_ref, x_ref, dm_ref,
     gain_ref, bias_ref, mk_ref, mv_ref, mr_ref,
-    out_ref, firsts, tail_ref, sums, acc,
+    out_ref, firsts, tail_ref, sums, acc, held, sems,
 ):
-    for i, (grads, weight) in enumerate(((dk_ref, wk_ref), (dv_ref, wv_ref), (dr_ref, wr_ref))):
+    first = pl.program_id(0) == 0
+    copies = [
+        pltpu.make_async_copy(ref, held.at[i], sems.at[i]) for i, ref in enumerate((wk_ref, wv_ref, wr_ref))
+    ]
+
+    @pl.when(first)
+    def _():
+        for copy in copies:
+            copy.start()
+
+    for i, grads in enumerate((dk_ref, dv_ref, dr_ref)):
+
+        @pl.when(first)
+        def _(i=i):
+            copies[i].wait()
+
         acc[i] = lax.dot_general(
-            grads[...], weight[...], (((1,), (1,)), ((), ())), preferred_element_type=F32
+            grads[...], held[i], (((1,), (1,)), ((), ())), preferred_element_type=F32
         )
     gain, bias = gain_ref[...], bias_ref[...]
     mixes = (mk_ref[...], mv_ref[...], mr_ref[...])
@@ -743,7 +774,7 @@
     span = total // seqs
     big = pl.BlockSpec((span, D), lambda s: (s, 0))
     row = pl.BlockSpec((1, D), lambda s: (0, 0))
-    full = pl.BlockSpec((D, D), lambda s: (0, 0))
+    full = pl.BlockSpec(memory_space=pl.ANY)
     return pl.pallas_call(
         mix_kernel,
         grid=(seqs,),
@@ -760,7 +791,11 @@
             jax.ShapeDtypeStruct((seqs, 3, 1, D), F32),
             jax.ShapeDtypeStruct((seqs, 5, ROWS, D), F32),
         ],
-        scratch_shapes=[pltpu.VMEM((3, span, D), F32)],
+        scratch_shapes=[
+            pltpu.VMEM((3, span, D), F32),
+            pltpu.VMEM((3, D, D), BF16),
+            pltpu.SemaphoreType.DMA((3,)),
+        ],
         compiler_params=pltpu.CompilerParams(vmem_limit_bytes=58 << 20),
         cost_estimate=LIGHT,
     )(d_keys, d_vals, d_recepts, w_k, w_v, w_r, tokens, d_middle, gain, bias, mix_k, mix_v, mix_r)
@@ -772,28 +807,33 @@
     return lax.dynamic_update_slice(whole, rows.astype(values.dtype), (0, at, 0)).reshape(values.shape)
 
 
-def cut_kernel(_, k, v, r, o, fk1, fk2, kv_out, ro_out, f1_out, f2_out):
+def cut_kernel(_, k, v, r, o, fk1, fk2, rows, kv_out, ro_out, f1_out, f2_out, row_out):
     kv_out[0], kv_out[1] = k[...], v[...]
     ro_out[0], ro_out[1] = r[...], o[...]
     f1_out[...], f2_out[...] = fk1[...], fk2[...]
-
-
-def cut(my_seq, quarter, key, value, recept, output, feed_key):
+    last = rows.shape[1] - 1
+    row_out[...] = rows[...].astype(F32)[:, last:, :]
+
+
+def cut(my_seq, quarter, key, value, recept, output, feed_key, tokens):
+    seqs, span, _ = tokens.shape
     shard, ff = feed_key.shape
     part = pl.BlockSpec((quarter, D), lambda i, at: (at[0], 0))
     side = lambda which: pl.BlockSpec((shard, ff // PIECES), lambda i, at: (0, 2 * at[0] + which))
     full = lambda *shape: pl.BlockSpec(shape, lambda i, at: (0,) * len(shape))
-    shapes = [(2, quarter, D), (2, quarter, D)] + [(shard, ff // PIECES)] * 2
+    shapes = [(2, quarter, D), (2, quarter, D)] + [(shard, ff // PIECES)] * 2 + [(seqs, 1, D)]
+    kinds = [BF16] * 4 + [F32]
     return pl.pallas_call(
         cut_kernel,
         grid_spec=pltpu.PrefetchScalarGridSpec(
             num_scalar_prefetch=1,
             grid=(1,),
-            in_specs=[part] * 4 + [side(0), side(1)],
+            in_specs=[part] * 4
+            + [side(0), side(1), pl.BlockSpec((seqs, 2 * ROWS, D), lambda i, at: (0, span // (2 * ROWS) - 1, 0))],
             out_specs=[full(*shape) for shape in shapes],
         ),
-        out_shape=[jax.ShapeDtypeStruct(shape, BF16) for shape in shapes],
-    )(my_seq[None], key, value, recept, output, feed_key, feed_key)
+        out_shape=[jax.ShapeDtypeStruct(shape, kind) for shape, kind in zip(shapes, kinds)],
+    )(my_seq[None], key, value, recept, output, feed_key, feed_key, tokens)
 
 
 def dot(left, right):
@@ -873,13 +913,13 @@
         return lax.dynamic_slice_in_dim(weight, my_seq * quarter, quarter, 0)
 
     hid = feed_value_weight.shape[0]
-    kv, ro, f1, f2 = [
-        Growing(part)
-        for part in cut(
-            my_seq, quarter, key_weight, value_weight, recept_weight, output_weight,
-            feed_key_weight,
-        )
-    ]
+    halves = lambda w: half(w.reshape(2, w.shape[0] // 2, D), lax.axis_index(c), 0)
+    gathered = lambda w: lax.all_gather(w, dp_axes + (c,), axis=0, tiled=True)
+    w_fr = gathered(halves(feed_recept_weight))
+    *cuts, last_token = cut(
+        my_seq, quarter, key_weight, value_weight, recept_weight, output_weight, feed_key_weight, tokens
+    )
+    kv, ro, f1, f2 = [Growing(part) for part in cuts]
     kv.start(z_axes[0])
     ro.start(z_axes[0])
     kv.value, tokens, *vectors = tie(
@@ -889,9 +929,9 @@
     )
     vectors = Growing(jnp.stack(vectors))
     vectors.start(z_axes[0])
-    edge1 = from_behind(tokens[:, -1:], seq_axes, 1)
+    edge1 = from_behind(last_token, seq_axes, 1)
     for z in z_axes[1:]:
-        settle([kv, ro, vectors])
+        (edge1,) = settle([kv, ro, vectors], edge1)
         kv.start(z)
         ro.start(z)
         vectors.start(z)
@@ -901,10 +941,7 @@
     vectors.start(x)
     f1.start(z_axes[0])
     f2.start(z_axes[0])
-    halves = lambda w: half(w.reshape(2, w.shape[0] // 2, D), lax.axis_index(c), 0)
-    gathered = lambda w: lax.all_gather(w, dp_axes + (c,), axis=0, tiled=True)
-    (fr_part,) = settle([kv, ro, vectors, f1, f2], halves(feed_recept_weight))
-    w_fr = gathered(fr_part)
+    settle([kv, ro, vectors, f1, f2])
     kv.start(y)
     ro.start(x)
     for z in z_axes[1:]:
@@ -912,18 +949,16 @@
         f2.start(z)
         if z != z_axes[-1]:
             settle([f1, f2])
-    (fv_part,) = settle([f1, f2, kv, ro], halves(feed_value_weight))
+    fv_part, w_fr = settle([f1, f2, kv, ro], halves(feed_value_weight), w_fr)
     w_fv = gathered(fv_part)
-    kv.start(c)
-    ro.start(c)
-    f1.start(x)
-    f2y = swap(f2.value, y)
-    (f2y,) = settle([kv, ro, f1], f2y)
+    kv.prepare(c)
+    ro.prepare(c)
+    f1.prepare(x)
+    f2y = Plain(f2.value, y)
+    tokens, vectors.value = fire([kv, ro, f1, f2y], tokens, vectors.value)
+    settle([kv, ro])
     pick = lambda v, i: jnp.moveaxis(v, -3, 0)[i].reshape(D, D)
     w_k, w_v, w_r, w_o = pick(kv.value, 0), pick(kv.value, 1), pick(ro.value, 0), pick(ro.value, 1)
-    f1_0 = row_major(f1.value).reshape(D, -1)
-    f2.value = jnp.stack([f2.value, f2y], axis=len(f2.held))
-
     vectors = jnp.swapaxes(vectors.value.reshape(dp, 11, D // dp), 0, 1).reshape(11, D).astype(F32)
     gain1, bias1, mix_k, mix_v, mix_r, log_rate, first, gain2, bias2, fmix_k, fmix_r = [
         vectors[i : i + 1] for i in range(11)
@@ -940,7 +975,7 @@
     inside = (my_seq > 0).astype(F32)
 
     xin = tokens.astype(F32)
-    edge1 = (normalize(edge1.astype(F32))[0] * gain1 + bias1) * inside
+    edge1 = (normalize(edge1)[0] * gain1 + bias1) * inside
     n1, inv1 = normalize(xin)
     a = n1 * gain1 + bias1
     a_prev = shifted(a, edge1)
@@ -959,6 +994,10 @@
     vals, recepts = vals.astype(BF16), recepts.astype(BF16)
     den_end = jnp.sum(left * power, axis=1)
     num0, den0 = earlier_state(span_decay, num_end, den_end, seq_axes, False)
+    num0, den0 = settle([f1, f2y], num0, den0)
+    f2y = f2y.got
+    f1_0 = row_major(f1.value).reshape(D, -1)
+    f2.value = jnp.stack([f2.value, f2y], axis=len(f2.held))
     f1_y = Plain(f1_0, y)
     f2.prepare(x)
     num0, den0 = fire([f1_y, f2], num0, den0)
@@ -968,7 +1007,7 @@
     f2_0 = row_major(jnp.moveaxis(f2.value, -3, 0)).reshape(2, D, -1)
     f1_c, f1_yc, f2_c = Plain(f1_0, c), Plain(f1_y, c), Plain(f2_0, c)
     (weighted,) = fire([f1_c, f1_yc, f2_c], weighted)
-    last_row = tokens[:, -1].astype(F32) + dot(deep(weighted)[:, -1], w_o)
+    last_row = last_token[:, 0] + dot(deep(weighted)[:, -1], w_o)
     edge2 = from_behind(last_row[:, None], seq_axes, 1)
     left_rows = (my_lens - my_seq * span).astype(jnp.int32)
     flat_tokens = flat(tokens)
@@ -1095,31 +1134,36 @@
     )
 
     small = jnp.concatenate([small1, small2])
-    small, input_grad = settle([r_kv, r_f], small, input_grad)
-    out_f = Growing(r_f.value)
-    out_f.start(y)
+    small, input_grad = settle([r_kv], small, input_grad)
     small = Summing(small)
     r_kv.start(z1)
     small.start(c)
-    (orf,) = settle([r_kv, small, out_f], orf)
-    out_f.start(c)
+    small.finish()
+    small.start(y)
+    (orf,) = settle([r_kv, small, r_f], orf)
     for z in reversed(z2):
         r_kv.start(z)
         if z != z2[0]:
             settle([r_kv])
-    small.start(y)
+    out_f = Growing(r_f.value)
+    out_f.start(y)
     orf_got = swap(orf, y)
+    small.start(x)
+    small.finish()
+    small.start(z1)
     (orf_got,) = settle([r_kv, small, out_f], orf_got)
+    out_f.start(c)
     orf = add_low(orf, orf_got)
     orf_c = swap(orf, c)
     own = r_kv.value
-    small.start(x)
+    last_z = list(reversed(z2))
+    for z in last_z[:-1]:
+        small.start(z)
+        small.finish()
+    small.start(last_z[-1])
     at_y, at_c = swap(own, y), swap(own, c)
     at_both = lax.ppermute(own, (y, c), [(i, 3 - i) for i in range(4)])
-    at_y, at_c, at_both, orf_c = settle([small], at_y, at_c, at_both, orf_c)
-    for z in (z1, *reversed(z2)):
-        small.start(z)
-        small.finish()
+    at_y, at_c, at_both, orf_c = settle([small, out_f], at_y, at_c, at_both, orf_c)
     small = small.value
     out_kv = join(join(own, at_c, c, 0), join(at_y, at_both, c, 0), y, 0)
 

time: 558 us -> 540 us (0.968)
  waiting for transfers between devices: 118 us -> 105 us
  blocking collectives: 10.7 us -> 20.6 us
  other arithmetic: 78.1 us -> 70.3 us
  local copies, waits for them, and re-layouts: 39.7 us -> 33.8 us
    select_n x1 -> x23, other arithmetic: 0.05 us -> 20.4 us  [join(): jnp.where(side == lax.axis_index(key), jnp.expand_dims(mine, at), jnp.exp...]
    another operation x47 -> x0, other arithmetic: 20 us -> none  [the longest x45 19.9 us: join(): jnp.stack([jnp.where(first, mine, other), jnp.where(first, other, mine)],...]
    ppermute x50, waiting for transfers between devices: 118 us -> 102 us  [swap(): return lax.ppermute(value, key, [(0, 1), (1, 0)])]
    all_gather x2, blocking collectives: 10.7 us -> 20.6 us  [earlier_state(): packed = lax.all_gather(jnp.concatenate([num, den], axis=0), axes)]
  transfers between devices with their start and end apart: 59 -> 59, of which waited for: 24 -> 23; matrix products, arithmetic and copies ran while one was open for 28% -> 26% of each run, Pallas kernels for 23% -> 23%
where the time goes in v3:
time: 540 us; the launch traced here: 535 us
  Pallas kernels  160 us (30%)
  waiting for transfers between devices  105 us (19%)
  other arithmetic  70.3 us (13%)
  matrix products  66.4 us (12%)
  starting transfers between devices  62.2 us (12%)
  local copies, waits for them, and re-layouts  33.8 us (6%)
  blocking collectives  20.6 us (4%)
  between operations  16.3 us (3%)
    ppermute x50, waiting for transfers between devices, swap(): return lax.ppermute(value, key, [(0, 1), (1, 0)])  102 us
    ppermute x50, starting transfers between devices, swap(): return lax.ppermute(value, key, [(0, 1), (1, 0)])  54.7 us
    dot_general x10, matrix products, dot_weight(): lax.dot_general(inputs, grads, (((0,), (0,)), ((), ())), preferred_elemen...  53.9 us
    pallas_call x1, Pallas kernels, down(): pl.pallas_call(down_kernel, grid_spec=pltpu.PrefetchScalarGridSpec(num_sc...  45.8 us
    pallas_call x1, Pallas kernels, feed_forward(): pl.pallas_call(feed_kernel, grid_spec=pltpu.PrefetchScalarGridSpec(num_sc...  34.5 us
    pallas_call x1, Pallas kernels, mix_back(): pl.pallas_call(mix_kernel, grid=(seqs,), in_specs=[big, big, big, full, f...  23.1 us
    all_gather x2, blocking collectives, earlier_state(): packed = lax.all_gather(jnp.concatenate([num, den], axis=0), axes)  20.6 us
    select_n x23, other arithmetic, join(): jnp.where(side == lax.axis_index(key), jnp.expand_dims(mine, at), jnp.exp...  20.4 us
  transfers between devices with their start and end apart: 59, of which 23 were waited for; matrix products, arithmetic and copies ran while one was open for 26% of the time, Pallas kernels for 23%

profile of v3, /device:TPU:0, one launch (start us, length us, event | category | flops | bytes accessed | tf_op | source)
XLA Modules:
  0.0 535.2 jit_solution(1079887884037429124)
XLA Ops:
  9.1 1.9 shard_map.389
  11.1 4.1 collective-permute-start
  15.4 2.9 collective-permute-start.2
  19.6 10.1 %collective-permute-done.2 = bf16[11,128]{1,0:T(8,128)(2,1)S(1)} collective-permute-done((bf16[11,128]{1,0:T(8,128)(2,1)S(1)}, bf16[11,128]{1,0:T(8,128)(2,1)S(1)}, u32[]{:S(2)}, u32[]{:S(2)}) %collective-permute-start.2) | collective-permute-done | bytes 2848 | tf_op jit(solution)/shard_map/ppermute | solution.py:25
  34.5 14.1 %collective-permute-done.6 = bf16[2,11,128]{2,0,1:T(2,128)(2,1)S(1)} collective-permute-done((bf16[2,11,128]{2,0,1:T(2,128)(2,1)S(1)}, bf16[2,11,128]{2,0,1:T(2,128)(2,1)S(1)}, u32[]{:S(2)}, u32[]{:S(2)}) %collective-permute-start.6) | collective-permute-done | bytes 5664 | tf_op jit(solution)/shard_map/ppermute | solution.py:25
  51.3 7.3 %collective-permute-start.10 = (bf16[128,512]{1,0:T(8,128)(2,1)S(1)}, bf16[128,512]{1,0:T(8,128)(2,1)S(1)}, u32[]{:S(2)}, u32[]{:S(2)}) collective-permute-start(bf16[128,512]{1,0:T(8,128)(2,1)S(1)} %copy-done.48), channel_id=1, source_target_pairs={{0,16},{16,0},{1,17},{17,1},{2,18},{18,2},{3,19},{19,3},{4,20},{20... | collective-permute-start | bytes 393224 | tf_op jit(solution)/shard_map/ppermute | solution.py:25
  59.0 3.6 collective-permute-done.9
  62.6 1.8 collective-permute-done.10
  64.3 2.8 collective-permute-done.11
  71.1 2.1 broadcast_select_fusion.10
  75.7 2.0 collective-permute-start.13
  78.5 6.7 %collective-permute-done.12 = bf16[2,128,512]{2,1,0:T(8,128)(2,1)} collective-permute-done((bf16[2,128,512]{2,1,0:T(8,128)(2,1)}, bf16[2,128,512]{2,1,0:T(8,128)(2,1)}, u32[]{:S(2)}, u32[]{:S(2)}) %collective-permute-start.12) | collective-permute-done | bytes 262176 | tf_op jit(solution)/shard_map/ppermute | solution.py:25
  85.2 3.4 collective-permute-done.13
  88.6 3.1 collective-permute-done.15
  91.7 5.8 %collective-permute-done.14 = bf16[2,2,2,2,32,1024]{5,4,2,1,0,3:T(8,128)(2,1)} collective-permute-done((bf16[2,2,2,2,32,1024]{5,4,2,1,0,3:T(8,128)(2,1)}, bf16[2,2,2,2,32,1024]{5,4,2,1,0,3:T(8,128)(2,1)}, u32[]{:S(2)}, u32[]{:S(2)}) %collective-permute-start.14) | collective-permute-done | bytes 1048608 | tf_op jit(solution)/shard_map/ppermute | solution.py:25
  104.4 2.0 broadcast_select_fusion.6
  106.7 1.7 collective-permute-start.17
  115.8 4.9 add_convert_fusion.1
  122.1 3.7 fusion.85
  125.7 4.8 multiply_reduce_fusion
  130.5 15.3 %all-gather.3 = f32[4,4,1024]{2,1,0:T(4,128)S(1)} all-gather(f32[1,4,1024]{2,1,0:T(4,128)S(1)} %maximum_bitcast_fusion), channel_id=3, replica_groups=mesh['d2'=2,'d1'=2,'d0'=2,'s1'=2,'s0'=2] {'s1','s0'}, dimensions={0}, use_global_device_ids=true | all-gather | bytes 81920 | tf_op jit(solution)/shard_map/all_gather | solution.py:879
  148.4 1.8 collective-permute-start.21
  153.3 3.7 convolution_convert_fusion.6.r_ref
  157.0 13.7 %shard_map.390 = (bf16[1024,1024]{1,0:T(8,128)(2,1)}, f32[1024,1024]{1,0:T(8,128)}, f32[1024,1024]{1,0:T(8,128)}) custom-call(f32[1024,1024]{1,0:T(8,128)} %get-tuple-element.455.k_ref, bf16[1024,1024]{1,0:T(8,128)(2,1)} %get-tuple-element.456.v_ref, bf16[1024,1024]{1,0:T(8,128)(2,1)} %convolution_convert_fusion.6.r_ref, f32[1,1024]{1,0:T(1,128)} %bitcast.457, ...), custom_call_target="tpu_custom_call" | custom-call | flops 1048576 | bytes 65536 | tf_op jit(solution)/shard_map/pallas_call | solution.py:286
  170.7 2.9 collective-permute-done.20.rest_2_
  173.6 6.1 %collective-permute-done.21 = bf16[2,2,2,128,512]{4,3,1,0,2:T(8,128)(2,1)} collective-permute-done((bf16[2,2,2,128,512]{4,3,1,0,2:T(8,128)(2,1)S(1)}, bf16[2,2,2,128,512]{4,3,1,0,2:T(8,128)(2,1)}, u32[]{:S(2)}, u32[]{:S(2)}) %collective-permute-start.21) | collective-permute-done | bytes 1048608 | tf_op jit(solution)/shard_map/ppermute | solution.py:25
  179.7 2.9 broadcast_select_fusion.2
  184.7 2.4 collective-permute-start.25
  188.4 11.1 %shard_map.391 = (f32[1024,1024]{1,0:T(8,128)}, bf16[1024,1024]{1,0:T(8,128)(2,1)}, bf16[1024,1024]{1,0:T(8,128)(2,1)}, f32[2,1,1024]{2,1,0:T(1,128)}, f32[2,8,1024]{2,1,0:T(8,128)}) custom-call(s32[2]{0:T(128)} %broadcast_subtract_fusion.5.left_ref, bf16[1024,1024]{1,0:T(8,128)(2,1)} %get-tuple-element.249.w_ref, bf16[1024,1024]{1,0:T(8,128)(2,1)} %bitcast.404, ...), custom_call_target="tpu_custom_call" | custom-call | flops 1048576 | bytes 65536 | tf_op jit(solution)/shard_map/pallas_call | solution.py:534
  205.4 34.5 %shard_map.392 = (bf16[1024,4096]{1,0:T(8,128)(2,1)}, bf16[1024,1024]{1,0:T(8,128)(2,1)}, bf16[1024,1024]{1,0:T(8,128)(2,1)}, bf16[1024,1024]{1,0:T(8,128)(2,1)}, f32[2,2,8,1024]{3,2,1,0:T(8,128)}) custom-call(s32[1]{0:T(128)} %bitcast._.s_ref, s32[2]{0:T(128)} %broadcast_subtract_fusion.5.left_ref, bf16[1024,1024]{1,0:T(8,128)(2,1)} %bitcast.439, ...), custom_call_target="tpu_custom_call" | custom-call | flops 1048576 | bytes 65536 | tf_op jit(solution)/shard_map/pallas_call | solution.py:433
  240.0 15.5 %convolution_convert_fusion = bf16[4096,1024]{1,0:T(8,128)(2,1)} fusion(bf16[1024,4096]{1,0:T(8,128)(2,1)} %get-tuple-element.262.sq_ref, bf16[1024,1024]{1,0:T(8,128)(2,1)} %get-tuple-element.261.dval_ref), kind=kOutput, calls=%fused_computation | convolution fusion | flops 8594128896 | bytes 18874368 | tf_op jit(solution)/shard_map/dot_general | solution.py:848
  255.5 45.8 %shard_map.393 = (bf16[4,1024,1024]{2,1,0:T(8,128)(2,1)}, f32[1024,1024]{1,0:T(8,128)}, bf16[1024,1024]{1,0:T(8,128)(2,1)}, f32[2,1,1024]{2,1,0:T(1,128)}, f32[2...) custom-call(s32[1]{0:T(128)} %bitcast._.s_ref, s32[2]{0:T(128)} %broadcast_subtract_fusion.5.left_ref, ...), custom_call_target="tpu_custom_call" | custom-call | flops 1048576 | bytes 65536 | tf_op jit(solution)/shard_map/pallas_call | solution.py:664
  301.3 5.4 %fusion.21 = bf16[1024,1024]{1,0:T(8,128)(2,1)} fusion(bf16[1024,1024]{1,0:T(8,128)(2,1)S(1)} %bitcast.440, bf16[4,1024,1024]{2,1,0:T(8,128)(2,1)} %get-tuple-element.268), kind=kOutput, calls=%fused_computation.46 | convolution fusion | flops 2148532224 | bytes 6291456 | tf_op jit(solution)/shard_map/dot_general | solution.py:848
  306.8 5.6 %fusion.18 = bf16[1024,1024]{1,0:T(8,128)(2,1)} fusion(bf16[1024,1024]{1,0:T(8,128)(2,1)S(1)} %bitcast.441, bf16[4,1024,1024]{2,1,0:T(8,128)(2,1)} %get-tuple-element.268), kind=kOutput, calls=%fused_computation.45 | convolution fusion | flops 2148532224 | bytes 6291456 | tf_op jit(solution)/shard_map/dot_general | solution.py:848
  314.3 5.3 convolution_convert_fusion.1
  319.6 4.0 fusion.27
  323.7 4.1 fusion.24
  327.8 3.9 add_convert_fusion.6
  336.7 2.8 collective-permute-start.29
  341.1 15.1 %shard_map.394 = (bf16[1024,1024]{1,0:T(8,128)(2,1)}, bf16[1024,1024]{1,0:T(8,128)(2,1)}, f32[2,8,1024]{2,1,0:T(8,128)}, f32[2,8,1024]{2,1,0:T(8,128)}) custom-call(bf16[1024,1024]{1,0:T(8,128)(2,1)} %bitcast.434, bf16[1024,1024]{1,0:T(8,128)(2,1)} %bitcast.405, f32[1024,1024]{1,0:T(8,128)} %get-tuple-element.455.k_ref, ...), custom_call_target="tpu_custom_call" | custom-call | flops 1048576 | bytes 65536 | tf_op jit(solution)/shard_map/pallas_call | solution.py:326
  357.2 5.5 %convolution_convert_fusion.5 = bf16[1024,1024]{1,0:T(8,128)(2,1)} fusion(bf16[1024,1024]{1,0:T(8,128)(2,1)S(1)} %copy-done.12, bf16[1024,1024]{1,0:T(8,128)(2,1)} %bitcast.435), kind=kOutput, calls=%fused_computation.53 | convolution fusion | flops 2148532224 | bytes 6291456 | tf_op jit(solution)/shard_map/dot_general | solution.py:848
  362.6 3.8 convolution_convert_fusion.4
  367.8 5.2 all-gather.4
  373.7 2.2 add_convert_fusion.5
  378.4 3.4 pad_maximum_fusion
  383.5 14.9 %shard_map.395 = (bf16[1024,1024]{1,0:T(8,128)(2,1)}, bf16[1024,1024]{1,0:T(8,128)(2,1)}, f32[2,8,1024]{2,1,0:T(8,128)}, f32[2,8,1024]{2,1,0:T(8,128)}) custom-call(f32[1024,1024]{1,0:T(8,128)} %get-tuple-element.455.k_ref, bf16[1024,1024]{1,0:T(8,128)(2,1)} %get-tuple-element.456.v_ref, f32[1024,1024]{1,0:T(8,128)} %get-tuple-element.282.a_ref, ...), custom_call_target="tpu_custom_call" | custom-call | flops 1048576 | bytes 65536 | tf_op jit(solution)/shard_map/pallas_call | solution.py:305
  398.4 1.7 fusion.31
  402.0 2.4 convolution_convert_fusion.3
  404.5 2.4 convolution_convert_fusion.2
  406.9 1.8 constant_dynamic-slice_fusion.7
  414.0 2.0 select_maximum_fusion
  419.3 6.2 %collective-permute-done.34 = bf16[256,1024]{1,0:T(8,128)(2,1)} collective-permute-done((bf16[256,1024]{1,0:T(8,128)(2,1)}, bf16[256,1024]{1,0:T(8,128)(2,1)}, u32[]{:S(2)}, u32[]{:S(2)}) %collective-permute-start.34) | collective-permute-done | bytes 524320 | tf_op jit(solution)/shard_map/ppermute | solution.py:25
  426.8 2.9 add_convert_fusion
  435.1 23.1 %shard_map.396 = (bf16[1024,1024]{1,0:T(8,128)(2,1)}, f32[2,3,1,1024]{3,2,1,0:T(1,128)}, f32[2,3,1,1024]{3,2,1,0:T(1,128)}, f32[2,5,8,1024]{3,2,1,0:T(8,128)}) custom-call(bf16[1024,1024]{1,0:T(8,128)(2,1)} %get-tuple-element.321.dk_ref, bf16[1024,1024]{1,0:T(8,128)(2,1)} %get-tuple-element.300.dv_ref, bf16[1024,1024]{1,0:T(8,128)(2,1)} %get-tuple-element.285.dr_ref, ...), custom_call_target="tpu_custom_call" | custom-call | flops 1048576 | bytes 65536 | tf_op jit(solution)/shard_map/pallas_call | solution.py:778
  460.9 1.7 fusion.5
  464.3 2.6 collective-permute-start.43
  470.0 11.6 %collective-permute-done.38 = bf16[2,2,2,32,1024]{4,3,2,1,0:T(8,128)(2,1)S(1)} collective-permute-done((bf16[2,2,2,32,1024]{4,3,2,1,0:T(8,128)(2,1)S(1)}, bf16[2,2,2,32,1024]{4,3,2,1,0:T(8,128)(2,1)S(1)}, u32[]{:S(2)}, u32[]{:S(2)}) %collective-permute-start.38) | collective-permute-done | bytes 524320 | tf_op jit(solution)/shard_map/ppermute | solution.py:25
  485.0 2.9 reduce-scatter.5.cloned.1.call-done
  488.3 5.3 collective-permute-done.41
  497.5 2.8 collective-permute-done.44
  501.9 2.8 collective-permute-done.46
  504.8 5.5 %collective-permute-done.48 = bf16[64,3072]{1,0:T(8,128)(2,1)S(1)} collective-permute-done((bf16[64,3072]{1,0:T(8,128)(2,1)}, bf16[64,3072]{1,0:T(8,128)(2,1)S(1)}, u32[]{:S(2)}, u32[]{:S(2)}) %collective-permute-start.48) | collective-permute-done | bytes 393248 | tf_op jit(solution)/shard_map/ppermute | solution.py:25
  512.2 4.6 collective-permute-done.49
  519.3 2.6 fusion.33
  (440 shorter events, 108.3 us)
Async XLA Ops:
  7.2 70.5 %copy-start = (bf16[512,1024]{1,0:T(8,128)(2,1)S(1)}, bf16[512,1024]{1,0:T(8,128)(2,1)}, u32[]{:S(2)}) copy-start(bf16[512,1024]{1,0:T(8,128)(2,1)} %param.43) | copy-start | bytes 3145732
  7.2 90.3 %all-gather.10.cloned.1.call-start = ((), (), s32[]{:S(2)}) async-start(), calls=%async_computation.5 | async-start | bytes 2228224 | tf_op jit(solution)/shard_map/all_gather | solution.py:917
  8.9 195.2 %all-gather.8.cloned.1.call-start = ((), (), s32[]{:S(2)}) async-start(), calls=%async_computation.2 | async-start | bytes 8912896 | tf_op jit(solution)/shard_map/all_gather | solution.py:917
  11.1 47.5 %copy-start.49 = (bf16[128,512]{1,0:T(8,128)(2,1)S(1)}, bf16[128,512]{1,0:T(8,128)(2,1)}, u32[]{:S(2)}) copy-start(bf16[128,512]{1,0:T(8,128)(2,1)} %get-tuple-element.214) | copy-start | bytes 393220
  11.1 18.6 %collective-permute-start = (bf16[2,32,1024]{2,1,0:T(8,128)(2,1)}, bf16[2,32,1024]{2,1,0:T(8,128)(2,1)S(1)}, u32[]{:S(2)}, u32[]{:S(2)}) collective-permute-start(bf16[2,32,1024]{2,1,0:T(8,128)(2,1)} %get-tuple-element.191), channel_id=1, source_target_pairs={{0,16},{16,0},{1,17},{17,1},{2,18},{18,2},{3,19},{19,3},{4,20},{20... | collective-permute-start | bytes 393224 | tf_op jit(solution)/shard_map/ppermute | solution.py:25
  15.2 14.5 %collective-permute-start.1 = (bf16[2,32,1024]{2,1,0:T(8,128)(2,1)}, bf16[2,32,1024]{2,1,0:T(8,128)(2,1)S(1)}, u32[]{:S(2)}, u32[]{:S(2)}) collective-permute-start(bf16[2,32,1024]{2,1,0:T(8,128)(2,1)} %get-tuple-element.192), channel_id=1, source_target_pairs={{0,16},{16,0},{1,17},{17,1},{2,18},{18,2},{3,19},{19,3},{4,20},{20... | collective-permute-start | bytes 393224 | tf_op jit(solution)/shard_map/ppermute | solution.py:25
  15.4 14.3 %collective-permute-start.2 = (bf16[11,128]{1,0:T(8,128)(2,1)S(1)}, bf16[11,128]{1,0:T(8,128)(2,1)S(1)}, u32[]{:S(2)}, u32[]{:S(2)}) collective-permute-start(bf16[11,128]{1,0:T(8,128)(2,1)S(1)} %stack.96), channel_id=1, source_target_pairs={{0,16},{16,0},{1,17},{17,1},{2,18},{18,2},{3,19},{19,3},{4,20},{20... | collective-permute-start | bytes 8456 | tf_op jit(solution)/shard_map/ppermute | solution.py:25
  18.3 11.4 %collective-permute-start.3 = (f32[2,1,1024]{2,1,0:T(1,128)}, f32[2,1,1024]{2,1,0:T(1,128)S(1)}, u32[]{:S(2)}, u32[]{:S(2)}) collective-permute-start(f32[2,1,1024]{2,1,0:T(1,128)} %get-tuple-element.204), channel_id=1, source_target_pairs={{0,1},{1,2},{2,3},{4,5},{5,6},{6,7},{8,9},{9,10},{10,11},{12,13},{... | collective-permute-start | bytes 24584 | tf_op jit(solution)/shard_map/ppermute | solution.py:861
  30.8 17.8 %collective-permute-start.5 = (bf16[2,2,32,1024]{3,2,0,1:T(8,128)(2,1)S(1)}, bf16[2,2,32,1024]{3,2,0,1:T(8,128)(2,1)S(1)}, u32[]{:S(2)}, u32[]{:S(2)}) collective-permute-start(bf16[2,2,32,1024]{3,2,0,1:T(8,128)(2,1)S(1)} %get-tuple-element.453), channel_id=1, source_target_pairs={{0,8},{8,0},{1,9},{9,1},{2,10},{10,2},{3,11},{11,3},{4,12},{12,4},... | collective-permute-start | bytes 786440 | tf_op jit(solution)/shard_map/ppermute | solution.py:25
  32.4 16.2 %collective-permute-start.4 = (bf16[2,2,32,1024]{3,2,0,1:T(8,128)(2,1)S(1)}, bf16[2,2,32,1024]{3,2,0,1:T(8,128)(2,1)S(1)}, u32[]{:S(2)}, u32[]{:S(2)}) collective-permute-start(bf16[2,2,32,1024]{3,2,0,1:T(8,128)(2,1)S(1)} %get-tuple-element.454), channel_id=1, source_target_pairs={{0,8},{8,0},{1,9},{9,1},{2,10},{10,2},{3,11},{11,3},{4,12},{12,4},... | collective-permute-start | bytes 786440 | tf_op jit(solution)/shard_map/ppermute | solution.py:25
  32.9 15.7 %collective-permute-start.6 = (bf16[2,11,128]{2,0,1:T(2,128)(2,1)S(1)}, bf16[2,11,128]{2,0,1:T(2,128)(2,1)S(1)}, u32[]{:S(2)}, u32[]{:S(2)}) collective-permute-start(bf16[2,11,128]{2,0,1:T(2,128)(2,1)S(1)} %broadcast_select_fusion.27), channel_id=1, source_target_pairs={{0,8},{8,0},{1,9},{9,1},{2,10},{10,2},{3,11},{11,3},{4,12},{12,4},... | collective-permute-start | bytes 16904 | tf_op jit(solution)/shard_map/ppermute | solution.py:25
  48.8 18.4 %collective-permute-start.8 = (bf16[2,2,2,32,1024]{4,3,1,0,2:T(8,128)(2,1)S(1)}, bf16[2,2,2,32,1024]{4,3,1,0,2:T(8,128)(2,1)S(1)}, u32[]{:S(2)}, u32[]{:S(2)}) collective-permute-start(bf16[2,2,2,32,1024]{4,3,1,0,2:T(8,128)(2,1)S(1)} %get-tuple-element.451), channel_id=1, source_target_pairs={{0,2},{2,0},{1,3},{3,1},{4,6},{6,4},{5,7},{7,5},{8,10},{10,8},{9,1... | collective-permute-start | bytes 1572872 | tf_op jit(solution)/shard_map/ppermute | solution.py:25
  49.9 17.3 %collective-permute-start.7 = (bf16[2,2,2,32,1024]{4,3,1,0,2:T(8,128)(2,1)S(1)}, bf16[2,2,2,32,1024]{4,3,1,0,2:T(8,128)(2,1)S(1)}, u32[]{:S(2)}, u32[]{:S(2)}) collective-permute-start(bf16[2,2,2,32,1024]{4,3,1,0,2:T(8,128)(2,1)S(1)} %get-tuple-element.452), channel_id=1, source_target_pairs={{0,4},{4,0},{1,5},{5,1},{2,6},{6,2},{3,7},{7,3},{8,12},{12,8},{9,1... | collective-permute-start | bytes 1572872 | tf_op jit(solution)/shard_map/ppermute | solution.py:25
  51.3 53.0 %copy-start.64 = (pred[2]{0:T(512)(128)(4,1)}, pred[2]{0:T(512)(128)(4,1)S(1)}, u32[]{:S(2)}) copy-start(pred[2]{0:T(512)(128)(4,1)S(1)} %iota_compare_fusion.2) | copy-start | bytes 10
  51.3 13.0 %collective-permute-start.10 = (bf16[128,512]{1,0:T(8,128)(2,1)S(1)}, bf16[128,512]{1,0:T(8,128)(2,1)S(1)}, u32[]{:S(2)}, u32[]{:S(2)}) collective-permute-start(bf16[128,512]{1,0:T(8,128)(2,1)S(1)} %copy-done.48), channel_id=1, source_target_pairs={{0,16},{16,0},{1,17},{17,1},{2,18},{18,2},{3,19},{19,3},{4,20},{20... | collective-permute-start | bytes 393224 | tf_op jit(solution)/shard_map/ppermute | solution.py:25
  58.6 8.5 %collective-permute-start.11 = (bf16[128,512]{1,0:T(8,128)(2,1)S(1)}, bf16[128,512]{1,0:T(8,128)(2,1)S(1)}, u32[]{:S(2)}, u32[]{:S(2)}) collective-permute-start(bf16[128,512]{1,0:T(8,128)(2,1)S(1)} %copy-done.49), channel_id=1, source_target_pairs={{0,16},{16,0},{1,17},{17,1},{2,18},{18,2},{3,19},{19,3},{4,20},{20... | collective-permute-start | bytes 393224 | tf_op jit(solution)/shard_map/ppermute | solution.py:25
  58.8 3.7 collective-permute-start.9
  69.8 21.9 %collective-permute-start.15 = (bf16[2,2,2,2,32,1024]{5,4,2,1,0,3:T(8,128)(2,1)}, bf16[2,2,2,2,32,1024]{5,4,2,1,0,3:T(8,128)(2,1)S(1)}, u32[]{:S(2)}, u32[]{:S(2)}) collective-permute-start(bf16[2,2,2,2,32,1024]{5,4,2,1,0,3:T(8,128)(2,1)} %broadcast_select_fusion.9), channel_id=1, source_target_pairs={{0,4},{4,0},{1,5},{5,1},{2,6},{6,2},{3,7},{7,3},{8,12},{12,8},{9,1... | collective-permute-start | bytes 3145736 | tf_op jit(solution)/shard_map/ppermute | solution.py:25
  73.3 24.3 %collective-permute-start.14 = (bf16[2,2,2,2,32,1024]{5,4,2,1,0,3:T(8,128)(2,1)}, bf16[2,2,2,2,32,1024]{5,4,2,1,0,3:T(8,128)(2,1)}, u32[]{:S(2)}, u32[]{:S(2)}) collective-permute-start(bf16[2,2,2,2,32,1024]{5,4,2,1,0,3:T(8,128)(2,1)} %broadcast_select_fusion.10), channel_id=1, source_target_pairs={{0,2},{2,0},{1,3},{3,1},{4,6},{6,4},{5,7},{7,5},{8,10},{10,8},{9,1... | collective-permute-start | bytes 3145736 | tf_op jit(solution)/shard_map/ppermute | solution.py:25
  75.7 9.6 %collective-permute-start.12 = (bf16[2,128,512]{2,1,0:T(8,128)(2,1)}, bf16[2,128,512]{2,1,0:T(8,128)(2,1)}, u32[]{:S(2)}, u32[]{:S(2)}) collective-permute-start(bf16[2,128,512]{2,1,0:T(8,128)(2,1)} %get-tuple-element.450), channel_id=1, source_target_pairs={{0,8},{8,0},{1,9},{9,1},{2,10},{10,2},{3,11},{11,3},{4,12},{12,4},... | collective-permute-start | bytes 786440 | tf_op jit(solution)/shard_map/ppermute | solution.py:25
  75.7 12.9 %collective-permute-start.13 = (bf16[2,128,512]{2,1,0:T(8,128)(2,1)S(1)}, bf16[2,128,512]{2,1,0:T(8,128)(2,1)}, u32[]{:S(2)}, u32[]{:S(2)}) collective-permute-start(bf16[2,128,512]{2,1,0:T(8,128)(2,1)S(1)} %get-tuple-element.449), channel_id=1, source_target_pairs={{0,8},{8,0},{1,9},{9,1},{2,10},{10,2},{3,11},{11,3},{4,12},{12,4},... | collective-permute-start | bytes 786440 | tf_op jit(solution)/shard_map/ppermute | solution.py:25
  97.6 300.8 %reduce-scatter.3.cloned.1.call-start = ((), (), s32[]{:S(2)}) async-start(), calls=%async_computation.3 | async-start | bytes 8912896 | tf_op jit(solution)/shard_map/reduce_scatter | solution.py:1031
  106.4 39.5 %collective-permute-start.16 = (bf16[2,2,128,512]{3,2,1,0:T(8,128)(2,1)S(1)}, bf16[2,2,128,512]{3,2,1,0:T(8,128)(2,1)S(1)}, u32[]{:S(2)}, u32[]{:S(2)}) collective-permute-start(bf16[2,2,128,512]{3,2,1,0:T(8,128)(2,1)S(1)} %get-tuple-element.225), channel_id=1, source_target_pairs={{0,4},{4,0},{1,5},{5,1},{2,6},{6,2},{3,7},{7,3},{8,12},{12,8},{9,1... | collective-permute-start | bytes 1572872 | tf_op jit(solution)/shard_map/ppermute | solution.py:25
  106.7 39.1 %collective-permute-start.17 = (bf16[2,2,128,512]{3,2,1,0:T(8,128)(2,1)S(1)}, bf16[2,2,128,512]{3,2,1,0:T(8,128)(2,1)S(1)}, u32[]{:S(2)}, u32[]{:S(2)}) collective-permute-start(bf16[2,2,128,512]{3,2,1,0:T(8,128)(2,1)S(1)} %get-tuple-element.226), channel_id=1, source_target_pairs={{0,2},{2,0},{1,3},{3,1},{4,6},{6,4},{5,7},{7,5},{8,10},{10,8},{9,1... | collective-permute-start | bytes 1572872 | tf_op jit(solution)/shard_map/ppermute | solution.py:25
  108.5 12.2 %collective-permute-start.18 = (bf16[2,2,2,2,2,32,1024]{6,5,3,2,1,0,4:T(8,128)(2,1)S(1)}, bf16[2,2,2,2,2,32,1024]{6,5,3,2,1,0,4:T(8,128)(2,1)S(1)}, u32[]{:S(2)}, u32[]{:S(2)}) collective-permute-start(bf16[2,2,2,2,2,32,1024]{6,5,3,2,1,0,4:T(8,128)(2,1)S(1)} %broadcast_select_fusion.6), channel_id=1, source_target_pairs={{0,1},{1,0},{2,3},{3,2},{4,5},{5,4},{6,7},{7,6},{8,9},{9,8},{10,11... | collective-permute-start | bytes 6291464 | tf_op jit(solution)/shard_map/ppermute | solution.py:25
  108.5 12.2 %collective-permute-start.19 = (bf16[2,2,2,2,2,32,1024]{6,5,3,2,1,0,4:T(8,128)(2,1)S(1)}, bf16[2,2,2,2,2,32,1024]{6,5,3,2,1,0,4:T(8,128)(2,1)S(1)}, u32[]{:S(2)}, u32[]{:S(2)}) collective-permute-start(bf16[2,2,2,2,2,32,1024]{6,5,3,2,1,0,4:T(8,128)(2,1)S(1)} %broadcast_select_fusion.5), channel_id=1, source_target_pairs={{0,1},{1,0},{2,3},{3,2},{4,5},{5,4},{6,7},{7,6},{8,9},{9,8},{10,11... | collective-permute-start | bytes 6291464 | tf_op jit(solution)/shard_map/ppermute | solution.py:25
  111.3 72.2 %copy-start.52 = (f32[1,8,128]{2,1,0:T(8,128)}, f32[1,8,128]{2,1,0:T(8,128)S(1)}, u32[]{:S(2)}) copy-start(f32[1,8,128]{2,1,0:T(8,128)S(1)} %get-tuple-element.425) | copy-start | bytes 12292
  111.3 77.0 %copy-start.53 = (f32[1,8,128]{2,1,0:T(8,128)}, f32[1,8,128]{2,1,0:T(8,128)S(1)}, u32[]{:S(2)}) copy-start(f32[1,8,128]{2,1,0:T(8,128)S(1)} %get-tuple-element.426) | copy-start | bytes 12292
  148.1 25.5 %collective-permute-start.20 = (bf16[1024,512]{1,0:T(8,128)(2,1)S(1)}, bf16[1024,512]{1,0:T(8,128)(2,1)}, u32[]{:S(2)}, u32[]{:S(2)}) collective-permute-start(bf16[1024,512]{1,0:T(8,128)(2,1)S(1)} %bitcast.409), channel_id=1, source_target_pairs={{0,2},{2,0},{1,3},{3,1},{4,6},{6,4},{5,7},{7,5},{8,10},{10,8},{9,1... | collective-permute-start | bytes 3145736 | tf_op jit(solution)/shard_map/ppermute | solution.py:25
  148.4 31.3 %collective-permute-start.21 = (bf16[2,2,2,128,512]{4,3,1,0,2:T(8,128)(2,1)S(1)}, bf16[2,2,2,128,512]{4,3,1,0,2:T(8,128)(2,1)}, u32[]{:S(2)}, u32[]{:S(2)}) collective-permute-start(bf16[2,2,2,128,512]{4,3,1,0,2:T(8,128)(2,1)S(1)} %get-tuple-element.238), channel_id=1, source_target_pairs={{0,4},{4,0},{1,5},{5,1},{2,6},{6,2},{3,7},{7,3},{8,12},{12,8},{9,1... | collective-permute-start | bytes 3145736 | tf_op jit(solution)/shard_map/ppermute | solution.py:25
  182.6 21.5 %collective-permute-start.24 = (bf16[2,1024,512]{2,1,0:T(8,128)(2,1)}, bf16[2,1024,512]{2,1,0:T(8,128)(2,1)}, u32[]{:S(2)}, u32[]{:S(2)}) collective-permute-start(bf16[2,1024,512]{2,1,0:T(8,128)(2,1)} %bitcast.60.rest_4_), channel_id=1, source_target_pairs={{0,1},{1,0},{2,3},{3,2},{4,5},{5,4},{6,7},{7,6},{8,9},{9,8},{10,11... | collective-permute-start | bytes 6291464 | tf_op jit(solution)/shard_map/ppermute | solution.py:25
  184.7 14.8 %collective-permute-start.25 = (f32[2,1,1024]{2,1,0:T(1,128)S(1)}, f32[2,1,1024]{2,1,0:T(1,128)S(1)}, u32[]{:S(2)}, u32[]{:S(2)}) collective-permute-start(f32[2,1,1024]{2,1,0:T(1,128)S(1)} %broadcast_in_dim.626), channel_id=1, source_target_pairs={{0,1},{1,2},{2,3},{4,5},{5,6},{6,7},{8,9},{9,10},{10,11},{12,13},{... | collective-permute-start | bytes 24584 | tf_op jit(solution)/shard_map/ppermute | solution.py:861
  187.1 17.0 %collective-permute-start.22 = (bf16[1024,512]{1,0:T(8,128)(2,1)S(1)}, bf16[1024,512]{1,0:T(8,128)(2,1)S(1)}, u32[]{:S(2)}, u32[]{:S(2)}) collective-permute-start(bf16[1024,512]{1,0:T(8,128)(2,1)S(1)} %bitcast.410), channel_id=1, source_target_pairs={{0,1},{1,0},{2,3},{3,2},{4,5},{5,4},{6,7},{7,6},{8,9},{9,8},{10,11... | collective-permute-start | bytes 3145736 | tf_op jit(solution)/shard_map/ppermute | solution.py:25
  188.3 15.8 %collective-permute-start.23 = (bf16[1024,512]{1,0:T(8,128)(2,1)}, bf16[1024,512]{1,0:T(8,128)(2,1)S(1)}, u32[]{:S(2)}, u32[]{:S(2)}) collective-permute-start(bf16[1024,512]{1,0:T(8,128)(2,1)} %collective-permute-done.20.rest_2_), channel_id=1, source_target_pairs={{0,1},{1,0},{2,3},{3,2},{4,5},{5,4},{6,7},{7,6},{8,9},{9,8},{10,11... | collective-permute-start | bytes 3145736 | tf_op jit(solution)/shard_map/ppermute | solution.py:25
  255.5 232.5 %reduce-scatter.5.cloned.1.call-start = ((), (), s32[]{:S(2)}) async-start(), calls=%async_computation.4 | async-start | bytes 6684672 | tf_op jit(solution)/shard_map/reduce_scatter | solution.py:1074
  312.3 15.4 %collective-permute-start.26 = (bf16[1024,1024]{1,0:T(8,128)(2,1)}, bf16[1024,1024]{1,0:T(8,128)(2,1)}, u32[]{:S(2)}, u32[]{:S(2)}) collective-permute-start(bf16[1024,1024]{1,0:T(8,128)(2,1)} %fusion.18), channel_id=1, source_target_pairs={{0,1},{1,0},{2,3},{3,2},{4,5},{5,4},{6,7},{7,6},{8,9},{9,8},{10,11... | collective-permute-start | bytes 6291464 | tf_op jit(solution)/shard_map/ppermute | solution.py:25
  312.8 15.0 %collective-permute-start.27 = (bf16[1024,1024]{1,0:T(8,128)(2,1)}, bf16[1024,1024]{1,0:T(8,128)(2,1)}, u32[]{:S(2)}, u32[]{:S(2)}) collective-permute-start(bf16[1024,1024]{1,0:T(8,128)(2,1)} %fusion.21), channel_id=1, source_target_pairs={{0,1},{1,0},{2,3},{3,2},{4,5},{5,4},{6,7},{7,6},{8,9},{9,8},{10,11... | collective-permute-start | bytes 6291464 | tf_op jit(solution)/shard_map/ppermute | solution.py:25
  312.9 26.6 %collective-permute-start.30 = (f32[2,1,1024]{2,1,0:T(1,128)S(1)}, f32[2,1,1024]{2,1,0:T(1,128)S(1)}, u32[]{:S(2)}, u32[]{:S(2)}) collective-permute-start(f32[2,1,1024]{2,1,0:T(1,128)S(1)} %get-tuple-element.435), channel_id=1, source_target_pairs={{1,0},{2,1},{3,2},{5,4},{6,5},{7,6},{9,8},{10,9},{11,10},{13,12},{... | collective-permute-start | bytes 24584 | tf_op jit(solution)/shard_map/ppermute | solution.py:861
  336.1 31.6 %collective-permute-start.28 = (bf16[2,2,2,128,512]{4,3,2,1,0:T(8,128)(2,1)}, bf16[2,2,2,128,512]{4,3,2,1,0:T(8,128)(2,1)S(1)}, u32[]{:S(2)}, u32[]{:S(2)}) collective-permute-start(bf16[2,2,2,128,512]{4,3,2,1,0:T(8,128)(2,1)} %pad_maximum_fusion.4), channel_id=1, source_target_pairs={{0,4},{4,0},{1,5},{5,1},{2,6},{6,2},{3,7},{7,3},{8,12},{12,8},{9,1... | collective-permute-start | bytes 3145736 | tf_op jit(solution)/shard_map/ppermute | solution.py:25
  336.7 31.0 %collective-permute-start.29 = (bf16[1024,512]{1,0:T(8,128)(2,1)}, bf16[1024,512]{1,0:T(8,128)(2,1)}, u32[]{:S(2)}, u32[]{:S(2)}) collective-permute-start(bf16[1024,512]{1,0:T(8,128)(2,1)} %get-tuple-element.277), channel_id=1, source_target_pairs={{0,2},{2,0},{1,3},{3,1},{4,6},{6,4},{5,7},{7,5},{8,10},{10,8},{9,1... | collective-permute-start | bytes 3145736 | tf_op jit(solution)/shard_map/ppermute | solution.py:25
  376.5 21.9 %collective-permute-start.31 = (bf16[2,2,128,512]{3,2,1,0:T(8,128)(2,1)S(1)}, bf16[2,2,128,512]{3,2,1,0:T(8,128)(2,1)}, u32[]{:S(2)}, u32[]{:S(2)}) collective-permute-start(bf16[2,2,128,512]{3,2,1,0:T(8,128)(2,1)S(1)} %dynamic-slice_bitcast_fusion.2), channel_id=1, source_target_pairs={{0,4},{4,0},{1,5},{5,1},{2,6},{6,2},{3,7},{7,3},{8,12},{12,8},{9,1... | collective-permute-start | bytes 1572872 | tf_op jit(solution)/shard_map/ppermute | solution.py:25
  377.2 21.1 %collective-permute-start.32 = (bf16[2,2,128,512]{3,2,1,0:T(8,128)(2,1)S(1)}, bf16[2,2,128,512]{3,2,1,0:T(8,128)(2,1)}, u32[]{:S(2)}, u32[]{:S(2)}) collective-permute-start(bf16[2,2,128,512]{3,2,1,0:T(8,128)(2,1)S(1)} %slice_bitcast_fusion.1), channel_id=1, source_target_pairs={{0,2},{2,0},{1,3},{3,1},{4,6},{6,4},{5,7},{7,5},{8,10},{10,8},{9,1... | collective-permute-start | bytes 1572872 | tf_op jit(solution)/shard_map/ppermute | solution.py:25
  410.2 15.3 %collective-permute-start.33 = (bf16[2,2,2,2,2,32,1024]{6,5,4,3,2,1,0:T(8,128)(2,1)}, bf16[2,2,2,2,2,32,1024]{6,5,4,3,2,1,0:T(8,128)(2,1)S(1)}, u32[]{:S(2)}, u32[]{:S(2)}) collective-permute-start(bf16[2,2,2,2,2,32,1024]{6,5,4,3,2,1,0:T(8,128)(2,1)} %pad_maximum_fusion.2), channel_id=1, source_target_pairs={{0,1},{1,0},{2,3},{3,2},{4,5},{5,4},{6,7},{7,6},{8,9},{9,8},{10,11... | collective-permute-start | bytes 6291464 | tf_op jit(solution)/shard_map/ppermute | solution.py:25
  411.2 14.3 %collective-permute-start.34 = (bf16[256,1024]{1,0:T(8,128)(2,1)}, bf16[256,1024]{1,0:T(8,128)(2,1)}, u32[]{:S(2)}, u32[]{:S(2)}) collective-permute-start(bf16[256,1024]{1,0:T(8,128)(2,1)} %reduce-scatter.3.cloned.1.call-done), channel_id=1, source_target_pairs={{0,2},{2,0},{1,3},{3,1},{4,6},{6,4},{5,7},{7,5},{8,10},{10,8},{9,1... | collective-permute-start | bytes 1572872 | tf_op jit(solution)/shard_map/ppermute | solution.py:25
  432.1 26.0 %collective-permute-start.35 = (bf16[2,2,2,2,32,1024]{5,4,3,2,1,0:T(8,128)(2,1)}, bf16[2,2,2,2,32,1024]{5,4,3,2,1,0:T(8,128)(2,1)}, u32[]{:S(2)}, u32[]{:S(2)}) collective-permute-start(bf16[2,2,2,2,32,1024]{5,4,3,2,1,0:T(8,128)(2,1)} %dynamic-slice_bitcast_fusion), channel_id=1, source_target_pairs={{0,2},{2,0},{1,3},{3,1},{4,6},{6,4},{5,7},{7,5},{8,10},{10,8},{9,1... | collective-permute-start | bytes 3145736 | tf_op jit(solution)/shard_map/ppermute | solution.py:25
  433.5 24.6 %collective-permute-start.36 = (bf16[2,2,128,512]{3,2,1,0:T(8,128)(2,1)}, bf16[2,2,128,512]{3,2,1,0:T(8,128)(2,1)}, u32[]{:S(2)}, u32[]{:S(2)}) collective-permute-start(bf16[2,2,128,512]{3,2,1,0:T(8,128)(2,1)} %pad_maximum_fusion.5), channel_id=1, source_target_pairs={{0,8},{8,0},{1,9},{9,1},{2,10},{10,2},{3,11},{11,3},{4,12},{12,4},... | collective-permute-start | bytes 1572872 | tf_op jit(solution)/shard_map/ppermute | solution.py:25
  435.0 23.1 %collective-permute-start.37 = (bf16[256,1024]{1,0:T(8,128)(2,1)S(1)}, bf16[256,1024]{1,0:T(8,128)(2,1)}, u32[]{:S(2)}, u32[]{:S(2)}) collective-permute-start(bf16[256,1024]{1,0:T(8,128)(2,1)S(1)} %add_convert_fusion.11), channel_id=1, source_target_pairs={{0,1},{1,0},{2,3},{3,2},{4,5},{5,4},{6,7},{7,6},{8,9},{9,8},{10,11... | collective-permute-start | bytes 1572872 | tf_op jit(solution)/shard_map/ppermute | solution.py:25
  462.7 5.6 %collective-permute-start.39 = (f32[2,1,1024]{2,1,0:T(1,128)S(1)}, f32[2,1,1024]{2,1,0:T(1,128)S(1)}, u32[]{:S(2)}, u32[]{:S(2)}) collective-permute-start(f32[2,1,1024]{2,1,0:T(1,128)S(1)} %fusion.61), channel_id=1, source_target_pairs={{1,0},{2,1},{3,2},{5,4},{6,5},{7,6},{9,8},{10,9},{11,10},{13,12},{... | collective-permute-start | bytes 24584 | tf_op jit(solution)/shard_map/ppermute | solution.py:861
  464.3 24.0 %collective-permute-start.43 = (bf16[2,128,512]{2,1,0:T(8,128)(2,1)}, bf16[2,128,512]{2,1,0:T(8,128)(2,1)S(1)}, u32[]{:S(2)}, u32[]{:S(2)}) collective-permute-start(bf16[2,128,512]{2,1,0:T(8,128)(2,1)} %dynamic-slice_bitcast_fusion.5), channel_id=1, source_target_pairs={{0,16},{16,0},{1,17},{17,1},{2,18},{18,2},{3,19},{19,3},{4,20},{20... | collective-permute-start | bytes 786440 | tf_op jit(solution)/shard_map/ppermute | solution.py:25
  466.9 14.7 %collective-permute-start.38 = (bf16[2,2,2,32,1024]{4,3,2,1,0:T(8,128)(2,1)S(1)}, bf16[2,2,2,32,1024]{4,3,2,1,0:T(8,128)(2,1)S(1)}, u32[]{:S(2)}, u32[]{:S(2)}) collective-permute-start(bf16[2,2,2,32,1024]{4,3,2,1,0:T(8,128)(2,1)S(1)} %dynamic-slice_bitcast_fusion.1), channel_id=1, source_target_pairs={{0,4},{4,0},{1,5},{5,1},{2,6},{6,2},{3,7},{7,3},{8,12},{12,8},{9,1... | collective-permute-start | bytes 1572872 | tf_op jit(solution)/shard_map/ppermute | solution.py:25
  481.9 11.8 %collective-permute-start.41 = (bf16[2,2,32,1024]{3,2,1,0:T(8,128)(2,1)S(1)}, bf16[2,2,32,1024]{3,2,1,0:T(8,128)(2,1)S(1)}, u32[]{:S(2)}, u32[]{:S(2)}) collective-permute-start(bf16[2,2,32,1024]{3,2,1,0:T(8,128)(2,1)S(1)} %dynamic-slice_bitcast_fusion.4), channel_id=1, source_target_pairs={{0,8},{8,0},{1,9},{9,1},{2,10},{10,2},{3,11},{11,3},{4,12},{12,4},... | collective-permute-start | bytes 786440 | tf_op jit(solution)/shard_map/ppermute | solution.py:25
  482.6 1.3 collective-permute-start.40
  483.8 4.5 collective-permute-start.42
  493.8 11.0 %collective-permute-start.47 = (bf16[2,128,512]{2,1,0:T(8,128)(2,1)S(1)}, bf16[2,128,512]{2,1,0:T(8,128)(2,1)S(1)}, u32[]{:S(2)}, u32[]{:S(2)}) collective-permute-start(bf16[2,128,512]{2,1,0:T(8,128)(2,1)S(1)} %fusion.35), channel_id=1, source_target_pairs={{0,2},{2,0},{1,3},{3,1},{4,6},{6,4},{5,7},{7,5},{8,10},{10,8},{9,1... | collective-permute-start | bytes 786440 | tf_op jit(solution)/shard_map/ppermute | solution.py:25
  494.9 15.3 %collective-permute-start.48 = (bf16[64,3072]{1,0:T(8,128)(2,1)}, bf16[64,3072]{1,0:T(8,128)(2,1)S(1)}, u32[]{:S(2)}, u32[]{:S(2)}) collective-permute-start(bf16[64,3072]{1,0:T(8,128)(2,1)} %reduce-scatter.5.cloned.1.call-done), channel_id=1, source_target_pairs={{0,2},{2,0},{1,3},{3,1},{4,6},{6,4},{5,7},{7,5},{8,10},{10,8},{9,1... | collective-permute-start | bytes 1179656 | tf_op jit(solution)/shard_map/ppermute | solution.py:25
  495.9 8.8 %collective-permute-start.45 = (bf16[2,32,1024]{2,1,0:T(8,128)(2,1)S(1)}, bf16[2,32,1024]{2,1,0:T(8,128)(2,1)S(1)}, u32[]{:S(2)}, u32[]{:S(2)}) collective-permute-start(bf16[2,32,1024]{2,1,0:T(8,128)(2,1)S(1)} %dynamic-slice_bitcast_fusion.6), channel_id=1, source_target_pairs={{0,16},{16,0},{1,17},{17,1},{2,18},{18,2},{3,19},{19,3},{4,20},{20... | collective-permute-start | bytes 393224 | tf_op jit(solution)/shard_map/ppermute | solution.py:25
  496.0 4.3 collective-permute-start.44
  500.4 4.4 collective-permute-start.46
  510.4 11.6 %collective-permute-start.50 = (bf16[2,2,128,512]{3,2,1,0:T(8,128)(2,1)S(1)}, bf16[2,2,128,512]{3,2,1,0:T(8,128)(2,1)S(1)}, u32[]{:S(2)}, u32[]{:S(2)}) collective-permute-start(bf16[2,2,128,512]{3,2,1,0:T(8,128)(2,1)S(1)} %broadcast_select_fusion.13), channel_id=1, source_target_pairs={{0,1},{1,0},{2,3},{3,2},{4,5},{5,4},{6,7},{7,6},{8,9},{9,8},{10,11... | collective-permute-start | bytes 1572872 | tf_op jit(solution)/shard_map/ppermute | solution.py:25
  510.6 11.4 %collective-permute-start.54 = (bf16[64,3072]{1,0:T(8,128)(2,1)S(1)}, bf16[64,3072]{1,0:T(8,128)(2,1)S(1)}, u32[]{:S(2)}, u32[]{:S(2)}) collective-permute-start(bf16[64,3072]{1,0:T(8,128)(2,1)S(1)} %add_convert_fusion.12), channel_id=1, source_target_pairs={{0,1},{1,0},{2,3},{3,2},{4,5},{5,4},{6,7},{7,6},{8,9},{9,8},{10,11... | collective-permute-start | bytes 1179656 | tf_op jit(solution)/shard_map/ppermute | solution.py:25
  511.2 5.6 %collective-permute-start.49 = (f32[12,1024]{1,0:T(8,128)S(1)}, f32[12,1024]{1,0:T(8,128)S(1)}, u32[]{:S(2)}, u32[]{:S(2)}) collective-permute-start(f32[12,1024]{1,0:T(8,128)S(1)} %add.349), channel_id=1, source_target_pairs={{0,16},{16,0},{1,17},{17,1},{2,18},{18,2},{3,19},{19,3},{4,20},{20... | collective-permute-start | bytes 147464 | tf_op jit(solution)/shard_map/ppermute | solution.py:25
  511.3 10.5 %collective-permute-start.53 = (bf16[2,32,1024]{2,1,0:T(8,128)(2,1)S(1)}, bf16[2,32,1024]{2,1,0:T(8,128)(2,1)S(1)}, u32[]{:S(2)}, u32[]{:S(2)}) collective-permute-start(bf16[2,32,1024]{2,1,0:T(8,128)(2,1)S(1)} %fusion.37), channel_id=1, source_target_pairs={{0,3},{1,2},{2,1},{3,0},{4,7},{5,6},{6,5},{7,4},{8,11},{9,10},{10,... | collective-permute-start | bytes 393224 | tf_op jit(solution)/shard_map/ppermute | solution.py:1165
  511.7 10.1 %collective-permute-start.52 = (bf16[2,32,1024]{2,1,0:T(8,128)(2,1)S(1)}, bf16[2,32,1024]{2,1,0:T(8,128)(2,1)S(1)}, u32[]{:S(2)}, u32[]{:S(2)}) collective-permute-start(bf16[2,32,1024]{2,1,0:T(8,128)(2,1)S(1)} %fusion.37), channel_id=1, source_target_pairs={{0,1},{1,0},{2,3},{3,2},{4,5},{5,4},{6,7},{7,6},{8,9},{9,8},{10,11... | collective-permute-start | bytes 393224 | tf_op jit(solution)/shard_map/ppermute | solution.py:25
  516.8 5.2 collective-permute-start.51
  (86 other events, 824.8 us)
Sparse Core Ops, SparseCore 0:
  10.8 47.0 all-gather.9
  97.7 84.4 all-gather.7
  255.6 108.6 reduce-scatter.2
  382.0 105.9 reduce-scatter.4

commit v4 on v3

--- a/solution.py
+++ b/solution.py
@@ -349,14 +349,17 @@
 
 def load_pieces(refs, held, sems):
     left, right = refs[:4], refs[4:]
-    per = PIECES // held.shape[0]
-    width = held.shape[2] // per
+    per = 4 // held.shape[0]
+    whole = held.shape[2] // per
     copies = []
     for p in range(4):
-        for side, ref in enumerate((left[p], right[p % 2].at[p // 2])):
-            i = 2 * p + side
-            to = held.at[i // per, :, pl.ds((i % per) * width, width)]
-            copies.append(pltpu.make_async_copy(ref, to, sems.at[i]))
+        at = (p % per) * whole
+        for ref in (left[p], right[p % 2].at[p // 2]):
+            width = ref.shape[-1]
+            copies.append(
+                pltpu.make_async_copy(ref, held.at[p // per, :, pl.ds(at, width)], sems.at[len(copies)])
+            )
+            at += width
     return copies
 
 
@@ -426,7 +429,7 @@
 
 def feed_forward(my_seq, left, inputs, pieces, weight, gate_inputs, gate_weight, middle, cotangent, seqs):
     total = inputs.shape[0]
-    width = 2 * pieces[0].shape[1]
+    width = pieces[0].shape[1] + pieces[4].shape[2]
     span = total // seqs
     ff = 4 * width
     big = pl.BlockSpec((span, D), lambda i, *_: (i, 0))
@@ -807,10 +810,11 @@
     return lax.dynamic_update_slice(whole, rows.astype(values.dtype), (0, at, 0)).reshape(values.shape)
 
 
-def cut_kernel(_, k, v, r, o, fk1, fk2, rows, kv_out, ro_out, f1_out, f2_out, row_out):
+def cut_kernel(_, k, v, r, o, fk, rows, kv_out, ro_out, f1_out, f2_out, row_out):
     kv_out[0], kv_out[1] = k[...], v[...]
     ro_out[0], ro_out[1] = r[...], o[...]
-    f1_out[...], f2_out[...] = fk1[...], fk2[...]
+    left = f1_out.shape[1]
+    f1_out[...], f2_out[...] = fk[:, :left], fk[:, left:]
     last = rows.shape[1] - 1
     row_out[...] = rows[...].astype(F32)[:, last:, :]
 
@@ -819,9 +823,10 @@
     seqs, span, _ = tokens.shape
     shard, ff = feed_key.shape
     part = pl.BlockSpec((quarter, D), lambda i, at: (at[0], 0))
-    side = lambda which: pl.BlockSpec((shard, ff // PIECES), lambda i, at: (0, 2 * at[0] + which))
+    side = pl.BlockSpec((shard, ff // 4), lambda i, at: (0, at[0]))
+    left = ff // 32 * 5
     full = lambda *shape: pl.BlockSpec(shape, lambda i, at: (0,) * len(shape))
-    shapes = [(2, quarter, D), (2, quarter, D)] + [(shard, ff // PIECES)] * 2 + [(seqs, 1, D)]
+    shapes = [(2, quarter, D), (2, quarter, D)] + [(shard, left), (shard, ff // 4 - left), (seqs, 1, D)]
     kinds = [BF16] * 4 + [F32]
     return pl.pallas_call(
         cut_kernel,
@@ -829,11 +834,11 @@
             num_scalar_prefetch=1,
             grid=(1,),
             in_specs=[part] * 4
-            + [side(0), side(1), pl.BlockSpec((seqs, 2 * ROWS, D), lambda i, at: (0, span // (2 * ROWS) - 1, 0))],
+            + [side, pl.BlockSpec((seqs, 2 * ROWS, D), lambda i, at: (0, span // (2 * ROWS) - 1, 0))],
             out_specs=[full(*shape) for shape in shapes],
         ),
         out_shape=[jax.ShapeDtypeStruct(shape, kind) for shape, kind in zip(shapes, kinds)],
-    )(my_seq[None], key, value, recept, output, feed_key, feed_key, tokens)
+    )(my_seq[None], key, value, recept, output, feed_key, tokens)
 
 
 def dot(left, right):
@@ -1151,7 +1156,8 @@
     small.start(x)
     small.finish()
     small.start(z1)
-    (orf_got,) = settle([r_kv, small, out_f], orf_got)
+    grad_fv = out_v.value.reshape(hid, D).astype(F32)
+    orf_got, grad_fv = settle([r_kv, small, out_f], orf_got, grad_fv)
     out_f.start(c)
     orf = add_low(orf, orf_got)
     orf_c = swap(orf, c)
@@ -1170,7 +1176,6 @@
     wide_out = lambda v, i: v[:, :, i].reshape(shard, -1)
     out_f = out_f.value.reshape(2 * seq, shard, side)
     grad_fk = jnp.concatenate([out_f[i] for i in range(2 * seq)], axis=1).astype(F32)
-    grad_fv = out_v.value.reshape(hid, D).astype(F32)
     orf = join(orf, orf_c, c, 0).reshape(shard, 3 * D).astype(F32)
     grad_o, grad_r, grad_fr = [orf[:, i * D : i * D + D] for i in range(3)]
     grad_k, grad_v = [wide_out(out_kv, i).astype(F32) for i in range(2)]

time: 540 us -> 534 us (0.989)
  other arithmetic: 70.3 us -> 76.4 us
    select_n x23 -> x25, other arithmetic: 20.4 us -> 21 us  [join(): jnp.where(side == lax.axis_index(key), jnp.expand_dims(mine, at), jnp.exp...]
  transfers between devices with their start and end apart: 59 -> 59, of which waited for: 23 -> 21; matrix products, arithmetic and copies ran while one was open for 26% -> 27% of each run, Pallas kernels for 23% -> 24%
where the time goes in v4:
time: 534 us; the launch traced here: 532 us
  Pallas kernels  161 us (30%)
  waiting for transfers between devices  101 us (19%)
  other arithmetic  76.4 us (14%)
  matrix products  66.6 us (12%)
  starting transfers between devices  57.3 us (11%)
  local copies, waits for them, and re-layouts  32.5 us (6%)
  blocking collectives  20.6 us (4%)
  between operations  16.5 us (3%)
    ppermute x50, waiting for transfers between devices, swap(): return lax.ppermute(value, key, [(0, 1), (1, 0)])  100 us
    dot_general x10, matrix products, dot_weight(): lax.dot_general(inputs, grads, (((0,), (0,)), ((), ())), preferred_elemen...  54 us
    ppermute x50, starting transfers between devices, swap(): return lax.ppermute(value, key, [(0, 1), (1, 0)])  49.3 us
    pallas_call x1, Pallas kernels, down(): pl.pallas_call(down_kernel, grid_spec=pltpu.PrefetchScalarGridSpec(num_sc...  46.6 us
    pallas_call x1, Pallas kernels, feed_forward(): pl.pallas_call(feed_kernel, grid_spec=pltpu.PrefetchScalarGridSpec(num_sc...  34.6 us
    pallas_call x1, Pallas kernels, mix_back(): pl.pallas_call(mix_kernel, grid=(seqs,), in_specs=[big, big, big, full, f...  23.1 us
    select_n x25, other arithmetic, join(): jnp.where(side == lax.axis_index(key), jnp.expand_dims(mine, at), jnp.exp...  21 us
    all_gather x2, blocking collectives, earlier_state(): packed = lax.all_gather(jnp.concatenate([num, den], axis=0), axes)  20.6 us
  transfers between devices with their start and end apart: 59, of which 21 were waited for; matrix products, arithmetic and copies ran while one was open for 27% of the time, Pallas kernels for 24%

profile of v4, /device:TPU:0, one launch (start us, length us, event | category | flops | bytes accessed | tf_op | source)
XLA Modules:
  0.0 531.7 jit_solution(3188061797679108094)
XLA Ops:
  9.1 1.9 shard_map.389
  11.1 4.1 collective-permute-start
  15.4 2.9 collective-permute-start.2
  19.6 10.1 %collective-permute-done.2 = bf16[11,128]{1,0:T(8,128)(2,1)S(1)} collective-permute-done((bf16[11,128]{1,0:T(8,128)(2,1)S(1)}, bf16[11,128]{1,0:T(8,128)(2,1)S(1)}, u32[]{:S(2)}, u32[]{:S(2)}) %collective-permute-start.2) | collective-permute-done | bytes 2848 | tf_op jit(solution)/shard_map/ppermute | solution.py:25
  34.5 14.0 %collective-permute-done.6 = bf16[2,11,128]{2,0,1:T(2,128)(2,1)S(1)} collective-permute-done((bf16[2,11,128]{2,0,1:T(2,128)(2,1)S(1)}, bf16[2,11,128]{2,0,1:T(2,128)(2,1)S(1)}, u32[]{:S(2)}, u32[]{:S(2)}) %collective-permute-start.6) | collective-permute-done | bytes 5664 | tf_op jit(solution)/shard_map/ppermute | solution.py:25
  51.3 7.3 %collective-permute-start.10 = (bf16[128,640]{1,0:T(8,128)(2,1)S(1)}, bf16[128,640]{1,0:T(8,128)(2,1)S(1)}, u32[]{:S(2)}, u32[]{:S(2)}) collective-permute-start(bf16[128,640]{1,0:T(8,128)(2,1)S(1)} %copy-done.42), channel_id=1, source_target_pairs={{0,16},{16,0},{1,17},{17,1},{2,18},{18,2},{3,19},{19,3},{4,20},{20... | collective-permute-start | bytes 491528 | tf_op jit(solution)/shard_map/ppermute | solution.py:25
  58.9 3.5 collective-permute-done.9
  62.4 4.7 collective-permute-done.11
  70.1 2.1 broadcast_select_fusion.11
  72.2 2.6 collective-permute-start.14
  75.8 2.1 collective-permute-start.13
  78.7 10.1 %collective-permute-done.13 = bf16[2,128,384]{2,1,0:T(8,128)(2,1)S(1)} collective-permute-done((bf16[2,128,384]{2,1,0:T(8,128)(2,1)S(1)}, bf16[2,128,384]{2,1,0:T(8,128)(2,1)S(1)}, u32[]{:S(2)}, u32[]{:S(2)}) %collective-permute-start.13) | collective-permute-done | bytes 196640 | tf_op jit(solution)/shard_map/ppermute | solution.py:25
  88.7 3.6 collective-permute-done.15
  92.4 5.4 %collective-permute-done.14 = bf16[2,2,2,2,32,1024]{5,4,2,1,0,3:T(8,128)(2,1)} collective-permute-done((bf16[2,2,2,2,32,1024]{5,4,2,1,0,3:T(8,128)(2,1)}, bf16[2,2,2,2,32,1024]{5,4,2,1,0,3:T(8,128)(2,1)}, u32[]{:S(2)}, u32[]{:S(2)}) %collective-permute-start.14) | collective-permute-done | bytes 1048608 | tf_op jit(solution)/shard_map/ppermute | solution.py:25
  106.3 1.9 broadcast_select_fusion.5
  108.2 1.8 collective-permute-start.17
  116.8 3.9 add_convert_fusion.1
  120.8 2.6 broadcast_select_fusion
  123.9 3.7 fusion.85
  127.6 4.9 multiply_reduce_fusion
  132.5 15.4 %all-gather.3 = f32[4,4,1024]{2,1,0:T(4,128)S(1)} all-gather(f32[1,4,1024]{2,1,0:T(4,128)S(1)} %maximum_bitcast_fusion), channel_id=3, replica_groups=mesh['d2'=2,'d1'=2,'d0'=2,'s1'=2,'s0'=2] {'s1','s0'}, dimensions={0}, use_global_device_ids=true | all-gather | bytes 81920 | tf_op jit(solution)/shard_map/all_gather | solution.py:884
  152.4 1.7 collective-permute-start.21
  154.1 2.8 fusion.77
  157.0 3.7 convolution_convert_fusion.6.r_ref
  160.7 13.7 %shard_map.390 = (bf16[1024,1024]{1,0:T(8,128)(2,1)}, f32[1024,1024]{1,0:T(8,128)}, f32[1024,1024]{1,0:T(8,128)}) custom-call(f32[1024,1024]{1,0:T(8,128)} %get-tuple-element.453.k_ref, bf16[1024,1024]{1,0:T(8,128)(2,1)} %get-tuple-element.454.v_ref, bf16[1024,1024]{1,0:T(8,128)(2,1)} %convolution_convert_fusion.6.r_ref, f32[1,1024]{1,0:T(1,128)} %bitcast.456, ...), custom_call_target="tpu_custom_call" | custom-call | flops 1048576 | bytes 65536 | tf_op jit(solution)/shard_map/pallas_call | solution.py:286
  174.3 7.3 %collective-permute-done.20.rest_2_ = bf16[1024,640]{1,0:T(8,128)(2,1)} collective-permute-done((bf16[1024,640]{1,0:T(8,128)(2,1)}, bf16[1024,640]{1,0:T(8,128)(2,1)}, u32[]{:S(2)}, u32[]{:S(2)}) %collective-permute-start.20) | collective-permute-done | bytes 1310752 | tf_op jit(solution)/shard_map/ppermute | solution.py:25
  184.9 2.3 collective-permute-start.25
  187.3 11.1 %shard_map.391 = (f32[1024,1024]{1,0:T(8,128)}, bf16[1024,1024]{1,0:T(8,128)(2,1)}, bf16[1024,1024]{1,0:T(8,128)(2,1)}, f32[2,1,1024]{2,1,0:T(1,128)}, f32[2,8,1024]{2,1,0:T(8,128)}) custom-call(s32[2]{0:T(128)} %broadcast_subtract_fusion.5.left_ref, bf16[1024,1024]{1,0:T(8,128)(2,1)} %get-tuple-element.250.w_ref, bf16[1024,1024]{1,0:T(8,128)(2,1)} %bitcast.404, ...), custom_call_target="tpu_custom_call" | custom-call | flops 1048576 | bytes 65536 | tf_op jit(solution)/shard_map/pallas_call | solution.py:537
  203.1 34.6 %shard_map.392 = (bf16[1024,4096]{1,0:T(8,128)(2,1)}, bf16[1024,1024]{1,0:T(8,128)(2,1)}, bf16[1024,1024]{1,0:T(8,128)(2,1)}, bf16[1024,1024]{1,0:T(8,128)(2,1)}, f32[2,2,8,1024]{3,2,1,0:T(8,128)}) custom-call(s32[1]{0:T(128)} %bitcast._.s_ref, s32[2]{0:T(128)} %broadcast_subtract_fusion.5.left_ref, bf16[1024,1024]{1,0:T(8,128)(2,1)} %bitcast.438, ...), custom_call_target="tpu_custom_call" | custom-call | flops 1048576 | bytes 65536 | tf_op jit(solution)/shard_map/pallas_call | solution.py:436
  237.7 15.5 %convolution_convert_fusion = bf16[4096,1024]{1,0:T(8,128)(2,1)} fusion(bf16[1024,4096]{1,0:T(8,128)(2,1)} %get-tuple-element.263.sq_ref, bf16[1024,1024]{1,0:T(8,128)(2,1)} %get-tuple-element.262.dval_ref), kind=kOutput, calls=%fused_computation | convolution fusion | flops 8594128896 | bytes 18874368 | tf_op jit(solution)/shard_map/dot_general | solution.py:853
  253.2 46.6 %shard_map.393 = (bf16[4,1024,1024]{2,1,0:T(8,128)(2,1)}, f32[1024,1024]{1,0:T(8,128)}, bf16[1024,1024]{1,0:T(8,128)(2,1)}, f32[2,1,1024]{2,1,0:T(1,128)}, f32[2...) custom-call(s32[1]{0:T(128)} %bitcast._.s_ref, s32[2]{0:T(128)} %broadcast_subtract_fusion.5.left_ref, ...), custom_call_target="tpu_custom_call" | custom-call | flops 1048576 | bytes 65536 | tf_op jit(solution)/shard_map/pallas_call | solution.py:667
  299.8 5.5 %fusion.21 = bf16[1024,1024]{1,0:T(8,128)(2,1)} fusion(bf16[1024,1024]{1,0:T(8,128)(2,1)S(1)} %bitcast.439, bf16[4,1024,1024]{2,1,0:T(8,128)(2,1)} %get-tuple-element.269), kind=kOutput, calls=%fused_computation.45 | convolution fusion | flops 2148532224 | bytes 6291456 | tf_op jit(solution)/shard_map/dot_general | solution.py:853
  305.3 5.5 %fusion.18 = bf16[1024,1024]{1,0:T(8,128)(2,1)} fusion(bf16[1024,1024]{1,0:T(8,128)(2,1)S(1)} %bitcast.440, bf16[4,1024,1024]{2,1,0:T(8,128)(2,1)} %get-tuple-element.269), kind=kOutput, calls=%fused_computation.44 | convolution fusion | flops 2148532224 | bytes 6291456 | tf_op jit(solution)/shard_map/dot_general | solution.py:853
  312.8 5.3 %convolution_convert_fusion.1 = bf16[1024,1024]{1,0:T(8,128)(2,1)} fusion(bf16[1024,1024]{1,0:T(8,128)(2,1)} %bitcast.445, bf16[1024,1024]{1,0:T(8,128)(2,1)S(1)} %copy-done.14), kind=kOutput, calls=%fused_computation.48 | convolution fusion | flops 2148532224 | bytes 6291456 | tf_op jit(solution)/shard_map/dot_general | solution.py:853
  318.2 4.1 fusion.27
  322.3 4.0 fusion.24
  326.3 3.9 add_convert_fusion.6
  336.3 2.4 collective-permute-start.29
  340.9 15.0 %shard_map.394 = (bf16[1024,1024]{1,0:T(8,128)(2,1)}, bf16[1024,1024]{1,0:T(8,128)(2,1)}, f32[2,8,1024]{2,1,0:T(8,128)}, f32[2,8,1024]{2,1,0:T(8,128)}) custom-call(bf16[1024,1024]{1,0:T(8,128)(2,1)} %bitcast.433, bf16[1024,1024]{1,0:T(8,128)(2,1)} %bitcast.405, f32[1024,1024]{1,0:T(8,128)} %get-tuple-element.453.k_ref, ...), custom_call_target="tpu_custom_call" | custom-call | flops 1048576 | bytes 65536 | tf_op jit(solution)/shard_map/pallas_call | solution.py:326
  356.8 5.5 %convolution_convert_fusion.5 = bf16[1024,1024]{1,0:T(8,128)(2,1)} fusion(bf16[1024,1024]{1,0:T(8,128)(2,1)S(1)} %copy-done.10, bf16[1024,1024]{1,0:T(8,128)(2,1)} %bitcast.434), kind=kOutput, calls=%fused_computation.52 | convolution fusion | flops 2148532224 | bytes 6291456 | tf_op jit(solution)/shard_map/dot_general | solution.py:853
  362.3 3.8 convolution_convert_fusion.4
  366.1 5.2 all-gather.4
  372.0 2.4 add_convert_fusion.5
  374.6 1.7 add_convert_fusion.4
  378.0 3.4 pad_maximum_fusion
  383.6 15.2 %shard_map.395 = (bf16[1024,1024]{1,0:T(8,128)(2,1)}, bf16[1024,1024]{1,0:T(8,128)(2,1)}, f32[2,8,1024]{2,1,0:T(8,128)}, f32[2,8,1024]{2,1,0:T(8,128)}) custom-call(f32[1024,1024]{1,0:T(8,128)} %get-tuple-element.453.k_ref, bf16[1024,1024]{1,0:T(8,128)(2,1)} %get-tuple-element.454.v_ref, f32[1024,1024]{1,0:T(8,128)} %get-tuple-element.283.a_ref, ...), custom_call_target="tpu_custom_call" | custom-call | flops 1048576 | bytes 65536 | tf_op jit(solution)/shard_map/pallas_call | solution.py:305
  398.9 1.7 fusion.31
  402.4 2.4 convolution_convert_fusion.3
  404.9 2.4 convolution_convert_fusion.2
  407.3 1.8 constant_dynamic-slice_fusion.7
  413.5 2.0 select_maximum_fusion
  419.5 7.2 %collective-permute-done.34 = bf16[256,1024]{1,0:T(8,128)(2,1)} collective-permute-done((bf16[256,1024]{1,0:T(8,128)(2,1)}, bf16[256,1024]{1,0:T(8,128)(2,1)}, u32[]{:S(2)}, u32[]{:S(2)}) %collective-permute-start.34) | collective-permute-done | bytes 524320 | tf_op jit(solution)/shard_map/ppermute | solution.py:25
  428.0 2.9 add_convert_fusion
  434.4 23.1 %shard_map.396 = (bf16[1024,1024]{1,0:T(8,128)(2,1)}, f32[2,3,1,1024]{3,2,1,0:T(1,128)}, f32[2,3,1,1024]{3,2,1,0:T(1,128)}, f32[2,5,8,1024]{3,2,1,0:T(8,128)}) custom-call(bf16[1024,1024]{1,0:T(8,128)(2,1)} %get-tuple-element.322.dk_ref, bf16[1024,1024]{1,0:T(8,128)(2,1)} %get-tuple-element.301.dv_ref, bf16[1024,1024]{1,0:T(8,128)(2,1)} %get-tuple-element.286.dr_ref, ...), custom_call_target="tpu_custom_call" | custom-call | flops 1048576 | bytes 65536 | tf_op jit(solution)/shard_map/pallas_call | solution.py:781
  461.3 1.7 fusion.5
  468.7 12.0 %collective-permute-done.38 = bf16[2,2,2,32,1024]{4,3,2,1,0:T(8,128)(2,1)S(1)} collective-permute-done((bf16[2,2,2,32,1024]{4,3,2,1,0:T(8,128)(2,1)S(1)}, bf16[2,2,2,32,1024]{4,3,2,1,0:T(8,128)(2,1)S(1)}, u32[]{:S(2)}, u32[]{:S(2)}) %collective-permute-start.38) | collective-permute-done | bytes 524320 | tf_op jit(solution)/shard_map/ppermute | solution.py:25
  482.4 1.7 collective-permute-start.42
  484.5 2.3 collective-permute-done.42
  486.8 3.2 collective-permute-done.41
  494.9 3.5 collective-permute-done.44
  499.6 2.6 fusion.33
  502.8 4.0 collective-permute-done.48
  509.5 3.8 collective-permute-done.49
  516.4 2.1 collective-permute-done.51
  (466 shorter events, 103.8 us)
Async XLA Ops:
  7.2 70.7 %copy-start = (bf16[512,1024]{1,0:T(8,128)(2,1)S(1)}, bf16[512,1024]{1,0:T(8,128)(2,1)}, u32[]{:S(2)}) copy-start(bf16[512,1024]{1,0:T(8,128)(2,1)} %param.43) | copy-start | bytes 3145732
  7.2 90.6 %all-gather.10.cloned.1.call-start = ((), (), s32[]{:S(2)}) async-start(), calls=%async_computation.5 | async-start | bytes 2228224 | tf_op jit(solution)/shard_map/all_gather | solution.py:922
  8.9 194.2 %all-gather.8.cloned.1.call-start = ((), (), s32[]{:S(2)}) async-start(), calls=%async_computation.2 | async-start | bytes 8912896 | tf_op jit(solution)/shard_map/all_gather | solution.py:922
  11.1 47.8 %copy-start.47 = (bf16[128,384]{1,0:T(8,128)(2,1)S(1)}, bf16[128,384]{1,0:T(8,128)(2,1)}, u32[]{:S(2)}) copy-start(bf16[128,384]{1,0:T(8,128)(2,1)} %get-tuple-element.215) | copy-start | bytes 294916
  11.1 18.6 %collective-permute-start = (bf16[2,32,1024]{2,1,0:T(8,128)(2,1)}, bf16[2,32,1024]{2,1,0:T(8,128)(2,1)S(1)}, u32[]{:S(2)}, u32[]{:S(2)}) collective-permute-start(bf16[2,32,1024]{2,1,0:T(8,128)(2,1)} %get-tuple-element.192), channel_id=1, source_target_pairs={{0,16},{16,0},{1,17},{17,1},{2,18},{18,2},{3,19},{19,3},{4,20},{20... | collective-permute-start | bytes 393224 | tf_op jit(solution)/shard_map/ppermute | solution.py:25
  15.2 14.5 %collective-permute-start.1 = (bf16[2,32,1024]{2,1,0:T(8,128)(2,1)}, bf16[2,32,1024]{2,1,0:T(8,128)(2,1)S(1)}, u32[]{:S(2)}, u32[]{:S(2)}) collective-permute-start(bf16[2,32,1024]{2,1,0:T(8,128)(2,1)} %get-tuple-element.193), channel_id=1, source_target_pairs={{0,16},{16,0},{1,17},{17,1},{2,18},{18,2},{3,19},{19,3},{4,20},{20... | collective-permute-start | bytes 393224 | tf_op jit(solution)/shard_map/ppermute | solution.py:25
  15.4 14.3 %collective-permute-start.2 = (bf16[11,128]{1,0:T(8,128)(2,1)S(1)}, bf16[11,128]{1,0:T(8,128)(2,1)S(1)}, u32[]{:S(2)}, u32[]{:S(2)}) collective-permute-start(bf16[11,128]{1,0:T(8,128)(2,1)S(1)} %stack.96), channel_id=1, source_target_pairs={{0,16},{16,0},{1,17},{17,1},{2,18},{18,2},{3,19},{19,3},{4,20},{20... | collective-permute-start | bytes 8456 | tf_op jit(solution)/shard_map/ppermute | solution.py:25
  18.3 11.4 %collective-permute-start.3 = (f32[2,1,1024]{2,1,0:T(1,128)}, f32[2,1,1024]{2,1,0:T(1,128)S(1)}, u32[]{:S(2)}, u32[]{:S(2)}) collective-permute-start(f32[2,1,1024]{2,1,0:T(1,128)} %get-tuple-element.205), channel_id=1, source_target_pairs={{0,1},{1,2},{2,3},{4,5},{5,6},{6,7},{8,9},{9,10},{10,11},{12,13},{... | collective-permute-start | bytes 24584 | tf_op jit(solution)/shard_map/ppermute | solution.py:866
  29.7 70.3 %copy-start.48 = (f32[2,1,1024]{2,1,0:T(1,128)}, f32[2,1,1024]{2,1,0:T(1,128)S(1)}, u32[]{:S(2)}) copy-start(f32[2,1,1024]{2,1,0:T(1,128)S(1)} %collective-permute-done.3) | copy-start | bytes 24580
  30.8 17.8 %collective-permute-start.5 = (bf16[2,2,32,1024]{3,2,0,1:T(8,128)(2,1)S(1)}, bf16[2,2,32,1024]{3,2,0,1:T(8,128)(2,1)S(1)}, u32[]{:S(2)}, u32[]{:S(2)}) collective-permute-start(bf16[2,2,32,1024]{3,2,0,1:T(8,128)(2,1)S(1)} %get-tuple-element.451), channel_id=1, source_target_pairs={{0,8},{8,0},{1,9},{9,1},{2,10},{10,2},{3,11},{11,3},{4,12},{12,4},... | collective-permute-start | bytes 786440 | tf_op jit(solution)/shard_map/ppermute | solution.py:25
  32.4 16.1 %collective-permute-start.4 = (bf16[2,2,32,1024]{3,2,0,1:T(8,128)(2,1)S(1)}, bf16[2,2,32,1024]{3,2,0,1:T(8,128)(2,1)S(1)}, u32[]{:S(2)}, u32[]{:S(2)}) collective-permute-start(bf16[2,2,32,1024]{3,2,0,1:T(8,128)(2,1)S(1)} %get-tuple-element.452), channel_id=1, source_target_pairs={{0,8},{8,0},{1,9},{9,1},{2,10},{10,2},{3,11},{11,3},{4,12},{12,4},... | collective-permute-start | bytes 786440 | tf_op jit(solution)/shard_map/ppermute | solution.py:25
  32.9 15.6 %collective-permute-start.6 = (bf16[2,11,128]{2,0,1:T(2,128)(2,1)S(1)}, bf16[2,11,128]{2,0,1:T(2,128)(2,1)S(1)}, u32[]{:S(2)}, u32[]{:S(2)}) collective-permute-start(bf16[2,11,128]{2,0,1:T(2,128)(2,1)S(1)} %broadcast_select_fusion.27), channel_id=1, source_target_pairs={{0,8},{8,0},{1,9},{9,1},{2,10},{10,2},{3,11},{11,3},{4,12},{12,4},... | collective-permute-start | bytes 16904 | tf_op jit(solution)/shard_map/ppermute | solution.py:25
  48.7 18.4 %collective-permute-start.8 = (bf16[2,2,2,32,1024]{4,3,1,0,2:T(8,128)(2,1)S(1)}, bf16[2,2,2,32,1024]{4,3,1,0,2:T(8,128)(2,1)S(1)}, u32[]{:S(2)}, u32[]{:S(2)}) collective-permute-start(bf16[2,2,2,32,1024]{4,3,1,0,2:T(8,128)(2,1)S(1)} %get-tuple-element.449), channel_id=1, source_target_pairs={{0,2},{2,0},{1,3},{3,1},{4,6},{6,4},{5,7},{7,5},{8,10},{10,8},{9,1... | collective-permute-start | bytes 1572872 | tf_op jit(solution)/shard_map/ppermute | solution.py:25
  49.9 17.3 %collective-permute-start.7 = (bf16[2,2,2,32,1024]{4,3,1,0,2:T(8,128)(2,1)S(1)}, bf16[2,2,2,32,1024]{4,3,1,0,2:T(8,128)(2,1)S(1)}, u32[]{:S(2)}, u32[]{:S(2)}) collective-permute-start(bf16[2,2,2,32,1024]{4,3,1,0,2:T(8,128)(2,1)S(1)} %get-tuple-element.450), channel_id=1, source_target_pairs={{0,4},{4,0},{1,5},{5,1},{2,6},{6,2},{3,7},{7,3},{8,12},{12,8},{9,1... | collective-permute-start | bytes 1572872 | tf_op jit(solution)/shard_map/ppermute | solution.py:25
  51.3 55.0 %copy-start.73 = (pred[2]{0:T(512)(128)(4,1)}, pred[2]{0:T(512)(128)(4,1)S(1)}, u32[]{:S(2)}) copy-start(pred[2]{0:T(512)(128)(4,1)S(1)} %iota_compare_fusion.2) | copy-start | bytes 10
  51.3 15.9 %collective-permute-start.10 = (bf16[128,640]{1,0:T(8,128)(2,1)S(1)}, bf16[128,640]{1,0:T(8,128)(2,1)S(1)}, u32[]{:S(2)}, u32[]{:S(2)}) collective-permute-start(bf16[128,640]{1,0:T(8,128)(2,1)S(1)} %copy-done.42), channel_id=1, source_target_pairs={{0,16},{16,0},{1,17},{17,1},{2,18},{18,2},{3,19},{19,3},{4,20},{20... | collective-permute-start | bytes 491528 | tf_op jit(solution)/shard_map/ppermute | solution.py:25
  58.7 3.7 collective-permute-start.9
  58.8 8.3 %collective-permute-start.11 = (bf16[128,384]{1,0:T(8,128)(2,1)S(1)}, bf16[128,384]{1,0:T(8,128)(2,1)S(1)}, u32[]{:S(2)}, u32[]{:S(2)}) collective-permute-start(bf16[128,384]{1,0:T(8,128)(2,1)S(1)} %copy-done.47), channel_id=1, source_target_pairs={{0,16},{16,0},{1,17},{17,1},{2,18},{18,2},{3,19},{19,3},{4,20},{20... | collective-permute-start | bytes 294920 | tf_op jit(solution)/shard_map/ppermute | solution.py:25
  69.8 22.6 %collective-permute-start.15 = (bf16[2,2,2,2,32,1024]{5,4,2,1,0,3:T(8,128)(2,1)}, bf16[2,2,2,2,32,1024]{5,4,2,1,0,3:T(8,128)(2,1)S(1)}, u32[]{:S(2)}, u32[]{:S(2)}) collective-permute-start(bf16[2,2,2,2,32,1024]{5,4,2,1,0,3:T(8,128)(2,1)} %broadcast_select_fusion.10), channel_id=1, source_target_pairs={{0,4},{4,0},{1,5},{5,1},{2,6},{6,2},{3,7},{7,3},{8,12},{12,8},{9,1... | collective-permute-start | bytes 3145736 | tf_op jit(solution)/shard_map/ppermute | solution.py:25
  72.2 25.5 %collective-permute-start.14 = (bf16[2,2,2,2,32,1024]{5,4,2,1,0,3:T(8,128)(2,1)}, bf16[2,2,2,2,32,1024]{5,4,2,1,0,3:T(8,128)(2,1)}, u32[]{:S(2)}, u32[]{:S(2)}) collective-permute-start(bf16[2,2,2,2,32,1024]{5,4,2,1,0,3:T(8,128)(2,1)} %broadcast_select_fusion.11), channel_id=1, source_target_pairs={{0,2},{2,0},{1,3},{3,1},{4,6},{6,4},{5,7},{7,5},{8,10},{10,8},{9,1... | collective-permute-start | bytes 3145736 | tf_op jit(solution)/shard_map/ppermute | solution.py:25
  75.7 13.1 %collective-permute-start.12 = (bf16[2,128,640]{2,1,0:T(8,128)(2,1)}, bf16[2,128,640]{2,1,0:T(8,128)(2,1)}, u32[]{:S(2)}, u32[]{:S(2)}) collective-permute-start(bf16[2,128,640]{2,1,0:T(8,128)(2,1)} %broadcast_select_fusion.19), channel_id=1, source_target_pairs={{0,8},{8,0},{1,9},{9,1},{2,10},{10,2},{3,11},{11,3},{4,12},{12,4},... | collective-permute-start | bytes 983048 | tf_op jit(solution)/shard_map/ppermute | solution.py:25
  75.8 13.0 %collective-permute-start.13 = (bf16[2,128,384]{2,1,0:T(8,128)(2,1)S(1)}, bf16[2,128,384]{2,1,0:T(8,128)(2,1)S(1)}, u32[]{:S(2)}, u32[]{:S(2)}) collective-permute-start(bf16[2,128,384]{2,1,0:T(8,128)(2,1)S(1)} %broadcast_select_fusion.24), channel_id=1, source_target_pairs={{0,8},{8,0},{1,9},{9,1},{2,10},{10,2},{3,11},{11,3},{4,12},{12,4},... | collective-permute-start | bytes 589832 | tf_op jit(solution)/shard_map/ppermute | solution.py:25
  97.8 301.0 %reduce-scatter.3.cloned.1.call-start = ((), (), s32[]{:S(2)}) async-start(), calls=%async_computation.3 | async-start | bytes 8912896 | tf_op jit(solution)/shard_map/reduce_scatter | solution.py:1036
  108.2 39.8 %collective-permute-start.17 = (bf16[2,2,128,384]{3,2,1,0:T(8,128)(2,1)S(1)}, bf16[2,2,128,384]{3,2,1,0:T(8,128)(2,1)S(1)}, u32[]{:S(2)}, u32[]{:S(2)}) collective-permute-start(bf16[2,2,128,384]{3,2,1,0:T(8,128)(2,1)S(1)} %broadcast_select_fusion.18), channel_id=1, source_target_pairs={{0,2},{2,0},{1,3},{3,1},{4,6},{6,4},{5,7},{7,5},{8,10},{10,8},{9,1... | collective-permute-start | bytes 1179656 | tf_op jit(solution)/shard_map/ppermute | solution.py:25
  110.0 37.9 %collective-permute-start.16 = (bf16[2,2,128,640]{3,2,1,0:T(8,128)(2,1)S(1)}, bf16[2,2,128,640]{3,2,1,0:T(8,128)(2,1)S(1)}, u32[]{:S(2)}, u32[]{:S(2)}) collective-permute-start(bf16[2,2,128,640]{3,2,1,0:T(8,128)(2,1)S(1)} %broadcast_select_fusion.12), channel_id=1, source_target_pairs={{0,4},{4,0},{1,5},{5,1},{2,6},{6,2},{3,7},{7,3},{8,12},{12,8},{9,1... | collective-permute-start | bytes 1966088 | tf_op jit(solution)/shard_map/ppermute | solution.py:25
  110.3 10.5 %collective-permute-start.18 = (bf16[2,2,2,2,2,32,1024]{6,5,3,2,1,0,4:T(8,128)(2,1)S(1)}, bf16[2,2,2,2,2,32,1024]{6,5,3,2,1,0,4:T(8,128)(2,1)S(1)}, u32[]{:S(2)}, u32[]{:S(2)}) collective-permute-start(bf16[2,2,2,2,2,32,1024]{6,5,3,2,1,0,4:T(8,128)(2,1)S(1)} %broadcast_select_fusion.5), channel_id=1, source_target_pairs={{0,1},{1,0},{2,3},{3,2},{4,5},{5,4},{6,7},{7,6},{8,9},{9,8},{10,11... | collective-permute-start | bytes 6291464 | tf_op jit(solution)/shard_map/ppermute | solution.py:25
  110.3 10.5 %collective-permute-start.19 = (bf16[2,2,2,2,2,32,1024]{6,5,3,2,1,0,4:T(8,128)(2,1)S(1)}, bf16[2,2,2,2,2,32,1024]{6,5,3,2,1,0,4:T(8,128)(2,1)S(1)}, u32[]{:S(2)}, u32[]{:S(2)}) collective-permute-start(bf16[2,2,2,2,2,32,1024]{6,5,3,2,1,0,4:T(8,128)(2,1)S(1)} %broadcast_select_fusion.4), channel_id=1, source_target_pairs={{0,1},{1,0},{2,3},{3,2},{4,5},{5,4},{6,7},{7,6},{8,9},{9,8},{10,11... | collective-permute-start | bytes 6291464 | tf_op jit(solution)/shard_map/ppermute | solution.py:25
  150.3 31.3 %collective-permute-start.20 = (bf16[1024,640]{1,0:T(8,128)(2,1)}, bf16[1024,640]{1,0:T(8,128)(2,1)}, u32[]{:S(2)}, u32[]{:S(2)}) collective-permute-start(bf16[1024,640]{1,0:T(8,128)(2,1)} %bitcast.46.rest_0_), channel_id=1, source_target_pairs={{0,2},{2,0},{1,3},{3,1},{4,6},{6,4},{5,7},{7,5},{8,10},{10,8},{9,1... | collective-permute-start | bytes 3932168 | tf_op jit(solution)/shard_map/ppermute | solution.py:25
  152.4 21.9 %collective-permute-start.21 = (bf16[2,2,2,128,384]{4,3,1,0,2:T(8,128)(2,1)}, bf16[2,2,2,128,384]{4,3,1,0,2:T(8,128)(2,1)}, u32[]{:S(2)}, u32[]{:S(2)}) collective-permute-start(bf16[2,2,2,128,384]{4,3,1,0,2:T(8,128)(2,1)} %get-tuple-element.239), channel_id=1, source_target_pairs={{0,4},{4,0},{1,5},{5,1},{2,6},{6,2},{3,7},{7,3},{8,12},{12,8},{9,1... | collective-permute-start | bytes 2359304 | tf_op jit(solution)/shard_map/ppermute | solution.py:25
  183.0 20.1 %collective-permute-start.24 = (bf16[2,1024,384]{2,1,0:T(8,128)(2,1)S(1)}, bf16[2,1024,384]{2,1,0:T(8,128)(2,1)}, u32[]{:S(2)}, u32[]{:S(2)}) collective-permute-start(bf16[2,1024,384]{2,1,0:T(8,128)(2,1)S(1)} %bitcast.409), channel_id=1, source_target_pairs={{0,1},{1,0},{2,3},{3,2},{4,5},{5,4},{6,7},{7,6},{8,9},{9,8},{10,11... | collective-permute-start | bytes 4718600 | tf_op jit(solution)/shard_map/ppermute | solution.py:25
  183.9 19.2 %collective-permute-start.22 = (bf16[1024,640]{1,0:T(8,128)(2,1)}, bf16[1024,640]{1,0:T(8,128)(2,1)}, u32[]{:S(2)}, u32[]{:S(2)}) collective-permute-start(bf16[1024,640]{1,0:T(8,128)(2,1)} %bitcast.46.rest_0_), channel_id=1, source_target_pairs={{0,1},{1,0},{2,3},{3,2},{4,5},{5,4},{6,7},{7,6},{8,9},{9,8},{10,11... | collective-permute-start | bytes 3932168 | tf_op jit(solution)/shard_map/ppermute | solution.py:25
  184.4 18.7 %collective-permute-start.23 = (bf16[1024,640]{1,0:T(8,128)(2,1)}, bf16[1024,640]{1,0:T(8,128)(2,1)}, u32[]{:S(2)}, u32[]{:S(2)}) collective-permute-start(bf16[1024,640]{1,0:T(8,128)(2,1)} %collective-permute-done.20.rest_2_), channel_id=1, source_target_pairs={{0,1},{1,0},{2,3},{3,2},{4,5},{5,4},{6,7},{7,6},{8,9},{9,8},{10,11... | collective-permute-start | bytes 3932168 | tf_op jit(solution)/shard_map/ppermute | solution.py:25
  184.9 13.6 %collective-permute-start.25 = (f32[2,1,1024]{2,1,0:T(1,128)S(1)}, f32[2,1,1024]{2,1,0:T(1,128)S(1)}, u32[]{:S(2)}, u32[]{:S(2)}) collective-permute-start(f32[2,1,1024]{2,1,0:T(1,128)S(1)} %broadcast_in_dim.638), channel_id=1, source_target_pairs={{0,1},{1,2},{2,3},{4,5},{5,6},{6,7},{8,9},{9,10},{10,11},{12,13},{... | collective-permute-start | bytes 24584 | tf_op jit(solution)/shard_map/ppermute | solution.py:866
  253.2 231.0 %reduce-scatter.5.cloned.1.call-start = ((), (), s32[]{:S(2)}) async-start(), calls=%async_computation.4 | async-start | bytes 6684672 | tf_op jit(solution)/shard_map/reduce_scatter | solution.py:1079
  253.2 46.6 %copy-start.16 = (bf16[2,512,1024]{2,1,0:T(8,128)(2,1)S(1)}, bf16[2,512,1024]{2,1,0:T(8,128)(2,1)}, u32[]{:S(2)}) copy-start(bf16[2,512,1024]{2,1,0:T(8,128)(2,1)} %dynamic_update_slice.15) | copy-start | bytes 6291460
  310.8 15.5 %collective-permute-start.26 = (bf16[1024,1024]{1,0:T(8,128)(2,1)}, bf16[1024,1024]{1,0:T(8,128)(2,1)}, u32[]{:S(2)}, u32[]{:S(2)}) collective-permute-start(bf16[1024,1024]{1,0:T(8,128)(2,1)} %fusion.18), channel_id=1, source_target_pairs={{0,1},{1,0},{2,3},{3,2},{4,5},{5,4},{6,7},{7,6},{8,9},{9,8},{10,11... | collective-permute-start | bytes 6291464 | tf_op jit(solution)/shard_map/ppermute | solution.py:25
  310.9 15.4 %collective-permute-start.27 = (bf16[1024,1024]{1,0:T(8,128)(2,1)}, bf16[1024,1024]{1,0:T(8,128)(2,1)}, u32[]{:S(2)}, u32[]{:S(2)}) collective-permute-start(bf16[1024,1024]{1,0:T(8,128)(2,1)} %fusion.21), channel_id=1, source_target_pairs={{0,1},{1,0},{2,3},{3,2},{4,5},{5,4},{6,7},{7,6},{8,9},{9,8},{10,11... | collective-permute-start | bytes 6291464 | tf_op jit(solution)/shard_map/ppermute | solution.py:25
  311.4 27.3 %collective-permute-start.30 = (f32[2,1,1024]{2,1,0:T(1,128)S(1)}, f32[2,1,1024]{2,1,0:T(1,128)S(1)}, u32[]{:S(2)}, u32[]{:S(2)}) collective-permute-start(f32[2,1,1024]{2,1,0:T(1,128)S(1)} %get-tuple-element.437), channel_id=1, source_target_pairs={{1,0},{2,1},{3,2},{5,4},{6,5},{7,6},{9,8},{10,9},{11,10},{13,12},{... | collective-permute-start | bytes 24584 | tf_op jit(solution)/shard_map/ppermute | solution.py:866
  334.7 31.3 %collective-permute-start.28 = (bf16[2,2,2,128,512]{4,3,2,1,0:T(8,128)(2,1)}, bf16[2,2,2,128,512]{4,3,2,1,0:T(8,128)(2,1)S(1)}, u32[]{:S(2)}, u32[]{:S(2)}) collective-permute-start(bf16[2,2,2,128,512]{4,3,2,1,0:T(8,128)(2,1)} %pad_maximum_fusion.3), channel_id=1, source_target_pairs={{0,4},{4,0},{1,5},{5,1},{2,6},{6,2},{3,7},{7,3},{8,12},{12,8},{9,1... | collective-permute-start | bytes 3145736 | tf_op jit(solution)/shard_map/ppermute | solution.py:25
  336.3 29.8 %collective-permute-start.29 = (bf16[1024,512]{1,0:T(8,128)(2,1)}, bf16[1024,512]{1,0:T(8,128)(2,1)}, u32[]{:S(2)}, u32[]{:S(2)}) collective-permute-start(bf16[1024,512]{1,0:T(8,128)(2,1)} %get-tuple-element.278), channel_id=1, source_target_pairs={{0,2},{2,0},{1,3},{3,1},{4,6},{6,4},{5,7},{7,5},{8,10},{10,8},{9,1... | collective-permute-start | bytes 3145736 | tf_op jit(solution)/shard_map/ppermute | solution.py:25
  376.3 22.5 %collective-permute-start.31 = (bf16[2,2,128,512]{3,2,1,0:T(8,128)(2,1)S(1)}, bf16[2,2,128,512]{3,2,1,0:T(8,128)(2,1)}, u32[]{:S(2)}, u32[]{:S(2)}) collective-permute-start(bf16[2,2,128,512]{3,2,1,0:T(8,128)(2,1)S(1)} %dynamic-slice_bitcast_fusion.2), channel_id=1, source_target_pairs={{0,4},{4,0},{1,5},{5,1},{2,6},{6,2},{3,7},{7,3},{8,12},{12,8},{9,1... | collective-permute-start | bytes 1572872 | tf_op jit(solution)/shard_map/ppermute | solution.py:25
  377.0 21.9 %collective-permute-start.32 = (bf16[2,2,128,512]{3,2,1,0:T(8,128)(2,1)S(1)}, bf16[2,2,128,512]{3,2,1,0:T(8,128)(2,1)}, u32[]{:S(2)}, u32[]{:S(2)}) collective-permute-start(bf16[2,2,128,512]{3,2,1,0:T(8,128)(2,1)S(1)} %slice_bitcast_fusion.1), channel_id=1, source_target_pairs={{0,2},{2,0},{1,3},{3,1},{4,6},{6,4},{5,7},{7,5},{8,10},{10,8},{9,1... | collective-permute-start | bytes 1572872 | tf_op jit(solution)/shard_map/ppermute | solution.py:25
  410.6 16.1 %collective-permute-start.33 = (bf16[2,2,2,2,2,32,1024]{6,5,4,3,2,1,0:T(8,128)(2,1)}, bf16[2,2,2,2,2,32,1024]{6,5,4,3,2,1,0:T(8,128)(2,1)S(1)}, u32[]{:S(2)}, u32[]{:S(2)}) collective-permute-start(bf16[2,2,2,2,2,32,1024]{6,5,4,3,2,1,0:T(8,128)(2,1)} %pad_maximum_fusion.2), channel_id=1, source_target_pairs={{0,1},{1,0},{2,3},{3,2},{4,5},{5,4},{6,7},{7,6},{8,9},{9,8},{10,11... | collective-permute-start | bytes 6291464 | tf_op jit(solution)/shard_map/ppermute | solution.py:25
  412.1 14.7 %collective-permute-start.34 = (bf16[256,1024]{1,0:T(8,128)(2,1)}, bf16[256,1024]{1,0:T(8,128)(2,1)}, u32[]{:S(2)}, u32[]{:S(2)}) collective-permute-start(bf16[256,1024]{1,0:T(8,128)(2,1)} %reduce-scatter.3.cloned.1.call-done), channel_id=1, source_target_pairs={{0,2},{2,0},{1,3},{3,1},{4,6},{6,4},{5,7},{7,5},{8,10},{10,8},{9,1... | collective-permute-start | bytes 1572872 | tf_op jit(solution)/shard_map/ppermute | solution.py:25
  433.5 25.2 %collective-permute-start.35 = (bf16[2,2,2,2,32,1024]{5,4,3,2,1,0:T(8,128)(2,1)}, bf16[2,2,2,2,32,1024]{5,4,3,2,1,0:T(8,128)(2,1)}, u32[]{:S(2)}, u32[]{:S(2)}) collective-permute-start(bf16[2,2,2,2,32,1024]{5,4,3,2,1,0:T(8,128)(2,1)} %dynamic-slice_bitcast_fusion), channel_id=1, source_target_pairs={{0,2},{2,0},{1,3},{3,1},{4,6},{6,4},{5,7},{7,5},{8,10},{10,8},{9,1... | collective-permute-start | bytes 3145736 | tf_op jit(solution)/shard_map/ppermute | solution.py:25
  434.3 23.2 %collective-permute-start.36 = (bf16[2,2,128,512]{3,2,1,0:T(8,128)(2,1)}, bf16[2,2,128,512]{3,2,1,0:T(8,128)(2,1)}, u32[]{:S(2)}, u32[]{:S(2)}) collective-permute-start(bf16[2,2,128,512]{3,2,1,0:T(8,128)(2,1)} %pad_maximum_fusion.5), channel_id=1, source_target_pairs={{0,8},{8,0},{1,9},{9,1},{2,10},{10,2},{3,11},{11,3},{4,12},{12,4},... | collective-permute-start | bytes 1572872 | tf_op jit(solution)/shard_map/ppermute | solution.py:25
  434.3 23.2 %collective-permute-start.37 = (bf16[256,1024]{1,0:T(8,128)(2,1)S(1)}, bf16[256,1024]{1,0:T(8,128)(2,1)}, u32[]{:S(2)}, u32[]{:S(2)}) collective-permute-start(bf16[256,1024]{1,0:T(8,128)(2,1)S(1)} %add_convert_fusion.11), channel_id=1, source_target_pairs={{0,1},{1,0},{2,3},{3,2},{4,5},{5,4},{6,7},{7,6},{8,9},{9,8},{10,11... | collective-permute-start | bytes 1572872 | tf_op jit(solution)/shard_map/ppermute | solution.py:25
  463.2 3.1 collective-permute-start.39
  464.7 19.8 %collective-permute-start.43 = (bf16[2,128,512]{2,1,0:T(8,128)(2,1)}, bf16[2,128,512]{2,1,0:T(8,128)(2,1)S(1)}, u32[]{:S(2)}, u32[]{:S(2)}) collective-permute-start(bf16[2,128,512]{2,1,0:T(8,128)(2,1)} %dynamic-slice_bitcast_fusion.5), channel_id=1, source_target_pairs={{0,16},{16,0},{1,17},{17,1},{2,18},{18,2},{3,19},{19,3},{4,20},{20... | collective-permute-start | bytes 786440 | tf_op jit(solution)/shard_map/ppermute | solution.py:25
  466.0 14.7 %collective-permute-start.38 = (bf16[2,2,2,32,1024]{4,3,2,1,0:T(8,128)(2,1)S(1)}, bf16[2,2,2,32,1024]{4,3,2,1,0:T(8,128)(2,1)S(1)}, u32[]{:S(2)}, u32[]{:S(2)}) collective-permute-start(bf16[2,2,2,32,1024]{4,3,2,1,0:T(8,128)(2,1)S(1)} %dynamic-slice_bitcast_fusion.1), channel_id=1, source_target_pairs={{0,4},{4,0},{1,5},{5,1},{2,6},{6,2},{3,7},{7,3},{8,12},{12,8},{9,1... | collective-permute-start | bytes 1572872 | tf_op jit(solution)/shard_map/ppermute | solution.py:25
  480.9 9.1 %collective-permute-start.41 = (bf16[2,2,32,1024]{3,2,1,0:T(8,128)(2,1)S(1)}, bf16[2,2,32,1024]{3,2,1,0:T(8,128)(2,1)S(1)}, u32[]{:S(2)}, u32[]{:S(2)}) collective-permute-start(bf16[2,2,32,1024]{3,2,1,0:T(8,128)(2,1)S(1)} %dynamic-slice_bitcast_fusion.4), channel_id=1, source_target_pairs={{0,8},{8,0},{1,9},{9,1},{2,10},{10,2},{3,11},{11,3},{4,12},{12,4},... | collective-permute-start | bytes 786440 | tf_op jit(solution)/shard_map/ppermute | solution.py:25
  481.2 1.3 collective-permute-start.40
  482.4 4.3 collective-permute-start.42
  490.1 12.7 %collective-permute-start.47 = (bf16[2,128,512]{2,1,0:T(8,128)(2,1)S(1)}, bf16[2,128,512]{2,1,0:T(8,128)(2,1)S(1)}, u32[]{:S(2)}, u32[]{:S(2)}) collective-permute-start(bf16[2,128,512]{2,1,0:T(8,128)(2,1)S(1)} %fusion.35), channel_id=1, source_target_pairs={{0,2},{2,0},{1,3},{3,1},{4,6},{6,4},{5,7},{7,5},{8,10},{10,8},{9,1... | collective-permute-start | bytes 786440 | tf_op jit(solution)/shard_map/ppermute | solution.py:25
  491.6 15.2 %collective-permute-start.48 = (bf16[64,3072]{1,0:T(8,128)(2,1)}, bf16[64,3072]{1,0:T(8,128)(2,1)S(1)}, u32[]{:S(2)}, u32[]{:S(2)}) collective-permute-start(bf16[64,3072]{1,0:T(8,128)(2,1)} %reduce-scatter.5.cloned.1.call-done), channel_id=1, source_target_pairs={{0,2},{2,0},{1,3},{3,1},{4,6},{6,4},{5,7},{7,5},{8,10},{10,8},{9,1... | collective-permute-start | bytes 1179656 | tf_op jit(solution)/shard_map/ppermute | solution.py:25
  493.3 9.6 %collective-permute-start.45 = (bf16[2,32,1024]{2,1,0:T(8,128)(2,1)S(1)}, bf16[2,32,1024]{2,1,0:T(8,128)(2,1)S(1)}, u32[]{:S(2)}, u32[]{:S(2)}) collective-permute-start(bf16[2,32,1024]{2,1,0:T(8,128)(2,1)S(1)} %dynamic-slice_bitcast_fusion.6), channel_id=1, source_target_pairs={{0,16},{16,0},{1,17},{17,1},{2,18},{18,2},{3,19},{19,3},{4,20},{20... | collective-permute-start | bytes 393224 | tf_op jit(solution)/shard_map/ppermute | solution.py:25
  494.1 4.3 collective-permute-start.44
  498.5 4.3 collective-permute-start.46
  506.9 11.6 %collective-permute-start.50 = (bf16[2,2,128,512]{3,2,1,0:T(8,128)(2,1)S(1)}, bf16[2,2,128,512]{3,2,1,0:T(8,128)(2,1)S(1)}, u32[]{:S(2)}, u32[]{:S(2)}) collective-permute-start(bf16[2,2,128,512]{3,2,1,0:T(8,128)(2,1)S(1)} %broadcast_select_fusion.14), channel_id=1, source_target_pairs={{0,1},{1,0},{2,3},{3,2},{4,5},{5,4},{6,7},{7,6},{8,9},{9,8},{10,11... | collective-permute-start | bytes 1572872 | tf_op jit(solution)/shard_map/ppermute | solution.py:25
  507.1 11.4 %collective-permute-start.54 = (bf16[64,3072]{1,0:T(8,128)(2,1)S(1)}, bf16[64,3072]{1,0:T(8,128)(2,1)S(1)}, u32[]{:S(2)}, u32[]{:S(2)}) collective-permute-start(bf16[64,3072]{1,0:T(8,128)(2,1)S(1)} %add_convert_fusion.12), channel_id=1, source_target_pairs={{0,1},{1,0},{2,3},{3,2},{4,5},{5,4},{6,7},{7,6},{8,9},{9,8},{10,11... | collective-permute-start | bytes 1179656 | tf_op jit(solution)/shard_map/ppermute | solution.py:25
  507.7 5.6 %collective-permute-start.49 = (f32[12,1024]{1,0:T(8,128)S(1)}, f32[12,1024]{1,0:T(8,128)S(1)}, u32[]{:S(2)}, u32[]{:S(2)}) collective-permute-start(f32[12,1024]{1,0:T(8,128)S(1)} %add.349), channel_id=1, source_target_pairs={{0,16},{16,0},{1,17},{17,1},{2,18},{18,2},{3,19},{19,3},{4,20},{20... | collective-permute-start | bytes 147464 | tf_op jit(solution)/shard_map/ppermute | solution.py:25
  507.8 8.6 %collective-permute-start.53 = (bf16[2,32,1024]{2,1,0:T(8,128)(2,1)S(1)}, bf16[2,32,1024]{2,1,0:T(8,128)(2,1)S(1)}, u32[]{:S(2)}, u32[]{:S(2)}) collective-permute-start(bf16[2,32,1024]{2,1,0:T(8,128)(2,1)S(1)} %fusion.37), channel_id=1, source_target_pairs={{0,3},{1,2},{2,1},{3,0},{4,7},{5,6},{6,5},{7,4},{8,11},{9,10},{10,... | collective-permute-start | bytes 393224 | tf_op jit(solution)/shard_map/ppermute | solution.py:1171
  509.0 7.4 %collective-permute-start.52 = (bf16[2,32,1024]{2,1,0:T(8,128)(2,1)S(1)}, bf16[2,32,1024]{2,1,0:T(8,128)(2,1)S(1)}, u32[]{:S(2)}, u32[]{:S(2)}) collective-permute-start(bf16[2,32,1024]{2,1,0:T(8,128)(2,1)S(1)} %fusion.37), channel_id=1, source_target_pairs={{0,1},{1,0},{2,3},{3,2},{4,5},{5,4},{6,7},{7,6},{8,9},{9,8},{10,11... | collective-permute-start | bytes 393224 | tf_op jit(solution)/shard_map/ppermute | solution.py:25
  513.3 5.2 collective-permute-start.51
  (98 other events, 848.1 us)
Sparse Core Ops, SparseCore 0:
  10.8 46.9 all-gather.9
  97.9 78.2 all-gather.7
  253.3 107.1 reduce-scatter.2
  381.5 100.3 reduce-scatter.4

commit v5 on v4

--- a/solution.py
+++ b/solution.py
@@ -268,7 +268,7 @@
     gb_ref[...] = gb[:ROWS] + gb[ROWS:]
 
 
-WIDTH = 256
+WIDTH = 512
 
 
 def wkv_specs(rows):

time: 534 us -> 534 us (level)
  waiting for transfers between devices: 101 us -> 108 us
  transfers between devices with their start and end apart: 59 -> 59, of which waited for: 21 -> 23; matrix products, arithmetic and copies ran while one was open for 27% -> 27% of each run, Pallas kernels for 24% -> 23%
where the time goes in v5:
time: 534 us; the launch traced here: 533 us
  Pallas kernels  156 us (29%)
  waiting for transfers between devices  108 us (20%)
  other arithmetic  76.4 us (14%)
  matrix products  66.6 us (12%)
  starting transfers between devices  56.1 us (11%)
  local copies, waits for them, and re-layouts  32.5 us (6%)
  blocking collectives  20.7 us (4%)
  between operations  16.5 us (3%)
    ppermute x50, waiting for transfers between devices, swap(): return lax.ppermute(value, key, [(0, 1), (1, 0)])  105 us
    dot_general x10, matrix products, dot_weight(): lax.dot_general(inputs, grads, (((0,), (0,)), ((), ())), preferred_elemen...  53.9 us
    ppermute x50, starting transfers between devices, swap(): return lax.ppermute(value, key, [(0, 1), (1, 0)])  48.3 us
    pallas_call x1, Pallas kernels, down(): pl.pallas_call(down_kernel, grid_spec=pltpu.PrefetchScalarGridSpec(num_sc...  46.6 us
    pallas_call x1, Pallas kernels, feed_forward(): pl.pallas_call(feed_kernel, grid_spec=pltpu.PrefetchScalarGridSpec(num_sc...  34.6 us
    pallas_call x1, Pallas kernels, mix_back(): pl.pallas_call(mix_kernel, grid=(seqs,), in_specs=[big, big, big, full, f...  23.1 us
    select_n x25, other arithmetic, join(): jnp.where(side == lax.axis_index(key), jnp.expand_dims(mine, at), jnp.exp...  21 us
    all_gather x2, blocking collectives, earlier_state(): packed = lax.all_gather(jnp.concatenate([num, den], axis=0), axes)  20.7 us
  transfers between devices with their start and end apart: 59, of which 23 were waited for; matrix products, arithmetic and copies ran while one was open for 27% of the time, Pallas kernels for 23%

profile of v5, /device:TPU:0, one launch (start us, length us, event | category | flops | bytes accessed | tf_op | source)
XLA Modules:
  0.0 532.8 jit_solution(5235421965692997555)
XLA Ops:
  9.1 1.9 shard_map.389
  11.1 4.1 collective-permute-start
  15.4 2.9 collective-permute-start.2
  19.6 10.1 %collective-permute-done.2 = bf16[11,128]{1,0:T(8,128)(2,1)S(1)} collective-permute-done((bf16[11,128]{1,0:T(8,128)(2,1)S(1)}, bf16[11,128]{1,0:T(8,128)(2,1)S(1)}, u32[]{:S(2)}, u32[]{:S(2)}) %collective-permute-start.2) | collective-permute-done | bytes 2848 | tf_op jit(solution)/shard_map/ppermute | solution.py:25
  34.5 14.0 %collective-permute-done.6 = bf16[2,11,128]{2,0,1:T(2,128)(2,1)S(1)} collective-permute-done((bf16[2,11,128]{2,0,1:T(2,128)(2,1)S(1)}, bf16[2,11,128]{2,0,1:T(2,128)(2,1)S(1)}, u32[]{:S(2)}, u32[]{:S(2)}) %collective-permute-start.6) | collective-permute-done | bytes 5664 | tf_op jit(solution)/shard_map/ppermute | solution.py:25
  51.3 7.3 %collective-permute-start.10 = (bf16[128,640]{1,0:T(8,128)(2,1)S(1)}, bf16[128,640]{1,0:T(8,128)(2,1)S(1)}, u32[]{:S(2)}, u32[]{:S(2)}) collective-permute-start(bf16[128,640]{1,0:T(8,128)(2,1)S(1)} %copy-done.42), channel_id=1, source_target_pairs={{0,16},{16,0},{1,17},{17,1},{2,18},{18,2},{3,19},{19,3},{4,20},{20... | collective-permute-start | bytes 491528 | tf_op jit(solution)/shard_map/ppermute | solution.py:25
  58.9 3.5 collective-permute-done.9
  62.4 4.7 collective-permute-done.11
  70.1 2.1 broadcast_select_fusion.11
  72.2 2.6 collective-permute-start.14
  75.8 2.1 collective-permute-start.13
  78.7 10.1 %collective-permute-done.13 = bf16[2,128,384]{2,1,0:T(8,128)(2,1)S(1)} collective-permute-done((bf16[2,128,384]{2,1,0:T(8,128)(2,1)S(1)}, bf16[2,128,384]{2,1,0:T(8,128)(2,1)S(1)}, u32[]{:S(2)}, u32[]{:S(2)}) %collective-permute-start.13) | collective-permute-done | bytes 196640 | tf_op jit(solution)/shard_map/ppermute | solution.py:25
  88.7 3.6 collective-permute-done.15
  92.4 5.4 %collective-permute-done.14 = bf16[2,2,2,2,32,1024]{5,4,2,1,0,3:T(8,128)(2,1)} collective-permute-done((bf16[2,2,2,2,32,1024]{5,4,2,1,0,3:T(8,128)(2,1)}, bf16[2,2,2,2,32,1024]{5,4,2,1,0,3:T(8,128)(2,1)}, u32[]{:S(2)}, u32[]{:S(2)}) %collective-permute-start.14) | collective-permute-done | bytes 1048608 | tf_op jit(solution)/shard_map/ppermute | solution.py:25
  106.3 1.9 broadcast_select_fusion.5
  108.2 1.8 collective-permute-start.17
  116.8 3.9 add_convert_fusion.1
  120.8 2.6 broadcast_select_fusion
  123.9 3.7 fusion.85
  127.6 4.9 multiply_reduce_fusion
  132.5 15.4 %all-gather.3 = f32[4,4,1024]{2,1,0:T(4,128)S(1)} all-gather(f32[1,4,1024]{2,1,0:T(4,128)S(1)} %maximum_bitcast_fusion), channel_id=3, replica_groups=mesh['d2'=2,'d1'=2,'d0'=2,'s1'=2,'s0'=2] {'s1','s0'}, dimensions={0}, use_global_device_ids=true | all-gather | bytes 81920 | tf_op jit(solution)/shard_map/all_gather | solution.py:884
  154.1 2.8 fusion.77
  157.0 3.7 convolution_convert_fusion.6.r_ref
  160.7 11.9 %shard_map.390 = (bf16[1024,1024]{1,0:T(8,128)(2,1)}, f32[1024,1024]{1,0:T(8,128)}, f32[1024,1024]{1,0:T(8,128)}) custom-call(f32[1024,1024]{1,0:T(8,128)} %get-tuple-element.453.k_ref, bf16[1024,1024]{1,0:T(8,128)(2,1)} %get-tuple-element.454.v_ref, bf16[1024,1024]{1,0:T(8,128)(2,1)} %convolution_convert_fusion.6.r_ref, f32[1,1024]{1,0:T(1,128)} %bitcast.456, ...), custom_call_target="tpu_custom_call" | custom-call | flops 1048576 | bytes 65536 | tf_op jit(solution)/shard_map/pallas_call | solution.py:286
  173.1 8.5 %collective-permute-done.20.rest_2_ = bf16[1024,640]{1,0:T(8,128)(2,1)} collective-permute-done((bf16[1024,640]{1,0:T(8,128)(2,1)}, bf16[1024,640]{1,0:T(8,128)(2,1)}, u32[]{:S(2)}, u32[]{:S(2)}) %collective-permute-start.20) | collective-permute-done | bytes 1310752 | tf_op jit(solution)/shard_map/ppermute | solution.py:25
  184.9 2.3 collective-permute-start.25
  187.3 11.1 %shard_map.391 = (f32[1024,1024]{1,0:T(8,128)}, bf16[1024,1024]{1,0:T(8,128)(2,1)}, bf16[1024,1024]{1,0:T(8,128)(2,1)}, f32[2,1,1024]{2,1,0:T(1,128)}, f32[2,8,1024]{2,1,0:T(8,128)}) custom-call(s32[2]{0:T(128)} %broadcast_subtract_fusion.5.left_ref, bf16[1024,1024]{1,0:T(8,128)(2,1)} %get-tuple-element.250.w_ref, bf16[1024,1024]{1,0:T(8,128)(2,1)} %bitcast.404, ...), custom_call_target="tpu_custom_call" | custom-call | flops 1048576 | bytes 65536 | tf_op jit(solution)/shard_map/pallas_call | solution.py:537
  203.2 34.6 %shard_map.392 = (bf16[1024,4096]{1,0:T(8,128)(2,1)}, bf16[1024,1024]{1,0:T(8,128)(2,1)}, bf16[1024,1024]{1,0:T(8,128)(2,1)}, bf16[1024,1024]{1,0:T(8,128)(2,1)}, f32[2,2,8,1024]{3,2,1,0:T(8,128)}) custom-call(s32[1]{0:T(128)} %bitcast._.s_ref, s32[2]{0:T(128)} %broadcast_subtract_fusion.5.left_ref, bf16[1024,1024]{1,0:T(8,128)(2,1)} %bitcast.438, ...), custom_call_target="tpu_custom_call" | custom-call | flops 1048576 | bytes 65536 | tf_op jit(solution)/shard_map/pallas_call | solution.py:436
  237.7 15.4 %convolution_convert_fusion = bf16[4096,1024]{1,0:T(8,128)(2,1)} fusion(bf16[1024,4096]{1,0:T(8,128)(2,1)} %get-tuple-element.263.sq_ref, bf16[1024,1024]{1,0:T(8,128)(2,1)} %get-tuple-element.262.dval_ref), kind=kOutput, calls=%fused_computation | convolution fusion | flops 8594128896 | bytes 18874368 | tf_op jit(solution)/shard_map/dot_general | solution.py:853
  253.3 46.6 %shard_map.393 = (bf16[4,1024,1024]{2,1,0:T(8,128)(2,1)}, f32[1024,1024]{1,0:T(8,128)}, bf16[1024,1024]{1,0:T(8,128)(2,1)}, f32[2,1,1024]{2,1,0:T(1,128)}, f32[2...) custom-call(s32[1]{0:T(128)} %bitcast._.s_ref, s32[2]{0:T(128)} %broadcast_subtract_fusion.5.left_ref, ...), custom_call_target="tpu_custom_call" | custom-call | flops 1048576 | bytes 65536 | tf_op jit(solution)/shard_map/pallas_call | solution.py:667
  299.9 5.5 %fusion.21 = bf16[1024,1024]{1,0:T(8,128)(2,1)} fusion(bf16[1024,1024]{1,0:T(8,128)(2,1)S(1)} %bitcast.439, bf16[4,1024,1024]{2,1,0:T(8,128)(2,1)} %get-tuple-element.269), kind=kOutput, calls=%fused_computation.45 | convolution fusion | flops 2148532224 | bytes 6291456 | tf_op jit(solution)/shard_map/dot_general | solution.py:853
  305.3 5.5 %fusion.18 = bf16[1024,1024]{1,0:T(8,128)(2,1)} fusion(bf16[1024,1024]{1,0:T(8,128)(2,1)S(1)} %bitcast.440, bf16[4,1024,1024]{2,1,0:T(8,128)(2,1)} %get-tuple-element.269), kind=kOutput, calls=%fused_computation.44 | convolution fusion | flops 2148532224 | bytes 6291456 | tf_op jit(solution)/shard_map/dot_general | solution.py:853
  312.9 5.3 %convolution_convert_fusion.1 = bf16[1024,1024]{1,0:T(8,128)(2,1)} fusion(bf16[1024,1024]{1,0:T(8,128)(2,1)} %bitcast.445, bf16[1024,1024]{1,0:T(8,128)(2,1)S(1)} %copy-done.14), kind=kOutput, calls=%fused_computation.48 | convolution fusion | flops 2148532224 | bytes 6291456 | tf_op jit(solution)/shard_map/dot_general | solution.py:853
  318.2 4.1 fusion.27
  322.3 4.0 fusion.24
  326.4 3.9 add_convert_fusion.6
  336.3 2.4 collective-permute-start.29
  340.9 13.4 %shard_map.394 = (bf16[1024,1024]{1,0:T(8,128)(2,1)}, bf16[1024,1024]{1,0:T(8,128)(2,1)}, f32[2,8,1024]{2,1,0:T(8,128)}, f32[2,8,1024]{2,1,0:T(8,128)}) custom-call(bf16[1024,1024]{1,0:T(8,128)(2,1)} %bitcast.433, bf16[1024,1024]{1,0:T(8,128)(2,1)} %bitcast.405, f32[1024,1024]{1,0:T(8,128)} %get-tuple-element.453.k_ref, ...), custom_call_target="tpu_custom_call" | custom-call | flops 1048576 | bytes 65536 | tf_op jit(solution)/shard_map/pallas_call | solution.py:326
  355.2 5.5 %convolution_convert_fusion.5 = bf16[1024,1024]{1,0:T(8,128)(2,1)} fusion(bf16[1024,1024]{1,0:T(8,128)(2,1)S(1)} %copy-done.10, bf16[1024,1024]{1,0:T(8,128)(2,1)} %bitcast.434), kind=kOutput, calls=%fused_computation.52 | convolution fusion | flops 2148532224 | bytes 6291456 | tf_op jit(solution)/shard_map/dot_general | solution.py:853
  360.7 3.8 convolution_convert_fusion.4
  365.7 5.2 all-gather.4
  371.6 2.4 add_convert_fusion.5
  374.2 1.7 add_convert_fusion.4
  376.3 1.8 collective-permute-start.32
  378.0 3.4 pad_maximum_fusion
  383.7 13.4 %shard_map.395 = (bf16[1024,1024]{1,0:T(8,128)(2,1)}, bf16[1024,1024]{1,0:T(8,128)(2,1)}, f32[2,8,1024]{2,1,0:T(8,128)}, f32[2,8,1024]{2,1,0:T(8,128)}) custom-call(f32[1024,1024]{1,0:T(8,128)} %get-tuple-element.453.k_ref, bf16[1024,1024]{1,0:T(8,128)(2,1)} %get-tuple-element.454.v_ref, f32[1024,1024]{1,0:T(8,128)} %get-tuple-element.283.a_ref, ...), custom_call_target="tpu_custom_call" | custom-call | flops 1048576 | bytes 65536 | tf_op jit(solution)/shard_map/pallas_call | solution.py:305
  397.1 1.7 fusion.31
  400.8 2.4 convolution_convert_fusion.3
  403.3 2.4 convolution_convert_fusion.2
  405.7 1.8 constant_dynamic-slice_fusion.7
  411.2 2.0 select_maximum_fusion
  417.2 8.0 %collective-permute-done.34 = bf16[256,1024]{1,0:T(8,128)(2,1)} collective-permute-done((bf16[256,1024]{1,0:T(8,128)(2,1)}, bf16[256,1024]{1,0:T(8,128)(2,1)}, u32[]{:S(2)}, u32[]{:S(2)}) %collective-permute-start.34) | collective-permute-done | bytes 524320 | tf_op jit(solution)/shard_map/ppermute | solution.py:25
  426.5 2.9 add_convert_fusion
  432.2 23.1 %shard_map.396 = (bf16[1024,1024]{1,0:T(8,128)(2,1)}, f32[2,3,1,1024]{3,2,1,0:T(1,128)}, f32[2,3,1,1024]{3,2,1,0:T(1,128)}, f32[2,5,8,1024]{3,2,1,0:T(8,128)}) custom-call(bf16[1024,1024]{1,0:T(8,128)(2,1)} %get-tuple-element.322.dk_ref, bf16[1024,1024]{1,0:T(8,128)(2,1)} %get-tuple-element.301.dv_ref, bf16[1024,1024]{1,0:T(8,128)(2,1)} %get-tuple-element.286.dr_ref, ...), custom_call_target="tpu_custom_call" | custom-call | flops 1048576 | bytes 65536 | tf_op jit(solution)/shard_map/pallas_call | solution.py:781
  467.1 11.8 %collective-permute-done.38 = bf16[2,2,2,32,1024]{4,3,2,1,0:T(8,128)(2,1)S(1)} collective-permute-done((bf16[2,2,2,32,1024]{4,3,2,1,0:T(8,128)(2,1)S(1)}, bf16[2,2,2,32,1024]{4,3,2,1,0:T(8,128)(2,1)S(1)}, u32[]{:S(2)}, u32[]{:S(2)}) %collective-permute-start.38) | collective-permute-done | bytes 524320 | tf_op jit(solution)/shard_map/ppermute | solution.py:25
  480.8 1.7 collective-permute-start.42
  482.5 2.4 reduce-scatter.5.cloned.1.call-done
  485.8 5.3 collective-permute-done.41
  495.6 3.2 collective-permute-done.44
  498.8 1.7 collective-permute-start.46
  500.6 2.6 fusion.33
  503.3 4.5 collective-permute-done.48
  510.3 4.1 collective-permute-done.49
  517.2 2.4 collective-permute-done.51
  (466 shorter events, 105.1 us)
Async XLA Ops:
  7.2 70.7 %copy-start = (bf16[512,1024]{1,0:T(8,128)(2,1)S(1)}, bf16[512,1024]{1,0:T(8,128)(2,1)}, u32[]{:S(2)}) copy-start(bf16[512,1024]{1,0:T(8,128)(2,1)} %param.43) | copy-start | bytes 3145732
  7.2 90.6 %all-gather.10.cloned.1.call-start = ((), (), s32[]{:S(2)}) async-start(), calls=%async_computation.5 | async-start | bytes 2228224 | tf_op jit(solution)/shard_map/all_gather | solution.py:922
  8.9 194.2 %all-gather.8.cloned.1.call-start = ((), (), s32[]{:S(2)}) async-start(), calls=%async_computation.2 | async-start | bytes 8912896 | tf_op jit(solution)/shard_map/all_gather | solution.py:922
  11.1 47.8 %copy-start.47 = (bf16[128,384]{1,0:T(8,128)(2,1)S(1)}, bf16[128,384]{1,0:T(8,128)(2,1)}, u32[]{:S(2)}) copy-start(bf16[128,384]{1,0:T(8,128)(2,1)} %get-tuple-element.215) | copy-start | bytes 294916
  11.1 18.6 %collective-permute-start = (bf16[2,32,1024]{2,1,0:T(8,128)(2,1)}, bf16[2,32,1024]{2,1,0:T(8,128)(2,1)S(1)}, u32[]{:S(2)}, u32[]{:S(2)}) collective-permute-start(bf16[2,32,1024]{2,1,0:T(8,128)(2,1)} %get-tuple-element.192), channel_id=1, source_target_pairs={{0,16},{16,0},{1,17},{17,1},{2,18},{18,2},{3,19},{19,3},{4,20},{20... | collective-permute-start | bytes 393224 | tf_op jit(solution)/shard_map/ppermute | solution.py:25
  15.2 14.5 %collective-permute-start.1 = (bf16[2,32,1024]{2,1,0:T(8,128)(2,1)}, bf16[2,32,1024]{2,1,0:T(8,128)(2,1)S(1)}, u32[]{:S(2)}, u32[]{:S(2)}) collective-permute-start(bf16[2,32,1024]{2,1,0:T(8,128)(2,1)} %get-tuple-element.193), channel_id=1, source_target_pairs={{0,16},{16,0},{1,17},{17,1},{2,18},{18,2},{3,19},{19,3},{4,20},{20... | collective-permute-start | bytes 393224 | tf_op jit(solution)/shard_map/ppermute | solution.py:25
  15.4 14.3 %collective-permute-start.2 = (bf16[11,128]{1,0:T(8,128)(2,1)S(1)}, bf16[11,128]{1,0:T(8,128)(2,1)S(1)}, u32[]{:S(2)}, u32[]{:S(2)}) collective-permute-start(bf16[11,128]{1,0:T(8,128)(2,1)S(1)} %stack.96), channel_id=1, source_target_pairs={{0,16},{16,0},{1,17},{17,1},{2,18},{18,2},{3,19},{19,3},{4,20},{20... | collective-permute-start | bytes 8456 | tf_op jit(solution)/shard_map/ppermute | solution.py:25
  18.3 11.4 %collective-permute-start.3 = (f32[2,1,1024]{2,1,0:T(1,128)}, f32[2,1,1024]{2,1,0:T(1,128)S(1)}, u32[]{:S(2)}, u32[]{:S(2)}) collective-permute-start(f32[2,1,1024]{2,1,0:T(1,128)} %get-tuple-element.205), channel_id=1, source_target_pairs={{0,1},{1,2},{2,3},{4,5},{5,6},{6,7},{8,9},{9,10},{10,11},{12,13},{... | collective-permute-start | bytes 24584 | tf_op jit(solution)/shard_map/ppermute | solution.py:866
  29.7 70.3 %copy-start.48 = (f32[2,1,1024]{2,1,0:T(1,128)}, f32[2,1,1024]{2,1,0:T(1,128)S(1)}, u32[]{:S(2)}) copy-start(f32[2,1,1024]{2,1,0:T(1,128)S(1)} %collective-permute-done.3) | copy-start | bytes 24580
  30.8 17.8 %collective-permute-start.5 = (bf16[2,2,32,1024]{3,2,0,1:T(8,128)(2,1)S(1)}, bf16[2,2,32,1024]{3,2,0,1:T(8,128)(2,1)S(1)}, u32[]{:S(2)}, u32[]{:S(2)}) collective-permute-start(bf16[2,2,32,1024]{3,2,0,1:T(8,128)(2,1)S(1)} %get-tuple-element.451), channel_id=1, source_target_pairs={{0,8},{8,0},{1,9},{9,1},{2,10},{10,2},{3,11},{11,3},{4,12},{12,4},... | collective-permute-start | bytes 786440 | tf_op jit(solution)/shard_map/ppermute | solution.py:25
  32.4 16.1 %collective-permute-start.4 = (bf16[2,2,32,1024]{3,2,0,1:T(8,128)(2,1)S(1)}, bf16[2,2,32,1024]{3,2,0,1:T(8,128)(2,1)S(1)}, u32[]{:S(2)}, u32[]{:S(2)}) collective-permute-start(bf16[2,2,32,1024]{3,2,0,1:T(8,128)(2,1)S(1)} %get-tuple-element.452), channel_id=1, source_target_pairs={{0,8},{8,0},{1,9},{9,1},{2,10},{10,2},{3,11},{11,3},{4,12},{12,4},... | collective-permute-start | bytes 786440 | tf_op jit(solution)/shard_map/ppermute | solution.py:25
  32.9 15.6 %collective-permute-start.6 = (bf16[2,11,128]{2,0,1:T(2,128)(2,1)S(1)}, bf16[2,11,128]{2,0,1:T(2,128)(2,1)S(1)}, u32[]{:S(2)}, u32[]{:S(2)}) collective-permute-start(bf16[2,11,128]{2,0,1:T(2,128)(2,1)S(1)} %broadcast_select_fusion.27), channel_id=1, source_target_pairs={{0,8},{8,0},{1,9},{9,1},{2,10},{10,2},{3,11},{11,3},{4,12},{12,4},... | collective-permute-start | bytes 16904 | tf_op jit(solution)/shard_map/ppermute | solution.py:25
  48.7 18.4 %collective-permute-start.8 = (bf16[2,2,2,32,1024]{4,3,1,0,2:T(8,128)(2,1)S(1)}, bf16[2,2,2,32,1024]{4,3,1,0,2:T(8,128)(2,1)S(1)}, u32[]{:S(2)}, u32[]{:S(2)}) collective-permute-start(bf16[2,2,2,32,1024]{4,3,1,0,2:T(8,128)(2,1)S(1)} %get-tuple-element.449), channel_id=1, source_target_pairs={{0,2},{2,0},{1,3},{3,1},{4,6},{6,4},{5,7},{7,5},{8,10},{10,8},{9,1... | collective-permute-start | bytes 1572872 | tf_op jit(solution)/shard_map/ppermute | solution.py:25
  49.9 17.3 %collective-permute-start.7 = (bf16[2,2,2,32,1024]{4,3,1,0,2:T(8,128)(2,1)S(1)}, bf16[2,2,2,32,1024]{4,3,1,0,2:T(8,128)(2,1)S(1)}, u32[]{:S(2)}, u32[]{:S(2)}) collective-permute-start(bf16[2,2,2,32,1024]{4,3,1,0,2:T(8,128)(2,1)S(1)} %get-tuple-element.450), channel_id=1, source_target_pairs={{0,4},{4,0},{1,5},{5,1},{2,6},{6,2},{3,7},{7,3},{8,12},{12,8},{9,1... | collective-permute-start | bytes 1572872 | tf_op jit(solution)/shard_map/ppermute | solution.py:25
  51.3 55.0 %copy-start.73 = (pred[2]{0:T(512)(128)(4,1)}, pred[2]{0:T(512)(128)(4,1)S(1)}, u32[]{:S(2)}) copy-start(pred[2]{0:T(512)(128)(4,1)S(1)} %iota_compare_fusion.2) | copy-start | bytes 10
  51.3 15.9 %collective-permute-start.10 = (bf16[128,640]{1,0:T(8,128)(2,1)S(1)}, bf16[128,640]{1,0:T(8,128)(2,1)S(1)}, u32[]{:S(2)}, u32[]{:S(2)}) collective-permute-start(bf16[128,640]{1,0:T(8,128)(2,1)S(1)} %copy-done.42), channel_id=1, source_target_pairs={{0,16},{16,0},{1,17},{17,1},{2,18},{18,2},{3,19},{19,3},{4,20},{20... | collective-permute-start | bytes 491528 | tf_op jit(solution)/shard_map/ppermute | solution.py:25
  58.7 3.7 collective-permute-start.9
  58.8 8.3 %collective-permute-start.11 = (bf16[128,384]{1,0:T(8,128)(2,1)S(1)}, bf16[128,384]{1,0:T(8,128)(2,1)S(1)}, u32[]{:S(2)}, u32[]{:S(2)}) collective-permute-start(bf16[128,384]{1,0:T(8,128)(2,1)S(1)} %copy-done.47), channel_id=1, source_target_pairs={{0,16},{16,0},{1,17},{17,1},{2,18},{18,2},{3,19},{19,3},{4,20},{20... | collective-permute-start | bytes 294920 | tf_op jit(solution)/shard_map/ppermute | solution.py:25
  69.8 22.6 %collective-permute-start.15 = (bf16[2,2,2,2,32,1024]{5,4,2,1,0,3:T(8,128)(2,1)}, bf16[2,2,2,2,32,1024]{5,4,2,1,0,3:T(8,128)(2,1)S(1)}, u32[]{:S(2)}, u32[]{:S(2)}) collective-permute-start(bf16[2,2,2,2,32,1024]{5,4,2,1,0,3:T(8,128)(2,1)} %broadcast_select_fusion.10), channel_id=1, source_target_pairs={{0,4},{4,0},{1,5},{5,1},{2,6},{6,2},{3,7},{7,3},{8,12},{12,8},{9,1... | collective-permute-start | bytes 3145736 | tf_op jit(solution)/shard_map/ppermute | solution.py:25
  72.2 25.5 %collective-permute-start.14 = (bf16[2,2,2,2,32,1024]{5,4,2,1,0,3:T(8,128)(2,1)}, bf16[2,2,2,2,32,1024]{5,4,2,1,0,3:T(8,128)(2,1)}, u32[]{:S(2)}, u32[]{:S(2)}) collective-permute-start(bf16[2,2,2,2,32,1024]{5,4,2,1,0,3:T(8,128)(2,1)} %broadcast_select_fusion.11), channel_id=1, source_target_pairs={{0,2},{2,0},{1,3},{3,1},{4,6},{6,4},{5,7},{7,5},{8,10},{10,8},{9,1... | collective-permute-start | bytes 3145736 | tf_op jit(solution)/shard_map/ppermute | solution.py:25
  75.7 13.1 %collective-permute-start.12 = (bf16[2,128,640]{2,1,0:T(8,128)(2,1)}, bf16[2,128,640]{2,1,0:T(8,128)(2,1)}, u32[]{:S(2)}, u32[]{:S(2)}) collective-permute-start(bf16[2,128,640]{2,1,0:T(8,128)(2,1)} %broadcast_select_fusion.19), channel_id=1, source_target_pairs={{0,8},{8,0},{1,9},{9,1},{2,10},{10,2},{3,11},{11,3},{4,12},{12,4},... | collective-permute-start | bytes 983048 | tf_op jit(solution)/shard_map/ppermute | solution.py:25
  75.8 13.0 %collective-permute-start.13 = (bf16[2,128,384]{2,1,0:T(8,128)(2,1)S(1)}, bf16[2,128,384]{2,1,0:T(8,128)(2,1)S(1)}, u32[]{:S(2)}, u32[]{:S(2)}) collective-permute-start(bf16[2,128,384]{2,1,0:T(8,128)(2,1)S(1)} %broadcast_select_fusion.24), channel_id=1, source_target_pairs={{0,8},{8,0},{1,9},{9,1},{2,10},{10,2},{3,11},{11,3},{4,12},{12,4},... | collective-permute-start | bytes 589832 | tf_op jit(solution)/shard_map/ppermute | solution.py:25
  97.8 299.3 %reduce-scatter.3.cloned.1.call-start = ((), (), s32[]{:S(2)}) async-start(), calls=%async_computation.3 | async-start | bytes 8912896 | tf_op jit(solution)/shard_map/reduce_scatter | solution.py:1036
  108.2 39.8 %collective-permute-start.17 = (bf16[2,2,128,384]{3,2,1,0:T(8,128)(2,1)S(1)}, bf16[2,2,128,384]{3,2,1,0:T(8,128)(2,1)S(1)}, u32[]{:S(2)}, u32[]{:S(2)}) collective-permute-start(bf16[2,2,128,384]{3,2,1,0:T(8,128)(2,1)S(1)} %broadcast_select_fusion.18), channel_id=1, source_target_pairs={{0,2},{2,0},{1,3},{3,1},{4,6},{6,4},{5,7},{7,5},{8,10},{10,8},{9,1... | collective-permute-start | bytes 1179656 | tf_op jit(solution)/shard_map/ppermute | solution.py:25
  110.0 38.0 %collective-permute-start.16 = (bf16[2,2,128,640]{3,2,1,0:T(8,128)(2,1)S(1)}, bf16[2,2,128,640]{3,2,1,0:T(8,128)(2,1)S(1)}, u32[]{:S(2)}, u32[]{:S(2)}) collective-permute-start(bf16[2,2,128,640]{3,2,1,0:T(8,128)(2,1)S(1)} %broadcast_select_fusion.12), channel_id=1, source_target_pairs={{0,4},{4,0},{1,5},{5,1},{2,6},{6,2},{3,7},{7,3},{8,12},{12,8},{9,1... | collective-permute-start | bytes 1966088 | tf_op jit(solution)/shard_map/ppermute | solution.py:25
  110.3 10.5 %collective-permute-start.18 = (bf16[2,2,2,2,2,32,1024]{6,5,3,2,1,0,4:T(8,128)(2,1)S(1)}, bf16[2,2,2,2,2,32,1024]{6,5,3,2,1,0,4:T(8,128)(2,1)S(1)}, u32[]{:S(2)}, u32[]{:S(2)}) collective-permute-start(bf16[2,2,2,2,2,32,1024]{6,5,3,2,1,0,4:T(8,128)(2,1)S(1)} %broadcast_select_fusion.5), channel_id=1, source_target_pairs={{0,1},{1,0},{2,3},{3,2},{4,5},{5,4},{6,7},{7,6},{8,9},{9,8},{10,11... | collective-permute-start | bytes 6291464 | tf_op jit(solution)/shard_map/ppermute | solution.py:25
  110.3 10.5 %collective-permute-start.19 = (bf16[2,2,2,2,2,32,1024]{6,5,3,2,1,0,4:T(8,128)(2,1)S(1)}, bf16[2,2,2,2,2,32,1024]{6,5,3,2,1,0,4:T(8,128)(2,1)S(1)}, u32[]{:S(2)}, u32[]{:S(2)}) collective-permute-start(bf16[2,2,2,2,2,32,1024]{6,5,3,2,1,0,4:T(8,128)(2,1)S(1)} %broadcast_select_fusion.4), channel_id=1, source_target_pairs={{0,1},{1,0},{2,3},{3,2},{4,5},{5,4},{6,7},{7,6},{8,9},{9,8},{10,11... | collective-permute-start | bytes 6291464 | tf_op jit(solution)/shard_map/ppermute | solution.py:25
  150.3 31.3 %collective-permute-start.20 = (bf16[1024,640]{1,0:T(8,128)(2,1)}, bf16[1024,640]{1,0:T(8,128)(2,1)}, u32[]{:S(2)}, u32[]{:S(2)}) collective-permute-start(bf16[1024,640]{1,0:T(8,128)(2,1)} %bitcast.46.rest_0_), channel_id=1, source_target_pairs={{0,2},{2,0},{1,3},{3,1},{4,6},{6,4},{5,7},{7,5},{8,10},{10,8},{9,1... | collective-permute-start | bytes 3932168 | tf_op jit(solution)/shard_map/ppermute | solution.py:25
  152.5 20.7 %collective-permute-start.21 = (bf16[2,2,2,128,384]{4,3,1,0,2:T(8,128)(2,1)}, bf16[2,2,2,128,384]{4,3,1,0,2:T(8,128)(2,1)}, u32[]{:S(2)}, u32[]{:S(2)}) collective-permute-start(bf16[2,2,2,128,384]{4,3,1,0,2:T(8,128)(2,1)} %get-tuple-element.239), channel_id=1, source_target_pairs={{0,4},{4,0},{1,5},{5,1},{2,6},{6,2},{3,7},{7,3},{8,12},{12,8},{9,1... | collective-permute-start | bytes 2359304 | tf_op jit(solution)/shard_map/ppermute | solution.py:25
  183.0 20.1 %collective-permute-start.24 = (bf16[2,1024,384]{2,1,0:T(8,128)(2,1)S(1)}, bf16[2,1024,384]{2,1,0:T(8,128)(2,1)}, u32[]{:S(2)}, u32[]{:S(2)}) collective-permute-start(bf16[2,1024,384]{2,1,0:T(8,128)(2,1)S(1)} %bitcast.409), channel_id=1, source_target_pairs={{0,1},{1,0},{2,3},{3,2},{4,5},{5,4},{6,7},{7,6},{8,9},{9,8},{10,11... | collective-permute-start | bytes 4718600 | tf_op jit(solution)/shard_map/ppermute | solution.py:25
  183.9 19.2 %collective-permute-start.22 = (bf16[1024,640]{1,0:T(8,128)(2,1)}, bf16[1024,640]{1,0:T(8,128)(2,1)}, u32[]{:S(2)}, u32[]{:S(2)}) collective-permute-start(bf16[1024,640]{1,0:T(8,128)(2,1)} %bitcast.46.rest_0_), channel_id=1, source_target_pairs={{0,1},{1,0},{2,3},{3,2},{4,5},{5,4},{6,7},{7,6},{8,9},{9,8},{10,11... | collective-permute-start | bytes 3932168 | tf_op jit(solution)/shard_map/ppermute | solution.py:25
  184.4 18.7 %collective-permute-start.23 = (bf16[1024,640]{1,0:T(8,128)(2,1)}, bf16[1024,640]{1,0:T(8,128)(2,1)}, u32[]{:S(2)}, u32[]{:S(2)}) collective-permute-start(bf16[1024,640]{1,0:T(8,128)(2,1)} %collective-permute-done.20.rest_2_), channel_id=1, source_target_pairs={{0,1},{1,0},{2,3},{3,2},{4,5},{5,4},{6,7},{7,6},{8,9},{9,8},{10,11... | collective-permute-start | bytes 3932168 | tf_op jit(solution)/shard_map/ppermute | solution.py:25
  184.9 13.6 %collective-permute-start.25 = (f32[2,1,1024]{2,1,0:T(1,128)S(1)}, f32[2,1,1024]{2,1,0:T(1,128)S(1)}, u32[]{:S(2)}, u32[]{:S(2)}) collective-permute-start(f32[2,1,1024]{2,1,0:T(1,128)S(1)} %broadcast_in_dim.638), channel_id=1, source_target_pairs={{0,1},{1,2},{2,3},{4,5},{5,6},{6,7},{8,9},{9,10},{10,11},{12,13},{... | collective-permute-start | bytes 24584 | tf_op jit(solution)/shard_map/ppermute | solution.py:866
  253.2 231.6 %reduce-scatter.5.cloned.1.call-start = ((), (), s32[]{:S(2)}) async-start(), calls=%async_computation.4 | async-start | bytes 6684672 | tf_op jit(solution)/shard_map/reduce_scatter | solution.py:1079
  253.3 46.6 %copy-start.16 = (bf16[2,512,1024]{2,1,0:T(8,128)(2,1)S(1)}, bf16[2,512,1024]{2,1,0:T(8,128)(2,1)}, u32[]{:S(2)}) copy-start(bf16[2,512,1024]{2,1,0:T(8,128)(2,1)} %dynamic_update_slice.15) | copy-start | bytes 6291460
  310.8 15.5 %collective-permute-start.26 = (bf16[1024,1024]{1,0:T(8,128)(2,1)}, bf16[1024,1024]{1,0:T(8,128)(2,1)}, u32[]{:S(2)}, u32[]{:S(2)}) collective-permute-start(bf16[1024,1024]{1,0:T(8,128)(2,1)} %fusion.18), channel_id=1, source_target_pairs={{0,1},{1,0},{2,3},{3,2},{4,5},{5,4},{6,7},{7,6},{8,9},{9,8},{10,11... | collective-permute-start | bytes 6291464 | tf_op jit(solution)/shard_map/ppermute | solution.py:25
  311.0 15.4 %collective-permute-start.27 = (bf16[1024,1024]{1,0:T(8,128)(2,1)}, bf16[1024,1024]{1,0:T(8,128)(2,1)}, u32[]{:S(2)}, u32[]{:S(2)}) collective-permute-start(bf16[1024,1024]{1,0:T(8,128)(2,1)} %fusion.21), channel_id=1, source_target_pairs={{0,1},{1,0},{2,3},{3,2},{4,5},{5,4},{6,7},{7,6},{8,9},{9,8},{10,11... | collective-permute-start | bytes 6291464 | tf_op jit(solution)/shard_map/ppermute | solution.py:25
  311.4 27.3 %collective-permute-start.30 = (f32[2,1,1024]{2,1,0:T(1,128)S(1)}, f32[2,1,1024]{2,1,0:T(1,128)S(1)}, u32[]{:S(2)}, u32[]{:S(2)}) collective-permute-start(f32[2,1,1024]{2,1,0:T(1,128)S(1)} %get-tuple-element.437), channel_id=1, source_target_pairs={{1,0},{2,1},{3,2},{5,4},{6,5},{7,6},{9,8},{10,9},{11,10},{13,12},{... | collective-permute-start | bytes 24584 | tf_op jit(solution)/shard_map/ppermute | solution.py:866
  334.7 31.0 %collective-permute-start.28 = (bf16[2,2,2,128,512]{4,3,2,1,0:T(8,128)(2,1)}, bf16[2,2,2,128,512]{4,3,2,1,0:T(8,128)(2,1)S(1)}, u32[]{:S(2)}, u32[]{:S(2)}) collective-permute-start(bf16[2,2,2,128,512]{4,3,2,1,0:T(8,128)(2,1)} %pad_maximum_fusion.3), channel_id=1, source_target_pairs={{0,4},{4,0},{1,5},{5,1},{2,6},{6,2},{3,7},{7,3},{8,12},{12,8},{9,1... | collective-permute-start | bytes 3145736 | tf_op jit(solution)/shard_map/ppermute | solution.py:25
  336.3 29.4 %collective-permute-start.29 = (bf16[1024,512]{1,0:T(8,128)(2,1)}, bf16[1024,512]{1,0:T(8,128)(2,1)}, u32[]{:S(2)}, u32[]{:S(2)}) collective-permute-start(bf16[1024,512]{1,0:T(8,128)(2,1)} %get-tuple-element.278), channel_id=1, source_target_pairs={{0,2},{2,0},{1,3},{3,1},{4,6},{6,4},{5,7},{7,5},{8,10},{10,8},{9,1... | collective-permute-start | bytes 3145736 | tf_op jit(solution)/shard_map/ppermute | solution.py:25
  375.9 21.2 %collective-permute-start.31 = (bf16[2,2,128,512]{3,2,1,0:T(8,128)(2,1)S(1)}, bf16[2,2,128,512]{3,2,1,0:T(8,128)(2,1)}, u32[]{:S(2)}, u32[]{:S(2)}) collective-permute-start(bf16[2,2,128,512]{3,2,1,0:T(8,128)(2,1)S(1)} %dynamic-slice_bitcast_fusion.2), channel_id=1, source_target_pairs={{0,4},{4,0},{1,5},{5,1},{2,6},{6,2},{3,7},{7,3},{8,12},{12,8},{9,1... | collective-permute-start | bytes 1572872 | tf_op jit(solution)/shard_map/ppermute | solution.py:25
  376.3 20.8 %collective-permute-start.32 = (bf16[2,2,128,512]{3,2,1,0:T(8,128)(2,1)S(1)}, bf16[2,2,128,512]{3,2,1,0:T(8,128)(2,1)}, u32[]{:S(2)}, u32[]{:S(2)}) collective-permute-start(bf16[2,2,128,512]{3,2,1,0:T(8,128)(2,1)S(1)} %slice_bitcast_fusion.1), channel_id=1, source_target_pairs={{0,2},{2,0},{1,3},{3,1},{4,6},{6,4},{5,7},{7,5},{8,10},{10,8},{9,1... | collective-permute-start | bytes 1572872 | tf_op jit(solution)/shard_map/ppermute | solution.py:25
  409.0 16.1 %collective-permute-start.33 = (bf16[2,2,2,2,2,32,1024]{6,5,4,3,2,1,0:T(8,128)(2,1)}, bf16[2,2,2,2,2,32,1024]{6,5,4,3,2,1,0:T(8,128)(2,1)S(1)}, u32[]{:S(2)}, u32[]{:S(2)}) collective-permute-start(bf16[2,2,2,2,2,32,1024]{6,5,4,3,2,1,0:T(8,128)(2,1)} %pad_maximum_fusion.2), channel_id=1, source_target_pairs={{0,1},{1,0},{2,3},{3,2},{4,5},{5,4},{6,7},{7,6},{8,9},{9,8},{10,11... | collective-permute-start | bytes 6291464 | tf_op jit(solution)/shard_map/ppermute | solution.py:25
  410.5 14.7 %collective-permute-start.34 = (bf16[256,1024]{1,0:T(8,128)(2,1)}, bf16[256,1024]{1,0:T(8,128)(2,1)}, u32[]{:S(2)}, u32[]{:S(2)}) collective-permute-start(bf16[256,1024]{1,0:T(8,128)(2,1)} %reduce-scatter.3.cloned.1.call-done), channel_id=1, source_target_pairs={{0,2},{2,0},{1,3},{3,1},{4,6},{6,4},{5,7},{7,5},{8,10},{10,8},{9,1... | collective-permute-start | bytes 1572872 | tf_op jit(solution)/shard_map/ppermute | solution.py:25
  431.9 25.2 %collective-permute-start.35 = (bf16[2,2,2,2,32,1024]{5,4,3,2,1,0:T(8,128)(2,1)}, bf16[2,2,2,2,32,1024]{5,4,3,2,1,0:T(8,128)(2,1)}, u32[]{:S(2)}, u32[]{:S(2)}) collective-permute-start(bf16[2,2,2,2,32,1024]{5,4,3,2,1,0:T(8,128)(2,1)} %dynamic-slice_bitcast_fusion), channel_id=1, source_target_pairs={{0,2},{2,0},{1,3},{3,1},{4,6},{6,4},{5,7},{7,5},{8,10},{10,8},{9,1... | collective-permute-start | bytes 3145736 | tf_op jit(solution)/shard_map/ppermute | solution.py:25
  432.2 23.2 %collective-permute-start.36 = (bf16[2,2,128,512]{3,2,1,0:T(8,128)(2,1)}, bf16[2,2,128,512]{3,2,1,0:T(8,128)(2,1)}, u32[]{:S(2)}, u32[]{:S(2)}) collective-permute-start(bf16[2,2,128,512]{3,2,1,0:T(8,128)(2,1)} %pad_maximum_fusion.5), channel_id=1, source_target_pairs={{0,8},{8,0},{1,9},{9,1},{2,10},{10,2},{3,11},{11,3},{4,12},{12,4},... | collective-permute-start | bytes 1572872 | tf_op jit(solution)/shard_map/ppermute | solution.py:25
  432.2 23.2 %collective-permute-start.37 = (bf16[256,1024]{1,0:T(8,128)(2,1)S(1)}, bf16[256,1024]{1,0:T(8,128)(2,1)}, u32[]{:S(2)}, u32[]{:S(2)}) collective-permute-start(bf16[256,1024]{1,0:T(8,128)(2,1)S(1)} %add_convert_fusion.11), channel_id=1, source_target_pairs={{0,1},{1,0},{2,3},{3,2},{4,5},{5,4},{6,7},{7,6},{8,9},{9,8},{10,11... | collective-permute-start | bytes 1572872 | tf_op jit(solution)/shard_map/ppermute | solution.py:25
  461.6 3.1 collective-permute-start.39
  463.1 22.7 %collective-permute-start.43 = (bf16[2,128,512]{2,1,0:T(8,128)(2,1)}, bf16[2,128,512]{2,1,0:T(8,128)(2,1)S(1)}, u32[]{:S(2)}, u32[]{:S(2)}) collective-permute-start(bf16[2,128,512]{2,1,0:T(8,128)(2,1)} %dynamic-slice_bitcast_fusion.5), channel_id=1, source_target_pairs={{0,16},{16,0},{1,17},{17,1},{2,18},{18,2},{3,19},{19,3},{4,20},{20... | collective-permute-start | bytes 786440 | tf_op jit(solution)/shard_map/ppermute | solution.py:25
  464.3 14.7 %collective-permute-start.38 = (bf16[2,2,2,32,1024]{4,3,2,1,0:T(8,128)(2,1)S(1)}, bf16[2,2,2,32,1024]{4,3,2,1,0:T(8,128)(2,1)S(1)}, u32[]{:S(2)}, u32[]{:S(2)}) collective-permute-start(bf16[2,2,2,32,1024]{4,3,2,1,0:T(8,128)(2,1)S(1)} %dynamic-slice_bitcast_fusion.1), channel_id=1, source_target_pairs={{0,4},{4,0},{1,5},{5,1},{2,6},{6,2},{3,7},{7,3},{8,12},{12,8},{9,1... | collective-permute-start | bytes 1572872 | tf_op jit(solution)/shard_map/ppermute | solution.py:25
  479.2 11.9 %collective-permute-start.41 = (bf16[2,2,32,1024]{3,2,1,0:T(8,128)(2,1)S(1)}, bf16[2,2,32,1024]{3,2,1,0:T(8,128)(2,1)S(1)}, u32[]{:S(2)}, u32[]{:S(2)}) collective-permute-start(bf16[2,2,32,1024]{3,2,1,0:T(8,128)(2,1)S(1)} %dynamic-slice_bitcast_fusion.4), channel_id=1, source_target_pairs={{0,8},{8,0},{1,9},{9,1},{2,10},{10,2},{3,11},{11,3},{4,12},{12,4},... | collective-permute-start | bytes 786440 | tf_op jit(solution)/shard_map/ppermute | solution.py:25
  479.5 1.3 collective-permute-start.40
  480.8 5.0 collective-permute-start.42
  491.2 12.2 %collective-permute-start.47 = (bf16[2,128,512]{2,1,0:T(8,128)(2,1)S(1)}, bf16[2,128,512]{2,1,0:T(8,128)(2,1)S(1)}, u32[]{:S(2)}, u32[]{:S(2)}) collective-permute-start(bf16[2,128,512]{2,1,0:T(8,128)(2,1)S(1)} %fusion.35), channel_id=1, source_target_pairs={{0,2},{2,0},{1,3},{3,1},{4,6},{6,4},{5,7},{7,5},{8,10},{10,8},{9,1... | collective-permute-start | bytes 786440 | tf_op jit(solution)/shard_map/ppermute | solution.py:25
  492.5 15.4 %collective-permute-start.48 = (bf16[64,3072]{1,0:T(8,128)(2,1)}, bf16[64,3072]{1,0:T(8,128)(2,1)S(1)}, u32[]{:S(2)}, u32[]{:S(2)}) collective-permute-start(bf16[64,3072]{1,0:T(8,128)(2,1)} %reduce-scatter.5.cloned.1.call-done), channel_id=1, source_target_pairs={{0,2},{2,0},{1,3},{3,1},{4,6},{6,4},{5,7},{7,5},{8,10},{10,8},{9,1... | collective-permute-start | bytes 1179656 | tf_op jit(solution)/shard_map/ppermute | solution.py:25
  494.3 9.0 %collective-permute-start.45 = (bf16[2,32,1024]{2,1,0:T(8,128)(2,1)S(1)}, bf16[2,32,1024]{2,1,0:T(8,128)(2,1)S(1)}, u32[]{:S(2)}, u32[]{:S(2)}) collective-permute-start(bf16[2,32,1024]{2,1,0:T(8,128)(2,1)S(1)} %dynamic-slice_bitcast_fusion.6), channel_id=1, source_target_pairs={{0,16},{16,0},{1,17},{17,1},{2,18},{18,2},{3,19},{19,3},{4,20},{20... | collective-permute-start | bytes 393224 | tf_op jit(solution)/shard_map/ppermute | solution.py:25
  494.4 4.3 collective-permute-start.44
  498.8 4.6 collective-permute-start.46
  508.0 11.6 %collective-permute-start.50 = (bf16[2,2,128,512]{3,2,1,0:T(8,128)(2,1)S(1)}, bf16[2,2,128,512]{3,2,1,0:T(8,128)(2,1)S(1)}, u32[]{:S(2)}, u32[]{:S(2)}) collective-permute-start(bf16[2,2,128,512]{3,2,1,0:T(8,128)(2,1)S(1)} %broadcast_select_fusion.14), channel_id=1, source_target_pairs={{0,1},{1,0},{2,3},{3,2},{4,5},{5,4},{6,7},{7,6},{8,9},{9,8},{10,11... | collective-permute-start | bytes 1572872 | tf_op jit(solution)/shard_map/ppermute | solution.py:25
  508.2 11.4 %collective-permute-start.54 = (bf16[64,3072]{1,0:T(8,128)(2,1)S(1)}, bf16[64,3072]{1,0:T(8,128)(2,1)S(1)}, u32[]{:S(2)}, u32[]{:S(2)}) collective-permute-start(bf16[64,3072]{1,0:T(8,128)(2,1)S(1)} %add_convert_fusion.12), channel_id=1, source_target_pairs={{0,1},{1,0},{2,3},{3,2},{4,5},{5,4},{6,7},{7,6},{8,9},{9,8},{10,11... | collective-permute-start | bytes 1179656 | tf_op jit(solution)/shard_map/ppermute | solution.py:25
  508.8 5.6 %collective-permute-start.49 = (f32[12,1024]{1,0:T(8,128)S(1)}, f32[12,1024]{1,0:T(8,128)S(1)}, u32[]{:S(2)}, u32[]{:S(2)}) collective-permute-start(f32[12,1024]{1,0:T(8,128)S(1)} %add.349), channel_id=1, source_target_pairs={{0,16},{16,0},{1,17},{17,1},{2,18},{18,2},{3,19},{19,3},{4,20},{20... | collective-permute-start | bytes 147464 | tf_op jit(solution)/shard_map/ppermute | solution.py:25
  508.9 8.3 %collective-permute-start.53 = (bf16[2,32,1024]{2,1,0:T(8,128)(2,1)S(1)}, bf16[2,32,1024]{2,1,0:T(8,128)(2,1)S(1)}, u32[]{:S(2)}, u32[]{:S(2)}) collective-permute-start(bf16[2,32,1024]{2,1,0:T(8,128)(2,1)S(1)} %fusion.37), channel_id=1, source_target_pairs={{0,3},{1,2},{2,1},{3,0},{4,7},{5,6},{6,5},{7,4},{8,11},{9,10},{10,... | collective-permute-start | bytes 393224 | tf_op jit(solution)/shard_map/ppermute | solution.py:1171
  509.8 7.4 %collective-permute-start.52 = (bf16[2,32,1024]{2,1,0:T(8,128)(2,1)S(1)}, bf16[2,32,1024]{2,1,0:T(8,128)(2,1)S(1)}, u32[]{:S(2)}, u32[]{:S(2)}) collective-permute-start(bf16[2,32,1024]{2,1,0:T(8,128)(2,1)S(1)} %fusion.37), channel_id=1, source_target_pairs={{0,1},{1,0},{2,3},{3,2},{4,5},{5,4},{6,7},{7,6},{8,9},{9,8},{10,11... | collective-permute-start | bytes 393224 | tf_op jit(solution)/shard_map/ppermute | solution.py:25
  514.4 5.2 collective-permute-start.51
  (98 other events, 861.1 us)
Sparse Core Ops, SparseCore 0:
  10.8 46.9 all-gather.9
  97.9 78.2 all-gather.7
  253.3 107.1 reduce-scatter.2
  381.6 103.2 reduce-scatter.4
